TPU v7x, 32 devices: a whole 2x2x4 slice. The times are simulated.
32 devices in a mesh: dp: 32 (over z, y, x, core).
Axes of the slice: x: 2, y: 2, z: 4, core: 2. Of those that a mesh axis runs over, the one named last changes fastest.
Arguments:
- tokens: bfloat16 [5120, 2048], P('dp'), may hold values from -6 to 6
- cotangent: bfloat16 [5120, 2048], P('dp'), may hold values from -6 to 6
- seq_lengths: int32 [5], replicated, may hold values from 1 to 2048, 5120 in all
- block_deal: int32 [32], replicated, may hold values from 0 to 31, each once
- in_proj: float32 [2048, 2048], P('dp'), may hold values from -0.125 to 0.125
- forget_proj: float32 [1024, 2048], P('dp'), may hold values from -0.125 to 0.125
- gate_proj: float32 [2048, 2048], P('dp'), may hold values from -0.125 to 0.125
- out_proj: float32 [2048, 2048], P('dp'), may hold values from -0.125 to 0.125
- ffn_gate: float32 [5632, 2048], P('dp'), may hold values from -0.125 to 0.125
- ffn_up: float32 [5632, 2048], P('dp'), may hold values from -0.125 to 0.125
- ffn_down: float32 [5632, 2048], P('dp'), may hold values from -0.078125 to 0.078125
- gain_mix: float32 [2048], P('dp'), may hold values from 0.5 to 1.5
- gain_out: float32 [2048], P('dp'), may hold values from 0.5 to 1.5
- gain_ffn: float32 [2048], P('dp'), may hold values from 0.5 to 1.5
- lower_bound: float32 [1024], P('dp'), may hold values from 0.95 to 0.9999
- rotation: float32 [1024], P('dp'), may hold values from -3.140625 to 3.140625
Outputs:
- mixed_out: bfloat16 [5120, 2048], P('dp')
- tokens_grad: bfloat16 [5120, 2048], P('dp')
- in_proj_grad: float32 [2048, 2048], P('dp')
- forget_proj_grad: float32 [1024, 2048], P('dp')
- gate_proj_grad: float32 [2048, 2048], P('dp')
- out_proj_grad: float32 [2048, 2048], P('dp')
- ffn_gate_grad: float32 [5632, 2048], P('dp')
- ffn_up_grad: float32 [5632, 2048], P('dp')
- ffn_down_grad: float32 [5632, 2048], P('dp')
- gain_mix_grad: float32 [2048], P('dp')
- gain_out_grad: float32 [2048], P('dp')
- gain_ffn_grad: float32 [2048], P('dp')
- lower_bound_grad: float32 [1024], P('dp')
- rotation_grad: float32 [1024], P('dp')
Inputs may be any that keep to these rules, and one draw needn't show every extreme that they name: `seq_lengths`: the lengths sum to 5120; the longest is exactly 2048. `block_deal`: every block of the stream is held by exactly one device.
All inputs are finite; a program needn't handle non-finite values.
Results may differ from a plain program's by a relative error of at most 0.011.
Values may be sent and summed in bfloat16 or wider, within the bound.
A program may use at most 448 MiB of HBM per device.

v0:
```python
from functools import partial

import jax
import jax.numpy as jnp
from jax import lax
from jax.sharding import PartitionSpec as P

EPS = 1e-06


def rms_scale(tensor, gain_vec):
    return tensor * lax.rsqrt(jnp.mean(tensor * tensor, axis=-1, keepdims=True) + EPS) * gain_vec


def contract(left_rows, right_rows):
    return lax.dot_general(
        left_rows, right_rows, (((1,), (1,)), ((), ())), preferred_element_type=jnp.float32
    )


def outer_rows(left_rows, right_rows):
    return lax.dot_general(
        left_rows, right_rows, (((0,), (0,)), ((), ())), preferred_element_type=jnp.float32
    )


def compose(earlier_map, later_map):
    early_re, early_im, shift_re, shift_im = earlier_map
    late_re, late_im, added_re, added_im = later_map
    return (
        late_re * early_re - late_im * early_im,
        late_re * early_im + late_im * early_re,
        late_re * shift_re - late_im * shift_im + added_re,
        late_re * shift_im + late_im * shift_re + added_im,
    )


def gate_terms(keep_mask, in_out, forget_out, lower_full, angle_full):
    half_width = forget_out.shape[1]
    magnitude = lower_full + (1.0 - lower_full) * jax.nn.sigmoid(forget_out)
    decay_re = keep_mask * magnitude * jnp.cos(angle_full)
    decay_im = keep_mask * magnitude * jnp.sin(angle_full)
    drive_re = jax.nn.silu(in_out[:, :half_width]) * (1.0 - magnitude)
    drive_im = jax.nn.silu(in_out[:, half_width:]) * (1.0 - magnitude)
    return (decay_re, decay_im, drive_re, drive_im)


def output_norm(state, gate_out, gain_vec):
    return rms_scale(state, gain_vec) * jax.nn.silu(gate_out)


def glu_unit(gate_value, up_value):
    return jax.nn.silu(gate_value) * up_value


def chain_carry(summary, block_order, block_place, reverse):
    ordered = tuple((jnp.take(member, block_order, axis=0) for member in summary))
    prefix = lax.associative_scan(compose, ordered, reverse=reverse, axis=0)
    dev_count = block_order.shape[0]
    if reverse:
        neighbor = block_place + 1
        is_valid = neighbor < dev_count
    else:
        neighbor = block_place - 1
        is_valid = neighbor >= 0
    safe_index = jnp.clip(neighbor, 0, dev_count - 1)
    carry_re = jnp.where(is_valid, prefix[2][safe_index], 0.0)[None, :]
    carry_im = jnp.where(is_valid, prefix[3][safe_index], 0.0)[None, :]
    return (carry_re, carry_im)


def weight_term(left_grads, right_values):
    return outer_rows(left_grads, right_values)


def scatter_ffn(left_grads, right_values):
    return lax.psum_scatter(
        weight_term(left_grads, right_values), "dp", scatter_dimension=0, tiled=True
    )


def scatter_mix(left_grads, right_values):
    return lax.psum_scatter(
        weight_term(left_grads, right_values), "dp", scatter_dimension=0, tiled=True
    )


def local(
    tokens,
    cotangent,
    seq_lengths,
    block_deal,
    in_proj,
    forget_proj,
    gate_proj,
    out_proj,
    ffn_gate,
    ffn_up,
    ffn_down,
    gain_mix,
    gain_out,
    gain_ffn,
    lower_bound,
    rotation,
):
    dev_count = lax.axis_size("dp")
    block_place = block_deal[lax.axis_index("dp")]
    row_count = tokens.shape[0]
    model_width = tokens.shape[1]
    half_width = model_width // 2
    indices = jnp.arange(dev_count, dtype=jnp.int32)
    block_order = jnp.sum(
        jnp.where(block_deal[None, :] == indices[:, None], indices[None, :], 0), axis=1
    )
    offsets = jnp.cumsum(seq_lengths) - seq_lengths
    positions = block_place * row_count + jnp.arange(row_count, dtype=jnp.int32)
    starts = jnp.any(positions[:, None] == offsets[None, :], axis=1)
    keep_mask = jnp.where(starts, 0.0, 1.0).astype(jnp.float32)[:, None]
    mix_gain, norm_gain, ffn_gain, lower_full, angle_full = (
        lax.all_gather(gain_mix, "dp", axis=0, tiled=True),
        lax.all_gather(gain_out, "dp", axis=0, tiled=True),
        lax.all_gather(gain_ffn, "dp", axis=0, tiled=True),
        lax.all_gather(lower_bound, "dp", axis=0, tiled=True),
        lax.all_gather(rotation, "dp", axis=0, tiled=True),
    )
    inputs = tokens.astype(jnp.float32)
    normed_low = rms_scale(inputs, mix_gain).astype(jnp.bfloat16)
    mix_full = (
        lax.all_gather(in_proj.astype(jnp.bfloat16), "dp", axis=0, tiled=True),
        lax.all_gather(forget_proj.astype(jnp.bfloat16), "dp", axis=0, tiled=True),
        lax.all_gather(gate_proj.astype(jnp.bfloat16), "dp", axis=0, tiled=True),
    )
    in_out = contract(normed_low, mix_full[0])
    forget_out = contract(normed_low, mix_full[1])
    gate_out = contract(normed_low, mix_full[2])
    decay_re, decay_im, drive_re, drive_im = gate_terms(
        keep_mask, in_out, forget_out, lower_full, angle_full
    )
    local_scan = lax.associative_scan(compose, (decay_re, decay_im, drive_re, drive_im), axis=0)
    summary = (
        lax.all_gather(local_scan[0][row_count - 1 :], "dp", axis=0, tiled=True),
        lax.all_gather(local_scan[1][row_count - 1 :], "dp", axis=0, tiled=True),
        lax.all_gather(local_scan[2][row_count - 1 :], "dp", axis=0, tiled=True),
        lax.all_gather(local_scan[3][row_count - 1 :], "dp", axis=0, tiled=True),
    )
    start_re, start_im = chain_carry(summary, block_order, block_place, False)
    state_re = local_scan[0] * start_re - local_scan[1] * start_im + local_scan[2]
    state_im = local_scan[0] * start_im + local_scan[1] * start_re + local_scan[3]
    state = jnp.concatenate([state_re, state_im], axis=1)
    mid_low = output_norm(state, gate_out, norm_gain).astype(jnp.bfloat16)
    out_full = lax.all_gather(out_proj.astype(jnp.bfloat16), "dp", axis=0, tiled=True)
    residual = inputs + contract(mid_low, out_full)
    ffn_low = rms_scale(residual, ffn_gain).astype(jnp.bfloat16)
    ffn_full = (
        lax.all_gather(ffn_gate.astype(jnp.bfloat16), "dp", axis=0, tiled=True),
        lax.all_gather(ffn_up.astype(jnp.bfloat16), "dp", axis=0, tiled=True),
        lax.all_gather(ffn_down.astype(jnp.bfloat16), "dp", axis=0, tiled=True),
    )
    gate_value = contract(ffn_low, ffn_full[0])
    up_value = contract(ffn_low, ffn_full[1])
    hidden_low = glu_unit(gate_value, up_value).astype(jnp.bfloat16)
    mixed_out = (
        residual + jnp.dot(hidden_low, ffn_full[2], preferred_element_type=jnp.float32)
    ).astype(jnp.bfloat16)
    grad_output = cotangent.astype(jnp.float32)
    ffn_again = (
        lax.all_gather(ffn_gate.astype(jnp.bfloat16), "dp", axis=0, tiled=True),
        lax.all_gather(ffn_up.astype(jnp.bfloat16), "dp", axis=0, tiled=True),
        lax.all_gather(ffn_down.astype(jnp.bfloat16), "dp", axis=0, tiled=True),
    )
    grad_hidden = contract(cotangent, ffn_again[2])
    _, glu_pull = jax.vjp(glu_unit, gate_value, up_value)
    grad_gate, grad_up = glu_pull(grad_hidden)
    gate_grad_low = grad_gate.astype(jnp.bfloat16)
    up_grad_low = grad_up.astype(jnp.bfloat16)
    grad_ffn_in = jnp.dot(
        gate_grad_low, ffn_again[0], preferred_element_type=jnp.float32
    ) + jnp.dot(up_grad_low, ffn_again[1], preferred_element_type=jnp.float32)
    _, ffn_norm_pull = jax.vjp(rms_scale, residual, ffn_gain)
    residual_part, grad_ffn_gain = ffn_norm_pull(grad_ffn_in)
    grad_residual = grad_output + residual_part
    ffn_results = []
    for left_grads, right_values in (
        (gate_grad_low, ffn_low),
        (up_grad_low, ffn_low),
        (hidden_low, cotangent),
    ):
        column_parts = []
        for column_half in range(2):
            right_part = right_values[:, column_half * half_width : (column_half + 1) * half_width]
            column_parts.append(scatter_ffn(left_grads, right_part))
        ffn_results.append(jnp.concatenate(column_parts, axis=1))
    branch_low = grad_residual.astype(jnp.bfloat16)
    out_again = lax.all_gather(out_proj.astype(jnp.bfloat16), "dp", axis=0, tiled=True)
    grad_mid = jnp.dot(branch_low, out_again, preferred_element_type=jnp.float32)
    _, mid_pull = jax.vjp(output_norm, state, gate_out, norm_gain)
    grad_state, grad_gate_out, grad_norm_gain = mid_pull(grad_mid)
    ahead_re = jnp.concatenate([decay_re[1:], jnp.ones((1, half_width), jnp.float32)], axis=0)
    ahead_im = jnp.concatenate([-decay_im[1:], jnp.zeros((1, half_width), jnp.float32)], axis=0)
    back_scan = lax.associative_scan(
        compose,
        (ahead_re, ahead_im, grad_state[:, :half_width], grad_state[:, half_width:]),
        reverse=True,
        axis=0,
    )
    first_re = decay_re[:1]
    first_im = -decay_im[:1]
    send_scale_re = first_re * back_scan[0][:1] - first_im * back_scan[1][:1]
    send_scale_im = first_re * back_scan[1][:1] + first_im * back_scan[0][:1]
    send_shift_re = first_re * back_scan[2][:1] - first_im * back_scan[3][:1]
    send_shift_im = first_re * back_scan[3][:1] + first_im * back_scan[2][:1]
    back_summary = (
        lax.all_gather(send_scale_re, "dp", axis=0, tiled=True),
        lax.all_gather(send_scale_im, "dp", axis=0, tiled=True),
        lax.all_gather(send_shift_re, "dp", axis=0, tiled=True),
        lax.all_gather(send_shift_im, "dp", axis=0, tiled=True),
    )
    later_re, later_im = chain_carry(back_summary, block_order, block_place, True)
    adjoint_re = back_scan[0] * later_re - back_scan[1] * later_im + back_scan[2]
    adjoint_im = back_scan[0] * later_im + back_scan[1] * later_re + back_scan[3]
    before_re = jnp.concatenate([start_re, state_re[:-1]], axis=0)
    before_im = jnp.concatenate([start_im, state_im[:-1]], axis=0)
    grad_decay_re = adjoint_re * before_re + adjoint_im * before_im
    grad_decay_im = adjoint_im * before_re - adjoint_re * before_im
    _, gate_pull = jax.vjp(
        partial(gate_terms, keep_mask), in_out, forget_out, lower_full, angle_full
    )
    grad_in_out, grad_forget_out, grad_lower, grad_angle = gate_pull(
        (grad_decay_re, grad_decay_im, adjoint_re, adjoint_im)
    )
    in_grad_low = grad_in_out.astype(jnp.bfloat16)
    forget_grad_low = grad_forget_out.astype(jnp.bfloat16)
    gate_out_low = grad_gate_out.astype(jnp.bfloat16)
    mix_again = (
        lax.all_gather(in_proj.astype(jnp.bfloat16), "dp", axis=0, tiled=True),
        lax.all_gather(forget_proj.astype(jnp.bfloat16), "dp", axis=0, tiled=True),
        lax.all_gather(gate_proj.astype(jnp.bfloat16), "dp", axis=0, tiled=True),
    )
    grad_normed = jnp.dot(in_grad_low, mix_again[0], preferred_element_type=jnp.float32)
    grad_normed = grad_normed + jnp.dot(
        forget_grad_low, mix_again[1], preferred_element_type=jnp.float32
    )
    grad_normed = grad_normed + jnp.dot(
        gate_out_low, mix_again[2], preferred_element_type=jnp.float32
    )
    _, mix_norm_pull = jax.vjp(rms_scale, inputs, mix_gain)
    input_part, grad_mix_gain = mix_norm_pull(grad_normed)
    tokens_grad = (grad_residual + input_part).astype(jnp.bfloat16)
    mix_results = []
    for left_grads, right_values, weight_rows in (
        (in_grad_low, normed_low, in_proj.shape[0]),
        (forget_grad_low, normed_low, forget_proj.shape[0]),
        (gate_out_low, normed_low, gate_proj.shape[0]),
        (branch_low, mid_low, out_proj.shape[0]),
    ):
        mix_results.append(scatter_mix(left_grads, right_values))
    vector_grads = (
        lax.psum_scatter(grad_mix_gain, "dp", scatter_dimension=0, tiled=True),
        lax.psum_scatter(grad_norm_gain, "dp", scatter_dimension=0, tiled=True),
        lax.psum_scatter(grad_ffn_gain, "dp", scatter_dimension=0, tiled=True),
        lax.psum_scatter(grad_lower, "dp", scatter_dimension=0, tiled=True),
        lax.psum_scatter(grad_angle, "dp", scatter_dimension=0, tiled=True),
    )
    return (
        mixed_out,
        tokens_grad,
        mix_results[0],
        mix_results[1],
        mix_results[2],
        mix_results[3],
        ffn_results[0],
        ffn_results[1],
        ffn_results[2],
        vector_grads[0],
        vector_grads[1],
        vector_grads[2],
        vector_grads[3],
        vector_grads[4],
    )


def solution(mesh):
    in_specs = (
        P("dp", None),
        P("dp", None),
        P(),
        P(),
        P("dp", None),
        P("dp", None),
        P("dp", None),
        P("dp", None),
        P("dp", None),
        P("dp", None),
        P("dp", None),
        P("dp"),
        P("dp"),
        P("dp"),
        P("dp"),
        P("dp"),
    )
    out_specs = (
        P("dp", None),
        P("dp", None),
        P("dp", None),
        P("dp", None),
        P("dp", None),
        P("dp", None),
        P("dp", None),
        P("dp", None),
        P("dp", None),
        P("dp"),
        P("dp"),
        P("dp"),
        P("dp"),
        P("dp"),
    )
    return jax.shard_map(local, mesh=mesh, in_specs=in_specs, out_specs=out_specs, check_vma=False)
```

profile of v0, /device:TPU:1, one launch (start us, length us, event | category | flops | bytes accessed | tf_op | source)
XLA Modules:
  0.0 3020.9 jit_solution(8894861106596157147)
XLA Ops:
  19.7 41.7 %all-reduce.169 = (f32[2048]{0:T(1024)}, f32[2048]{0:T(1024)S(1)}, f32[1024]{0:T(1024)S(1)}, f32[1024]{0:T(1024)S(1)}, f32[2048]{0:T(1024)S(1)}) all-reduce(f32[2048]{0:T(1024)S(1)} %dynamic-update-slice.3, f32[2048]{0:T(1024)S(1)} %dynamic-update-slice.1, f32[1024]{0:T(1024)S(1)} %dynamic-update-slice, ...), channel_id=1, replica_groups=mesh['dp'=32] {'dp'}, use_global_device_ids=true, to_apply=%add.161 | all-reduce | flops 8192 | bytes 65536
  63.1 28.3 all-gather.18.cloned.1.call-done
  97.8 57.8 %all-gather.16.cloned.1.call-done = bf16[1024,2048]{1,0:T(8,128)(2,1)} async-done(((bf16[32,2048]{1,0:T(8,128)(2,1)}), bf16[1024,2048]{1,0:T(8,128)(2,1)}) %all-gather.16.cloned.1.call-update) | async-done | bytes 4194320 | tf_op jit(solution)/shard_map/all_gather | solution.py:130
  322.8 40.3 %all-gather = f32[32,1,1024]{2,1,0:T(1,128)S(1)} all-gather(f32[1,1,1024]{2,1,0:T(1,128)S(1)} %add_bitcast_fusion.3), channel_id=1, replica_groups=mesh['dp'=32] {'dp'}, dimensions={0}, use_global_device_ids=true | all-gather | bytes 135168 | tf_op jit(solution)/shard_map/all_gather | solution.py:143
  369.5 37.6 %all-gather.3 = f32[32,1,1024]{2,1,0:T(1,128)S(1)} all-gather(f32[1,1,1024]{2,1,0:T(1,128)S(1)} %add_bitcast_fusion), channel_id=1, replica_groups=mesh['dp'=32] {'dp'}, dimensions={0}, use_global_device_ids=true | all-gather | bytes 135168 | tf_op jit(solution)/shard_map/all_gather | solution.py:144
  525.3 39.8 %all-gather.1 = f32[32,1,1024]{2,1,0:T(1,128)S(1)} all-gather(f32[1,1,1024]{2,1,0:T(1,128)S(1)} %add_bitcast_fusion.2), channel_id=1, replica_groups=mesh['dp'=32] {'dp'}, dimensions={0}, use_global_device_ids=true | all-gather | bytes 135168 | tf_op jit(solution)/shard_map/all_gather | solution.py:141
  566.8 38.2 %all-gather.2 = f32[32,1,1024]{2,1,0:T(1,128)S(1)} all-gather(f32[1,1,1024]{2,1,0:T(1,128)S(1)} %add_bitcast_fusion.1), channel_id=1, replica_groups=mesh['dp'=32] {'dp'}, dimensions={0}, use_global_device_ids=true | all-gather | bytes 135168 | tf_op jit(solution)/shard_map/all_gather | solution.py:142
  627.2 14.3 fusion.78
  641.5 14.8 fusion.77
  656.3 97.7 %all-gather.28.cloned.1.call-done = bf16[5632,2048]{1,0:T(8,128)(2,1)} async-done(((bf16[176,2048]{1,0:T(8,128)(2,1)}), bf16[5632,2048]{1,0:T(8,128)(2,1)}) %all-gather.28.cloned.1.call-update) | async-done | bytes 23068688 | tf_op jit(solution)/shard_map/all_gather | solution.py:157
  754.0 15.7 multiply_convert_fusion
  769.7 11.0 fusion.42
  780.7 11.4 fusion.46
  792.2 11.0 fusion.44
  803.3 11.2 fusion.48
  814.5 11.1 fusion.32
  825.8 11.4 fusion.34
  854.8 39.7 %all-gather.5 = f32[32,1,1024]{2,1,0:T(1,128)S(1)} all-gather(f32[1,1,1024]{2,1,0:T(1,128)S(1)} %copy-done.153), channel_id=1, replica_groups=mesh['dp'=32] {'dp'}, dimensions={0}, use_global_device_ids=true | all-gather | bytes 135168 | tf_op jit(solution)/shard_map/all_gather | solution.py:213
  895.9 37.9 %all-gather.6 = f32[32,1,1024]{2,1,0:T(1,128)S(1)} all-gather(f32[1,1,1024]{2,1,0:T(1,128)S(1)} %copy-done.152), channel_id=1, replica_groups=mesh['dp'=32] {'dp'}, dimensions={0}, use_global_device_ids=true | all-gather | bytes 135168 | tf_op jit(solution)/shard_map/all_gather | solution.py:214
  946.0 10.8 multiply_reduce_fusion
  1076.9 38.9 %all-gather.4 = f32[32,1,1024]{2,1,0:T(1,128)S(1)} all-gather(f32[1,1,1024]{2,1,0:T(1,128)S(1)} %get-tuple-element.49), channel_id=1, replica_groups=mesh['dp'=32] {'dp'}, dimensions={0}, use_global_device_ids=true | all-gather | bytes 135168 | tf_op jit(solution)/shard_map/all_gather | solution.py:216
  1116.7 37.9 %all-gather.7 = f32[32,1,1024]{2,1,0:T(1,128)S(1)} all-gather(f32[1,1,1024]{2,1,0:T(1,128)S(1)} %get-tuple-element.50), channel_id=1, replica_groups=mesh['dp'=32] {'dp'}, dimensions={0}, use_global_device_ids=true | all-gather | bytes 135168 | tf_op jit(solution)/shard_map/all_gather | solution.py:215
  1271.9 44.6 %all-reduce.168 = (f32[2048]{0:T(1024)S(1)}, f32[2048]{0:T(1024)S(1)}, f32[2048]{0:T(1024)S(1)}, f32[1024]{0:T(1024)S(1)}, f32[1024]{0:T(1024)S(1)}) all-reduce(f32[2048]{0:T(1024)S(1)} %get-tuple-element.21, f32[2048]{0:T(1024)S(1)} %copy-done.185, f32[2048]{0:T(1024)S(1)} %copy-done.149, ...), channel_id=12, replica_groups=mesh['dp'=32] {'dp'}, use_global_device_ids=true, to_apply=%region_20.22.clone | all-reduce | flops 8192 | bytes 65536
  1322.1 10.8 fusion.5
  1335.5 205.5 %reduce-scatter.21.cloned.1.call-done = f32[176,1024]{1,0:T(8,128)} async-done(((f32[5632,1024]{1,0:T(8,128)}), f32[176,1024]{1,0:T(8,128)}) %reduce-scatter.21.cloned.1.call-update) | async-done | bytes 720912 | tf_op jit(solution)/shard_map/reduce_scatter | solution.py:77
  1541.1 255.1 %reduce-scatter.19.cloned.1.call-done = f32[176,1024]{1,0:T(8,128)} async-done(((f32[5632,1024]{1,0:T(8,128)}), f32[176,1024]{1,0:T(8,128)}) %reduce-scatter.19.cloned.1.call-update) | async-done | bytes 720912 | tf_op jit(solution)/shard_map/reduce_scatter | solution.py:77
  1798.7 251.0 %reduce-scatter.29.cloned.1.call-done = f32[176,1024]{1,0:T(8,128)} async-done(((f32[5632,1024]{1,0:T(8,128)}), f32[176,1024]{1,0:T(8,128)}) %reduce-scatter.29.cloned.1.call-update) | async-done | bytes 720912 | tf_op jit(solution)/shard_map/reduce_scatter | solution.py:77
  2049.7 253.7 %reduce-scatter.27.cloned.1.call-done = f32[176,1024]{1,0:T(8,128)} async-done(((f32[5632,1024]{1,0:T(8,128)}), f32[176,1024]{1,0:T(8,128)}) %reduce-scatter.27.cloned.1.call-update) | async-done | bytes 720912 | tf_op jit(solution)/shard_map/reduce_scatter | solution.py:77
  2306.0 146.0 %reduce-scatter.13.cloned.1.call-done = f32[32,2048]{1,0:T(8,128)} async-done(((f32[1024,2048]{1,0:T(8,128)}), f32[32,2048]{1,0:T(8,128)}) %reduce-scatter.13.cloned.1.call-update) | async-done | bytes 262160 | tf_op jit(solution)/shard_map/reduce_scatter | solution.py:83
  2452.0 187.4 %reduce-scatter.17.cloned.1.call-done = f32[64,2048]{1,0:T(8,128)} async-done(((f32[2048,2048]{1,0:T(8,128)}), f32[64,2048]{1,0:T(8,128)}) %reduce-scatter.17.cloned.1.call-update) | async-done | bytes 524304 | tf_op jit(solution)/shard_map/reduce_scatter | solution.py:83
  2639.4 187.2 %reduce-scatter.11.cloned.1.call-done = f32[64,2048]{1,0:T(8,128)} async-done(((f32[2048,2048]{1,0:T(8,128)}), f32[64,2048]{1,0:T(8,128)}) %reduce-scatter.11.cloned.1.call-update) | async-done | bytes 524304 | tf_op jit(solution)/shard_map/reduce_scatter | solution.py:83
  2826.7 187.2 %reduce-scatter.15.cloned.1.call-done = f32[64,2048]{1,0:T(8,128)} async-done(((f32[2048,2048]{1,0:T(8,128)}), f32[64,2048]{1,0:T(8,128)}) %reduce-scatter.15.cloned.1.call-update) | async-done | bytes 524304 | tf_op jit(solution)/shard_map/reduce_scatter | solution.py:83
  (1175 shorter events, 613.6 us)
Async XLA Ops:
  7.2 84.3 %all-gather.18.cloned.1.call-start = ((), (), s32[]{:S(2)}) async-start(), calls=%async_computation.11 | async-start | bytes 8650752 | tf_op jit(solution)/shard_map/all_gather | solution.py:129
  9.1 146.4 %all-gather.16.cloned.1.call-start = ((), (), s32[]{:S(2)}) async-start(), calls=%async_computation.10 | async-start | bytes 4325376 | tf_op jit(solution)/shard_map/all_gather | solution.py:130
  10.9 601.2 %all-gather.20.cloned.1.call-start = ((), (), s32[]{:S(2)}) async-start(), calls=%async_computation.12 | async-start | bytes 8650752 | tf_op jit(solution)/shard_map/all_gather | solution.py:131
  11.8 608.6 %all-gather.22.cloned.1.call-start = ((), (), s32[]{:S(2)}) async-start(), calls=%async_computation.13 | async-start | bytes 8650752 | tf_op jit(solution)/shard_map/all_gather | solution.py:151
  12.6 614.6 %all-gather.26.cloned.1.call-start = ((), (), s32[]{:S(2)}) async-start(), calls=%async_computation.15 | async-start | bytes 23789568 | tf_op jit(solution)/shard_map/all_gather | solution.py:156
  13.7 627.8 %all-gather.24.cloned.1.call-start = ((), (), s32[]{:S(2)}) async-start(), calls=%async_computation.14 | async-start | bytes 23789568 | tf_op jit(solution)/shard_map/all_gather | solution.py:155
  15.3 738.7 %all-gather.28.cloned.1.call-start = ((), (), s32[]{:S(2)}) async-start(), calls=%async_computation.16 | async-start | bytes 23789568 | tf_op jit(solution)/shard_map/all_gather | solution.py:157
  16.3 1316.6 %reduce-scatter.25.cloned.1.call-start = ((), (), s32[]{:S(2)}) async-start(), calls=%async_computation.24 | async-start | bytes 23789568 | tf_op jit(solution)/shard_map/reduce_scatter | solution.py:77
  61.5 94.1 %copy-start.145 = (f32[1024]{0:T(1024)}, f32[1024]{0:T(1024)S(1)}, u32[]{:S(2)}) copy-start(f32[1024]{0:T(1024)S(1)} %get-tuple-element.32) | copy-start | bytes 12292
  61.5 551.3 %copy-start.108 = (f32[2048]{0:T(1024)}, f32[2048]{0:T(1024)S(1)}, u32[]{:S(2)}) copy-start(f32[2048]{0:T(1024)S(1)} %get-tuple-element.31) | copy-start | bytes 24580
  63.0 92.5 %copy-start.188 = (f32[160]{0:T(256)}, f32[160]{0:T(256)S(1)}, u32[]{:S(2)}) copy-start(f32[160]{0:T(256)S(1)} %broadcast_select_fusion.12) | copy-start | bytes 1924
  63.1 92.5 %copy-start.134 = (f32[160]{0:T(256)}, f32[160]{0:T(256)S(1)}, u32[]{:S(2)}) copy-start(f32[160]{0:T(256)S(1)} %fusion.57) | copy-start | bytes 1924
  63.1 92.5 %copy-start.141 = (f32[1024]{0:T(1024)}, f32[1024]{0:T(1024)S(1)}, u32[]{:S(2)}) copy-start(f32[1024]{0:T(1024)S(1)} %get-tuple-element.265) | copy-start | bytes 12292
  63.1 92.5 %copy-start.143 = (f32[1024]{0:T(1024)}, f32[1024]{0:T(1024)S(1)}, u32[]{:S(2)}) copy-start(f32[1024]{0:T(1024)S(1)} %get-tuple-element.266) | copy-start | bytes 12292
  63.1 92.5 %copy-start.147 = (f32[1024]{0:T(1024)}, f32[1024]{0:T(1024)S(1)}, u32[]{:S(2)}) copy-start(f32[1024]{0:T(1024)S(1)} %get-tuple-element.283) | copy-start | bytes 12292
  97.8 63.0 %copy-start.3 = (f32[160,2048]{1,0:T(8,128)}, f32[160,2048]{1,0:T(8,128)S(1)}, u32[]{:S(2)}) copy-start(f32[160,2048]{1,0:T(8,128)S(1)} %fusion.69) | copy-start | bytes 3932164
  160.8 360.8 %copy-start.14 = (f32[160,1024]{1,0:T(8,128)}, f32[160,1024]{1,0:T(8,128)S(1)}, u32[]{:S(2)}) copy-start(f32[160,1024]{1,0:T(8,128)S(1)} %get-tuple-element.89) | copy-start | bytes 1966084
  160.8 360.8 %copy-start.15 = (f32[160,1024]{1,0:T(8,128)}, f32[160,1024]{1,0:T(8,128)S(1)}, u32[]{:S(2)}) copy-start(f32[160,1024]{1,0:T(8,128)S(1)} %get-tuple-element.90) | copy-start | bytes 1966084
  258.9 209.0 %copy-start.60 = (f32[39,1024]{1,0:T(8,128)}, f32[39,1024]{1,0:T(8,128)S(1)}, u32[]{:S(2)}) copy-start(f32[39,1024]{1,0:T(8,128)S(1)} %slice.1575) | copy-start | bytes 479236
  410.5 72.0 %copy-start.18 = (f32[79,1024]{1,0:T(8,128)}, f32[79,1024]{1,0:T(8,128)S(1)}, u32[]{:S(2)}) copy-start(f32[79,1024]{1,0:T(8,128)S(1)} %slice.1627) | copy-start | bytes 970756
  413.9 68.6 %copy-start.20 = (f32[79,1024]{1,0:T(8,128)}, f32[79,1024]{1,0:T(8,128)S(1)}, u32[]{:S(2)}) copy-start(f32[79,1024]{1,0:T(8,128)S(1)} %slice.1564) | copy-start | bytes 970756
  641.5 112.5 %copy-start.50 = (bf16[160,2048]{1,0:T(8,128)(2,1)S(1)}, bf16[160,2048]{1,0:T(8,128)(2,1)}, u32[]{:S(2)}) copy-start(bf16[160,2048]{1,0:T(8,128)(2,1)} %param.19) | copy-start | bytes 1966084
  780.7 552.3 %reduce-scatter.23.cloned.1.call-start = ((), (), s32[]{:S(2)}) async-start(), calls=%async_computation.23 | async-start | bytes 23789568 | tf_op jit(solution)/shard_map/reduce_scatter | solution.py:77
  792.1 748.9 %reduce-scatter.21.cloned.1.call-start = ((), (), s32[]{:S(2)}) async-start(), calls=%async_computation.22 | async-start | bytes 23789568 | tf_op jit(solution)/shard_map/reduce_scatter | solution.py:77
  803.2 992.9 %reduce-scatter.19.cloned.1.call-start = ((), (), s32[]{:S(2)}) async-start(), calls=%async_computation.21 | async-start | bytes 23789568 | tf_op jit(solution)/shard_map/reduce_scatter | solution.py:77
  814.5 1235.2 %reduce-scatter.29.cloned.1.call-start = ((), (), s32[]{:S(2)}) async-start(), calls=%async_computation.26 | async-start | bytes 23789568 | tf_op jit(solution)/shard_map/reduce_scatter | solution.py:77
  825.7 1477.8 %reduce-scatter.27.cloned.1.call-start = ((), (), s32[]{:S(2)}) async-start(), calls=%async_computation.25 | async-start | bytes 23789568 | tf_op jit(solution)/shard_map/reduce_scatter | solution.py:77
  837.2 1614.8 %reduce-scatter.13.cloned.1.call-start = ((), (), s32[]{:S(2)}) async-start(), calls=%async_computation.18 | async-start | bytes 8650752 | tf_op jit(solution)/shard_map/reduce_scatter | solution.py:83
  1230.0 1409.5 %reduce-scatter.17.cloned.1.call-start = ((), (), s32[]{:S(2)}) async-start(), calls=%async_computation.20 | async-start | bytes 17301504 | tf_op jit(solution)/shard_map/reduce_scatter | solution.py:83
  1239.4 1587.3 %reduce-scatter.11.cloned.1.call-start = ((), (), s32[]{:S(2)}) async-start(), calls=%async_computation.17 | async-start | bytes 17301504 | tf_op jit(solution)/shard_map/reduce_scatter | solution.py:83
  1249.0 1764.9 %reduce-scatter.15.cloned.1.call-start = ((), (), s32[]{:S(2)}) async-start(), calls=%async_computation.19 | async-start | bytes 17301504 | tf_op jit(solution)/shard_map/reduce_scatter | solution.py:83
  1269.5 49.9 %copy-start.181 = (f32[160]{0:T(256)S(1)}, f32[160]{0:T(256)}, u32[]{:S(2)}) copy-start(f32[160]{0:T(256)} %copy-done.180) | copy-start | bytes 1924
  (183 other events, 1434.6 us)
Sparse Core Ops, SparseCore 0:
  11.5 79.9 all-gather.17
  94.9 60.6 all-gather.15
  158.4 75.9 all-gather.19
  237.2 76.0 all-gather.21
  315.9 144.4 all-gather.25
  463.7 144.5 all-gather.23
  611.2 142.7 all-gather.27
  780.8 249.1 reduce-scatter.24
  1032.3 254.6 reduce-scatter.22
  1289.1 251.8 reduce-scatter.20
  1543.4 252.7 reduce-scatter.18
  1798.3 251.3 reduce-scatter.28
  2052.0 251.3 reduce-scatter.26
  2306.2 145.7 reduce-scatter.12
  2454.7 184.6 reduce-scatter.16
  2642.1 184.4 reduce-scatter.10
  2829.4 184.4 reduce-scatter.14
where the time goes:
time: 3040 us; the launch traced here: 3020 us
  waiting for transfers between devices  1860 us (61%)
  blocking collectives  397 us (13%)
  local copies, waits for them, and re-layouts  361 us (12%)
  matrix products  219 us (7%)
  other arithmetic  166 us (5%)
    reduce_scatter x6, waiting for transfers between devices, scatter_ffn(): lax.psum_scatter(weight_term(left_grads, right_values), 'dp', scatter_dim...  965 us
    reduce_scatter x4, waiting for transfers between devices, scatter_mix(): lax.psum_scatter(weight_term(left_grads, right_values), 'dp', scatter_dim...  708 us
    slice x105, local copies, waits for them, and re-layouts, local(): lax.associative_scan(compose, (ahead_re, ahead_im, grad_state[:, :half_wi...  109 us
    dot_general x10, matrix products, outer_rows(): lax.dot_general(left_rows, right_rows, (((0,), (0,)), ((), ())), preferre...  100 us
    all_gather x1, waiting for transfers between devices, local(): lax.all_gather(ffn_down.astype(jnp.bfloat16), 'dp', axis=0, tiled=True)  97.7 us
    unnamed x2, blocking collectives  86.3 us
    dot_general x7, matrix products, contract(): lax.dot_general(left_rows, right_rows, (((1,), (1,)), ((), ())), preferre...  70.4 us
    slice x97, local copies, waits for them, and re-layouts, local(): lax.associative_scan(compose, (decay_re, decay_im, drive_re, drive_im), a...  64.3 us
  transfers between devices with their start and end apart: 17, of which 11 were waited for; matrix products, arithmetic and copies ran while one was open for 23% of the time, Pallas kernels for 0%

commit v1 on v0

v1 whole, which is shorter than its diff:
```python
from functools import partial

import jax
import jax.numpy as jnp
from jax import lax
from jax.experimental import pallas as pl
from jax.experimental.pallas import tpu as pltpu
from jax.sharding import PartitionSpec as P


EPS = 1e-06
LOW = jnp.bfloat16
F32 = jnp.float32
MESH = pl.DeviceIdType.MESH
ROWS = 32
LANES = 128


def contract(left_rows, right_rows):
    return lax.dot_general(
        left_rows, right_rows, (((1,), (1,)), ((), ())), preferred_element_type=F32
    )


def outer_rows(left_rows, right_rows):
    return lax.dot_general(
        left_rows, right_rows, (((0,), (0,)), ((), ())), preferred_element_type=F32
    )


class Layout:
    def __init__(self, n):
        self.n = n
        self.Y = n // 16
        self.C, self.X, self.ZL, self.ZH = 1, 2, 4 * self.Y, 8 * self.Y
        self.ybits = []
        bit = 4
        while bit < self.ZL:
            self.ybits.append(bit)
            bit *= 2
        self.wbits = [self.ZH] + self.ybits + [self.C]
        self.tmasks = [0, self.X, self.ZL, self.ZL | self.X]
        self.wmasks = [0]
        for bit in self.wbits:
            self.wmasks = self.wmasks + [m | bit for m in self.wmasks]
        self.bits = [1 << k for k in range(n.bit_length() - 1)]

    def flip(self, device, mask):
        for bit in self.bits:
            if mask & bit:
                device = device + bit * (1 - 2 * ((device // bit) % 2))
        return device

    def parts(self, device):
        c = device % 2
        x = (device // self.X) % 2
        y = (device // 4) % self.Y
        zlo = (device // self.ZL) % 2
        zhi = device // self.ZH
        return zhi, zlo, y, x, c

    def send(self, value, mask):
        return lax.ppermute(value, "dp", [(i, i ^ mask) for i in range(self.n)])

    def gather_t(self, value):
        return [value] + [self.send(value, m) for m in self.tmasks[1:]]

    def scatter_t(self, blocks):
        got = [self.send(b, m) for b, m in zip(blocks[1:], self.tmasks[1:])]
        total = blocks[0].astype(F32)
        for g in got:
            total = total + g.astype(F32)
        return total

    def gather_w(self, value):
        pieces = [value]
        for bit in self.wbits:
            pieces = pieces + [self.send(v, bit) for v in pieces]
        return pieces


def gather_kernel(lay, masks, slot_of, in_ref, out_ref, send_sems, recv_sems):
    me = lax.axis_index("dp")
    peers = [lay.flip(me, m) for m in masks]
    barrier = pltpu.get_barrier_semaphore()
    for peer in peers:
        pl.semaphore_signal(barrier, inc=1, device_id=(peer,), device_id_type=MESH)
    pl.semaphore_wait(barrier, len(peers))
    slot = slot_of(me)
    copies = []
    for i, peer in enumerate(peers):
        copy = pltpu.make_async_remote_copy(
            src_ref=in_ref,
            dst_ref=out_ref.at[slot],
            send_sem=send_sems.at[i],
            recv_sem=recv_sems.at[i],
            device_id=(peer,),
            device_id_type=MESH,
        )
        copy.start()
        copies.append(copy)
    out_ref[slot] = in_ref[...]
    for copy in copies:
        copy.wait()


def small_gather(lay, value, masks, slot_of, slots, collective_id):
    masks = [m for m in masks if m]
    vmem = pl.BlockSpec(memory_space=pltpu.VMEM)
    return pl.pallas_call(
        partial(gather_kernel, lay, masks, slot_of),
        out_shape=jax.ShapeDtypeStruct((slots,) + value.shape, value.dtype),
        in_specs=[vmem],
        out_specs=vmem,
        scratch_shapes=[
            pltpu.SemaphoreType.DMA((len(masks),)),
            pltpu.SemaphoreType.DMA((len(masks),)),
        ],
        compiler_params=pltpu.CompilerParams(collective_id=collective_id, has_side_effects=True),
    )(value)


def exchange_kernel(lay, masks, in_ref, out_ref, send_sems, recv_sems):
    me = lax.axis_index("dp")
    peers = [lay.flip(me, m) for m in masks]
    barrier = pltpu.get_barrier_semaphore()
    for peer in peers:
        pl.semaphore_signal(barrier, inc=1, device_id=(peer,), device_id_type=MESH)
    pl.semaphore_wait(barrier, len(peers))
    copies = []
    for i, peer in enumerate(peers):
        copy = pltpu.make_async_remote_copy(
            src_ref=in_ref.at[peer],
            dst_ref=out_ref.at[me],
            send_sem=send_sems.at[i],
            recv_sem=recv_sems.at[i],
            device_id=(peer,),
            device_id_type=MESH,
        )
        copy.start()
        copies.append(copy)
    out_ref[me] = in_ref[me]
    for copy in copies:
        copy.wait()


def small_exchange(lay, value, collective_id):
    masks = list(range(1, lay.n))
    vmem = pl.BlockSpec(memory_space=pltpu.VMEM)
    return pl.pallas_call(
        partial(exchange_kernel, lay, masks),
        out_shape=jax.ShapeDtypeStruct(value.shape, value.dtype),
        in_specs=[vmem],
        out_specs=vmem,
        scratch_shapes=[
            pltpu.SemaphoreType.DMA((len(masks),)),
            pltpu.SemaphoreType.DMA((len(masks),)),
        ],
        compiler_params=pltpu.CompilerParams(collective_id=collective_id, has_side_effects=True),
    )(value)


def sig(v):
    return 1.0 / (1.0 + jnp.exp(-v))


def lanes(base, h):
    return slice(base + h * LANES, base + (h + 1) * LANES)


def fold_rows(v):
    return jnp.sum(v.reshape(v.shape[0] // 8, 8, v.shape[1]), axis=0)


def forward_kernel(half, length, proj, keep, par, d_re, d_im, v_re, v_im, summ):
    total = d_re.shape[1]
    blocks = total // length
    tiles = half // LANES

    def terms(i, _):
        rows = pl.ds(pl.multiple_of(i * ROWS, ROWS), ROWS)
        kept = keep[rows, :]
        for h in range(tiles):
            at = slice(h * LANES, (h + 1) * LANES)
            lower = par[0:1, at]
            magnitude = lower + (1.0 - lower) * sig(proj[rows, lanes(4 * half, h)])
            rest = 1.0 - magnitude
            d_re[h, rows, :] = kept * magnitude * par[1:2, at]
            d_im[h, rows, :] = kept * magnitude * par[2:3, at]
            a = proj[rows, lanes(0, h)]
            b = proj[rows, lanes(half, h)]
            v_re[h, rows, :] = a * sig(a) * rest
            v_im[h, rows, :] = b * sig(b) * rest
        return 0

    lax.fori_loop(0, total // ROWS, terms, 0)

    def step(t, carry):
        rows = pl.ds(t, blocks, stride=length)
        out = []
        for h in range(tiles):
            p_re, p_im, s_re, s_im = carry[4 * h : 4 * h + 4]
            dr, di = d_re[h, rows, :], d_im[h, rows, :]
            out += [
                dr * p_re - di * p_im,
                dr * p_im + di * p_re,
                dr * s_re - di * s_im + v_re[h, rows, :],
                dr * s_im + di * s_re + v_im[h, rows, :],
            ]
        return tuple(out)

    zero = jnp.zeros((blocks, LANES), F32)
    ends = lax.fori_loop(0, length, step, (zero + 1.0, zero, zero, zero) * tiles, unroll=4)
    for j in range(blocks):
        summ[j, 4:8, :] = jnp.zeros((4, half), F32)
        for h in range(tiles):
            for k in range(4):
                summ[j, k : k + 1, lanes(0, h)] = ends[4 * h + k][j : j + 1, :]


def chain_blocks(half, n, blocks, ints, summ, back):
    tiles = half // LANES

    def chain(i, carry):
        p = i if back is None else n - 1 - i
        tile = summ[ints[p]]
        shift = tile[2:4, :] if back is None else back[ints[p]]
        out = []
        for h in range(tiles):
            at = slice(h * LANES, (h + 1) * LANES)
            old = carry[h * (2 + 2 * blocks) : (h + 1) * (2 + 2 * blocks)]
            c_re, c_im = old[0], old[1]
            a_re = tile[0:1, at]
            a_im = tile[1:2, at] if back is None else -tile[1:2, at]
            out.append(a_re * c_re - a_im * c_im + shift[0:1, at])
            out.append(a_re * c_im + a_im * c_re + shift[1:2, at])
            for j in range(blocks):
                here = ints[n + j] == p
                out.append(jnp.where(here, c_re, old[2 + 2 * j]))
                out.append(jnp.where(here, c_im, old[3 + 2 * j]))
        return tuple(out)

    first = summ[0]
    zero = first[0:1, 0:LANES] - first[0:1, 0:LANES]
    res = lax.fori_loop(0, n, chain, (zero,) * (tiles * (2 + 2 * blocks)))
    entry = []
    for h in range(tiles):
        old = res[h * (2 + 2 * blocks) : (h + 1) * (2 + 2 * blocks)]
        entry.append(jnp.concatenate([old[2 + 2 * j] for j in range(blocks)], axis=0))
        entry.append(jnp.concatenate([old[3 + 2 * j] for j in range(blocks)], axis=0))
    return tuple(entry)


def state_kernel(
    half, length, n, ints, summ, d_re, d_im, v_re, v_im, proj, gain,
    st_re, st_im, be_re, be_im, unit, squares,
):
    total = d_re.shape[1]
    blocks = total // length
    tiles = half // LANES

    def step(t, carry):
        rows = pl.ds(t, blocks, stride=length)
        out = []
        for h in range(tiles):
            s_re, s_im = carry[2 * h], carry[2 * h + 1]
            be_re[h, rows, :] = s_re
            be_im[h, rows, :] = s_im
            dr, di = d_re[h, rows, :], d_im[h, rows, :]
            n_re = dr * s_re - di * s_im + v_re[h, rows, :]
            n_im = dr * s_im + di * s_re + v_im[h, rows, :]
            st_re[h, rows, :] = n_re
            st_im[h, rows, :] = n_im
            out += [n_re, n_im]
        return tuple(out)

    entry = chain_blocks(half, n, blocks, ints, summ, None)
    lax.fori_loop(0, length, step, entry, unroll=4)

    def finish(i, _):
        rows = pl.ds(pl.multiple_of(i * ROWS, ROWS), ROWS)
        square = jnp.zeros((ROWS, 1), F32)
        for h in range(tiles):
            for part, st in ((0, st_re), (1, st_im)):
                v = st[h, rows, :]
                g = proj[rows, lanes((2 + part) * half, h)]
                at = lanes(part * half, h)
                unit[rows, at] = (v * gain[0:1, at] * (g * sig(g))).astype(LOW)
                square = square + jnp.sum(v * v, axis=1, keepdims=True)
        squares[rows, :] = square
        return 0

    lax.fori_loop(0, total // ROWS, finish, 0)


def back_kernel(
    half, length, grad_mid, st_re, st_im, proj, gain, scale, d_re, d_im,
    gs_re, gs_im, gate_low, mid, gain_grad, summ, acc,
):
    total = d_re.shape[1]
    blocks = total // length
    tiles = half // LANES
    acc[...] = jnp.zeros_like(acc)

    def terms(i, _):
        rows = pl.ds(pl.multiple_of(i * ROWS, ROWS), ROWS)
        r = scale[rows, 0:1]
        q = scale[rows, 1:2]
        for h in range(tiles):
            for part, st, gs in ((0, st_re, gs_re), (1, st_im, gs_im)):
                at = lanes(part * half, h)
                g = proj[rows, lanes((2 + part) * half, h)]
                v = st[h, rows, :]
                gv = gain[0:1, at]
                dm = grad_mid[rows, at]
                sg = sig(g)
                silu = g * sg
                du = dm * silu
                normed = v * r
                scaled = normed * gv
                mid[rows, at] = (scaled * silu).astype(LOW)
                gate_low[rows, at] = (dm * scaled * (sg * (1.0 + g * (1.0 - sg)))).astype(LOW)
                gs[h, rows, :] = du * gv * r - v * q
                acc[:, at] = acc[:, at] + fold_rows(du * normed)
        return 0

    lax.fori_loop(0, total // ROWS, terms, 0)
    gain_grad[...] = acc[...]

    def step(i, carry):
        rows = pl.ds(length - 1 - i, blocks, stride=length)
        out = []
        for h in range(tiles):
            a_re = gs_re[h, rows, :] + carry[2 * h]
            a_im = gs_im[h, rows, :] + carry[2 * h + 1]
            dr, di = d_re[h, rows, :], d_im[h, rows, :]
            out += [dr * a_re + di * a_im, dr * a_im - di * a_re]
        return tuple(out)

    zero = jnp.zeros((blocks, LANES), F32)
    ends = lax.fori_loop(0, length, step, (zero, zero) * tiles, unroll=4)
    for j in range(blocks):
        summ[j, 2:8, :] = jnp.zeros((6, half), F32)
        for h in range(tiles):
            for k in range(2):
                summ[j, k : k + 1, lanes(0, h)] = ends[2 * h + k][j : j + 1, :]


def adjoint_kernel(
    half, length, n, ints, summ, back, gs_re, gs_im, d_re, d_im, be_re, be_im, proj, keep, par, gate_low,
    grads, lower_grad, angle_grad, ad_re, ad_im, acc,
):
    total = d_re.shape[1]
    blocks = total // length
    tiles = half // LANES

    def step(i, carry):
        rows = pl.ds(length - 1 - i, blocks, stride=length)
        out = []
        for h in range(tiles):
            a_re = gs_re[h, rows, :] + carry[2 * h]
            a_im = gs_im[h, rows, :] + carry[2 * h + 1]
            ad_re[h, rows, :] = a_re
            ad_im[h, rows, :] = a_im
            dr, di = d_re[h, rows, :], d_im[h, rows, :]
            out += [dr * a_re + di * a_im, dr * a_im - di * a_re]
        return tuple(out)

    entry = chain_blocks(half, n, blocks, ints, summ, back)
    lax.fori_loop(0, length, step, entry, unroll=4)
    acc[...] = jnp.zeros_like(acc)

    def terms(i, _):
        rows = pl.ds(pl.multiple_of(i * ROWS, ROWS), ROWS)
        kept = keep[rows, :]
        for h in range(tiles):
            at = slice(h * LANES, (h + 1) * LANES)
            lower, cos, sin = par[0:1, at], par[1:2, at], par[2:3, at]
            sf = sig(proj[rows, lanes(4 * half, h)])
            magnitude = lower + (1.0 - lower) * sf
            rest = 1.0 - magnitude
            a = proj[rows, lanes(0, h)]
            b = proj[rows, lanes(half, h)]
            sa, sb = sig(a), sig(b)
            ar, ai = ad_re[h, rows, :], ad_im[h, rows, :]
            br, bi = be_re[h, rows, :], be_im[h, rows, :]
            g_re = ar * br + ai * bi
            g_im = ai * br - ar * bi
            g_mag = kept * (g_re * cos + g_im * sin) - (ar * (a * sa) + ai * (b * sb))
            acc[0:8, at] = acc[0:8, at] + fold_rows(g_mag * (1.0 - sf))
            acc[8:16, at] = acc[8:16, at] + fold_rows(kept * magnitude * (g_im * cos - g_re * sin))
            grads[rows, lanes(0, h)] = (ar * rest * (sa * (1.0 + a * (1.0 - sa)))).astype(LOW)
            grads[rows, lanes(half, h)] = (ai * rest * (sb * (1.0 + b * (1.0 - sb)))).astype(LOW)
            grads[rows, lanes(4 * half, h)] = (g_mag * (1.0 - lower) * sf * (1.0 - sf)).astype(LOW)
        grads[rows, 2 * half : 4 * half] = gate_low[rows, :]
        return 0

    lax.fori_loop(0, total // ROWS, terms, 0)
    lower_grad[...] = acc[0:8, :]
    angle_grad[...] = acc[8:16, :]


VMEM = pl.BlockSpec(memory_space=pltpu.VMEM)
SMEM = pl.BlockSpec(memory_space=pltpu.SMEM)


def plain_call(body, outs, n_in, smem=0, scratch=(), name=None):
    return pl.pallas_call(
        body,
        out_shape=tuple(jax.ShapeDtypeStruct(s, d) for s, d in outs),
        in_specs=[SMEM] * smem + [VMEM] * (n_in - smem),
        out_specs=tuple(VMEM for _ in outs),
        scratch_shapes=list(scratch),
        compiler_params=pltpu.CompilerParams(vmem_limit_bytes=48 << 20),
        cost_estimate=pl.CostEstimate(flops=20_000_000, bytes_accessed=12_000_000, transcendentals=0),
        name=name,
    )


def local(
    n,
    tokens,
    cotangent,
    seq_lengths,
    block_deal,
    in_proj,
    forget_proj,
    gate_proj,
    out_proj,
    ffn_gate,
    ffn_up,
    ffn_down,
    gain_mix,
    gain_out,
    gain_ffn,
    lower_bound,
    rotation,
):
    lay = Layout(n)
    Y = lay.Y
    W = n // 4
    me = lax.axis_index("dp")
    zhi, zlo, y, x, c = lay.parts(me)
    mine_t = zlo * 2 + x
    length, width = tokens.shape
    half = width // 8
    total = 4 * length
    r_in, r_f = in_proj.shape[0], forget_proj.shape[0]

    def w_slot(device):
        zh, _, yy, _, cc = lay.parts(device)
        return (zh * Y + yy) * 2 + cc

    indices = jnp.arange(n, dtype=jnp.int32)
    order = jnp.sum(jnp.where(block_deal[None, :] == indices[:, None], indices[None, :], 0), axis=1)
    t_devices = jnp.stack([lay.flip(me, m) for m in lay.tmasks])
    t_places = jnp.sum(
        jnp.where(t_devices[:, None] == indices[None, :], block_deal[None, :], 0), axis=1
    )
    o_parts = lay.parts(order)
    t_rel = ((o_parts[1] + zlo) % 2) * 2 + (o_parts[3] + x) % 2
    ints = jnp.concatenate([w_slot(order) * 4 + t_rel, t_places]).astype(jnp.int32)
    offsets = jnp.cumsum(seq_lengths) - seq_lengths
    positions = (
        t_places[:, None] * length + jnp.arange(length, dtype=jnp.int32)[None, :]
    ).reshape(-1)
    starts = jnp.any(positions[:, None] == offsets[None, :], axis=1)
    keep = jnp.where(starts, 0.0, 1.0).astype(F32)[:, None]

    packed = jnp.concatenate([gain_mix, gain_ffn, gain_out, lower_bound, rotation])
    pack_rows = -(-packed.shape[0] // 128)
    packed = jnp.pad(packed, (0, 8 * 128 - packed.shape[0])).reshape(8, 128)
    every = small_gather(lay, packed, list(range(n)), lambda d: d, n, 0)
    every = every[:, :pack_rows, :].reshape(n, pack_rows * 128)
    g_mix = every[:, 0:r_in].reshape(1, width)
    g_ffn = every[:, r_in : 2 * r_in].reshape(1, width)
    g_out = every[:, 2 * r_in : 3 * r_in].reshape(2, 2, Y, 2, 2 * r_in)
    g_out = lax.dynamic_index_in_dim(g_out, zlo, 1, keepdims=False)
    g_out = lax.dynamic_index_in_dim(g_out, x, 2, keepdims=False).reshape(1, 2 * half)

    def channels(vector):
        vector = vector.reshape(2, Y, 2, half // Y)
        vector = lax.dynamic_index_in_dim(vector, zlo, 0, keepdims=False)
        return lax.dynamic_index_in_dim(vector, x, 1, keepdims=False).reshape(1, half)

    lower = channels(every[:, 3 * r_in : 3 * r_in + r_f])
    angle = channels(every[:, 3 * r_in + r_f : 3 * r_in + 2 * r_f])
    par = jnp.concatenate(
        [lower, jnp.cos(angle), jnp.sin(angle), jnp.zeros((5, half), F32)], axis=0
    )

    forget_to = [(2 * e + b, b * (n // 2) + e) for e in range(n // 2) for b in range(2)]
    forget_from = [(d, s) for s, d in forget_to]
    forget_low = lax.ppermute(forget_proj.astype(LOW), "dp", forget_to)
    tok_all = jnp.concatenate(lay.gather_t(tokens), axis=0)
    out_cols = out_proj.astype(LOW).reshape(r_in, 2, 2, Y, 2, 2 * r_in)
    out_cols = out_cols.transpose(2, 4, 0, 1, 3, 5).reshape(4, r_in, 2 * half)

    def out_for(mask):
        slot = ((zlo + (1 if mask & lay.ZL else 0)) % 2) * 2 + (x + (1 if mask & lay.X else 0)) % 2
        return lax.dynamic_index_in_dim(out_cols, slot, 0, keepdims=False)

    out_low = jnp.stack(
        [out_for(0)] + [lay.send(out_for(m), m) for m in lay.tmasks[1:]]
    )
    mix_low = jnp.concatenate([in_proj.astype(LOW), gate_proj.astype(LOW), forget_low], axis=0)
    mix_pieces = lay.gather_w(mix_low)
    out_pieces = lay.gather_w(out_low)

    slots = [w_slot(lay.flip(me, m)) for m in lay.wmasks]
    mix_buf = jnp.zeros((W,) + mix_low.shape, LOW)
    for slot, piece in zip(slots, mix_pieces):
        mix_buf = lax.dynamic_update_slice(mix_buf, piece[None], (slot, 0, 0))
    w_in = mix_buf[:, :r_in].reshape(2 * half, width)
    w_gate = mix_buf[:, r_in : 2 * r_in].reshape(2 * half, width)
    w_forget = (
        mix_buf[:, 2 * r_in :]
        .reshape(2, W // 2, r_f, width)
        .transpose(1, 0, 2, 3)
        .reshape(half, width)
    )
    w_mix = jnp.concatenate([w_in, w_gate, w_forget], axis=0)
    out_buf = jnp.zeros((n, r_in, 2 * half), LOW)
    for mask, piece in zip(lay.wmasks, out_pieces):
        for j, t_mask in enumerate(lay.tmasks):
            out_buf = lax.dynamic_update_slice(
                out_buf, piece[j][None], (lay.flip(me, mask ^ t_mask), 0, 0)
            )
    w_out = out_buf.reshape(width, 2 * half)

    f_gate, f_up, f_down, cot_own, _, _ = lax.optimization_barrier(
        (ffn_gate.astype(LOW), ffn_up.astype(LOW), ffn_down.astype(LOW), cotangent, mix_pieces[1], tok_all)
    )
    gate_pieces = lay.gather_w(f_gate)
    f_up, _ = lax.optimization_barrier((f_up, gate_pieces[1]))
    up_pieces = lay.gather_w(f_up)
    f_down, _ = lax.optimization_barrier((f_down, up_pieces[1]))
    down_pieces = lay.gather_w(f_down)
    w_gu = jnp.concatenate(gate_pieces + up_pieces, axis=0)
    w_down = jnp.concatenate(down_pieces, axis=0)
    hid = w_down.shape[0]
    cot_all = jnp.concatenate(lay.gather_t(cot_own), axis=0)

    inputs = tokens.astype(F32)
    r_tok = lax.rsqrt(jnp.mean(inputs * inputs, axis=-1, keepdims=True) + EPS)
    all32 = tok_all.astype(F32)
    normed = (
        all32 * lax.rsqrt(jnp.mean(all32 * all32, axis=-1, keepdims=True) + EPS) * g_mix
    ).astype(LOW)
    proj = contract(normed, w_mix)
    wide = ((half // LANES, total, LANES), F32)
    d_re, d_im, v_re, v_im, summ = plain_call(
        partial(forward_kernel, half, length),
        [wide] * 4 + [((4, 8, half), F32)],
        3,
        name="gates",
    )(proj, keep, par)
    summ_all = small_gather(lay, summ, lay.wmasks, w_slot, W, 1).reshape(n, 8, half)
    st_re, st_im, be_re, be_im, unit, squares = plain_call(
        partial(state_kernel, half, length, n),
        [wide] * 4 + [((total, 2 * half), LOW), ((total, 1), F32)],
        8,
        smem=1,
        name="states",
    )(ints, summ_all, d_re, d_im, v_re, v_im, proj, g_out)
    branch_low = contract(unit, w_out).astype(LOW)

    def t_blocks(value):
        return [value[j * length : (j + 1) * length] for j in range(4)]

    square = lay.scatter_t(t_blocks(squares))
    branch = lay.scatter_t(t_blocks(branch_low))
    r_state = lax.rsqrt(square / width + EPS)
    residual = inputs + r_state * branch
    r_res = lax.rsqrt(jnp.mean(residual * residual, axis=-1, keepdims=True) + EPS)
    ffn_low = (residual * r_res * g_ffn).astype(LOW)

    ffn_all = jnp.concatenate(lay.gather_t(ffn_low), axis=0)
    gate_up = contract(ffn_all, w_gu)
    gate_value, up_value = gate_up[:, :hid], gate_up[:, hid:]
    s_gate = jax.nn.sigmoid(gate_value)
    silu_gate = gate_value * s_gate
    hidden_low = (silu_gate * up_value).astype(LOW)
    grad_hidden = contract(cot_all, w_down)
    grad_gu = jnp.concatenate(
        [
            (grad_hidden * up_value * s_gate * (1.0 + gate_value * (1.0 - s_gate))).astype(LOW),
            (grad_hidden * silu_gate).astype(LOW),
        ],
        axis=1,
    )
    du_low = jnp.dot(grad_gu, w_gu, preferred_element_type=F32).astype(LOW)
    du = lay.scatter_t(t_blocks(du_low))
    mixed_low = jnp.dot(hidden_low, w_down, preferred_element_type=F32).astype(LOW)
    mixed_out = (residual + lay.scatter_t(t_blocks(mixed_low))).astype(LOW)

    def scatter_w(partial_grad):
        for bit in reversed(lay.wbits):
            rows = partial_grad.shape[0] // 2
            got = lay.send(partial_grad[rows:], bit)
            partial_grad = partial_grad[:rows].astype(F32) + got.astype(F32)
            if bit != lay.wbits[0]:
                partial_grad = partial_grad.astype(LOW)
        return partial_grad

    grad_w_gu = outer_rows(grad_gu, ffn_all).astype(LOW)
    grad_w_down = outer_rows(hidden_low, cot_all).astype(LOW)
    ffn_gate_grad = scatter_w(grad_w_gu[:hid])
    ffn_up_grad = scatter_w(grad_w_gu[hid:])
    ffn_down_grad = scatter_w(grad_w_down)

    du_gain = du * g_ffn
    grad_residual = (
        cotangent.astype(F32)
        + r_res * du_gain
        - residual * (r_res * r_res * r_res) * jnp.mean(residual * du_gain, axis=-1, keepdims=True)
    )
    ffn_gain_part = jnp.sum(du * residual * r_res, axis=0)
    grad_low = grad_residual.astype(LOW)
    inner = jnp.sum(grad_low.astype(F32) * branch, axis=-1, keepdims=True) / width
    scale = jnp.concatenate([r_state, r_state * r_state * r_state * inner], axis=1)

    grad_all = jnp.concatenate(lay.gather_t(grad_low), axis=0)
    scale_all = jnp.concatenate(lay.gather_t(scale), axis=0)
    grad_mid = jnp.dot(grad_all, w_out, preferred_element_type=F32)
    gs_re, gs_im, gate_low, mid, out_gain_part, back = plain_call(
        partial(back_kernel, half, length),
        [wide] * 2
        + [((total, 2 * half), LOW)] * 2
        + [((8, 2 * half), F32), ((4, 8, half), F32)],
        8,
        scratch=[pltpu.VMEM((8, 2 * half), F32)],
        name="back_gates",
    )(grad_mid, st_re, st_im, proj, g_out, scale_all, d_re, d_im)
    back_all = small_gather(lay, back, lay.wmasks, w_slot, W, 2).reshape(n, 8, half)
    grads, lower_part, angle_part = plain_call(
        partial(adjoint_kernel, half, length, n),
        [((total, 5 * half), LOW), ((8, half), F32), ((8, half), F32)],
        13,
        smem=1,
        scratch=[pltpu.VMEM((half // LANES, total, LANES), F32)] * 2 + [pltpu.VMEM((16, half), F32)],
        name="adjoints",
    )(ints, summ_all, back_all, gs_re, gs_im, d_re, d_im, be_re, be_im, proj, keep, par, gate_low)
    du_mix_low = jnp.dot(grads, w_mix, preferred_element_type=F32).astype(LOW)
    du_mix = lay.scatter_t(t_blocks(du_mix_low))
    dg_mix = du_mix * g_mix
    tokens_grad = (
        grad_residual
        + r_tok * dg_mix
        - inputs * (r_tok * r_tok * r_tok) * jnp.mean(inputs * dg_mix, axis=-1, keepdims=True)
    ).astype(LOW)
    mix_gain_part = jnp.sum(du_mix * inputs * r_tok, axis=0)

    def scatter_abs(part):
        shape = part.shape
        axes = len(lay.wbits)
        bits = {0: zhi, axes - 1: c}
        for k, bit in enumerate(reversed(lay.ybits)):
            bits[1 + k] = (me // bit) % 2
        names = {0: lay.ZH, axes - 1: lay.C}
        for k, bit in enumerate(reversed(lay.ybits)):
            names[1 + k] = bit
        part = part.reshape((2,) * axes + shape[3:])
        for k in reversed(range(axes)):
            kept = lax.dynamic_index_in_dim(part, bits[k], k, keepdims=False)
            away = lax.dynamic_index_in_dim(part, 1 - bits[k], k, keepdims=False)
            got = lay.send(away, names[k])
            part = kept.astype(F32) + got.astype(F32)
            if k:
                part = part.astype(LOW)
        return part

    grad_w_out = outer_rows(grad_all, mid).astype(LOW)
    grad_w_out = grad_w_out.reshape(2, 2, Y, 2, 2, r_in, 2 * half).transpose(0, 2, 4, 1, 3, 5, 6)
    out_part = scatter_abs(grad_w_out).reshape(4, r_in, 2 * half)

    def out_back(mask):
        slot = ((zlo + (1 if mask & lay.ZL else 0)) % 2) * 2 + (x + (1 if mask & lay.X else 0)) % 2
        return lax.dynamic_index_in_dim(out_part, slot, 0, keepdims=False), slot

    out_grad = jnp.zeros((4, r_in, 2 * half), F32)
    for mask in lay.tmasks:
        value, slot = out_back(mask)
        if mask:
            value = lay.send(value, mask)
        out_grad = lax.dynamic_update_slice(out_grad, value[None], (slot, 0, 0))
    out_proj_grad = (
        out_grad.reshape(2, 2, r_in, 2, Y, 2 * r_in).transpose(2, 3, 0, 4, 1, 5).reshape(r_in, width)
    )

    grad_w_mix = outer_rows(grads, normed).astype(LOW)
    grad_w_mix = jnp.concatenate(
        [
            grad_w_mix[: 2 * half].reshape(W, r_in, width),
            grad_w_mix[2 * half : 4 * half].reshape(W, r_in, width),
            grad_w_mix[4 * half :]
            .reshape(W // 2, 2, r_f, width)
            .transpose(1, 0, 2, 3)
            .reshape(W, r_f, width),
        ],
        axis=1,
    ).reshape(2, Y, 2, 2 * r_in + r_f, width)
    mix_part = scatter_abs(grad_w_mix)
    in_proj_grad = mix_part[:r_in]
    gate_proj_grad = mix_part[r_in : 2 * r_in]
    forget_proj_grad = lax.ppermute(mix_part[2 * r_in :], "dp", forget_from)

    t_hot = ((jnp.arange(2)[:, None] == zlo) & (jnp.arange(2)[None, :] == x)).astype(F32)
    out_gain_part = jnp.sum(out_gain_part, axis=0).reshape(2, 1, Y, 1, 2 * r_in)
    out_gain_part = (out_gain_part * t_hot[None, :, None, :, None]).reshape(n, r_in)

    def spread(vector):
        vector = jnp.sum(vector, axis=0).reshape(1, Y, 1, half // Y)
        return (vector * t_hot[:, None, :, None]).reshape(n, r_f)

    to_owner = jnp.concatenate(
        [
            mix_gain_part.reshape(n, r_in),
            ffn_gain_part.reshape(n, r_in),
            out_gain_part,
            spread(lower_part),
            spread(angle_part),
        ],
        axis=1,
    )
    to_owner = jnp.pad(to_owner, ((0, 0), (0, 1024 - to_owner.shape[1]))).reshape(n, 8, 128)
    owned = jnp.sum(small_exchange(lay, to_owner, 3), axis=0).reshape(-1)
    return (
        mixed_out,
        tokens_grad,
        in_proj_grad,
        forget_proj_grad,
        gate_proj_grad,
        out_proj_grad,
        ffn_gate_grad,
        ffn_up_grad,
        ffn_down_grad,
        owned[0:r_in],
        owned[2 * r_in : 3 * r_in],
        owned[r_in : 2 * r_in],
        owned[3 * r_in : 3 * r_in + r_f],
        owned[3 * r_in + r_f : 3 * r_in + 2 * r_f],
    )


def solution(mesh):
    rows, vector = P("dp", None), P("dp")
    in_specs = (rows, rows, P(), P()) + (rows,) * 7 + (vector,) * 5
    out_specs = (rows,) * 9 + (vector,) * 5
    return jax.shard_map(
        partial(local, mesh.shape["dp"]),
        mesh=mesh,
        in_specs=in_specs,
        out_specs=out_specs,
        check_vma=False,
    )
```

time: 3040 us -> 808 us (0.27)
  waiting for transfers between devices: 1860 us -> 346 us
  blocking collectives: 397 us -> 0 us
  local copies, waits for them, and re-layouts: 361 us -> 116 us
  matrix products: 219 us -> 95.1 us
  other arithmetic: 166 us -> 46.6 us
  starting transfers between devices: 0.96 us -> 99.3 us
  Pallas kernels: 0 us -> 91 us
    reduce_scatter x10 -> x0, waiting for transfers between devices: 1670 us -> none  [the longest x6 965 us: scatter_ffn(): lax.psum_scatter(weight_term(left_grads, right_values), 'dp', scatter_dim...]
    ppermute x0 -> x88, waiting for transfers between devices: none -> 346 us  [the longest x86 331 us: send(): return lax.ppermute(value, 'dp', [(i, i ^ mask) for i in range(self.n)])]
    all_gather x8 -> x0, blocking collectives: 310 us -> none  [the longest x1 40.3 us: local(): lax.all_gather(local_scan[2][row_count - 1:], 'dp', axis=0, tiled=True)]
    all_gather x7 -> x0, waiting for transfers between devices: 184 us -> none  [the longest x1 97.7 us: local(): lax.all_gather(ffn_down.astype(jnp.bfloat16), 'dp', axis=0, tiled=True)]
    slice x316 -> x25, local copies, waits for them, and re-layouts: 203 us -> 23.6 us  [the longest x8 9.36 us: scatter_w(): got = lay.send(partial_grad[rows:], bit)]
    ppermute x0 -> x88, starting transfers between devices: none -> 99.3 us  [the longest x86 92.4 us: send(): return lax.ppermute(value, 'dp', [(i, i ^ mask) for i in range(self.n)])]
    pad x128 -> x0, local copies, waits for them, and re-layouts: 97.7 us -> none  [the longest x48 64.2 us: local(): lax.associative_scan(compose, (ahead_re, ahead_im, grad_state[:, :half_wi...]
    pallas_call x0 -> x8, Pallas kernels: none -> 91 us  [the longest x3 51.6 us: small_gather(): pl.pallas_call(partial(gather_kernel, lay, masks, slot_of), out_shape=jax...]
  transfers between devices with their start and end apart: 17 -> 88, of which waited for: 11 -> 35; matrix products, arithmetic and copies ran while one was open for 23% -> 26% of each run, Pallas kernels for 0% -> 11%
where the time goes in v1:
time: 808 us; the launch traced here: 797 us
  waiting for transfers between devices  346 us (43%)
  local copies, waits for them, and re-layouts  116 us (14%)
  starting transfers between devices  99.3 us (12%)
  matrix products  95.1 us (12%)
  Pallas kernels  91 us (11%)
  other arithmetic  46.6 us (6%)
    ppermute x86, waiting for transfers between devices, send(): return lax.ppermute(value, 'dp', [(i, i ^ mask) for i in range(self.n)])  331 us
    ppermute x86, starting transfers between devices, send(): return lax.ppermute(value, 'dp', [(i, i ^ mask) for i in range(self.n)])  92.4 us
    unnamed x214, local copies, waits for them, and re-layouts  52 us
    pallas_call x3, Pallas kernels, small_gather(): pl.pallas_call(partial(gather_kernel, lay, masks, slot_of), out_shape=jax...  51.6 us
    dot_general x4, matrix products, contract(): lax.dot_general(left_rows, right_rows, (((1,), (1,)), ((), ())), preferre...  34.4 us
    dot_general x4, matrix products, outer_rows(): lax.dot_general(left_rows, right_rows, (((0,), (0,)), ((), ())), preferre...  32.3 us
    dynamic_update_slice x31, local copies, waits for them, and re-layouts, local(): lax.dynamic_update_slice(out_buf, piece[j][None], (lay.flip(me, mask ^ t_...  21.2 us
  transfers between devices with their start and end apart: 88, of which 35 were waited for; matrix products, arithmetic and copies ran while one was open for 26% of the time, Pallas kernels for 11%

profile of v1, /device:TPU:1, one launch (start us, length us, event | category | flops | bytes accessed | tf_op | source)
XLA Modules:
  0.0 797.5 jit_solution(17251721577127824282)
XLA Ops:
  12.2 16.6 %shard_map.263 = f32[32,8,128]{2,1,0:T(8,128)} custom-call(f32[8,128]{1,0:T(8,128)} %pad_bitcast_fusion.1.in_ref), custom_call_target="tpu_custom_call" | custom-call | tf_op jit(solution)/shard_map/pallas_call | solution.py:110
  50.0 7.8 collective-permute-done.3
  57.8 9.5 %collective-permute-start.18 = (bf16[4,64,512]{2,1,0:T(8,128)(2,1)S(1)}, bf16[4,64,512]{2,1,0:T(8,128)(2,1)S(1)}, u32[]{:S(2)}, u32[]{:S(2)}) collective-permute-start(bf16[4,64,512]{2,1,0:T(8,128)(2,1)S(1)} %pad_maximum_fusion.13), channel_id=1, source_target_pairs={{0,4},{1,5},{2,6},{3,7},{4,0},{5,1},{6,2},{7,3},{8,12},{9,13},{10,... | collective-permute-start | bytes 786440 | tf_op jit(solution)/shard_map/ppermute | solution.py:63
  97.0 11.8 %collective-permute-done.4 = bf16[160,2048]{1,0:T(8,128)(2,1)S(1)} collective-permute-done((bf16[160,2048]{1,0:T(8,128)(2,1)S(1)}, bf16[160,2048]{1,0:T(8,128)(2,1)S(1)}, u32[]{:S(2)}, u32[]{:S(2)}) %collective-permute-start.4) | collective-permute-done | bytes 655392 | tf_op jit(solution)/shard_map/ppermute | solution.py:63
  115.2 25.2 %collective-permute-done.6 = bf16[160,2048]{1,0:T(8,128)(2,1)S(1)} collective-permute-done((bf16[160,2048]{1,0:T(8,128)(2,1)S(1)}, bf16[160,2048]{1,0:T(8,128)(2,1)S(1)}, u32[]{:S(2)}, u32[]{:S(2)}) %collective-permute-start.6) | collective-permute-done | bytes 655392 | tf_op jit(solution)/shard_map/ppermute | solution.py:63
  146.0 13.6 %collective-permute-done.55 = bf16[160,2048]{1,0:T(8,128)(2,1)S(1)} collective-permute-done((bf16[160,2048]{1,0:T(8,128)(2,1)S(1)}, bf16[160,2048]{1,0:T(8,128)(2,1)S(1)}, u32[]{:S(2)}, u32[]{:S(2)}) %collective-permute-start.55) | collective-permute-done | bytes 655392 | tf_op jit(solution)/shard_map/ppermute | solution.py:63
  161.4 11.4 %collective-permute-done.56 = bf16[160,2048]{1,0:T(8,128)(2,1)S(1)} collective-permute-done((bf16[160,2048]{1,0:T(8,128)(2,1)S(1)}, bf16[160,2048]{1,0:T(8,128)(2,1)S(1)}, u32[]{:S(2)}, u32[]{:S(2)}) %collective-permute-start.56) | collective-permute-done | bytes 655392 | tf_op jit(solution)/shard_map/ppermute | solution.py:63
  195.0 19.0 %shard_map.264 = f32[8,4,8,256]{3,2,1,0:T(8,128)} custom-call(f32[4,8,256]{2,1,0:T(8,128)} %copy-done.17), custom_call_target="tpu_custom_call" | custom-call | tf_op jit(solution)/shard_map/pallas_call | solution.py:110
  216.0 7.5 states.1
  255.1 27.7 %collective-permute-done.26 = bf16[160,2048]{1,0:T(8,128)(2,1)S(1)} collective-permute-done((bf16[160,2048]{1,0:T(8,128)(2,1)S(1)}, bf16[160,2048]{1,0:T(8,128)(2,1)S(1)}, u32[]{:S(2)}, u32[]{:S(2)}) %collective-permute-start.26) | collective-permute-done | bytes 655392 | tf_op jit(solution)/shard_map/ppermute | solution.py:63
  293.4 10.0 %collective-permute-done.39 = bf16[176,2048]{1,0:T(8,128)(2,1)S(1)} collective-permute-done((bf16[176,2048]{1,0:T(8,128)(2,1)}, bf16[176,2048]{1,0:T(8,128)(2,1)S(1)}, u32[]{:S(2)}, u32[]{:S(2)}) %collective-permute-start.39) | collective-permute-done | bytes 720928 | tf_op jit(solution)/shard_map/ppermute | solution.py:63
  314.7 7.3 collective-permute-done.27
  329.3 8.5 %collective-permute-done.29 = bf16[160,2048]{1,0:T(8,128)(2,1)} collective-permute-done((bf16[160,2048]{1,0:T(8,128)(2,1)S(1)}, bf16[160,2048]{1,0:T(8,128)(2,1)}, u32[]{:S(2)}, u32[]{:S(2)}) %collective-permute-start.29) | collective-permute-done | bytes 655392 | tf_op jit(solution)/shard_map/ppermute | solution.py:63
  337.9 13.8 %fusion.18 = f32[640,2816]{1,0:T(8,128)} fusion(bf16[2816,2048]{1,0:T(8,128)(2,1)} %constant_dynamic-update-slice_fusion.4, bf16[160,2048]{1,0:T(8,128)(2,1)} %collective-permute-done.29, bf16[160,2048]{1,0:T(8,128)(2,1)S(1)} %collective-permute-done.28, bf16[160,2048]{1,0:T(8,128)(2,1)S(1)} %collective-permute-done.27, ...), kind=kOutput, calls=%fused_computation.81 | convolution fusion | flops 7392460800 | bytes 21364736 | tf_op jit(solution)/shard_map/dot_general | solution.py:20
  356.5 12.1 %multiply_convert_fusion.1 = (bf16[640,1408]{1,0:T(8,128)(2,1)S(1)}, bf16[640,1408]{1,0:T(8,128)(2,1)}, bf16[640,1408]{1,0:T(8,128)(2,1)S(1)}) fusion(f32[640,2816]{1,0:T(8,128)} %fusion.18, bf16[640,2048]{1,0:T(8,128)(2,1)} %copy-done.58, bf16[1408,2048]{1,0:T(8,128)(2,1)} %constant_dynamic-update-slice_fusion.20), kind=kOutput, calls=%fused_computation.16 | convolution fusion | flops 3704504320 | bytes 21004288 | tf_op jit(solution)/shard_map/dot_general | solution.py:20
  368.6 12.4 %convolution_convert_fusion.4 = bf16[640,2048]{1,0:T(8,128)(2,1)S(1)} fusion(bf16[2816,2048]{1,0:T(8,128)(2,1)} %constant_dynamic-update-slice_fusion.4, bf16[640,1408]{1,0:T(8,128)(2,1)} %get-tuple-element.84, bf16[640,1408]{1,0:T(8,128)(2,1)S(1)} %get-tuple-element.83), kind=kOutput, calls=%fused_computation.21 | convolution fusion | flops 7390494720 | bytes 17760256 | tf_op jit(solution)/shard_map/dot_general | solution.py:592
  398.3 14.5 %convolution_convert_fusion = bf16[2816,2048]{1,0:T(8,128)(2,1)} fusion(bf16[640,1408]{1,0:T(8,128)(2,1)} %get-tuple-element.84, bf16[640,1408]{1,0:T(8,128)(2,1)} %copy-done.83, bf16[160,2048]{1,0:T(8,128)(2,1)} %collective-permute-done.29, bf16[160,2048]{1,0:T(8,128)(2,1)} %copy-done.79, bf16[160,2048]{1,0:T(8,128)(2,1)} %copy-done.78, ...), kind=kOutput, calls=%fused_computation | convolution fusion | flops 7405436928 | bytes 17760256 | tf_op jit(solution)/shard_map/dot_general | solution.py:26
  412.8 19.8 %collective-permute-done.58 = bf16[160,2048]{1,0:T(8,128)(2,1)S(1)} collective-permute-done((bf16[160,2048]{1,0:T(8,128)(2,1)}, bf16[160,2048]{1,0:T(8,128)(2,1)S(1)}, u32[]{:S(2)}, u32[]{:S(2)}) %collective-permute-start.58) | collective-permute-done | bytes 655392 | tf_op jit(solution)/shard_map/ppermute | solution.py:63
  432.6 14.2 %collective-permute-done.59 = bf16[160,2048]{1,0:T(8,128)(2,1)S(1)} collective-permute-done((bf16[160,2048]{1,0:T(8,128)(2,1)}, bf16[160,2048]{1,0:T(8,128)(2,1)S(1)}, u32[]{:S(2)}, u32[]{:S(2)}) %collective-permute-start.59) | collective-permute-done | bytes 655392 | tf_op jit(solution)/shard_map/ppermute | solution.py:63
  453.0 7.5 convolution_convert_fusion.1
  476.0 13.9 %collective-permute-done.62 = bf16[160,2048]{1,0:T(8,128)(2,1)} collective-permute-done((bf16[160,2048]{1,0:T(8,128)(2,1)}, bf16[160,2048]{1,0:T(8,128)(2,1)}, u32[]{:S(2)}, u32[]{:S(2)}) %collective-permute-start.62) | collective-permute-done | bytes 655392 | tf_op jit(solution)/shard_map/ppermute | solution.py:63
  506.8 16.0 %shard_map.265 = f32[8,4,8,256]{3,2,1,0:T(8,128)} custom-call(f32[4,8,256]{2,1,0:T(8,128)} %copy-done.16), custom_call_target="tpu_custom_call" | custom-call | tf_op jit(solution)/shard_map/pallas_call | solution.py:110
  527.0 8.6 %adjoints.1 = (bf16[640,1280]{1,0:T(8,128)(2,1)}, f32[8,256]{1,0:T(8,128)S(1)}, f32[8,256]{1,0:T(8,128)S(1)}) custom-call(s32[36]{0:T(128)S(1)} %pad_add_fusion.1.ints, f32[32,8,256]{2,1,0:T(8,128)S(1)} %bitcast.142, f32[32,8,256]{2,1,0:T(8,128)S(1)} %bitcast.143, f32[2,640,128]{2,1,0:T(8,128)S(1)} %copy-done.4, f32[2,640,128]{2,1,0:T(8,128)S(1)} %copy-done.6, ...), custom_call_target="tpu_custom_call" | custom-call | flops 20000000 | bytes 12000000 | tf_op jit(solution)/shard_map/adjoints/pallas_call | solution.py:636
  572.9 11.5 %collective-permute-done.68 = bf16[160,2048]{1,0:T(8,128)(2,1)} collective-permute-done((bf16[160,2048]{1,0:T(8,128)(2,1)}, bf16[160,2048]{1,0:T(8,128)(2,1)}, u32[]{:S(2)}, u32[]{:S(2)}) %collective-permute-start.68) | collective-permute-done | bytes 655392 | tf_op jit(solution)/shard_map/ppermute | solution.py:63
  589.0 10.7 %shard_map.266 = f32[32,8,128]{2,1,0:T(8,128)} custom-call(f32[32,8,128]{2,1,0:T(8,128)} %bitcast.165), custom_call_target="tpu_custom_call" | custom-call | tf_op jit(solution)/shard_map/pallas_call | solution.py:150
  607.9 9.0 %collective-permute-done.74 = bf16[2,2,2,64,512]{4,3,2,1,0:T(8,128)(2,1)S(1)} collective-permute-done((bf16[2,2,2,64,512]{4,3,2,1,0:T(8,128)(2,1)S(1)}, bf16[2,2,2,64,512]{4,3,2,1,0:T(8,128)(2,1)S(1)}, u32[]{:S(2)}, u32[]{:S(2)}) %collective-permute-start.74) | collective-permute-done | bytes 524320 | tf_op jit(solution)/shard_map/ppermute | solution.py:63
  623.6 8.0 %collective-permute-done.75 = bf16[2,2,64,512]{3,2,1,0:T(8,128)(2,1)S(1)} collective-permute-done((bf16[2,2,64,512]{3,2,1,0:T(8,128)(2,1)S(1)}, bf16[2,2,64,512]{3,2,1,0:T(8,128)(2,1)S(1)}, u32[]{:S(2)}, u32[]{:S(2)}) %collective-permute-start.75) | collective-permute-done | bytes 262176 | tf_op jit(solution)/shard_map/ppermute | solution.py:63
  661.1 24.1 %collective-permute-done.83 = bf16[352,2048]{1,0:T(8,128)(2,1)} collective-permute-done((bf16[352,2048]{1,0:T(8,128)(2,1)}, bf16[352,2048]{1,0:T(8,128)(2,1)}, u32[]{:S(2)}, u32[]{:S(2)}) %collective-permute-start.83) | collective-permute-done | bytes 1441824 | tf_op jit(solution)/shard_map/ppermute | solution.py:63
  689.4 26.7 %collective-permute-done.80 = bf16[352,2048]{1,0:T(8,128)(2,1)} collective-permute-done((bf16[352,2048]{1,0:T(8,128)(2,1)}, bf16[352,2048]{1,0:T(8,128)(2,1)}, u32[]{:S(2)}, u32[]{:S(2)}) %collective-permute-start.80) | collective-permute-done | bytes 1441824 | tf_op jit(solution)/shard_map/ppermute | solution.py:63
  721.6 22.5 %collective-permute-done.70 = bf16[2,160,2048]{2,1,0:T(8,128)(2,1)S(1)} collective-permute-done((bf16[2,160,2048]{2,1,0:T(8,128)(2,1)S(1)}, bf16[2,160,2048]{2,1,0:T(8,128)(2,1)S(1)}, u32[]{:S(2)}, u32[]{:S(2)}) %collective-permute-start.70) | collective-permute-done | bytes 1310752 | tf_op jit(solution)/shard_map/ppermute | solution.py:63
  748.2 22.9 %collective-permute-done.81 = bf16[176,2048]{1,0:T(8,128)(2,1)S(1)} collective-permute-done((bf16[176,2048]{1,0:T(8,128)(2,1)S(1)}, bf16[176,2048]{1,0:T(8,128)(2,1)S(1)}, u32[]{:S(2)}, u32[]{:S(2)}) %collective-permute-start.81) | collective-permute-done | bytes 720928 | tf_op jit(solution)/shard_map/ppermute | solution.py:63
  772.4 12.8 %collective-permute-done.71 = bf16[160,2048]{1,0:T(8,128)(2,1)S(1)} collective-permute-done((bf16[160,2048]{1,0:T(8,128)(2,1)S(1)}, bf16[160,2048]{1,0:T(8,128)(2,1)S(1)}, u32[]{:S(2)}, u32[]{:S(2)}) %collective-permute-start.71) | collective-permute-done | bytes 655392 | tf_op jit(solution)/shard_map/ppermute | solution.py:63
  (554 shorter events, 336.7 us)
Async XLA Ops:
  0.6 92.6 %collective-permute-start = (bf16[160,2048]{1,0:T(8,128)(2,1)}, bf16[160,2048]{1,0:T(8,128)(2,1)}, u32[]{:S(2)}, u32[]{:S(2)}) collective-permute-start(bf16[160,2048]{1,0:T(8,128)(2,1)} %param.16), channel_id=1, source_target_pairs={{0,2},{1,3},{2,0},{3,1},{4,6},{5,7},{6,4},{7,5},{8,10},{9,11},{10,... | collective-permute-start | bytes 1966088 | tf_op jit(solution)/shard_map/ppermute | solution.py:63
  2.8 92.4 %collective-permute-start.1 = (bf16[160,2048]{1,0:T(8,128)(2,1)}, bf16[160,2048]{1,0:T(8,128)(2,1)}, u32[]{:S(2)}, u32[]{:S(2)}) collective-permute-start(bf16[160,2048]{1,0:T(8,128)(2,1)} %param.16), channel_id=1, source_target_pairs={{0,8},{1,9},{2,10},{3,11},{4,12},{5,13},{6,14},{7,15},{8,0},{9,1},... | collective-permute-start | bytes 1966088 | tf_op jit(solution)/shard_map/ppermute | solution.py:63
  8.2 37.3 %collective-permute-start.16 = (bf16[64,512]{1,0:T(8,128)(2,1)}, bf16[64,512]{1,0:T(8,128)(2,1)}, u32[]{:S(2)}, u32[]{:S(2)}) collective-permute-start(bf16[64,512]{1,0:T(8,128)(2,1)} %get-tuple-element.113), channel_id=1, source_target_pairs={{0,10},{1,11},{2,8},{3,9},{4,14},{5,15},{6,12},{7,13},{8,2},{9,3},... | collective-permute-start | bytes 196616 | tf_op jit(solution)/shard_map/ppermute | solution.py:63
  40.4 55.9 %collective-permute-start.2 = (bf16[160,2048]{1,0:T(8,128)(2,1)S(1)}, bf16[160,2048]{1,0:T(8,128)(2,1)S(1)}, u32[]{:S(2)}, u32[]{:S(2)}) collective-permute-start(bf16[160,2048]{1,0:T(8,128)(2,1)S(1)} %copy-done.26), channel_id=1, source_target_pairs={{0,10},{1,11},{2,8},{3,9},{4,14},{5,15},{6,12},{7,13},{8,2},{9,3},... | collective-permute-start | bytes 1966088 | tf_op jit(solution)/shard_map/ppermute | solution.py:63
  93.2 48.5 %collective-permute-start.7 = (bf16[160,2048]{1,0:T(8,128)(2,1)S(1)}, bf16[160,2048]{1,0:T(8,128)(2,1)S(1)}, u32[]{:S(2)}, u32[]{:S(2)}) collective-permute-start(bf16[160,2048]{1,0:T(8,128)(2,1)S(1)} %pad_maximum_fusion.8), channel_id=1, source_target_pairs={{0,1},{1,0},{2,3},{3,2},{4,5},{5,4},{6,7},{7,6},{8,9},{9,8},{10,11... | collective-permute-start | bytes 1966088 | tf_op jit(solution)/shard_map/ppermute | solution.py:63
  108.9 64.0 %collective-permute-start.30 = (bf16[176,2048]{1,0:T(8,128)(2,1)}, bf16[176,2048]{1,0:T(8,128)(2,1)}, u32[]{:S(2)}, u32[]{:S(2)}) collective-permute-start(bf16[176,2048]{1,0:T(8,128)(2,1)} %convert_element_type.298), channel_id=1, source_target_pairs={{0,16},{1,17},{2,18},{3,19},{4,20},{5,21},{6,22},{7,23},{8,24},{9,... | collective-permute-start | bytes 2162696 | tf_op jit(solution)/shard_map/ppermute | solution.py:63
  108.9 68.3 %collective-permute-start.31 = (bf16[176,2048]{1,0:T(8,128)(2,1)}, bf16[176,2048]{1,0:T(8,128)(2,1)}, u32[]{:S(2)}, u32[]{:S(2)}) collective-permute-start(bf16[176,2048]{1,0:T(8,128)(2,1)} %convert_element_type.298), channel_id=1, source_target_pairs={{0,4},{1,5},{2,6},{3,7},{4,0},{5,1},{6,2},{7,3},{8,12},{9,13},{10,... | collective-permute-start | bytes 2162696 | tf_op jit(solution)/shard_map/ppermute | solution.py:63
  145.2 95.0 %collective-permute-start.33 = (bf16[176,2048]{1,0:T(8,128)(2,1)}, bf16[176,2048]{1,0:T(8,128)(2,1)}, u32[]{:S(2)}, u32[]{:S(2)}) collective-permute-start(bf16[176,2048]{1,0:T(8,128)(2,1)} %convert_element_type.298), channel_id=1, source_target_pairs={{0,1},{1,0},{2,3},{3,2},{4,5},{5,4},{6,7},{7,6},{8,9},{9,8},{10,11... | collective-permute-start | bytes 2162696 | tf_op jit(solution)/shard_map/ppermute | solution.py:63
  172.9 62.0 %collective-permute-start.37 = (bf16[176,2048]{1,0:T(8,128)(2,1)}, bf16[176,2048]{1,0:T(8,128)(2,1)}, u32[]{:S(2)}, u32[]{:S(2)}) collective-permute-start(bf16[176,2048]{1,0:T(8,128)(2,1)} %convert_element_type.299), channel_id=1, source_target_pairs={{0,16},{1,17},{2,18},{3,19},{4,20},{5,21},{6,22},{7,23},{8,24},{9,... | collective-permute-start | bytes 2162696 | tf_op jit(solution)/shard_map/ppermute | solution.py:63
  174.3 63.0 %collective-permute-start.32 = (bf16[176,2048]{1,0:T(8,128)(2,1)}, bf16[176,2048]{1,0:T(8,128)(2,1)}, u32[]{:S(2)}, u32[]{:S(2)}) collective-permute-start(bf16[176,2048]{1,0:T(8,128)(2,1)} %collective-permute-done.30), channel_id=1, source_target_pairs={{0,4},{1,5},{2,6},{3,7},{4,0},{5,1},{6,2},{7,3},{8,12},{9,13},{10,... | collective-permute-start | bytes 2162696 | tf_op jit(solution)/shard_map/ppermute | solution.py:63
  240.2 42.7 %collective-permute-start.26 = (bf16[160,2048]{1,0:T(8,128)(2,1)S(1)}, bf16[160,2048]{1,0:T(8,128)(2,1)S(1)}, u32[]{:S(2)}, u32[]{:S(2)}) collective-permute-start(bf16[160,2048]{1,0:T(8,128)(2,1)S(1)} %copy-done.54), channel_id=1, source_target_pairs={{0,10},{1,11},{2,8},{3,9},{4,14},{5,15},{6,12},{7,13},{8,2},{9,3},... | collective-permute-start | bytes 1966088 | tf_op jit(solution)/shard_map/ppermute | solution.py:63
  243.2 48.6 %collective-permute-start.38 = (bf16[176,2048]{1,0:T(8,128)(2,1)}, bf16[176,2048]{1,0:T(8,128)(2,1)S(1)}, u32[]{:S(2)}, u32[]{:S(2)}) collective-permute-start(bf16[176,2048]{1,0:T(8,128)(2,1)} %convert_element_type.299), channel_id=1, source_target_pairs={{0,4},{1,5},{2,6},{3,7},{4,0},{5,1},{6,2},{7,3},{8,12},{9,13},{10,... | collective-permute-start | bytes 2162696 | tf_op jit(solution)/shard_map/ppermute | solution.py:63
  246.4 59.2 %collective-permute-start.40 = (bf16[176,2048]{1,0:T(8,128)(2,1)}, bf16[176,2048]{1,0:T(8,128)(2,1)S(1)}, u32[]{:S(2)}, u32[]{:S(2)}) collective-permute-start(bf16[176,2048]{1,0:T(8,128)(2,1)} %convert_element_type.299), channel_id=1, source_target_pairs={{0,1},{1,0},{2,3},{3,2},{4,5},{5,4},{6,7},{7,6},{8,9},{9,8},{10,11... | collective-permute-start | bytes 2162696 | tf_op jit(solution)/shard_map/ppermute | solution.py:63
  251.5 56.3 %collective-permute-start.44 = (bf16[176,2048]{1,0:T(8,128)(2,1)S(1)}, bf16[176,2048]{1,0:T(8,128)(2,1)S(1)}, u32[]{:S(2)}, u32[]{:S(2)}) collective-permute-start(bf16[176,2048]{1,0:T(8,128)(2,1)S(1)} %copy-done.39), channel_id=1, source_target_pairs={{0,16},{1,17},{2,18},{3,19},{4,20},{5,21},{6,22},{7,23},{8,24},{9,... | collective-permute-start | bytes 2162696 | tf_op jit(solution)/shard_map/ppermute | solution.py:63
  254.3 56.5 %collective-permute-start.45 = (bf16[176,2048]{1,0:T(8,128)(2,1)S(1)}, bf16[176,2048]{1,0:T(8,128)(2,1)S(1)}, u32[]{:S(2)}, u32[]{:S(2)}) collective-permute-start(bf16[176,2048]{1,0:T(8,128)(2,1)S(1)} %copy-done.39), channel_id=1, source_target_pairs={{0,4},{1,5},{2,6},{3,7},{4,0},{5,1},{6,2},{7,3},{8,12},{9,13},{10,... | collective-permute-start | bytes 2162696 | tf_op jit(solution)/shard_map/ppermute | solution.py:63
  312.7 39.9 %collective-permute-start.47 = (bf16[176,2048]{1,0:T(8,128)(2,1)S(1)}, bf16[176,2048]{1,0:T(8,128)(2,1)S(1)}, u32[]{:S(2)}, u32[]{:S(2)}) collective-permute-start(bf16[176,2048]{1,0:T(8,128)(2,1)S(1)} %copy-done.39), channel_id=1, source_target_pairs={{0,1},{1,0},{2,3},{3,2},{4,5},{5,4},{6,7},{7,6},{8,9},{9,8},{10,11... | collective-permute-start | bytes 2162696 | tf_op jit(solution)/shard_map/ppermute | solution.py:63
  388.7 58.9 %collective-permute-start.51 = (bf16[160,2048]{1,0:T(8,128)(2,1)}, bf16[160,2048]{1,0:T(8,128)(2,1)S(1)}, u32[]{:S(2)}, u32[]{:S(2)}) collective-permute-start(bf16[160,2048]{1,0:T(8,128)(2,1)} %get-tuple-element.96), channel_id=1, source_target_pairs={{0,2},{1,3},{2,0},{3,1},{4,6},{5,7},{6,4},{7,5},{8,10},{9,11},{10,... | collective-permute-start | bytes 1966088 | tf_op jit(solution)/shard_map/ppermute | solution.py:63
  389.8 57.8 %collective-permute-start.52 = (bf16[160,2048]{1,0:T(8,128)(2,1)}, bf16[160,2048]{1,0:T(8,128)(2,1)}, u32[]{:S(2)}, u32[]{:S(2)}) collective-permute-start(bf16[160,2048]{1,0:T(8,128)(2,1)} %get-tuple-element.98), channel_id=1, source_target_pairs={{0,8},{1,9},{2,10},{3,11},{4,12},{5,13},{6,14},{7,15},{8,0},{9,1},... | collective-permute-start | bytes 1966088 | tf_op jit(solution)/shard_map/ppermute | solution.py:63
  390.1 57.5 %collective-permute-start.53 = (bf16[160,2048]{1,0:T(8,128)(2,1)}, bf16[160,2048]{1,0:T(8,128)(2,1)}, u32[]{:S(2)}, u32[]{:S(2)}) collective-permute-start(bf16[160,2048]{1,0:T(8,128)(2,1)} %get-tuple-element.97), channel_id=1, source_target_pairs={{0,10},{1,11},{2,8},{3,9},{4,14},{5,15},{6,12},{7,13},{8,2},{9,3},... | collective-permute-start | bytes 1966088 | tf_op jit(solution)/shard_map/ppermute | solution.py:63
  391.3 41.3 %collective-permute-start.58 = (bf16[160,2048]{1,0:T(8,128)(2,1)}, bf16[160,2048]{1,0:T(8,128)(2,1)S(1)}, u32[]{:S(2)}, u32[]{:S(2)}) collective-permute-start(bf16[160,2048]{1,0:T(8,128)(2,1)} %get-tuple-element.95), channel_id=1, source_target_pairs={{0,8},{1,9},{2,10},{3,11},{4,12},{5,13},{6,14},{7,15},{8,0},{9,1},... | collective-permute-start | bytes 1966088 | tf_op jit(solution)/shard_map/ppermute | solution.py:63
  397.5 49.3 %collective-permute-start.59 = (bf16[160,2048]{1,0:T(8,128)(2,1)}, bf16[160,2048]{1,0:T(8,128)(2,1)S(1)}, u32[]{:S(2)}, u32[]{:S(2)}) collective-permute-start(bf16[160,2048]{1,0:T(8,128)(2,1)} %get-tuple-element.94), channel_id=1, source_target_pairs={{0,10},{1,11},{2,8},{3,9},{4,14},{5,15},{6,12},{7,13},{8,2},{9,3},... | collective-permute-start | bytes 1966088 | tf_op jit(solution)/shard_map/ppermute | solution.py:63
  470.6 146.7 %collective-permute-start.85 = (bf16[704,2048]{1,0:T(8,128)(2,1)}, bf16[704,2048]{1,0:T(8,128)(2,1)}, u32[]{:S(2)}, u32[]{:S(2)}) collective-permute-start(bf16[704,2048]{1,0:T(8,128)(2,1)} %slice.431), channel_id=1, source_target_pairs={{0,1},{1,0},{2,3},{3,2},{4,5},{5,4},{6,7},{7,6},{8,9},{9,8},{10,11... | collective-permute-start | bytes 8650760 | tf_op jit(solution)/shard_map/ppermute | solution.py:63
  475.0 158.1 %collective-permute-start.79 = (bf16[704,2048]{1,0:T(8,128)(2,1)}, bf16[704,2048]{1,0:T(8,128)(2,1)}, u32[]{:S(2)}, u32[]{:S(2)}) collective-permute-start(bf16[704,2048]{1,0:T(8,128)(2,1)} %get-tuple-element.82), channel_id=1, source_target_pairs={{0,1},{1,0},{2,3},{3,2},{4,5},{5,4},{6,7},{7,6},{8,9},{9,8},{10,11... | collective-permute-start | bytes 8650760 | tf_op jit(solution)/shard_map/ppermute | solution.py:63
  569.5 63.6 %collective-permute-start.82 = (bf16[704,2048]{1,0:T(8,128)(2,1)}, bf16[704,2048]{1,0:T(8,128)(2,1)}, u32[]{:S(2)}, u32[]{:S(2)}) collective-permute-start(bf16[704,2048]{1,0:T(8,128)(2,1)} %get-tuple-element.81), channel_id=1, source_target_pairs={{0,1},{1,0},{2,3},{3,2},{4,5},{5,4},{6,7},{7,6},{8,9},{9,8},{10,11... | collective-permute-start | bytes 8650760 | tf_op jit(solution)/shard_map/ppermute | solution.py:63
  584.4 70.0 %collective-permute-start.69 = (bf16[2,2,160,2048]{3,2,0,1:T(8,128)(2,1)}, bf16[2,2,160,2048]{3,2,0,1:T(8,128)(2,1)}, u32[]{:S(2)}, u32[]{:S(2)}) collective-permute-start(bf16[2,2,160,2048]{3,2,0,1:T(8,128)(2,1)} %dynamic-slice_bitcast_fusion), channel_id=1, source_target_pairs={{0,1},{1,0},{2,3},{3,2},{4,5},{5,4},{6,7},{7,6},{8,9},{9,8},{10,11... | collective-permute-start | bytes 7864328 | tf_op jit(solution)/shard_map/ppermute | solution.py:63
  638.8 46.4 %collective-permute-start.83 = (bf16[352,2048]{1,0:T(8,128)(2,1)}, bf16[352,2048]{1,0:T(8,128)(2,1)}, u32[]{:S(2)}, u32[]{:S(2)}) collective-permute-start(bf16[352,2048]{1,0:T(8,128)(2,1)} %slice.427), channel_id=1, source_target_pairs={{0,4},{1,5},{2,6},{3,7},{4,0},{5,1},{6,2},{7,3},{8,12},{9,13},{10,... | collective-permute-start | bytes 4325384 | tf_op jit(solution)/shard_map/ppermute | solution.py:63
  640.9 75.2 %collective-permute-start.80 = (bf16[352,2048]{1,0:T(8,128)(2,1)}, bf16[352,2048]{1,0:T(8,128)(2,1)}, u32[]{:S(2)}, u32[]{:S(2)}) collective-permute-start(bf16[352,2048]{1,0:T(8,128)(2,1)} %slice.421), channel_id=1, source_target_pairs={{0,4},{1,5},{2,6},{3,7},{4,0},{5,1},{6,2},{7,3},{8,12},{9,13},{10,... | collective-permute-start | bytes 4325384 | tf_op jit(solution)/shard_map/ppermute | solution.py:63
  658.2 85.9 %collective-permute-start.70 = (bf16[2,160,2048]{2,1,0:T(8,128)(2,1)S(1)}, bf16[2,160,2048]{2,1,0:T(8,128)(2,1)S(1)}, u32[]{:S(2)}, u32[]{:S(2)}) collective-permute-start(bf16[2,160,2048]{2,1,0:T(8,128)(2,1)S(1)} %dynamic-slice_bitcast_fusion.1), channel_id=1, source_target_pairs={{0,4},{1,5},{2,6},{3,7},{4,0},{5,1},{6,2},{7,3},{8,12},{9,13},{10,... | collective-permute-start | bytes 3932168 | tf_op jit(solution)/shard_map/ppermute | solution.py:63
  661.0 59.3 %collective-permute-start.87 = (bf16[176,2048]{1,0:T(8,128)(2,1)S(1)}, bf16[176,2048]{1,0:T(8,128)(2,1)S(1)}, u32[]{:S(2)}, u32[]{:S(2)}) collective-permute-start(bf16[176,2048]{1,0:T(8,128)(2,1)S(1)} %slice.435), channel_id=1, source_target_pairs={{0,16},{1,17},{2,18},{3,19},{4,20},{5,21},{6,22},{7,23},{8,24},{9,... | collective-permute-start | bytes 2162696 | tf_op jit(solution)/shard_map/ppermute | solution.py:63
  687.2 59.7 %collective-permute-start.84 = (bf16[176,2048]{1,0:T(8,128)(2,1)S(1)}, bf16[176,2048]{1,0:T(8,128)(2,1)S(1)}, u32[]{:S(2)}, u32[]{:S(2)}) collective-permute-start(bf16[176,2048]{1,0:T(8,128)(2,1)S(1)} %slice.429), channel_id=1, source_target_pairs={{0,16},{1,17},{2,18},{3,19},{4,20},{5,21},{6,22},{7,23},{8,24},{9,... | collective-permute-start | bytes 2162696 | tf_op jit(solution)/shard_map/ppermute | solution.py:63
  718.1 53.0 %collective-permute-start.81 = (bf16[176,2048]{1,0:T(8,128)(2,1)S(1)}, bf16[176,2048]{1,0:T(8,128)(2,1)S(1)}, u32[]{:S(2)}, u32[]{:S(2)}) collective-permute-start(bf16[176,2048]{1,0:T(8,128)(2,1)S(1)} %slice.423), channel_id=1, source_target_pairs={{0,16},{1,17},{2,18},{3,19},{4,20},{5,21},{6,22},{7,23},{8,24},{9,... | collective-permute-start | bytes 2162696 | tf_op jit(solution)/shard_map/ppermute | solution.py:63
  744.7 40.5 %collective-permute-start.71 = (bf16[160,2048]{1,0:T(8,128)(2,1)S(1)}, bf16[160,2048]{1,0:T(8,128)(2,1)S(1)}, u32[]{:S(2)}, u32[]{:S(2)}) collective-permute-start(bf16[160,2048]{1,0:T(8,128)(2,1)S(1)} %dynamic-slice_bitcast_fusion.3), channel_id=1, source_target_pairs={{0,16},{1,17},{2,18},{3,19},{4,20},{5,21},{6,22},{7,23},{8,24},{9,... | collective-permute-start | bytes 1966088 | tf_op jit(solution)/shard_map/ppermute | solution.py:63
  (147 other events, 2270.7 us)

commit v2 on v1

--- a/solution.py
+++ b/solution.py
@@ -39,6 +39,7 @@
             self.ybits.append(bit)
             bit *= 2
         self.wbits = [self.ZH] + self.ybits + [self.C]
+        self.rbits = [self.C] + self.ybits + [self.ZH]
         self.tmasks = [0, self.X, self.ZL, self.ZL | self.X]
         self.wmasks = [0]
         for bit in self.wbits:
@@ -120,44 +121,337 @@
     )(value)
 
 
-def exchange_kernel(lay, masks, in_ref, out_ref, send_sems, recv_sems):
-    me = lax.axis_index("dp")
-    peers = [lay.flip(me, m) for m in masks]
-    barrier = pltpu.get_barrier_semaphore()
-    for peer in peers:
-        pl.semaphore_signal(barrier, inc=1, device_id=(peer,), device_id_type=MESH)
-    pl.semaphore_wait(barrier, len(peers))
-    copies = []
-    for i, peer in enumerate(peers):
+class Net:
+    def __init__(self, lay, peers, send_sems, recv_sems, local_sems):
+        self.lay, self.send_sems, self.recv_sems, self.local_sems = lay, send_sems, recv_sems, local_sems
+        self.me = lax.axis_index("dp")
+        self.used, self.used_local, self.open, self.local = 0, 0, [], []
+        barrier = pltpu.get_barrier_semaphore()
+        for mask in peers:
+            pl.semaphore_signal(
+                barrier, inc=1, device_id=(lay.flip(self.me, mask),), device_id_type=MESH
+            )
+        pl.semaphore_wait(barrier, len(peers))
+
+    def put(self, src, dst, mask):
         copy = pltpu.make_async_remote_copy(
-            src_ref=in_ref.at[peer],
-            dst_ref=out_ref.at[me],
-            send_sem=send_sems.at[i],
-            recv_sem=recv_sems.at[i],
-            device_id=(peer,),
+            src_ref=src,
+            dst_ref=dst,
+            send_sem=self.send_sems.at[self.used],
+            recv_sem=self.recv_sems.at[self.used],
+            device_id=(self.lay.flip(self.me, mask),),
             device_id_type=MESH,
         )
         copy.start()
-        copies.append(copy)
-    out_ref[me] = in_ref[me]
+        self.used += 1
+        self.open.append(copy)
+        return copy
+
+    def load(self, src, dst):
+        copy = pltpu.make_async_copy(src, dst, self.local_sems.at[self.used_local])
+        copy.start()
+        self.used_local += 1
+        return copy
+
+    def keep(self, src, dst):
+        self.local.append(self.load(src, dst))
+
+    def finish(self):
+        for copy in self.open:
+            copy.wait_send()
+        for copy in self.local:
+            copy.wait()
+
+
+class WeightGather:
+    def __init__(self, net, own, place):
+        self.net, self.own, self.place = net, own, place
+        self.bits = net.lay.wbits
+        self.pending = {}
+
+    def start(self):
+        for bit in self.bits:
+            self.pending[bit] = self.net.put(self.own, self.place(self.net.me), bit)
+        self.net.keep(self.own, self.place(self.net.me))
+
+    def masks(self):
+        out = [0]
+        for bit in self.bits[:-1]:
+            out = out + [m | bit for m in out]
+        return sorted(out[1:], key=lambda m: (bin(m).count("1"), -m))
+
+    def forward(self, mask):
+        self.pending[mask].wait_recv()
+        last = max(i for i, bit in enumerate(self.bits) if mask & bit)
+        here = self.place(self.net.lay.flip(self.net.me, mask))
+        for bit in self.bits[last + 1 :]:
+            self.pending[mask | bit] = self.net.put(here, here, bit)
+
+    def end(self):
+        for mask, copy in self.pending.items():
+            if mask & self.bits[-1]:
+                copy.wait_recv()
+
+
+def token_gather(net, own, out):
+    lay = net.lay
+    net.keep(own, out.at[0])
+    return [net.put(own, out.at[j], m) for j, m in enumerate(lay.tmasks) if j]
+
+
+def token_scatter(net, blocks, out):
+    return [net.put(blocks.at[j], out.at[j - 1], m) for j, m in enumerate(net.lay.tmasks) if j]
+
+
+def arrived(copies):
     for copy in copies:
-        copy.wait()
-
-
-def small_exchange(lay, value, collective_id):
-    masks = list(range(1, lay.n))
-    vmem = pl.BlockSpec(memory_space=pltpu.VMEM)
+        copy.wait_recv()
+
+
+def net_call(body, lay, values, outs, copies, local, collective_id, name, scratch=()):
+    hbm = pl.BlockSpec(memory_space=pl.ANY)
     return pl.pallas_call(
-        partial(exchange_kernel, lay, masks),
-        out_shape=jax.ShapeDtypeStruct(value.shape, value.dtype),
-        in_specs=[vmem],
-        out_specs=vmem,
+        body,
+        out_shape=tuple(jax.ShapeDtypeStruct(s, d) for s, d in outs),
+        in_specs=[hbm] * len(values),
+        out_specs=tuple(hbm for _ in outs),
         scratch_shapes=[
-            pltpu.SemaphoreType.DMA((len(masks),)),
-            pltpu.SemaphoreType.DMA((len(masks),)),
+            *scratch,
+            pltpu.SemaphoreType.DMA((copies,)),
+            pltpu.SemaphoreType.DMA((copies,)),
+            pltpu.SemaphoreType.DMA((local,)),
         ],
-        compiler_params=pltpu.CompilerParams(collective_id=collective_id, has_side_effects=True),
-    )(value)
+        compiler_params=pltpu.CompilerParams(
+            collective_id=collective_id,
+            has_side_effects=True,
+            vmem_limit_bytes=(56 << 20) if scratch else None,
+        ),
+        name=name,
+    )(*values)
+
+
+def w_slot(lay, device):
+    zhi, _, y, _, c = lay.parts(device)
+    return (zhi * lay.Y + y) * 2 + c
+
+
+def f_slot(lay, device):
+    zhi, _, y, _, c = lay.parts(device)
+    return (y * 2 + c) * 2 + zhi
+
+
+def t_slot(lay, device):
+    _, zlo, _, x, _ = lay.parts(device)
+    return zlo * 2 + x
+
+
+def start_kernel(
+    lay, units, tok, cot, w_in, w_gate, w_forget, w_out, f_gate, pack,
+    tok_all, cot_all, mix_all, out_own, out_all, f_gate_all, every, send_sems, recv_sems, local_sems,
+):
+    n, W = lay.n, lay.n // 4
+    net = Net(lay, list(range(1, n)), send_sems, recv_sems, local_sems)
+    me = net.me
+
+    def region(base):
+        return lambda d: mix_all.at[pl.ds(base + w_slot(lay, d) * units, units)]
+
+    g_in = WeightGather(net, w_in, region(0))
+    g_gate = WeightGather(net, w_gate, region(W * units))
+    g_forget = WeightGather(
+        net, w_forget, lambda d: mix_all.at[pl.ds(2 * W * units + f_slot(lay, d), 1)]
+    )
+    g_out = WeightGather(net, out_own, lambda d: out_all.at[w_slot(lay, d)])
+    g_ffn = WeightGather(net, f_gate, lambda d: f_gate_all.at[w_slot(lay, d)])
+    g_in.start()
+    g_gate.start()
+    tok_in = token_gather(net, tok, tok_all)
+    mine = t_slot(lay, me)
+    own = net.load(w_out.at[mine], out_own.at[mine])
+    out_in = [
+        net.put(w_out.at[t_slot(lay, lay.flip(me, m))], out_own.at[mine], m) for m in lay.tmasks[1:]
+    ]
+    g_forget.start()
+    all_in = [net.put(pack, every.at[me], m) for m in range(1, n)]
+    net.keep(pack, every.at[me])
+    for mask in g_in.masks():
+        g_in.forward(mask)
+        g_gate.forward(mask)
+    for mask in g_forget.masks():
+        g_forget.forward(mask)
+    own.wait()
+    arrived(out_in)
+    g_out.start()
+    g_ffn.start()
+    arrived(tok_in)
+    cot_in = token_gather(net, cot, cot_all)
+    for mask in g_out.masks():
+        g_out.forward(mask)
+    for mask in g_ffn.masks():
+        g_ffn.forward(mask)
+    for gather in (g_in, g_gate, g_forget, g_out, g_ffn):
+        gather.end()
+    arrived(cot_in)
+    arrived(all_in)
+    net.finish()
+
+
+def group_peers(lay):
+    return lay.tmasks[1:] + lay.wbits
+
+
+def scatter_kernel(lay, blocks, small, weight, got, got_small, weight_all, send_sems, recv_sems, local_sems):
+    net = Net(lay, group_peers(lay), send_sems, recv_sems, local_sems)
+    gather = WeightGather(net, weight, lambda d: weight_all.at[w_slot(lay, d)])
+    waits = token_scatter(net, blocks, got) + token_scatter(net, small, got_small)
+    gather.start()
+    for mask in gather.masks():
+        gather.forward(mask)
+    gather.end()
+    arrived(waits)
+    net.finish()
+
+
+def gather_both_kernel(lay, own, weight, own_all, weight_all, send_sems, recv_sems, local_sems):
+    net = Net(lay, group_peers(lay), send_sems, recv_sems, local_sems)
+    gather = WeightGather(net, weight, lambda d: weight_all.at[w_slot(lay, d)])
+    waits = token_gather(net, own, own_all)
+    gather.start()
+    for mask in gather.masks():
+        gather.forward(mask)
+    gather.end()
+    arrived(waits)
+    net.finish()
+
+
+def add_rows(out, left, right):
+    rows = left.shape[0]
+    tile = 16 if rows % 16 == 0 else rows
+
+    def body(i, _):
+        at = pl.ds(pl.multiple_of(i * tile, tile), tile)
+        out[at, :] = (left[at, :].astype(F32) + right[at, :].astype(F32)).astype(out.dtype)
+        return 0
+
+    lax.fori_loop(0, rows // tile, body, 0)
+
+
+class WeightReduce:
+    def __init__(self, net, part, place, local, stages, total, out):
+        self.net, self.part, self.place = net, part, place
+        self.local, self.stages, self.total, self.out = local, stages, total, out
+        self.bits = net.lay.rbits
+        self.sent, self.waited = [], -1
+
+    def side(self, k):
+        return (self.net.me // self.bits[k]) % 2
+
+    def start(self):
+        at = self.side(0)
+        count = self.stages[0].shape[0]
+        self.sent = [
+            self.net.put(self.part.at[self.place(2 * i + 1 - at)], self.stages[0].at[i], self.bits[0])
+            for i in range(count)
+        ]
+        self.loads = [
+            self.net.load(self.part.at[self.place(2 * i + at)], self.local.at[i]) for i in range(count)
+        ]
+
+    def wait(self, k):
+        if self.waited < k:
+            arrived(self.sent)
+            self.waited = k
+
+    def add(self, k):
+        stage = self.stages[k]
+        count = stage.shape[0]
+        if k == 0:
+            for copy in self.loads:
+                copy.wait()
+        at = self.side(k)
+        mine = self.side(k + 1) if count > 1 else 0
+
+        def one(i):
+            old = self.local.at[i] if k == 0 else self.stages[k - 1].at[2 * i + at]
+            if count == 1:
+                add_rows(self.total, stage.at[i], old)
+            else:
+                add_rows(stage.at[i], stage.at[i], old)
+
+        if count == 1:
+            one(0)
+        else:
+            for i in range(count // 2):
+                one(2 * i + 1 - mine)
+            for i in range(count // 2):
+                one(2 * i + mine)
+
+    def send(self, k):
+        at = self.side(k)
+        self.sent = [
+            self.net.put(self.stages[k - 1].at[2 * i + 1 - at], self.stages[k].at[i], self.bits[k])
+            for i in range(self.stages[k].shape[0])
+        ]
+
+    def store(self):
+        if self.out is not None:
+            self.net.keep(self.total, self.out)
+
+
+def reduce_kernel(lay, n_parts, *refs):
+    W = lay.n // 4
+    depth = len(lay.rbits)
+    parts, refs = refs[:n_parts], refs[n_parts:]
+    (du, mixed, vectors), refs = refs[:3], refs[3:]
+    outs, refs = refs[: n_parts - 1], refs[n_parts - 1 :]
+    (out_cols, got_du, got_mixed, all_vectors), refs = refs[:4], refs[4:]
+    scratch, (send_sems, recv_sems, local_sems) = refs[:-3], refs[-3:]
+    net = Net(lay, list(range(1, lay.n)), send_sems, recv_sems, local_sems)
+    me = net.me
+    jobs = []
+    for i, part in enumerate(parts):
+        local, *stages = scratch[i * (depth + 2) : i * (depth + 2) + depth + 1]
+        total = scratch[i * (depth + 2) + depth + 1]
+        place = (lambda k: k) if i else (lambda k: ((k // 2) % lay.Y * 2 + k % 2) * 2 + k // (2 * lay.Y))
+        out = None if i == 1 else outs[i - (i > 1)]
+        jobs.append(WeightReduce(net, part, place, local, stages, total, out))
+    waits = token_scatter(net, du, got_du)
+    for job in jobs:
+        job.start()
+    waits += [net.put(vectors.at[lay.flip(me, m)], all_vectors.at[me], m) for m in range(1, lay.n)]
+    net.keep(vectors.at[me], all_vectors.at[me])
+
+    def finish(job, i):
+        job.store()
+        if i == 1:
+            rows = job.total.shape[0] // 4
+            mine = t_slot(lay, me)
+
+            def cut(slot):
+                return job.total.at[pl.ds(pl.multiple_of(slot * rows, rows), rows)]
+
+            net.keep(cut(mine), out_cols.at[mine])
+            for m in lay.tmasks[1:]:
+                waits.append(net.put(cut(t_slot(lay, lay.flip(me, m))), out_cols.at[mine], m))
+
+    for tick in range(n_parts + depth - 1):
+        for k in range(depth):
+            i = tick - k
+            valid = 0 <= i < n_parts
+            if valid:
+                jobs[i].wait(k)
+                jobs[i].add(k)
+            if k + 1 < depth:
+                if 0 <= i - 1 < n_parts:
+                    jobs[i - 1].wait(k + 1)
+                if valid:
+                    jobs[i].send(k + 1)
+            elif valid:
+                finish(jobs[i], i)
+        if tick == 1:
+            waits += token_scatter(net, mixed, got_mixed)
+    arrived(waits)
+    net.finish()
 
 
 def sig(v):
@@ -287,7 +581,7 @@
                 at = lanes(part * half, h)
                 unit[rows, at] = (v * gain[0:1, at] * (g * sig(g))).astype(LOW)
                 square = square + jnp.sum(v * v, axis=1, keepdims=True)
-        squares[rows, :] = square
+        squares[rows, :] = jnp.broadcast_to(square, (ROWS, LANES))
         return 0
 
     lax.fori_loop(0, total // ROWS, finish, 0)
@@ -447,10 +741,6 @@
     total = 4 * length
     r_in, r_f = in_proj.shape[0], forget_proj.shape[0]
 
-    def w_slot(device):
-        zh, _, yy, _, cc = lay.parts(device)
-        return (zh * Y + yy) * 2 + cc
-
     indices = jnp.arange(n, dtype=jnp.int32)
     order = jnp.sum(jnp.where(block_deal[None, :] == indices[:, None], indices[None, :], 0), axis=1)
     t_devices = jnp.stack([lay.flip(me, m) for m in lay.tmasks])
@@ -459,7 +749,7 @@
     )
     o_parts = lay.parts(order)
     t_rel = ((o_parts[1] + zlo) % 2) * 2 + (o_parts[3] + x) % 2
-    ints = jnp.concatenate([w_slot(order) * 4 + t_rel, t_places]).astype(jnp.int32)
+    ints = jnp.concatenate([w_slot(lay, order) * 4 + t_rel, t_places]).astype(jnp.int32)
     offsets = jnp.cumsum(seq_lengths) - seq_lengths
     positions = (
         t_places[:, None] * length + jnp.arange(length, dtype=jnp.int32)[None, :]
@@ -470,7 +760,46 @@
     packed = jnp.concatenate([gain_mix, gain_ffn, gain_out, lower_bound, rotation])
     pack_rows = -(-packed.shape[0] // 128)
     packed = jnp.pad(packed, (0, 8 * 128 - packed.shape[0])).reshape(8, 128)
-    every = small_gather(lay, packed, list(range(n)), lambda d: d, n, 0)
+    forget_to = [(2 * e + b, b * (n // 2) + e) for e in range(n // 2) for b in range(2)]
+    forget_from = [(d, s) for s, d in forget_to]
+    forget_low = lax.ppermute(forget_proj.astype(LOW), "dp", forget_to)
+    out_cols = out_proj.astype(LOW).reshape(r_in, 2, 2, Y, 2, 2 * r_in)
+    out_cols = out_cols.transpose(2, 4, 0, 1, 3, 5).reshape(4, r_in, 2 * half)
+    units = r_in // r_f
+    r_ffn = ffn_gate.shape[0]
+    tok_all, cot_all, w_mix, _, w_out, w_ffn_gate, every = net_call(
+        partial(start_kernel, lay, units),
+        lay,
+        (
+            tokens,
+            cotangent,
+            in_proj.astype(LOW).reshape(units, r_f, width),
+            gate_proj.astype(LOW).reshape(units, r_f, width),
+            forget_low.reshape(1, r_f, width),
+            out_cols,
+            ffn_gate.astype(LOW),
+            packed,
+        ),
+        [
+            ((4, length, width), LOW),
+            ((4, length, width), LOW),
+            ((W * (2 * units + 1), r_f, width), LOW),
+            ((4, r_in, 2 * half), LOW),
+            ((W, 4, r_in, 2 * half), LOW),
+            ((W, r_ffn, width), LOW),
+            ((n, 8, 128), F32),
+        ],
+        5 * (W - 1) + 9 + n - 1,
+        16,
+        0,
+        "start",
+    )
+    tok_all = tok_all.reshape(total, width)
+    cot_all = cot_all.reshape(total, width)
+    w_mix = w_mix.reshape(5 * half, width)
+    w_out = w_out.reshape(2, Y, 2, 2, 2, r_in, 2 * half).transpose(0, 3, 1, 4, 2, 5, 6)
+    w_out = w_out.reshape(width, 2 * half)
+    w_ffn_gate = w_ffn_gate.reshape(W * r_ffn, width)
     every = every[:, :pack_rows, :].reshape(n, pack_rows * 128)
     g_mix = every[:, 0:r_in].reshape(1, width)
     g_ffn = every[:, r_in : 2 * r_in].reshape(1, width)
@@ -489,64 +818,11 @@
         [lower, jnp.cos(angle), jnp.sin(angle), jnp.zeros((5, half), F32)], axis=0
     )
 
-    forget_to = [(2 * e + b, b * (n // 2) + e) for e in range(n // 2) for b in range(2)]
-    forget_from = [(d, s) for s, d in forget_to]
-    forget_low = lax.ppermute(forget_proj.astype(LOW), "dp", forget_to)
-    tok_all = jnp.concatenate(lay.gather_t(tokens), axis=0)
-    out_cols = out_proj.astype(LOW).reshape(r_in, 2, 2, Y, 2, 2 * r_in)
-    out_cols = out_cols.transpose(2, 4, 0, 1, 3, 5).reshape(4, r_in, 2 * half)
-
-    def out_for(mask):
-        slot = ((zlo + (1 if mask & lay.ZL else 0)) % 2) * 2 + (x + (1 if mask & lay.X else 0)) % 2
-        return lax.dynamic_index_in_dim(out_cols, slot, 0, keepdims=False)
-
-    out_low = jnp.stack(
-        [out_for(0)] + [lay.send(out_for(m), m) for m in lay.tmasks[1:]]
-    )
-    mix_low = jnp.concatenate([in_proj.astype(LOW), gate_proj.astype(LOW), forget_low], axis=0)
-    mix_pieces = lay.gather_w(mix_low)
-    out_pieces = lay.gather_w(out_low)
-
-    slots = [w_slot(lay.flip(me, m)) for m in lay.wmasks]
-    mix_buf = jnp.zeros((W,) + mix_low.shape, LOW)
-    for slot, piece in zip(slots, mix_pieces):
-        mix_buf = lax.dynamic_update_slice(mix_buf, piece[None], (slot, 0, 0))
-    w_in = mix_buf[:, :r_in].reshape(2 * half, width)
-    w_gate = mix_buf[:, r_in : 2 * r_in].reshape(2 * half, width)
-    w_forget = (
-        mix_buf[:, 2 * r_in :]
-        .reshape(2, W // 2, r_f, width)
-        .transpose(1, 0, 2, 3)
-        .reshape(half, width)
-    )
-    w_mix = jnp.concatenate([w_in, w_gate, w_forget], axis=0)
-    out_buf = jnp.zeros((n, r_in, 2 * half), LOW)
-    for mask, piece in zip(lay.wmasks, out_pieces):
-        for j, t_mask in enumerate(lay.tmasks):
-            out_buf = lax.dynamic_update_slice(
-                out_buf, piece[j][None], (lay.flip(me, mask ^ t_mask), 0, 0)
-            )
-    w_out = out_buf.reshape(width, 2 * half)
-
-    f_gate, f_up, f_down, cot_own, _, _ = lax.optimization_barrier(
-        (ffn_gate.astype(LOW), ffn_up.astype(LOW), ffn_down.astype(LOW), cotangent, mix_pieces[1], tok_all)
-    )
-    gate_pieces = lay.gather_w(f_gate)
-    f_up, _ = lax.optimization_barrier((f_up, gate_pieces[1]))
-    up_pieces = lay.gather_w(f_up)
-    f_down, _ = lax.optimization_barrier((f_down, up_pieces[1]))
-    down_pieces = lay.gather_w(f_down)
-    w_gu = jnp.concatenate(gate_pieces + up_pieces, axis=0)
-    w_down = jnp.concatenate(down_pieces, axis=0)
-    hid = w_down.shape[0]
-    cot_all = jnp.concatenate(lay.gather_t(cot_own), axis=0)
-
     inputs = tokens.astype(F32)
     r_tok = lax.rsqrt(jnp.mean(inputs * inputs, axis=-1, keepdims=True) + EPS)
     all32 = tok_all.astype(F32)
-    normed = (
-        all32 * lax.rsqrt(jnp.mean(all32 * all32, axis=-1, keepdims=True) + EPS) * g_mix
-    ).astype(LOW)
+    r_all = lax.rsqrt(jnp.mean(all32 * all32, axis=-1, keepdims=True) + EPS)
+    normed = (all32 * r_all * g_mix).astype(LOW)
     proj = contract(normed, w_mix)
     wide = ((half // LANES, total, LANES), F32)
     d_re, d_im, v_re, v_im, summ = plain_call(
@@ -555,10 +831,10 @@
         3,
         name="gates",
     )(proj, keep, par)
-    summ_all = small_gather(lay, summ, lay.wmasks, w_slot, W, 1).reshape(n, 8, half)
+    summ_all = small_gather(lay, summ, lay.wmasks, partial(w_slot, lay), W, 1).reshape(n, 8, half)
     st_re, st_im, be_re, be_im, unit, squares = plain_call(
         partial(state_kernel, half, length, n),
-        [wide] * 4 + [((total, 2 * half), LOW), ((total, 1), F32)],
+        [wide] * 4 + [((total, 2 * half), LOW), ((total, LANES), F32)],
         8,
         smem=1,
         name="states",
@@ -568,46 +844,57 @@
     def t_blocks(value):
         return [value[j * length : (j + 1) * length] for j in range(4)]
 
-    square = lay.scatter_t(t_blocks(squares))
-    branch = lay.scatter_t(t_blocks(branch_low))
+    got, got_squares, w_ffn_up = net_call(
+        partial(scatter_kernel, lay),
+        lay,
+        (branch_low.reshape(4, length, width), squares.reshape(4, length, LANES), ffn_up.astype(LOW)),
+        [((3, length, width), LOW), ((3, length, LANES), F32), ((W, r_ffn, width), LOW)],
+        W - 1 + 6,
+        2,
+        4,
+        "branch",
+    )
+    w_ffn_up = w_ffn_up.reshape(W * r_ffn, width)
+
+    def own_sum(whole, arrived_parts):
+        value = whole[:length].astype(F32)
+        for j in range(3):
+            value = value + arrived_parts[j].astype(F32)
+        return value
+
+    square = own_sum(squares, got_squares)[:, 0:1]
+    branch = own_sum(branch_low, got)
     r_state = lax.rsqrt(square / width + EPS)
     residual = inputs + r_state * branch
     r_res = lax.rsqrt(jnp.mean(residual * residual, axis=-1, keepdims=True) + EPS)
     ffn_low = (residual * r_res * g_ffn).astype(LOW)
 
-    ffn_all = jnp.concatenate(lay.gather_t(ffn_low), axis=0)
-    gate_up = contract(ffn_all, w_gu)
-    gate_value, up_value = gate_up[:, :hid], gate_up[:, hid:]
+    ffn_all, w_down = net_call(
+        partial(gather_both_kernel, lay),
+        lay,
+        (ffn_low, ffn_down.astype(LOW)),
+        [((4, length, width), LOW), ((W, r_ffn, width), LOW)],
+        W - 1 + 3,
+        2,
+        5,
+        "ffn_in",
+    )
+    ffn_all = ffn_all.reshape(total, width)
+    w_down = w_down.reshape(W * r_ffn, width)
+    gate_value = contract(ffn_all, w_ffn_gate)
+    up_value = contract(ffn_all, w_ffn_up)
     s_gate = jax.nn.sigmoid(gate_value)
     silu_gate = gate_value * s_gate
     hidden_low = (silu_gate * up_value).astype(LOW)
     grad_hidden = contract(cot_all, w_down)
-    grad_gu = jnp.concatenate(
-        [
-            (grad_hidden * up_value * s_gate * (1.0 + gate_value * (1.0 - s_gate))).astype(LOW),
-            (grad_hidden * silu_gate).astype(LOW),
-        ],
-        axis=1,
-    )
-    du_low = jnp.dot(grad_gu, w_gu, preferred_element_type=F32).astype(LOW)
+    grad_gate = (grad_hidden * up_value * s_gate * (1.0 + gate_value * (1.0 - s_gate))).astype(LOW)
+    grad_up = (grad_hidden * silu_gate).astype(LOW)
+    du_low = (
+        jnp.dot(grad_gate, w_ffn_gate, preferred_element_type=F32)
+        + jnp.dot(grad_up, w_ffn_up, preferred_element_type=F32)
+    ).astype(LOW)
     du = lay.scatter_t(t_blocks(du_low))
     mixed_low = jnp.dot(hidden_low, w_down, preferred_element_type=F32).astype(LOW)
-    mixed_out = (residual + lay.scatter_t(t_blocks(mixed_low))).astype(LOW)
-
-    def scatter_w(partial_grad):
-        for bit in reversed(lay.wbits):
-            rows = partial_grad.shape[0] // 2
-            got = lay.send(partial_grad[rows:], bit)
-            partial_grad = partial_grad[:rows].astype(F32) + got.astype(F32)
-            if bit != lay.wbits[0]:
-                partial_grad = partial_grad.astype(LOW)
-        return partial_grad
-
-    grad_w_gu = outer_rows(grad_gu, ffn_all).astype(LOW)
-    grad_w_down = outer_rows(hidden_low, cot_all).astype(LOW)
-    ffn_gate_grad = scatter_w(grad_w_gu[:hid])
-    ffn_up_grad = scatter_w(grad_w_gu[hid:])
-    ffn_down_grad = scatter_w(grad_w_down)
 
     du_gain = du * g_ffn
     grad_residual = (
@@ -632,7 +919,7 @@
         scratch=[pltpu.VMEM((8, 2 * half), F32)],
         name="back_gates",
     )(grad_mid, st_re, st_im, proj, g_out, scale_all, d_re, d_im)
-    back_all = small_gather(lay, back, lay.wmasks, w_slot, W, 2).reshape(n, 8, half)
+    back_all = small_gather(lay, back, lay.wmasks, partial(w_slot, lay), W, 2).reshape(n, 8, half)
     grads, lower_part, angle_part = plain_call(
         partial(adjoint_kernel, half, length, n),
         [((total, 5 * half), LOW), ((8, half), F32), ((8, half), F32)],
@@ -642,68 +929,9 @@
         name="adjoints",
     )(ints, summ_all, back_all, gs_re, gs_im, d_re, d_im, be_re, be_im, proj, keep, par, gate_low)
     du_mix_low = jnp.dot(grads, w_mix, preferred_element_type=F32).astype(LOW)
-    du_mix = lay.scatter_t(t_blocks(du_mix_low))
-    dg_mix = du_mix * g_mix
-    tokens_grad = (
-        grad_residual
-        + r_tok * dg_mix
-        - inputs * (r_tok * r_tok * r_tok) * jnp.mean(inputs * dg_mix, axis=-1, keepdims=True)
-    ).astype(LOW)
-    mix_gain_part = jnp.sum(du_mix * inputs * r_tok, axis=0)
-
-    def scatter_abs(part):
-        shape = part.shape
-        axes = len(lay.wbits)
-        bits = {0: zhi, axes - 1: c}
-        for k, bit in enumerate(reversed(lay.ybits)):
-            bits[1 + k] = (me // bit) % 2
-        names = {0: lay.ZH, axes - 1: lay.C}
-        for k, bit in enumerate(reversed(lay.ybits)):
-            names[1 + k] = bit
-        part = part.reshape((2,) * axes + shape[3:])
-        for k in reversed(range(axes)):
-            kept = lax.dynamic_index_in_dim(part, bits[k], k, keepdims=False)
-            away = lax.dynamic_index_in_dim(part, 1 - bits[k], k, keepdims=False)
-            got = lay.send(away, names[k])
-            part = kept.astype(F32) + got.astype(F32)
-            if k:
-                part = part.astype(LOW)
-        return part
-
-    grad_w_out = outer_rows(grad_all, mid).astype(LOW)
-    grad_w_out = grad_w_out.reshape(2, 2, Y, 2, 2, r_in, 2 * half).transpose(0, 2, 4, 1, 3, 5, 6)
-    out_part = scatter_abs(grad_w_out).reshape(4, r_in, 2 * half)
-
-    def out_back(mask):
-        slot = ((zlo + (1 if mask & lay.ZL else 0)) % 2) * 2 + (x + (1 if mask & lay.X else 0)) % 2
-        return lax.dynamic_index_in_dim(out_part, slot, 0, keepdims=False), slot
-
-    out_grad = jnp.zeros((4, r_in, 2 * half), F32)
-    for mask in lay.tmasks:
-        value, slot = out_back(mask)
-        if mask:
-            value = lay.send(value, mask)
-        out_grad = lax.dynamic_update_slice(out_grad, value[None], (slot, 0, 0))
-    out_proj_grad = (
-        out_grad.reshape(2, 2, r_in, 2, Y, 2 * r_in).transpose(2, 3, 0, 4, 1, 5).reshape(r_in, width)
-    )
-
-    grad_w_mix = outer_rows(grads, normed).astype(LOW)
-    grad_w_mix = jnp.concatenate(
-        [
-            grad_w_mix[: 2 * half].reshape(W, r_in, width),
-            grad_w_mix[2 * half : 4 * half].reshape(W, r_in, width),
-            grad_w_mix[4 * half :]
-            .reshape(W // 2, 2, r_f, width)
-            .transpose(1, 0, 2, 3)
-            .reshape(W, r_f, width),
-        ],
-        axis=1,
-    ).reshape(2, Y, 2, 2 * r_in + r_f, width)
-    mix_part = scatter_abs(grad_w_mix)
-    in_proj_grad = mix_part[:r_in]
-    gate_proj_grad = mix_part[r_in : 2 * r_in]
-    forget_proj_grad = lax.ppermute(mix_part[2 * r_in :], "dp", forget_from)
+    mix_gain_part = jnp.sum(
+        du_mix_low.astype(F32) * (all32 * r_all), axis=0
+    )
 
     t_hot = ((jnp.arange(2)[:, None] == zlo) & (jnp.arange(2)[None, :] == x)).astype(F32)
     out_gain_part = jnp.sum(out_gain_part, axis=0).reshape(2, 1, Y, 1, 2 * r_in)
@@ -724,7 +952,67 @@
         axis=1,
     )
     to_owner = jnp.pad(to_owner, ((0, 0), (0, 1024 - to_owner.shape[1]))).reshape(n, 8, 128)
-    owned = jnp.sum(small_exchange(lay, to_owner, 3), axis=0).reshape(-1)
+
+    grad_w_out = outer_rows(grad_all, mid).astype(LOW).reshape(2, 2, Y, 2, 2, r_in, 2 * half)
+    grad_w_out = grad_w_out.transpose(0, 2, 4, 1, 3, 5, 6).reshape(W, 4 * r_in, 2 * half)
+    grad_w_mix = outer_rows(grads, normed).astype(LOW)
+    parts = [
+        grad_w_mix[4 * half :].reshape(W, r_f, width),
+        grad_w_out,
+        outer_rows(grad_gate, ffn_all).astype(LOW).reshape(W, r_ffn, width),
+        outer_rows(grad_up, ffn_all).astype(LOW).reshape(W, r_ffn, width),
+        outer_rows(hidden_low, cot_all).astype(LOW).reshape(W, r_ffn, width),
+        grad_w_mix[: 2 * half].reshape(W, r_in, width),
+        grad_w_mix[2 * half : 4 * half].reshape(W, r_in, width),
+    ]
+    scratch, copies, local_copies = [], 6 + 3 + n - 1, 2
+    for part in parts:
+        blocks, shape = W // 2, part.shape[1:]
+        scratch.append(pltpu.VMEM((blocks,) + shape, LOW))
+        local_copies += blocks + 1
+        for _ in lay.rbits:
+            scratch.append(pltpu.VMEM((blocks,) + shape, LOW))
+            copies += blocks
+            blocks //= 2
+        scratch.append(pltpu.VMEM(shape, F32))
+    forget_part, *w_grads, out_cols_grad, got_du, got_mixed, owned = net_call(
+        partial(reduce_kernel, lay, len(parts)),
+        lay,
+        (
+            *parts,
+            du_mix_low.reshape(4, length, width),
+            mixed_low.reshape(4, length, width),
+            to_owner,
+        ),
+        [(part.shape[1:], F32) for i, part in enumerate(parts) if i != 1]
+        + [
+            ((4, r_in, 2 * half), F32),
+            ((3, length, width), LOW),
+            ((3, length, width), LOW),
+            ((n, 8, 128), F32),
+        ],
+        copies,
+        local_copies,
+        3,
+        "reduce",
+        scratch,
+    )
+    ffn_gate_grad, ffn_up_grad, ffn_down_grad, in_proj_grad, gate_proj_grad = w_grads
+    forget_proj_grad = lax.ppermute(forget_part, "dp", forget_from)
+    out_proj_grad = (
+        out_cols_grad.reshape(2, 2, r_in, 2, Y, 2 * r_in)
+        .transpose(2, 3, 0, 4, 1, 5)
+        .reshape(r_in, width)
+    )
+    owned = jnp.sum(owned, axis=0).reshape(-1)
+    mixed_out = (residual + own_sum(mixed_low, got_mixed)).astype(LOW)
+    du_mix = own_sum(du_mix_low, got_du)
+    dg_mix = du_mix * g_mix
+    tokens_grad = (
+        grad_residual
+        + r_tok * dg_mix
+        - inputs * (r_tok * r_tok * r_tok) * jnp.mean(inputs * dg_mix, axis=-1, keepdims=True)
+    ).astype(LOW)
     return (
         mixed_out,
         tokens_grad,

time: 808 us -> 733 us (0.907)
  Pallas kernels: 91 us -> 482 us
  waiting for transfers between devices: 346 us -> 32.3 us
  local copies, waits for them, and re-layouts: 116 us -> 43.6 us
  starting transfers between devices: 99.3 us -> 36.3 us
  other arithmetic: 46.6 us -> 34.8 us
    pallas_call x1 -> x4, Pallas kernels: 10.7 us -> 427 us  [net_call(): pl.pallas_call(body, out_shape=tuple((jax.ShapeDtypeStruct(s, d) for s, d...]
    ppermute x86 -> x9, waiting for transfers between devices: 331 us -> 31 us  [send(): return lax.ppermute(value, 'dp', [(i, i ^ mask) for i in range(self.n)])]
    ppermute x86 -> x9, starting transfers between devices: 92.4 us -> 27.9 us  [send(): return lax.ppermute(value, 'dp', [(i, i ^ mask) for i in range(self.n)])]
    unnamed x214 -> x149, local copies, waits for them, and re-layouts: 52 us -> 23.4 us
    pallas_call x3 -> x2, Pallas kernels: 51.6 us -> 25 us  [small_gather(): pl.pallas_call(partial(gather_kernel, lay, masks, slot_of), out_shape=jax...]
    dynamic_update_slice x41 -> x0, local copies, waits for them, and re-layouts: 21.6 us -> none  [the longest x31 21.2 us: local(): lax.dynamic_update_slice(out_buf, piece[j][None], (lay.flip(me, mask ^ t_...]
    convert_element_type x11 -> x4, other arithmetic: 21.3 us -> 4.69 us  [the longest x1 2.57 us: local(): mixed_out = (residual + own_sum(mixed_low, got_mixed)).astype(LOW)]
    slice x14 -> x2, local copies, waits for them, and re-layouts: 11.8 us -> 1.09 us  [the longest x1 1.08 us: local(): grad_w_mix[4 * half:].reshape(W, r_f, width)]
  transfers between devices with their start and end apart: 88 -> 11, of which waited for: 35 -> 4; matrix products, arithmetic and copies ran while one was open for 26% -> 7% of each run, Pallas kernels for 11% -> 0%
where the time goes in v2:
time: 733 us; the launch traced here: 727 us
  Pallas kernels  482 us (66%)
  matrix products  96.1 us (13%)
  local copies, waits for them, and re-layouts  43.6 us (6%)
  starting transfers between devices  36.3 us (5%)
  other arithmetic  34.8 us (5%)
  waiting for transfers between devices  32.3 us (4%)
    pallas_call x4, Pallas kernels, net_call(): pl.pallas_call(body, out_shape=tuple((jax.ShapeDtypeStruct(s, d) for s, d...  427 us
    dot_general x5, matrix products, contract(): lax.dot_general(left_rows, right_rows, (((1,), (1,)), ((), ())), preferre...  34.3 us
    ppermute x9, waiting for transfers between devices, send(): return lax.ppermute(value, 'dp', [(i, i ^ mask) for i in range(self.n)])  31 us
    dot_general x5, matrix products, outer_rows(): lax.dot_general(left_rows, right_rows, (((0,), (0,)), ((), ())), preferre...  30.9 us
    ppermute x9, starting transfers between devices, send(): return lax.ppermute(value, 'dp', [(i, i ^ mask) for i in range(self.n)])  27.9 us
    pallas_call x2, Pallas kernels, small_gather(): pl.pallas_call(partial(gather_kernel, lay, masks, slot_of), out_shape=jax...  25 us
    unnamed x149, local copies, waits for them, and re-layouts  23.4 us
  transfers between devices with their start and end apart: 11, of which 4 were waited for; matrix products, arithmetic and copies ran while one was open for 7% of the time, Pallas kernels for 0%

profile of v2, /device:TPU:1, one launch (start us, length us, event | category | flops | bytes accessed | tf_op | source)
XLA Modules:
  0.0 726.7 jit_solution(18122022612587526116)
XLA Ops:
  1.7 5.6 collective-permute-start
  19.9 118.3 %start.1 = (bf16[4,160,2048]{2,1,0:T(8,128)(2,1)}, bf16[4,160,2048]{2,1,0:T(8,128)(2,1)}, bf16[40,32,2048]{2,1,0:T(8,128)(2,1)}, bf16[4,64,512]{2,1,0:T(8,128)(2...) custom-call(bf16[160,2048]{1,0:T(8,128)(2,1)} %tok.1, ...), custom_call_target="tpu_custom_call" | custom-call | tf_op jit(solution)/shard_map/start/pallas_call | solution.py:213
  144.5 5.3 fusion.36.proj
  149.9 5.6 gates.1
  157.9 10.9 %shard_map.263 = f32[8,4,8,256]{3,2,1,0:T(8,128)} custom-call(f32[4,8,256]{2,1,0:T(8,128)} %copy-done.17), custom_call_target="tpu_custom_call" | custom-call | tf_op jit(solution)/shard_map/pallas_call | solution.py:111
  170.8 8.2 %states.1 = (f32[2,640,128]{2,1,0:T(8,128)S(1)}, f32[2,640,128]{2,1,0:T(8,128)S(1)}, f32[2,640,128]{2,1,0:T(8,128)S(1)}, f32[2,640,128]{2,1,0:T(8,128)S(1)}, bf1...) custom-call(s32[36]{0:T(128)S(1)} %pad_add_fusion.1.ints, f32[32,8,256]{2,1,0:T(8,128)S(1)} %bitcast.156, ...), custom_call_target="tpu_custom_call" | custom-call | flops 20000000 | bytes 12000000 | tf_op jit(solution)/shard_map/states/pallas_call | solution.py:835
  179.0 3.0 convolution_convert_fusion.6
  182.0 50.5 %branch.1 = (bf16[3,160,2048]{2,1,0:T(8,128)(2,1)}, f32[3,160,128]{2,1,0:T(8,128)}, bf16[8,176,2048]{2,1,0:T(8,128)(2,1)}) custom-call(bf16[4,160,2048]{2,1,0:T(8,128)(2,1)} %bitcast.166, f32[4,160,128]{2,1,0:T(8,128)} %bitcast.159, bf16[176,2048]{1,0:T(8,128)(2,1)} %convert_element_type.199.weight), custom_call_target="tpu_custom_call" | custom-call | tf_op jit(solution)/shard_map/branch/pallas_call | solution.py:213
  233.6 3.5 multiply_reduce_fusion.5
  239.5 67.3 %ffn_in.1 = (bf16[4,160,2048]{2,1,0:T(8,128)(2,1)}, bf16[8,176,2048]{2,1,0:T(8,128)(2,1)}) custom-call(bf16[160,2048]{1,0:T(8,128)(2,1)} %multiply_convert_fusion.5.own, bf16[176,2048]{1,0:T(8,128)(2,1)} %convert_element_type.208.weight), custom_call_target="tpu_custom_call" | custom-call | tf_op jit(solution)/shard_map/ffn_in/pallas_call | solution.py:213
  306.9 9.8 %fusion.37 = f32[640,1408]{1,0:T(8,128)} fusion(bf16[640,2048]{1,0:T(8,128)(2,1)} %bitcast.206, bf16[1408,2048]{1,0:T(8,128)(2,1)} %bitcast.196), kind=kOutput, calls=%fused_computation.149 | convolution fusion | flops 3690987520 | bytes 11993088 | tf_op jit(solution)/shard_map/dot_general | solution.py:20
  316.7 6.1 fusion.38
  322.8 10.2 %multiply_convert_fusion.3 = (bf16[640,1408]{1,0:T(8,128)(2,1)S(1)}, bf16[640,1408]{1,0:T(8,128)(2,1)S(1)}, bf16[640,1408]{1,0:T(8,128)(2,1)}) fusion(f32[640,1408]{1,0:T(8,128)} %fusion.38, f32[640,1408]{1,0:T(8,128)} %fusion.37, bf16[640,2048]{1,0:T(8,128)(2,1)} %bitcast.207, bf16[1408,2048]{1,0:T(8,128)(2,1)S(1)} %bitcast.194), kind=kOutput, calls=%fused_computation.11 | convolution fusion | flops 3704504320 | bytes 21004288 | tf_op jit(solution)/shard_map/dot_general | solution.py:20
  332.9 4.2 fusion.39
  337.2 4.4 add_convert_fusion
  345.6 20.6 %collective-permute-start.2 = (bf16[160,2048]{1,0:T(8,128)(2,1)}, bf16[160,2048]{1,0:T(8,128)(2,1)}, u32[]{:S(2)}, u32[]{:S(2)}) collective-permute-start(bf16[160,2048]{1,0:T(8,128)(2,1)} %get-tuple-element.116), channel_id=1, source_target_pairs={{0,8},{1,9},{2,10},{3,11},{4,12},{5,13},{6,14},{7,15},{8,0},{9,1},... | collective-permute-start | bytes 1966088 | tf_op jit(solution)/shard_map/ppermute | solution.py:64
  367.1 9.1 %convolution_convert_fusion.5 = bf16[640,2048]{1,0:T(8,128)(2,1)} fusion(bf16[640,1408]{1,0:T(8,128)(2,1)} %get-tuple-element.109, bf16[1408,2048]{1,0:T(8,128)(2,1)} %bitcast.200), kind=kOutput, calls=%fused_computation.16 | convolution fusion | flops 3692298240 | bytes 10190848 | tf_op jit(solution)/shard_map/dot_general | solution.py:897
  376.3 6.8 convolution_convert_fusion.1
  383.1 13.2 %collective-permute-done.3 = bf16[160,2048]{1,0:T(8,128)(2,1)} collective-permute-done((bf16[160,2048]{1,0:T(8,128)(2,1)}, bf16[160,2048]{1,0:T(8,128)(2,1)}, u32[]{:S(2)}, u32[]{:S(2)}) %collective-permute-start.3) | collective-permute-done | bytes 655392 | tf_op jit(solution)/shard_map/ppermute | solution.py:64
  398.5 4.0 multiply_reduce_fusion.3
  403.1 9.6 %convolution_convert_fusion.2 = bf16[1408,2048]{1,0:T(8,128)(2,1)} fusion(bf16[640,1408]{1,0:T(8,128)(2,1)} %copy-done.64, bf16[640,2048]{1,0:T(8,128)(2,1)} %bitcast.208), kind=kOutput, calls=%fused_computation.2 | convolution fusion | flops 3693871104 | bytes 10190848 | tf_op jit(solution)/shard_map/dot_general | solution.py:26
  417.6 6.5 convolution_convert_fusion
  429.8 15.0 %collective-permute-done.6 = bf16[160,2048]{1,0:T(8,128)(2,1)} collective-permute-done((bf16[160,2048]{1,0:T(8,128)(2,1)}, bf16[160,2048]{1,0:T(8,128)(2,1)}, u32[]{:S(2)}, u32[]{:S(2)}) %collective-permute-start.6) | collective-permute-done | bytes 655392 | tf_op jit(solution)/shard_map/ppermute | solution.py:64
  444.8 5.0 fusion.9.grad_mid
  449.8 7.2 back_gates.1
  461.6 14.2 %shard_map.264 = f32[8,4,8,256]{3,2,1,0:T(8,128)} custom-call(f32[4,8,256]{2,1,0:T(8,128)} %copy-done.16), custom_call_target="tpu_custom_call" | custom-call | tf_op jit(solution)/shard_map/pallas_call | solution.py:111
  479.9 8.7 %adjoints.1 = (bf16[640,1280]{1,0:T(8,128)(2,1)}, f32[8,256]{1,0:T(8,128)S(1)}, f32[8,256]{1,0:T(8,128)S(1)}) custom-call(s32[36]{0:T(128)S(1)} %pad_add_fusion.1.ints, f32[32,8,256]{2,1,0:T(8,128)S(1)} %bitcast.157, f32[32,8,256]{2,1,0:T(8,128)S(1)} %bitcast.158, f32[2,640,128]{2,1,0:T(8,128)S(1)} %copy-done.3, f32[2,640,128]{2,1,0:T(8,128)S(1)} %copy-done.5, ...), custom_call_target="tpu_custom_call" | custom-call | flops 20000000 | bytes 12000000 | tf_op jit(solution)/shard_map/adjoints/pallas_call | solution.py:923
  488.6 8.2 %multiply_reduce_fusion = (f32[2048]{0:T(1024)S(1)}, bf16[640,2048]{1,0:T(8,128)(2,1)S(1)}, bf16[640,2048]{1,0:T(8,128)(2,1)}) fusion(bf16[4,160,2048]{2,1,0:T(8,128)(2,1)S(1)} %copy-done.25, f32[640]{0:T(1024)S(1)} %copy-done.50, f32[2048]{0:T(1024)S(1)} %copy-done.45, bf16[640,1280]{1,0:T(8,128)(2,1)} %get-tuple-element.81, bf16[1280,2048]{1,0:T(8,128)(2,1)} %bitcast.202), kind=kOutput, calls=%fused_computation.5 | convolution fusion | flops 3365926912 | bytes 14764544 | tf_op jit(solution)/shard_map/dot_general | solution.py:931
  496.9 4.5 convolution_convert_fusion.3
  506.3 3.5 convolution_convert_fusion.7
  511.4 190.8 %reduce.4 = (f32[32,2048]{1,0:T(8,128)}, f32[176,2048]{1,0:T(8,128)}, f32[176,2048]{1,0:T(8,128)}, f32[176,2048]{1,0:T(8,128)}, f32[64,2048]{1,0:T(8,128)}, /*in...) custom-call(bf16[8,32,2048]{2,1,0:T(8,128)(2,1)} %bitcast.170, ...), custom_call_target="tpu_custom_call" | custom-call | tf_op jit(solution)/shard_map/reduce/pallas_call | solution.py:213
  710.4 3.0 fusion.4
  (254 shorter events, 82.2 us)
Async XLA Ops:
  0.6 13.3 %copy-start.34 = (f32[176,2048]{1,0:T(8,128)S(1)}, f32[176,2048]{1,0:T(8,128)}, u32[]{:S(2)}) copy-start(f32[176,2048]{1,0:T(8,128)} %param.24) | copy-start | bytes 4325380
  1.7 17.5 %collective-permute-start = (bf16[32,2048]{1,0:T(8,128)(2,1)S(1)}, bf16[32,2048]{1,0:T(8,128)(2,1)S(1)}, u32[]{:S(2)}, u32[]{:S(2)}) collective-permute-start(bf16[32,2048]{1,0:T(8,128)(2,1)S(1)} %convert_element_type.192), channel_id=1, source_target_pairs={{0,0},{1,16},{2,1},{3,17},{4,2},{5,18},{6,3},{7,19},{8,4},{9,20},{... | collective-permute-start | bytes 393224 | tf_op jit(solution)/shard_map/ppermute | solution.py:765
  170.7 8.3 %copy-start.32 = (bf16[2,2,2,2,2,64,512]{6,5,2,4,1,3,0:T(8,128)(2,1)}, bf16[2,2,2,2,2,64,512]{6,5,2,4,1,3,0:T(8,128)(2,1)S(1)}, u32[]{:S(2)}) copy-start(bf16[2,2,2,2,2,64,512]{6,5,2,4,1,3,0:T(8,128)(2,1)S(1)} %copy.62) | copy-start | bytes 6291460
  306.9 9.8 %copy-start.56 = (bf16[8,176,2048]{2,1,0:T(8,128)(2,1)S(1)}, bf16[8,176,2048]{2,1,0:T(8,128)(2,1)}, u32[]{:S(2)}) copy-start(bf16[8,176,2048]{2,1,0:T(8,128)(2,1)} %get-tuple-element.71) | copy-start | bytes 17301508
  306.9 9.8 %copy-start.58 = (bf16[4,160,2048]{2,1,0:T(8,128)(2,1)S(1)}, bf16[4,160,2048]{2,1,0:T(8,128)(2,1)}, u32[]{:S(2)}) copy-start(bf16[4,160,2048]{2,1,0:T(8,128)(2,1)} %get-tuple-element.72) | copy-start | bytes 7864324
  306.9 15.9 %slice-start = ((s8[5767168]{0:T(1024)(128)(4,1)}), s8[4194304]{0:T(1024)(128)(4,1)S(1)}, s32[]{:S(2)}) async-start(s8[5767168]{0:T(1024)(128)(4,1)} %bitcast.192), calls=%async_computation | async-start | bytes 8388608
  316.6 16.3 %slice-start.2 = ((s8[5767168]{0:T(1024)(128)(4,1)}), s8[4194304]{0:T(1024)(128)(4,1)S(1)}, s32[]{:S(2)}) async-start(s8[5767168]{0:T(1024)(128)(4,1)} %bitcast.197), calls=%async_computation.2 | async-start | bytes 8388608
  322.8 10.2 %slice-start.3 = ((s8[5767168]{0:T(1024)(128)(4,1)}), s8[1572864]{0:T(1024)(128)(4,1)S(1)}, s32[]{:S(2)}) async-start(s8[5767168]{0:T(1024)(128)(4,1)} %bitcast.197), calls=%async_computation.3 | async-start | bytes 3145728
  344.4 38.6 %collective-permute-start.1 = (bf16[160,2048]{1,0:T(8,128)(2,1)}, bf16[160,2048]{1,0:T(8,128)(2,1)}, u32[]{:S(2)}, u32[]{:S(2)}) collective-permute-start(bf16[160,2048]{1,0:T(8,128)(2,1)} %get-tuple-element.114), channel_id=1, source_target_pairs={{0,2},{1,3},{2,0},{3,1},{4,6},{5,7},{6,4},{7,5},{8,10},{9,11},{10,... | collective-permute-start | bytes 1966088 | tf_op jit(solution)/shard_map/ppermute | solution.py:64
  345.6 37.5 %collective-permute-start.2 = (bf16[160,2048]{1,0:T(8,128)(2,1)}, bf16[160,2048]{1,0:T(8,128)(2,1)}, u32[]{:S(2)}, u32[]{:S(2)}) collective-permute-start(bf16[160,2048]{1,0:T(8,128)(2,1)} %get-tuple-element.116), channel_id=1, source_target_pairs={{0,8},{1,9},{2,10},{3,11},{4,12},{5,13},{6,14},{7,15},{8,0},{9,1},... | collective-permute-start | bytes 1966088 | tf_op jit(solution)/shard_map/ppermute | solution.py:64
  366.2 30.0 %collective-permute-start.3 = (bf16[160,2048]{1,0:T(8,128)(2,1)}, bf16[160,2048]{1,0:T(8,128)(2,1)}, u32[]{:S(2)}, u32[]{:S(2)}) collective-permute-start(bf16[160,2048]{1,0:T(8,128)(2,1)} %get-tuple-element.115), channel_id=1, source_target_pairs={{0,10},{1,11},{2,8},{3,9},{4,14},{5,15},{6,12},{7,13},{8,2},{9,3},... | collective-permute-start | bytes 1966088 | tf_op jit(solution)/shard_map/ppermute | solution.py:64
  367.1 9.1 %copy-start.60 = (bf16[4,160,2048]{2,1,0:T(8,128)(2,1)S(1)}, bf16[4,160,2048]{2,1,0:T(8,128)(2,1)}, u32[]{:S(2)}) copy-start(bf16[4,160,2048]{2,1,0:T(8,128)(2,1)} %get-tuple-element.68) | copy-start | bytes 7864324
  367.1 9.1 %copy-start.63 = (bf16[640,1408]{1,0:T(8,128)(2,1)S(1)}, bf16[640,1408]{1,0:T(8,128)(2,1)}, u32[]{:S(2)}) copy-start(bf16[640,1408]{1,0:T(8,128)(2,1)} %copy-done.62) | copy-start | bytes 5406724
  376.2 20.0 %copy-start.22 = (f32[160,2048]{1,0:T(8,128)S(1)}, f32[160,2048]{1,0:T(8,128)}, u32[]{:S(2)}) copy-start(f32[160,2048]{1,0:T(8,128)} %get-tuple-element.104) | copy-start | bytes 3932164
  376.2 20.0 %copy-start.30 = (bf16[640,2048]{1,0:T(8,128)(2,1)S(1)}, bf16[640,2048]{1,0:T(8,128)(2,1)}, u32[]{:S(2)}) copy-start(bf16[640,2048]{1,0:T(8,128)(2,1)} %copy-done.29) | copy-start | bytes 7864324
  383.0 15.4 %copy-start.27 = (bf16[3,160,2048]{2,1,0:T(8,128)(2,1)S(1)}, bf16[3,160,2048]{2,1,0:T(8,128)(2,1)}, u32[]{:S(2)}) copy-start(bf16[3,160,2048]{2,1,0:T(8,128)(2,1)} %get-tuple-element.67) | copy-start | bytes 5898244
  383.0 15.4 %copy-start.31 = (bf16[160,2048]{1,0:T(8,128)(2,1)S(1)}, bf16[160,2048]{1,0:T(8,128)(2,1)}, u32[]{:S(2)}) copy-start(bf16[160,2048]{1,0:T(8,128)(2,1)} %cot.1) | copy-start | bytes 1966084
  402.7 14.9 %copy-start.59 = (bf16[4,160,2048]{2,1,0:T(8,128)(2,1)S(1)}, bf16[4,160,2048]{2,1,0:T(8,128)(2,1)}, u32[]{:S(2)}) copy-start(bf16[4,160,2048]{2,1,0:T(8,128)(2,1)} %get-tuple-element.72) | copy-start | bytes 7864324
  402.7 14.9 %copy-start.65 = (bf16[640,1408]{1,0:T(8,128)(2,1)S(1)}, bf16[640,1408]{1,0:T(8,128)(2,1)}, u32[]{:S(2)}) copy-start(bf16[640,1408]{1,0:T(8,128)(2,1)} %get-tuple-element.109) | copy-start | bytes 5406724
  402.7 13.7 %collective-permute-start.7 = (f32[160,2]{0,1:T(2,128)S(1)}, f32[160,2]{0,1:T(2,128)S(1)}, u32[]{:S(2)}, u32[]{:S(2)}) collective-permute-start(f32[160,2]{0,1:T(2,128)S(1)} %pad_maximum_fusion.4), channel_id=1, source_target_pairs={{0,2},{1,3},{2,0},{3,1},{4,6},{5,7},{6,4},{7,5},{8,10},{9,11},{10,... | collective-permute-start | bytes 3848 | tf_op jit(solution)/shard_map/ppermute | solution.py:64
  412.7 12.8 %collective-permute-start.8 = (f32[160,2]{0,1:T(2,128)S(1)}, f32[160,2]{0,1:T(2,128)S(1)}, u32[]{:S(2)}, u32[]{:S(2)}) collective-permute-start(f32[160,2]{0,1:T(2,128)S(1)} %pad_maximum_fusion.4), channel_id=1, source_target_pairs={{0,8},{1,9},{2,10},{3,11},{4,12},{5,13},{6,14},{7,15},{8,0},{9,1},... | collective-permute-start | bytes 3848 | tf_op jit(solution)/shard_map/ppermute | solution.py:64
  413.8 11.6 %collective-permute-start.9 = (f32[160,2]{0,1:T(2,128)S(1)}, f32[160,2]{0,1:T(2,128)S(1)}, u32[]{:S(2)}, u32[]{:S(2)}) collective-permute-start(f32[160,2]{0,1:T(2,128)S(1)} %pad_maximum_fusion.4), channel_id=1, source_target_pairs={{0,10},{1,11},{2,8},{3,9},{4,14},{5,15},{6,12},{7,13},{8,2},{9,3},... | collective-permute-start | bytes 3848 | tf_op jit(solution)/shard_map/ppermute | solution.py:64
  414.9 14.9 %collective-permute-start.4 = (bf16[160,2048]{1,0:T(8,128)(2,1)}, bf16[160,2048]{1,0:T(8,128)(2,1)}, u32[]{:S(2)}, u32[]{:S(2)}) collective-permute-start(bf16[160,2048]{1,0:T(8,128)(2,1)} %get-tuple-element.101), channel_id=1, source_target_pairs={{0,2},{1,3},{2,0},{3,1},{4,6},{5,7},{6,4},{7,5},{8,10},{9,11},{10,... | collective-permute-start | bytes 1966088 | tf_op jit(solution)/shard_map/ppermute | solution.py:64
  415.3 14.5 %collective-permute-start.5 = (bf16[160,2048]{1,0:T(8,128)(2,1)}, bf16[160,2048]{1,0:T(8,128)(2,1)}, u32[]{:S(2)}, u32[]{:S(2)}) collective-permute-start(bf16[160,2048]{1,0:T(8,128)(2,1)} %get-tuple-element.101), channel_id=1, source_target_pairs={{0,8},{1,9},{2,10},{3,11},{4,12},{5,13},{6,14},{7,15},{8,0},{9,1},... | collective-permute-start | bytes 1966088 | tf_op jit(solution)/shard_map/ppermute | solution.py:64
  416.5 28.3 %collective-permute-start.6 = (bf16[160,2048]{1,0:T(8,128)(2,1)}, bf16[160,2048]{1,0:T(8,128)(2,1)}, u32[]{:S(2)}, u32[]{:S(2)}) collective-permute-start(bf16[160,2048]{1,0:T(8,128)(2,1)} %get-tuple-element.101), channel_id=1, source_target_pairs={{0,10},{1,11},{2,8},{3,9},{4,14},{5,15},{6,12},{7,13},{8,2},{9,3},... | collective-permute-start | bytes 1966088 | tf_op jit(solution)/shard_map/ppermute | solution.py:64
  427.0 22.8 %copy-start.12 = (f32[2,640,128]{2,1,0:T(8,128)S(1)}, f32[2,640,128]{2,1,0:T(8,128)}, u32[]{:S(2)}) copy-start(f32[2,640,128]{2,1,0:T(8,128)} %copy-done.11) | copy-start | bytes 1966084
  427.0 22.8 %copy-start.14 = (f32[2,640,128]{2,1,0:T(8,128)S(1)}, f32[2,640,128]{2,1,0:T(8,128)}, u32[]{:S(2)}) copy-start(f32[2,640,128]{2,1,0:T(8,128)} %copy-done.13) | copy-start | bytes 1966084
  479.9 8.7 %copy-start.25 = (bf16[4,160,2048]{2,1,0:T(8,128)(2,1)S(1)}, bf16[4,160,2048]{2,1,0:T(8,128)(2,1)}, u32[]{:S(2)}) copy-start(bf16[4,160,2048]{2,1,0:T(8,128)(2,1)} %get-tuple-element.55) | copy-start | bytes 7864324
  479.9 8.7 %copy-start.45 = (f32[2048]{0:T(1024)S(1)}, f32[2048]{0:T(1024)}, u32[]{:S(2)}) copy-start(f32[2048]{0:T(1024)} %copy-done.44) | copy-start | bytes 24580
  479.9 8.7 %copy-start.50 = (f32[640]{0:T(1024)S(1)}, f32[640]{0:T(1024)}, u32[]{:S(2)}) copy-start(f32[640]{0:T(1024)} %rsqrt.40) | copy-start | bytes 7684
  511.4 190.8 %copy-start.26 = (bf16[160,2048]{1,0:T(8,128)(2,1)S(1)}, bf16[160,2048]{1,0:T(8,128)(2,1)}, u32[]{:S(2)}) copy-start(bf16[160,2048]{1,0:T(8,128)(2,1)} %tok.1) | copy-start | bytes 1966084
  707.5 11.4 %collective-permute-start.10 = (f32[32,2048]{1,0:T(8,128)}, f32[32,2048]{1,0:T(8,128)}, u32[]{:S(2)}, u32[]{:S(2)}) collective-permute-start(f32[32,2048]{1,0:T(8,128)} %get-tuple-element.89), channel_id=1, source_target_pairs={{0,0},{16,1},{1,2},{17,3},{2,4},{18,5},{3,6},{19,7},{4,8},{20,9},{... | collective-permute-start | bytes 786440 | tf_op jit(solution)/shard_map/ppermute | solution.py:1001
  (49 other events, 124.1 us)

commit v3 on v2

--- a/solution.py
+++ b/solution.py
@@ -26,6 +26,10 @@
     return lax.dot_general(
         left_rows, right_rows, (((0,), (0,)), ((), ())), preferred_element_type=F32
     )
+
+
+def tie(value, *others):
+    return lax.optimization_barrier((value,) + others)[0]
 
 
 class Layout:
@@ -45,6 +49,9 @@
         for bit in self.wbits:
             self.wmasks = self.wmasks + [m | bit for m in self.wmasks]
         self.bits = [1 << k for k in range(n.bit_length() - 1)]
+
+    def rel_slot(self, mask):
+        return ((mask % 2) * self.Y + (mask // 4) % self.Y) * 2 + mask // self.ZH
 
     def flip(self, device, mask):
         for bit in self.bits:
@@ -118,12 +125,14 @@
             pltpu.SemaphoreType.DMA((len(masks),)),
         ],
         compiler_params=pltpu.CompilerParams(collective_id=collective_id, has_side_effects=True),
+        cost_estimate=estimate(10),
     )(value)
 
 
 class Net:
-    def __init__(self, lay, peers, send_sems, recv_sems, local_sems):
+    def __init__(self, lay, peers, send_sems, recv_sems, local_sems, rooms=()):
         self.lay, self.send_sems, self.recv_sems, self.local_sems = lay, send_sems, recv_sems, local_sems
+        self.rooms, self.moving = list(rooms), []
         self.me = lax.axis_index("dp")
         self.used, self.used_local, self.open, self.local = 0, 0, [], []
         barrier = pltpu.get_barrier_semaphore()
@@ -156,6 +165,16 @@
     def keep(self, src, dst):
         self.local.append(self.load(src, dst))
 
+    def move(self, src, dst):
+        room = self.rooms.pop(0)
+        self.moving.append((self.load(src, room), room, dst))
+
+    def settle(self):
+        for copy, room, dst in self.moving:
+            copy.wait()
+            self.keep(room, dst)
+        self.moving = []
+
     def finish(self):
         for copy in self.open:
             copy.wait_send()
@@ -164,28 +183,40 @@
 
 
 class WeightGather:
-    def __init__(self, net, own, place):
-        self.net, self.own, self.place = net, own, place
+    def __init__(self, net, own, place, ahead=None):
+        self.net, self.own, self.place, self.ahead = net, own, place, ahead
         self.bits = net.lay.wbits
         self.pending = {}
 
     def start(self):
-        for bit in self.bits:
-            self.pending[bit] = self.net.put(self.own, self.place(self.net.me), bit)
-        self.net.keep(self.own, self.place(self.net.me))
+        me = self.net.me
+        if self.ahead is None:
+            self.pending[self.bits[0]] = self.net.put(
+                self.own, self.place(me, self.bits[0]), self.bits[0]
+            )
+        for bit in self.bits[1:]:
+            self.pending[bit] = self.net.put(self.own, self.place(me, bit), bit)
+        self.net.move(self.own, self.place(me, 0))
+        if self.ahead is not None:
+            self.pass_on(self.bits[0], self.ahead)
+            self.net.move(self.ahead, self.place(self.net.lay.flip(me, self.bits[0]), self.bits[0]))
 
     def masks(self):
         out = [0]
         for bit in self.bits[:-1]:
             out = out + [m | bit for m in out]
-        return sorted(out[1:], key=lambda m: (bin(m).count("1"), -m))
+        out = sorted(out[1:], key=lambda m: (bin(m).count("1"), -m))
+        return [m for m in out if self.ahead is None or m != self.bits[0]]
+
+    def pass_on(self, mask, block):
+        last = max(i for i, bit in enumerate(self.bits) if mask & bit)
+        source = self.net.lay.flip(self.net.me, mask)
+        for bit in self.bits[last + 1 :]:
+            self.pending[mask | bit] = self.net.put(block, self.place(source, mask | bit), bit)
 
     def forward(self, mask):
         self.pending[mask].wait_recv()
-        last = max(i for i, bit in enumerate(self.bits) if mask & bit)
-        here = self.place(self.net.lay.flip(self.net.me, mask))
-        for bit in self.bits[last + 1 :]:
-            self.pending[mask | bit] = self.net.put(here, here, bit)
+        self.pass_on(mask, self.place(self.net.lay.flip(self.net.me, mask), mask))
 
     def end(self):
         for mask, copy in self.pending.items():
@@ -193,10 +224,20 @@
                 copy.wait_recv()
 
 
-def token_gather(net, own, out):
+def token_start(net, own, out):
     lay = net.lay
-    net.keep(own, out.at[0])
-    return [net.put(own, out.at[j], m) for j, m in enumerate(lay.tmasks) if j]
+    first = [net.put(own, out.at[1], lay.X), net.put(own, out.at[2], lay.ZL)]
+    net.move(own, out.at[0])
+    return first
+
+
+def token_finish(net, first, out):
+    lay, half = net.lay, out.shape[1] // 2
+    top, low = pl.ds(0, half), pl.ds(half, half)
+    arrived(first[:1])
+    copies = [net.put(out.at[1, top], out.at[3, top], lay.ZL)]
+    arrived(first[1:])
+    return copies + [net.put(out.at[2, low], out.at[3, low], lay.X)]
 
 
 def token_scatter(net, blocks, out):
@@ -208,7 +249,11 @@
         copy.wait_recv()
 
 
-def net_call(body, lay, values, outs, copies, local, collective_id, name, scratch=()):
+def estimate(micros):
+    return pl.CostEstimate(flops=micros * 1_000_000_000, bytes_accessed=0, transcendentals=0)
+
+
+def net_call(body, lay, values, outs, copies, local, collective_id, name, micros, scratch=(), limit=None):
     hbm = pl.BlockSpec(memory_space=pl.ANY)
     return pl.pallas_call(
         body,
@@ -224,8 +269,9 @@
         compiler_params=pltpu.CompilerParams(
             collective_id=collective_id,
             has_side_effects=True,
-            vmem_limit_bytes=(56 << 20) if scratch else None,
+            vmem_limit_bytes=limit,
         ),
+        cost_estimate=estimate(micros),
         name=name,
     )(*values)
 
@@ -245,53 +291,92 @@
     return zlo * 2 + x
 
 
+class Turn:
+    def __init__(self, net, target, src, dst):
+        self.remote = target != net.me
+        self.away = pltpu.make_async_remote_copy(
+            src_ref=src,
+            dst_ref=dst,
+            send_sem=net.send_sems.at[net.used],
+            recv_sem=net.recv_sems.at[net.used],
+            device_id=(target,),
+            device_id_type=MESH,
+        )
+        self.here = pltpu.make_async_copy(src, dst, net.local_sems.at[net.used_local])
+        net.used += 1
+        net.used_local += 1
+
+        @pl.when(self.remote)
+        def _():
+            self.away.start()
+
+        @pl.when(jnp.logical_not(self.remote))
+        def _():
+            self.here.start()
+
+    def wait(self):
+        @pl.when(self.remote)
+        def _():
+            self.away.wait()
+
+        @pl.when(jnp.logical_not(self.remote))
+        def _():
+            self.here.wait()
+
+
+def forget_to(lay, device):
+    return (device % 2) * (lay.n // 2) + device // 2
+
+
+def forget_from(lay, device):
+    return 2 * (device % (lay.n // 2)) + device // (lay.n // 2)
+
+
 def start_kernel(
-    lay, units, tok, cot, w_in, w_gate, w_forget, w_out, f_gate, pack,
-    tok_all, cot_all, mix_all, out_own, out_all, f_gate_all, every, send_sems, recv_sems, local_sems,
+    lay, units, tok, w_in, w_gate, w_forget, w_out, pack,
+    tok_all, mix_all, forget_own, out_own, out_all, every, *rest,
 ):
     n, W = lay.n, lay.n // 4
-    net = Net(lay, list(range(1, n)), send_sems, recv_sems, local_sems)
+    *rooms, send_sems, recv_sems, local_sems = rest
+    net = Net(lay, list(range(1, n)), send_sems, recv_sems, local_sems, rooms)
     me = net.me
 
     def region(base):
-        return lambda d: mix_all.at[pl.ds(base + w_slot(lay, d) * units, units)]
+        return lambda d, m: mix_all.at[pl.ds(base + w_slot(lay, d) * units, units)]
 
     g_in = WeightGather(net, w_in, region(0))
     g_gate = WeightGather(net, w_gate, region(W * units))
     g_forget = WeightGather(
-        net, w_forget, lambda d: mix_all.at[pl.ds(2 * W * units + f_slot(lay, d), 1)]
-    )
-    g_out = WeightGather(net, out_own, lambda d: out_all.at[w_slot(lay, d)])
-    g_ffn = WeightGather(net, f_gate, lambda d: f_gate_all.at[w_slot(lay, d)])
+        net, forget_own, lambda d, m: mix_all.at[pl.ds(2 * W * units + f_slot(lay, d), 1)]
+    )
+    g_out = WeightGather(net, out_own, lambda d, m: out_all.at[w_slot(lay, d)])
+    turn = Turn(net, forget_to(lay, me), w_forget, forget_own)
     g_in.start()
     g_gate.start()
-    tok_in = token_gather(net, tok, tok_all)
     mine = t_slot(lay, me)
     own = net.load(w_out.at[mine], out_own.at[mine])
     out_in = [
         net.put(w_out.at[t_slot(lay, lay.flip(me, m))], out_own.at[mine], m) for m in lay.tmasks[1:]
     ]
-    g_forget.start()
+    first = token_start(net, tok, tok_all)
     all_in = [net.put(pack, every.at[me], m) for m in range(1, n)]
     net.keep(pack, every.at[me])
+    turn.wait()
+    g_forget.start()
+    own.wait()
+    arrived(out_in)
+    g_out.start()
+    net.settle()
     for mask in g_in.masks():
         g_in.forward(mask)
         g_gate.forward(mask)
+    rest = token_finish(net, first, tok_all)
     for mask in g_forget.masks():
         g_forget.forward(mask)
-    own.wait()
-    arrived(out_in)
-    g_out.start()
-    g_ffn.start()
-    arrived(tok_in)
-    cot_in = token_gather(net, cot, cot_all)
-    for mask in g_out.masks():
         g_out.forward(mask)
-    for mask in g_ffn.masks():
-        g_ffn.forward(mask)
-    for gather in (g_in, g_gate, g_forget, g_out, g_ffn):
+    for gather in (g_in, g_gate, g_forget, g_out):
         gather.end()
-    arrived(cot_in)
+    arrived(rest)
     arrived(all_in)
     net.finish()
 
@@ -300,27 +385,49 @@
     return lay.tmasks[1:] + lay.wbits
 
 
-def scatter_kernel(lay, blocks, small, weight, got, got_small, weight_all, send_sems, recv_sems, local_sems):
-    net = Net(lay, group_peers(lay), send_sems, recv_sems, local_sems)
-    gather = WeightGather(net, weight, lambda d: weight_all.at[w_slot(lay, d)])
+def rel_gather(net, own, ahead, out):
+    return WeightGather(net, own, lambda d, m: out.at[net.lay.rel_slot(m)], ahead)
+
+
+def scatter_kernel(lay, blocks, small, weight, ahead, other, got, got_small, weight_all, other_got, *rest):
+    *rooms, send_sems, recv_sems, local_sems = rest
+    net = Net(lay, group_peers(lay), send_sems, recv_sems, local_sems, rooms)
+    gather = rel_gather(net, weight, ahead, weight_all)
     waits = token_scatter(net, blocks, got) + token_scatter(net, small, got_small)
     gather.start()
+    net.settle()
+    for mask in gather.masks():
+        gather.forward(mask)
+    waits.append(net.put(other, other_got, lay.ybits[0]))
+    gather.end()
+    arrived(waits)
+    net.finish()
+
+
+def gather_kernel_both(lay, own, weight, ahead, own_all, weight_all, *rest):
+    *rooms, send_sems, recv_sems, local_sems = rest
+    net = Net(lay, group_peers(lay), send_sems, recv_sems, local_sems, rooms)
+    first = token_start(net, own, own_all)
+    gather = rel_gather(net, weight, ahead, weight_all)
+    gather.start()
+    net.settle()
+    rest = token_finish(net, first, own_all)
     for mask in gather.masks():
         gather.forward(mask)
     gather.end()
-    arrived(waits)
+    arrived(rest)
     net.finish()
 
 
-def gather_both_kernel(lay, own, weight, own_all, weight_all, send_sems, recv_sems, local_sems):
-    net = Net(lay, group_peers(lay), send_sems, recv_sems, local_sems)
-    gather = WeightGather(net, weight, lambda d: weight_all.at[w_slot(lay, d)])
-    waits = token_gather(net, own, own_all)
-    gather.start()
-    for mask in gather.masks():
-        gather.forward(mask)
-    gather.end()
-    arrived(waits)
+def gather_kernel_two(lay, own, small, own_all, small_all, *rest):
+    *rooms, send_sems, recv_sems, local_sems = rest
+    net = Net(lay, lay.tmasks[1:], send_sems, recv_sems, local_sems, rooms)
+    first = token_start(net, own, own_all)
+    net.move(small, small_all.at[0])
+    waits = [net.put(small, small_all.at[j], m) for j, m in enumerate(lay.tmasks) if j]
+    net.settle()
+    rest = token_finish(net, first, own_all)
+    arrived(waits + rest)
     net.finish()
 
 
@@ -337,24 +444,30 @@
 
 
 class WeightReduce:
-    def __init__(self, net, part, place, local, stages, total, out):
-        self.net, self.part, self.place = net, part, place
-        self.local, self.stages, self.total, self.out = local, stages, total, out
-        self.bits = net.lay.rbits
+    def __init__(self, net, bits, part, place, local, stages, total, away=None):
+        self.net, self.bits, self.part, self.place, self.away = net, bits, part, place, away
+        self.local, self.stages, self.total = local, stages, total
         self.sent, self.waited = [], -1
 
-    def side(self, k):
-        return (self.net.me // self.bits[k]) % 2
+    def pick(self, k, i, away):
+        if self.away is not None:
+            return i + (self.stages[k].shape[0] if away and k else 0)
+        side = (self.net.me // self.bits[k]) % 2
+        return 2 * i + (1 - side if away else side)
 
     def start(self):
-        at = self.side(0)
         count = self.stages[0].shape[0]
         self.sent = [
-            self.net.put(self.part.at[self.place(2 * i + 1 - at)], self.stages[0].at[i], self.bits[0])
+            self.net.put(
+                (self.part if self.away is None else self.away).at[self.place(self.pick(0, i, True))],
+                self.stages[0].at[i],
+                self.bits[0],
+            )
             for i in range(count)
         ]
         self.loads = [
-            self.net.load(self.part.at[self.place(2 * i + at)], self.local.at[i]) for i in range(count)
+            self.net.load(self.part.at[self.place(self.pick(0, i, False))], self.local.at[i])
+            for i in range(count)
         ]
 
     def wait(self, k):
@@ -368,89 +481,100 @@
         if k == 0:
             for copy in self.loads:
                 copy.wait()
-        at = self.side(k)
-        mine = self.side(k + 1) if count > 1 else 0
 
         def one(i):
-            old = self.local.at[i] if k == 0 else self.stages[k - 1].at[2 * i + at]
-            if count == 1:
-                add_rows(self.total, stage.at[i], old)
-            else:
-                add_rows(stage.at[i], stage.at[i], old)
+            old = self.local.at[i] if k == 0 else self.stages[k - 1].at[self.pick(k, i, False)]
+            add_rows(self.total if count == 1 else stage.at[i], stage.at[i], old)
 
         if count == 1:
             one(0)
         else:
-            for i in range(count // 2):
-                one(2 * i + 1 - mine)
-            for i in range(count // 2):
-                one(2 * i + mine)
+            for away in (True, False):
+                for i in range(count // 2):
+                    one(self.pick(k + 1, i, away))
 
     def send(self, k):
-        at = self.side(k)
         self.sent = [
-            self.net.put(self.stages[k - 1].at[2 * i + 1 - at], self.stages[k].at[i], self.bits[k])
+            self.net.put(self.stages[k - 1].at[self.pick(k, i, True)], self.stages[k].at[i], self.bits[k])
             for i in range(self.stages[k].shape[0])
         ]
 
-    def store(self):
-        if self.out is not None:
-            self.net.keep(self.total, self.out)
-
-
-def reduce_kernel(lay, n_parts, *refs):
-    W = lay.n // 4
-    depth = len(lay.rbits)
-    parts, refs = refs[:n_parts], refs[n_parts:]
-    (du, mixed, vectors), refs = refs[:3], refs[3:]
-    outs, refs = refs[: n_parts - 1], refs[n_parts - 1 :]
-    (out_cols, got_du, got_mixed, all_vectors), refs = refs[:4], refs[4:]
-    scratch, (send_sems, recv_sems, local_sems) = refs[:-3], refs[-3:]
+
+PARTS = (("forget", 0), ("out", 0), ("down", 1), ("gate", 0), ("in", 0))
+
+
+def forget_place(lay, slot):
+    return ((slot // 2) % lay.Y * 2 + slot % 2) * 2 + slot // (2 * lay.Y)
+
+
+def reduce_kernel(lay, *refs):
+    count = len(PARTS)
+    parts, refs = refs[:count], refs[count:]
+    (away, up, du, vectors), refs = refs[:4], refs[4:]
+    outs, refs = refs[:count], refs[count:]
+    (got_up, got_du, all_vectors), refs = refs[:3], refs[3:]
+    scratch, (send_sems, recv_sems, local_sems) = list(refs[:-3]), refs[-3:]
     net = Net(lay, list(range(1, lay.n)), send_sems, recv_sems, local_sems)
     me = net.me
-    jobs = []
-    for i, part in enumerate(parts):
-        local, *stages = scratch[i * (depth + 2) : i * (depth + 2) + depth + 1]
-        total = scratch[i * (depth + 2) + depth + 1]
-        place = (lambda k: k) if i else (lambda k: ((k // 2) % lay.Y * 2 + k % 2) * 2 + k // (2 * lay.Y))
-        out = None if i == 1 else outs[i - (i > 1)]
-        jobs.append(WeightReduce(net, part, place, local, stages, total, out))
-    waits = token_scatter(net, du, got_du)
-    for job in jobs:
-        job.start()
+    jobs, turns, waits = [], [], []
+    for (name, first), part in zip(PARTS, parts):
+        bits = lay.rbits[first:]
+        local = scratch.pop(0)
+        stages = [scratch.pop(0) for _ in bits]
+        place = partial(forget_place, lay) if name == "forget" else lambda k: k
+        jobs.append(
+            WeightReduce(
+                net, bits, part, place, local, stages, scratch.pop(0), away if name == "down" else None
+            )
+        )
+    jobs[0].start()
+    jobs[1].start()
+    jobs[2].start()
+    waits += [net.put(up, got_up, lay.ZH)]
+    waits += token_scatter(net, du, got_du)
+    jobs[3].start()
+    jobs[4].start()
     waits += [net.put(vectors.at[lay.flip(me, m)], all_vectors.at[me], m) for m in range(1, lay.n)]
     net.keep(vectors.at[me], all_vectors.at[me])
 
-    def finish(job, i):
-        job.store()
-        if i == 1:
-            rows = job.total.shape[0] // 4
+    def finish(i):
+        total, out = jobs[i].total, outs[i]
+        if PARTS[i][0] == "forget":
+            turns.append(Turn(net, forget_from(lay, me), total, out))
+        elif PARTS[i][0] == "out":
+            rows = total.shape[0] // 4
             mine = t_slot(lay, me)
 
             def cut(slot):
-                return job.total.at[pl.ds(pl.multiple_of(slot * rows, rows), rows)]
-
-            net.keep(cut(mine), out_cols.at[mine])
+                return total.at[pl.ds(pl.multiple_of(slot * rows, rows), rows)]
+
+            net.keep(cut(mine), out.at[mine])
             for m in lay.tmasks[1:]:
-                waits.append(net.put(cut(t_slot(lay, lay.flip(me, m))), out_cols.at[mine], m))
-
-    for tick in range(n_parts + depth - 1):
-        for k in range(depth):
-            i = tick - k
-            valid = 0 <= i < n_parts
-            if valid:
+                waits.append(net.put(cut(t_slot(lay, lay.flip(me, m))), out.at[mine], m))
+        else:
+            net.keep(total, out)
+
+    depth = len(lay.rbits)
+    for tick in range(count + depth - 1):
+        for stage in range(depth):
+            i = tick - stage
+            valid = 0 <= i < count
+            k = stage - PARTS[i][1] if valid else 0
+            if valid and k >= 0:
                 jobs[i].wait(k)
                 jobs[i].add(k)
-            if k + 1 < depth:
-                if 0 <= i - 1 < n_parts:
-                    jobs[i - 1].wait(k + 1)
-                if valid:
+            if stage + 1 < depth:
+                if 0 <= i - 1 < count:
+                    ahead = stage + 1 - PARTS[i - 1][1]
+                    if ahead >= 0:
+                        jobs[i - 1].wait(ahead)
+                if valid and k >= 0:
                     jobs[i].send(k + 1)
             elif valid:
-                finish(jobs[i], i)
-        if tick == 1:
-            waits += token_scatter(net, mixed, got_mixed)
+                finish(i)
     arrived(waits)
+    for turn in turns:
+        turn.wait()
     net.finish()
 
 
@@ -706,7 +830,7 @@
         out_specs=tuple(VMEM for _ in outs),
         scratch_shapes=list(scratch),
         compiler_params=pltpu.CompilerParams(vmem_limit_bytes=48 << 20),
-        cost_estimate=pl.CostEstimate(flops=20_000_000, bytes_accessed=12_000_000, transcendentals=0),
+        cost_estimate=estimate(7),
         name=name,
     )
 
@@ -760,46 +884,50 @@
     packed = jnp.concatenate([gain_mix, gain_ffn, gain_out, lower_bound, rotation])
     pack_rows = -(-packed.shape[0] // 128)
     packed = jnp.pad(packed, (0, 8 * 128 - packed.shape[0])).reshape(8, 128)
-    forget_to = [(2 * e + b, b * (n // 2) + e) for e in range(n // 2) for b in range(2)]
-    forget_from = [(d, s) for s, d in forget_to]
-    forget_low = lax.ppermute(forget_proj.astype(LOW), "dp", forget_to)
     out_cols = out_proj.astype(LOW).reshape(r_in, 2, 2, Y, 2, 2 * r_in)
     out_cols = out_cols.transpose(2, 4, 0, 1, 3, 5).reshape(4, r_in, 2 * half)
     units = r_in // r_f
     r_ffn = ffn_gate.shape[0]
-    tok_all, cot_all, w_mix, _, w_out, w_ffn_gate, every = net_call(
+    tok_all, w_mix, _, _, w_out, every = net_call(
         partial(start_kernel, lay, units),
         lay,
         (
             tokens,
-            cotangent,
             in_proj.astype(LOW).reshape(units, r_f, width),
             gate_proj.astype(LOW).reshape(units, r_f, width),
-            forget_low.reshape(1, r_f, width),
+            forget_proj.astype(LOW).reshape(1, r_f, width),
             out_cols,
-            ffn_gate.astype(LOW),
             packed,
         ),
         [
             ((4, length, width), LOW),
-            ((4, length, width), LOW),
             ((W * (2 * units + 1), r_f, width), LOW),
+            ((1, r_f, width), LOW),
             ((4, r_in, 2 * half), LOW),
             ((W, 4, r_in, 2 * half), LOW),
-            ((W, r_ffn, width), LOW),
             ((n, 8, 128), F32),
         ],
-        5 * (W - 1) + 9 + n - 1,
-        16,
+        4 * (W - 1) + 8 + n - 1,
+        24,
         0,
         "start",
-    )
+        60,
+        [
+            pltpu.VMEM((units, r_f, width), LOW),
+            pltpu.VMEM((units, r_f, width), LOW),
+            pltpu.VMEM((length, width), LOW),
+            pltpu.VMEM((1, r_f, width), LOW),
+            pltpu.VMEM((4, r_in, 2 * half), LOW),
+        ],
+    )
+    f_gate, f_up, f_down = lax.optimization_barrier(
+        (ffn_gate.astype(LOW), ffn_up.astype(LOW), ffn_down.astype(LOW), every)
+    )[:3]
+    gate_z = lay.send(f_gate, lay.ZH)
     tok_all = tok_all.reshape(total, width)
-    cot_all = cot_all.reshape(total, width)
     w_mix = w_mix.reshape(5 * half, width)
     w_out = w_out.reshape(2, Y, 2, 2, 2, r_in, 2 * half).transpose(0, 3, 1, 4, 2, 5, 6)
     w_out = w_out.reshape(width, 2 * half)
-    w_ffn_gate = w_ffn_gate.reshape(W * r_ffn, width)
     every = every[:, :pack_rows, :].reshape(n, pack_rows * 128)
     g_mix = every[:, 0:r_in].reshape(1, width)
     g_ffn = every[:, r_in : 2 * r_in].reshape(1, width)
@@ -832,6 +960,8 @@
         name="gates",
     )(proj, keep, par)
     summ_all = small_gather(lay, summ, lay.wmasks, partial(w_slot, lay), W, 1).reshape(n, 8, half)
+    cot_blocks = lay.gather_t(tie(cotangent, summ_all))
+    up_z = lay.send(tie(f_up, gate_z, summ_all), lay.ZH)
     st_re, st_im, be_re, be_im, unit, squares = plain_call(
         partial(state_kernel, half, length, n),
         [wide] * 4 + [((total, 2 * half), LOW), ((total, LANES), F32)],
@@ -844,17 +974,25 @@
     def t_blocks(value):
         return [value[j * length : (j + 1) * length] for j in range(4)]
 
-    got, got_squares, w_ffn_up = net_call(
+    got, got_squares, w_ffn_gate, down_y = net_call(
         partial(scatter_kernel, lay),
         lay,
-        (branch_low.reshape(4, length, width), squares.reshape(4, length, LANES), ffn_up.astype(LOW)),
-        [((3, length, width), LOW), ((3, length, LANES), F32), ((W, r_ffn, width), LOW)],
-        W - 1 + 6,
-        2,
+        (branch_low.reshape(4, length, width), squares.reshape(4, length, LANES), f_gate, gate_z, f_down),
+        [
+            ((3, length, width), LOW),
+            ((3, length, LANES), F32),
+            ((W, r_ffn, width), LOW),
+            ((r_ffn, width), LOW),
+        ],
+        W - 1 + 7,
+        4,
         4,
         "branch",
-    )
-    w_ffn_up = w_ffn_up.reshape(W * r_ffn, width)
+        40,
+        [pltpu.VMEM((r_ffn, width), LOW)] * 2,
+    )
+    w_ffn_gate = w_ffn_gate.reshape(W * r_ffn, width)
+    down_z = lay.send(tie(f_down, up_z, got), lay.ZH)
 
     def own_sum(whole, arrived_parts):
         value = whole[:length].astype(F32)
@@ -869,18 +1007,27 @@
     r_res = lax.rsqrt(jnp.mean(residual * residual, axis=-1, keepdims=True) + EPS)
     ffn_low = (residual * r_res * g_ffn).astype(LOW)
 
-    ffn_all, w_down = net_call(
-        partial(gather_both_kernel, lay),
+    ffn_all, w_ffn_up = net_call(
+        partial(gather_kernel_both, lay),
         lay,
-        (ffn_low, ffn_down.astype(LOW)),
+        (ffn_low, f_up, up_z),
         [((4, length, width), LOW), ((W, r_ffn, width), LOW)],
-        W - 1 + 3,
-        2,
+        W - 1 + 4,
+        6,
         5,
         "ffn_in",
+        40,
+        [pltpu.VMEM((length, width), LOW)] + [pltpu.VMEM((r_ffn, width), LOW)] * 2,
     )
     ffn_all = ffn_all.reshape(total, width)
-    w_down = w_down.reshape(W * r_ffn, width)
+    w_ffn_up = w_ffn_up.reshape(W * r_ffn, width)
+    down_pieces = [f_down, down_z]
+    for bit in lay.ybits:
+        first = [down_y] if bit == lay.ybits[0] else []
+        down_pieces = down_pieces + first + [lay.send(v, bit) for v in down_pieces[len(first) :]]
+    down_pieces[0] = tie(f_down, down_z)
+    cot_all = jnp.concatenate(cot_blocks, axis=0)
+    w_down = jnp.concatenate(down_pieces + [lay.send(v, lay.C) for v in down_pieces], axis=0)
     gate_value = contract(ffn_all, w_ffn_gate)
     up_value = contract(ffn_all, w_ffn_up)
     s_gate = jax.nn.sigmoid(gate_value)
@@ -894,7 +1041,30 @@
         + jnp.dot(grad_up, w_ffn_up, preferred_element_type=F32)
     ).astype(LOW)
     du = lay.scatter_t(t_blocks(du_low))
-    mixed_low = jnp.dot(hidden_low, w_down, preferred_element_type=F32).astype(LOW)
+
+    def join(kept, got):
+        return kept.astype(F32) + got.astype(F32)
+
+    def split_sum(kept, got):
+        rows = kept.shape[0] // 2
+        return join(kept[:rows], got[:rows]).astype(LOW), join(kept[rows:], got[rows:]).astype(LOW)
+
+    def over_core(part):
+        rows = part.shape[0] // 2
+        return split_sum(part[:rows], lay.send(part[rows:], lay.C))
+
+    def over_y(kept, away):
+        for bit in lay.ybits:
+            kept, away = split_sum(kept, lay.send(away, bit))
+        return kept, away
+
+    left_gate, left_up, left_hidden, _ = lax.optimization_barrier(
+        (grad_gate, grad_up, hidden_low, du_low)
+    )
+    gate_kept, gate_away = over_core(outer_rows(left_gate, ffn_all).astype(LOW))
+    up_kept, up_away = over_core(outer_rows(left_up, ffn_all).astype(LOW))
+    down_part = outer_rows(left_hidden, cot_all).astype(LOW)
+    mixed_low = jnp.dot(left_hidden, w_down, preferred_element_type=F32).astype(LOW)
 
     du_gain = du * g_ffn
     grad_residual = (
@@ -903,12 +1073,30 @@
         - residual * (r_res * r_res * r_res) * jnp.mean(residual * du_gain, axis=-1, keepdims=True)
     )
     ffn_gain_part = jnp.sum(du * residual * r_res, axis=0)
-    grad_low = grad_residual.astype(LOW)
+    grad_low = tie(grad_residual.astype(LOW), gate_away)
     inner = jnp.sum(grad_low.astype(F32) * branch, axis=-1, keepdims=True) / width
-    scale = jnp.concatenate([r_state, r_state * r_state * r_state * inner], axis=1)
-
-    grad_all = jnp.concatenate(lay.gather_t(grad_low), axis=0)
-    scale_all = jnp.concatenate(lay.gather_t(scale), axis=0)
+    scale = jnp.where(
+        jnp.arange(LANES)[None, :] == 0, r_state, r_state * r_state * r_state * inner
+    )
+
+    grad_all, scale_all = net_call(
+        partial(gather_kernel_two, lay),
+        lay,
+        (grad_low, scale),
+        [((4, length, width), LOW), ((4, length, LANES), F32)],
+        7,
+        4,
+        6,
+        "grad_in",
+        27,
+        [pltpu.VMEM((length, width), LOW), pltpu.VMEM((length, LANES), F32)],
+    )
+    gate_kept, gate_away = over_y(gate_kept, gate_away)
+    mixed_blocks = t_blocks(tie(mixed_low, grad_all))
+    mixed = lay.scatter_t(mixed_blocks)
+    mixed_out = (residual + mixed).astype(LOW)
+    grad_all = grad_all.reshape(total, width)
+    scale_all = scale_all.reshape(total, LANES)
     grad_mid = jnp.dot(grad_all, w_out, preferred_element_type=F32)
     gs_re, gs_im, gate_low, mid, out_gain_part, back = plain_call(
         partial(back_kernel, half, length),
@@ -919,6 +1107,7 @@
         scratch=[pltpu.VMEM((8, 2 * half), F32)],
         name="back_gates",
     )(grad_mid, st_re, st_im, proj, g_out, scale_all, d_re, d_im)
+    back = tie(back, gate_away)
     back_all = small_gather(lay, back, lay.wmasks, partial(w_slot, lay), W, 2).reshape(n, 8, half)
     grads, lower_part, angle_part = plain_call(
         partial(adjoint_kernel, half, length, n),
@@ -956,38 +1145,44 @@
     grad_w_out = outer_rows(grad_all, mid).astype(LOW).reshape(2, 2, Y, 2, 2, r_in, 2 * half)
     grad_w_out = grad_w_out.transpose(0, 2, 4, 1, 3, 5, 6).reshape(W, 4 * r_in, 2 * half)
     grad_w_mix = outer_rows(grads, normed).astype(LOW)
+    down_kept, down_away = over_core(down_part)
+    up_kept, up_away = over_y(up_kept, tie(up_away, back_all))
+    gate_got = lay.send(tie(gate_away, back_all), lay.ZH)
+    du_mix_low = tie(du_mix_low, mixed_out, gate_got)
     parts = [
         grad_w_mix[4 * half :].reshape(W, r_f, width),
         grad_w_out,
-        outer_rows(grad_gate, ffn_all).astype(LOW).reshape(W, r_ffn, width),
-        outer_rows(grad_up, ffn_all).astype(LOW).reshape(W, r_ffn, width),
-        outer_rows(hidden_low, cot_all).astype(LOW).reshape(W, r_ffn, width),
+        down_kept.reshape(W // 4, r_ffn, width),
+        grad_w_mix[2 * half : 4 * half].reshape(W, r_in, width),
         grad_w_mix[: 2 * half].reshape(W, r_in, width),
-        grad_w_mix[2 * half : 4 * half].reshape(W, r_in, width),
     ]
-    scratch, copies, local_copies = [], 6 + 3 + n - 1, 2
-    for part in parts:
-        blocks, shape = W // 2, part.shape[1:]
+    scratch, copies, local_copies = [], 6 + 3 + n + 2, 4
+    for (_, first), part in zip(PARTS, parts):
+        blocks, shape = W // 2 >> first, part.shape[1:]
         scratch.append(pltpu.VMEM((blocks,) + shape, LOW))
         local_copies += blocks + 1
-        for _ in lay.rbits:
+        for _ in lay.rbits[first:]:
             scratch.append(pltpu.VMEM((blocks,) + shape, LOW))
             copies += blocks
             blocks //= 2
         scratch.append(pltpu.VMEM(shape, F32))
-    forget_part, *w_grads, out_cols_grad, got_du, got_mixed, owned = net_call(
-        partial(reduce_kernel, lay, len(parts)),
+    forget_proj_grad, out_cols_grad, ffn_down_grad, gate_proj_grad, in_proj_grad, got_up, got_du, owned = net_call(
+        partial(reduce_kernel, lay),
         lay,
         (
             *parts,
+            down_away.reshape(W // 4, r_ffn, width),
+            up_away,
             du_mix_low.reshape(4, length, width),
-            mixed_low.reshape(4, length, width),
             to_owner,
         ),
-        [(part.shape[1:], F32) for i, part in enumerate(parts) if i != 1]
-        + [
+        [
+            ((r_f, width), F32),
             ((4, r_in, 2 * half), F32),
-            ((3, length, width), LOW),
+            ((r_ffn, width), F32),
+            ((r_in, width), F32),
+            ((r_in, width), F32),
+            ((r_ffn, width), LOW),
             ((3, length, width), LOW),
             ((n, 8, 128), F32),
         ],
@@ -995,17 +1190,18 @@
         local_copies,
         3,
         "reduce",
+        120,
         scratch,
-    )
-    ffn_gate_grad, ffn_up_grad, ffn_down_grad, in_proj_grad, gate_proj_grad = w_grads
-    forget_proj_grad = lax.ppermute(forget_part, "dp", forget_from)
+        56 << 20,
+    )
+    ffn_gate_grad = join(gate_kept, gate_got)
+    ffn_up_grad = join(up_kept, got_up)
     out_proj_grad = (
         out_cols_grad.reshape(2, 2, r_in, 2, Y, 2 * r_in)
         .transpose(2, 3, 0, 4, 1, 5)
         .reshape(r_in, width)
     )
     owned = jnp.sum(owned, axis=0).reshape(-1)
-    mixed_out = (residual + own_sum(mixed_low, got_mixed)).astype(LOW)
     du_mix = own_sum(du_mix_low, got_du)
     dg_mix = du_mix * g_mix
     tokens_grad = (

time: 733 us -> 650 us (0.89)
  Pallas kernels: 482 us -> 364 us
  local copies, waits for them, and re-layouts: 43.6 us -> 66 us
  other arithmetic: 34.8 us -> 55.7 us
  starting transfers between devices: 36.3 us -> 17.6 us
  waiting for transfers between devices: 32.3 us -> 45.3 us
    pallas_call x4 -> x5, Pallas kernels: 427 us -> 308 us  [net_call(): pl.pallas_call(body, out_shape=tuple((jax.ShapeDtypeStruct(s, d) for s, d...]
    convert_element_type x2 -> x7, other arithmetic: 3.64 us -> 26.7 us  [the longest x2 10.5 us: split_sum(): join(kept[:rows], got[:rows]).astype(LOW)]
    ppermute x9 -> x23, waiting for transfers between devices: 31 us -> 45.3 us  [send(): return lax.ppermute(value, 'dp', [(i, i ^ mask) for i in range(self.n)])]
    ppermute x9 -> x23, starting transfers between devices: 27.9 us -> 17.6 us  [send(): return lax.ppermute(value, 'dp', [(i, i ^ mask) for i in range(self.n)])]
    ppermute x2 -> x0, starting transfers between devices: 8.39 us -> none  [the longest x1 5.61 us: local(): forget_low = lax.ppermute(forget_proj.astype(LOW), 'dp', forget_to)]
    slice x1 -> x4, local copies, waits for them, and re-layouts: 2.55 us -> 10.4 us  [the longest x3 5.46 us: over_core(): return split_sum(part[:rows], lay.send(part[rows:], lay.C))]
    unnamed x149 -> x195, local copies, waits for them, and re-layouts: 23.4 us -> 30.5 us
  transfers between devices with their start and end apart: 11 -> 23, of which waited for: 4 -> 6; matrix products, arithmetic and copies ran while one was open for 7% -> 20% of each run, Pallas kernels for 0% -> 20%
where the time goes in v3:
time: 650 us; the launch traced here: 642 us
  Pallas kernels  364 us (56%)
  matrix products  91.7 us (14%)
  local copies, waits for them, and re-layouts  66 us (10%)
  other arithmetic  55.7 us (9%)
  waiting for transfers between devices  45.3 us (7%)
  starting transfers between devices  17.6 us (3%)
    pallas_call x5, Pallas kernels, net_call(): pl.pallas_call(body, out_shape=tuple((jax.ShapeDtypeStruct(s, d) for s, d...  308 us
    ppermute x23, waiting for transfers between devices, send(): return lax.ppermute(value, 'dp', [(i, i ^ mask) for i in range(self.n)])  45.3 us
    dot_general x5, matrix products, contract(): lax.dot_general(left_rows, right_rows, (((1,), (1,)), ((), ())), preferre...  35.6 us
    unnamed x195, local copies, waits for them, and re-layouts  30.5 us
    pallas_call x2, Pallas kernels, small_gather(): pl.pallas_call(partial(gather_kernel, lay, masks, slot_of), out_shape=jax...  26.5 us
    dot_general x5, matrix products, outer_rows(): lax.dot_general(left_rows, right_rows, (((0,), (0,)), ((), ())), preferre...  25.8 us
    ppermute x23, starting transfers between devices, send(): return lax.ppermute(value, 'dp', [(i, i ^ mask) for i in range(self.n)])  17.6 us
  transfers between devices with their start and end apart: 23, of which 6 were waited for; matrix products, arithmetic and copies ran while one was open for 20% of the time, Pallas kernels for 20%

profile of v3, /device:TPU:1, one launch (start us, length us, event | category | flops | bytes accessed | tf_op | source)
XLA Modules:
  0.0 642.0 jit_solution(9962520601834929032)
XLA Ops:
  6.0 62.8 %start.1 = (bf16[4,160,2048]{2,1,0:T(8,128)(2,1)}, bf16[40,32,2048]{2,1,0:T(8,128)(2,1)}, bf16[1,32,2048]{2,1,0:T(8,128)(2,1)}, bf16[4,64,512]{2,1,0:T(8,128)(2,...) custom-call(bf16[160,2048]{1,0:T(8,128)(2,1)} %tok.1, bf16[2,32,2048]{2,1,0:T(8,128)(2,1)} %bitcast.174, ...), custom_call_target="tpu_custom_call" | custom-call | flops 60000002048 | tf_op jit(solution)/shard_map/start/pallas_call | solution.py:258
  76.1 5.4 fusion.34.proj
  81.6 5.7 gates.1
  88.8 11.5 %shard_map.263 = f32[8,4,8,256]{3,2,1,0:T(8,128)} custom-call(f32[4,8,256]{2,1,0:T(8,128)} %copy-done.27), custom_call_target="tpu_custom_call" | custom-call | flops 10000000000 | tf_op jit(solution)/shard_map/pallas_call | solution.py:118
  111.7 7.4 %states.1 = (f32[2,640,128]{2,1,0:T(8,128)S(1)}, f32[2,640,128]{2,1,0:T(8,128)S(1)}, f32[2,640,128]{2,1,0:T(8,128)S(1)}, f32[2,640,128]{2,1,0:T(8,128)S(1)}, bf1...) custom-call(s32[36]{0:T(128)S(1)} %pad_add_fusion.1.ints, f32[32,8,256]{2,1,0:T(8,128)S(1)} %bitcast.152, ...), custom_call_target="tpu_custom_call" | custom-call | flops 7000000000 | tf_op jit(solution)/shard_map/states/pallas_call | solution.py:965
  121.7 4.7 convolution_convert_fusion.6
  133.4 13.8 %collective-permute-done.3 = bf16[160,2048]{1,0:T(8,128)(2,1)} collective-permute-done((bf16[160,2048]{1,0:T(8,128)(2,1)}, bf16[160,2048]{1,0:T(8,128)(2,1)}, u32[]{:S(2)}, u32[]{:S(2)}) %collective-permute-start.3) | collective-permute-done | bytes 655392 | tf_op jit(solution)/shard_map/ppermute | solution.py:71
  149.8 49.4 %branch.1 = (bf16[3,160,2048]{2,1,0:T(8,128)(2,1)}, f32[3,160,128]{2,1,0:T(8,128)}, bf16[8,176,2048]{2,1,0:T(8,128)(2,1)}, bf16[176,2048]{1,0:T(8,128)(2,1)}) custom-call(bf16[4,160,2048]{2,1,0:T(8,128)(2,1)} %bitcast.170, f32[4,160,128]{2,1,0:T(8,128)} %bitcast.148, bf16[176,2048]{1,0:T(8,128)(2,1)} %convert_element_type.291.weight, ...), custom_call_target="tpu_custom_call" | custom-call | flops 40000000000 | tf_op jit(solution)/shard_map/branch/pallas_call | solution.py:258
  207.8 41.0 %ffn_in.1 = (bf16[4,160,2048]{2,1,0:T(8,128)(2,1)}, bf16[8,176,2048]{2,1,0:T(8,128)(2,1)}) custom-call(bf16[160,2048]{1,0:T(8,128)(2,1)} %multiply_convert_fusion.5.own, bf16[176,2048]{1,0:T(8,128)(2,1)} %convert_element_type.292.weight, bf16[176,2048]{1,0:T(8,128)(2,1)} %collective-permute-done.4.ahead), custom_call_target="tpu_custom_call" | custom-call | flops 40000000000 | tf_op jit(solution)/shard_map/ffn_in/pallas_call | solution.py:258
  248.9 9.7 %fusion.36 = f32[640,1408]{1,0:T(8,128)} fusion(bf16[640,2048]{1,0:T(8,128)(2,1)} %bitcast.193, bf16[1408,2048]{1,0:T(8,128)(2,1)} %bitcast.185), kind=kOutput, calls=%fused_computation.170 | convolution fusion | flops 3690987520 | bytes 11993088 | tf_op jit(solution)/shard_map/dot_general | solution.py:20
  258.6 6.0 fusion.35
  268.1 14.7 %collective-permute-done.6 = bf16[176,2048]{1,0:T(8,128)(2,1)S(1)} collective-permute-done((bf16[176,2048]{1,0:T(8,128)(2,1)S(1)}, bf16[176,2048]{1,0:T(8,128)(2,1)S(1)}, u32[]{:S(2)}, u32[]{:S(2)}) %collective-permute-start.6) | collective-permute-done | bytes 720928 | tf_op jit(solution)/shard_map/ppermute | solution.py:71
  285.8 9.7 %multiply_convert_fusion.2 = (bf16[640,1408]{1,0:T(8,128)(2,1)}, bf16[640,1408]{1,0:T(8,128)(2,1)}, bf16[640,1408]{1,0:T(8,128)(2,1)}) fusion(f32[640,1408]{1,0:T(8,128)} %fusion.35, f32[640,1408]{1,0:T(8,128)} %fusion.36, bf16[640,2048]{1,0:T(8,128)(2,1)S(1)} %copy-done.63, bf16[1408,2048]{1,0:T(8,128)(2,1)S(1)} %constant_dynamic-update-slice_fusion.4), kind=kOutput, calls=%fused_computation.10 | convolution fusion | flops 3704504320 | bytes 21004288 | tf_op jit(solution)/shard_map/dot_general | solution.py:20
  295.5 6.9 %fusion.37 = f32[640,2048]{1,0:T(8,128)S(1)} fusion(bf16[640,1408]{1,0:T(8,128)(2,1)} %get-tuple-element.113, bf16[1408,2048]{1,0:T(8,128)(2,1)} %bitcast.189), kind=kOutput, calls=%fused_computation.171 | convolution fusion | flops 3690987520 | bytes 12812288 | tf_op jit(solution)/shard_map/dot_general | solution.py:1041
  302.5 4.4 add_convert_fusion
  309.6 6.4 convolution_convert_fusion.3
  322.2 4.9 convolution_convert_fusion
  331.8 5.1 convolution_convert_fusion.1
  340.5 5.5 convolution_convert_fusion.5
  355.1 6.0 add_convert_fusion.5
  365.0 25.8 %grad_in.1 = (bf16[4,160,2048]{2,1,0:T(8,128)(2,1)}, f32[4,160,128]{2,1,0:T(8,128)}) custom-call(bf16[160,2048]{1,0:T(8,128)(2,1)} %copy-done.47, f32[160,128]{1,0:T(8,128)} %broadcast_select_fusion.small), custom_call_target="tpu_custom_call" | custom-call | flops 27000000512 | tf_op jit(solution)/shard_map/grad_in/pallas_call | solution.py:258
  394.9 4.5 fusion.38.grad_mid
  400.9 4.6 add_convert_fusion.2
  405.5 7.6 %back_gates.1 = (f32[2,640,128]{2,1,0:T(8,128)S(1)}, f32[2,640,128]{2,1,0:T(8,128)S(1)}, bf16[640,512]{1,0:T(8,128)(2,1)S(1)}, bf16[640,512]{1,0:T(8,128)(2,1)S(...) custom-call(f32[640,512]{1,0:T(8,128)} %fusion.38.grad_mid, f32[2,640,128]{2,1,0:T(8,128)S(1)} %copy-done.20, ...), custom_call_target="tpu_custom_call" | custom-call | flops 7000000000 | tf_op jit(solution)/shard_map/back_gates/pallas_call | solution.py:1101
  419.8 5.7 add_convert_fusion.3
  430.8 15.1 %shard_map.264 = f32[8,4,8,256]{3,2,1,0:T(8,128)} custom-call(f32[4,8,256]{2,1,0:T(8,128)} %copy-done.26), custom_call_target="tpu_custom_call" | custom-call | flops 10000000000 | tf_op jit(solution)/shard_map/pallas_call | solution.py:118
  450.1 8.5 %adjoints.1 = (bf16[640,1280]{1,0:T(8,128)(2,1)}, f32[8,256]{1,0:T(8,128)S(1)}, f32[8,256]{1,0:T(8,128)S(1)}) custom-call(s32[36]{0:T(128)S(1)} %copy-done.10, f32[32,8,256]{2,1,0:T(8,128)S(1)} %bitcast.153, f32[32,8,256]{2,1,0:T(8,128)S(1)} %bitcast.154, f32[2,640,128]{2,1,0:T(8,128)S(1)} %copy-done.14, f32[2,640,128]{2,1,0:T(8,128)S(1)} %copy-done.16, ...), custom_call_target="tpu_custom_call" | custom-call | flops 7000000000 | tf_op jit(solution)/shard_map/adjoints/pallas_call | solution.py:1112
  459.1 9.1 %multiply_reduce_fusion = (f32[2048]{0:T(1024)S(1)}, bf16[640,2048]{1,0:T(8,128)(2,1)S(1)}, bf16[640,2048]{1,0:T(8,128)(2,1)}) fusion(bf16[4,160,2048]{2,1,0:T(8,128)(2,1)} %get-tuple-element.70, f32[640]{0:T(1024)S(1)} %copy-done.67, f32[2048]{0:T(1024)S(1)} %copy-done.65, bf16[640,1280]{1,0:T(8,128)(2,1)} %get-tuple-element.109, ...), kind=kOutput, calls=%fused_computation.5 | convolution fusion | flops 3365926912 | bytes 14764544 | tf_op jit(solution)/shard_map/dot_general | solution.py:1120
  468.2 6.1 convolution_convert_fusion.2
  477.7 5.0 fusion.27
  482.7 9.6 %collective-permute-done.19 = bf16[176,2048]{1,0:T(8,128)(2,1)S(1)} collective-permute-done((bf16[176,2048]{1,0:T(8,128)(2,1)}, bf16[176,2048]{1,0:T(8,128)(2,1)S(1)}, u32[]{:S(2)}, u32[]{:S(2)}) %collective-permute-start.19) | collective-permute-done | bytes 720928 | tf_op jit(solution)/shard_map/ppermute | solution.py:71
  496.2 129.1 %reduce.6 = (f32[32,2048]{1,0:T(8,128)}, f32[4,64,512]{2,1,0:T(8,128)}, f32[176,2048]{1,0:T(8,128)}, f32[64,2048]{1,0:T(8,128)}, f32[64,2048]{1,0:T(8,128)}, /*i...) custom-call(bf16[8,32,2048]{2,1,0:T(8,128)(2,1)} %bitcast.168, ...), custom_call_target="tpu_custom_call" | custom-call | flops 120000004096 | tf_op jit(solution)/shard_map/reduce/pallas_call | solution.py:258
  (336 shorter events, 128.4 us)
Async XLA Ops:
  6.0 64.3 %copy-start.75 = (s32[32]{0:T(128)S(1)}, s32[32]{0:T(128)}, u32[]{:S(2)}) copy-start(s32[32]{0:T(128)} %param.19) | copy-start | bytes 388
  6.0 64.7 %copy-start.74 = (s32[5]{0:T(128)S(1)}, s32[5]{0:T(128)}, u32[]{:S(2)}) copy-start(s32[5]{0:T(128)} %param.18) | copy-start | bytes 64
  100.3 28.4 %collective-permute-start.1 = (bf16[160,2048]{1,0:T(8,128)(2,1)}, bf16[160,2048]{1,0:T(8,128)(2,1)}, u32[]{:S(2)}, u32[]{:S(2)}) collective-permute-start(bf16[160,2048]{1,0:T(8,128)(2,1)} %param.17), channel_id=1, source_target_pairs={{0,2},{1,3},{2,0},{3,1},{4,6},{5,7},{6,4},{7,5},{8,10},{9,11},{10,... | collective-permute-start | bytes 1966088 | tf_op jit(solution)/shard_map/ppermute | solution.py:71
  100.6 31.6 %collective-permute-start.2 = (bf16[160,2048]{1,0:T(8,128)(2,1)}, bf16[160,2048]{1,0:T(8,128)(2,1)}, u32[]{:S(2)}, u32[]{:S(2)}) collective-permute-start(bf16[160,2048]{1,0:T(8,128)(2,1)} %param.17), channel_id=1, source_target_pairs={{0,8},{1,9},{2,10},{3,11},{4,12},{5,13},{6,14},{7,15},{8,0},{9,1},... | collective-permute-start | bytes 1966088 | tf_op jit(solution)/shard_map/ppermute | solution.py:71
  100.6 46.6 %collective-permute-start.3 = (bf16[160,2048]{1,0:T(8,128)(2,1)}, bf16[160,2048]{1,0:T(8,128)(2,1)}, u32[]{:S(2)}, u32[]{:S(2)}) collective-permute-start(bf16[160,2048]{1,0:T(8,128)(2,1)} %param.17), channel_id=1, source_target_pairs={{0,10},{1,11},{2,8},{3,9},{4,14},{5,15},{6,12},{7,13},{8,2},{9,3},... | collective-permute-start | bytes 1966088 | tf_op jit(solution)/shard_map/ppermute | solution.py:71
  107.2 41.1 %collective-permute-start = (bf16[176,2048]{1,0:T(8,128)(2,1)}, bf16[176,2048]{1,0:T(8,128)(2,1)}, u32[]{:S(2)}, u32[]{:S(2)}) collective-permute-start(bf16[176,2048]{1,0:T(8,128)(2,1)} %convert_element_type.291.weight), channel_id=1, source_target_pairs={{0,16},{1,17},{2,18},{3,19},{4,20},{5,21},{6,22},{7,23},{8,24},{9,... | collective-permute-start | bytes 2162696 | tf_op jit(solution)/shard_map/ppermute | solution.py:71
  148.4 58.6 %collective-permute-start.4 = (bf16[176,2048]{1,0:T(8,128)(2,1)}, bf16[176,2048]{1,0:T(8,128)(2,1)}, u32[]{:S(2)}, u32[]{:S(2)}) collective-permute-start(bf16[176,2048]{1,0:T(8,128)(2,1)} %convert_element_type.292.weight), channel_id=1, source_target_pairs={{0,16},{1,17},{2,18},{3,19},{4,20},{5,21},{6,22},{7,23},{8,24},{9,... | collective-permute-start | bytes 2162696 | tf_op jit(solution)/shard_map/ppermute | solution.py:71
  149.8 52.8 %copy-start.34 = (bf16[160,2048]{1,0:T(8,128)(2,1)S(1)}, bf16[160,2048]{1,0:T(8,128)(2,1)}, u32[]{:S(2)}) copy-start(bf16[160,2048]{1,0:T(8,128)(2,1)} %tok.1) | copy-start | bytes 1966084
  199.2 84.7 %collective-permute-start.9 = (bf16[176,2048]{1,0:T(8,128)(2,1)}, bf16[176,2048]{1,0:T(8,128)(2,1)}, u32[]{:S(2)}, u32[]{:S(2)}) collective-permute-start(bf16[176,2048]{1,0:T(8,128)(2,1)} %get-tuple-element.90), channel_id=1, source_target_pairs={{0,1},{1,0},{2,3},{3,2},{4,5},{5,4},{6,7},{7,6},{8,9},{9,8},{10,11... | collective-permute-start | bytes 2162696 | tf_op jit(solution)/shard_map/ppermute | solution.py:71
  207.0 57.7 %collective-permute-start.5 = (bf16[176,2048]{1,0:T(8,128)(2,1)}, bf16[176,2048]{1,0:T(8,128)(2,1)S(1)}, u32[]{:S(2)}, u32[]{:S(2)}) collective-permute-start(bf16[176,2048]{1,0:T(8,128)(2,1)} %convert_element_type.293.other), channel_id=1, source_target_pairs={{0,16},{1,17},{2,18},{3,19},{4,20},{5,21},{6,22},{7,23},{8,24},{9,... | collective-permute-start | bytes 2162696 | tf_op jit(solution)/shard_map/ppermute | solution.py:71
  264.7 19.1 %collective-permute-start.7 = (bf16[176,2048]{1,0:T(8,128)(2,1)}, bf16[176,2048]{1,0:T(8,128)(2,1)S(1)}, u32[]{:S(2)}, u32[]{:S(2)}) collective-permute-start(bf16[176,2048]{1,0:T(8,128)(2,1)} %convert_element_type.293.other), channel_id=1, source_target_pairs={{0,1},{1,0},{2,3},{3,2},{4,5},{5,4},{6,7},{7,6},{8,9},{9,8},{10,11... | collective-permute-start | bytes 2162696 | tf_op jit(solution)/shard_map/ppermute | solution.py:71
  265.2 17.7 %collective-permute-start.6 = (bf16[176,2048]{1,0:T(8,128)(2,1)S(1)}, bf16[176,2048]{1,0:T(8,128)(2,1)S(1)}, u32[]{:S(2)}, u32[]{:S(2)}) collective-permute-start(bf16[176,2048]{1,0:T(8,128)(2,1)S(1)} %collective-permute-done.5), channel_id=1, source_target_pairs={{0,4},{1,5},{2,6},{3,7},{4,0},{5,1},{6,2},{7,3},{8,12},{9,13},{10,... | collective-permute-start | bytes 2162696 | tf_op jit(solution)/shard_map/ppermute | solution.py:71
  266.5 17.4 %collective-permute-start.8 = (bf16[176,2048]{1,0:T(8,128)(2,1)S(1)}, bf16[176,2048]{1,0:T(8,128)(2,1)S(1)}, u32[]{:S(2)}, u32[]{:S(2)}) collective-permute-start(bf16[176,2048]{1,0:T(8,128)(2,1)S(1)} %collective-permute-done.5), channel_id=1, source_target_pairs={{0,1},{1,0},{2,3},{3,2},{4,5},{5,4},{6,7},{7,6},{8,9},{9,8},{10,11... | collective-permute-start | bytes 2162696 | tf_op jit(solution)/shard_map/ppermute | solution.py:71
  282.8 2.7 collective-permute-start.10
  283.8 18.6 %slice-start.2 = ((s8[5767168]{0:T(1024)(128)(4,1)}), s8[4194304]{0:T(1024)(128)(4,1)S(1)}, s32[]{:S(2)}) async-start(s8[5767168]{0:T(1024)(128)(4,1)} %bitcast.186), calls=%async_computation.2 | async-start | bytes 8388608
  285.8 16.7 %slice-start.3 = ((s8[5767168]{0:T(1024)(128)(4,1)}), s8[1572864]{0:T(1024)(128)(4,1)S(1)}, s32[]{:S(2)}) async-start(s8[5767168]{0:T(1024)(128)(4,1)} %bitcast.186), calls=%async_computation.3 | async-start | bytes 3145728
  306.9 43.4 %copy-start.44 = (bf16[640,2048]{1,0:T(8,128)(2,1)}, bf16[640,2048]{1,0:T(8,128)(2,1)S(1)}, u32[]{:S(2)}) copy-start(bf16[640,2048]{1,0:T(8,128)(2,1)S(1)} %add_convert_fusion) | copy-start | bytes 7864324
  319.5 35.6 %collective-permute-start.14 = (bf16[704,2048]{1,0:T(8,128)(2,1)}, bf16[704,2048]{1,0:T(8,128)(2,1)}, u32[]{:S(2)}, u32[]{:S(2)}) collective-permute-start(bf16[704,2048]{1,0:T(8,128)(2,1)} %slice.256), channel_id=1, source_target_pairs={{0,1},{1,0},{2,3},{3,2},{4,5},{5,4},{6,7},{7,6},{8,9},{9,8},{10,11... | collective-permute-start | bytes 8650760 | tf_op jit(solution)/shard_map/ppermute | solution.py:71
  319.6 26.4 %collective-permute-start.11 = (bf16[160,2048]{1,0:T(8,128)(2,1)S(1)}, bf16[160,2048]{1,0:T(8,128)(2,1)S(1)}, u32[]{:S(2)}, u32[]{:S(2)}) collective-permute-start(bf16[160,2048]{1,0:T(8,128)(2,1)S(1)} %get-tuple-element.152), channel_id=1, source_target_pairs={{0,2},{1,3},{2,0},{3,1},{4,6},{5,7},{6,4},{7,5},{8,10},{9,11},{10,... | collective-permute-start | bytes 1966088 | tf_op jit(solution)/shard_map/ppermute | solution.py:71
  320.3 25.7 %collective-permute-start.12 = (bf16[160,2048]{1,0:T(8,128)(2,1)S(1)}, bf16[160,2048]{1,0:T(8,128)(2,1)S(1)}, u32[]{:S(2)}, u32[]{:S(2)}) collective-permute-start(bf16[160,2048]{1,0:T(8,128)(2,1)S(1)} %get-tuple-element.154), channel_id=1, source_target_pairs={{0,8},{1,9},{2,10},{3,11},{4,12},{5,13},{6,14},{7,15},{8,0},{9,1},... | collective-permute-start | bytes 1966088 | tf_op jit(solution)/shard_map/ppermute | solution.py:71
  320.9 29.4 %collective-permute-start.13 = (bf16[160,2048]{1,0:T(8,128)(2,1)S(1)}, bf16[160,2048]{1,0:T(8,128)(2,1)S(1)}, u32[]{:S(2)}, u32[]{:S(2)}) collective-permute-start(bf16[160,2048]{1,0:T(8,128)(2,1)S(1)} %get-tuple-element.153), channel_id=1, source_target_pairs={{0,10},{1,11},{2,8},{3,9},{4,14},{5,15},{6,12},{7,13},{8,2},{9,3},... | collective-permute-start | bytes 1966088 | tf_op jit(solution)/shard_map/ppermute | solution.py:71
  330.6 68.8 %collective-permute-start.21 = (bf16[704,2048]{1,0:T(8,128)(2,1)}, bf16[704,2048]{1,0:T(8,128)(2,1)}, u32[]{:S(2)}, u32[]{:S(2)}) collective-permute-start(bf16[704,2048]{1,0:T(8,128)(2,1)} %slice.271), channel_id=1, source_target_pairs={{0,1},{1,0},{2,3},{3,2},{4,5},{5,4},{6,7},{7,6},{8,9},{9,8},{10,11... | collective-permute-start | bytes 8650760 | tf_op jit(solution)/shard_map/ppermute | solution.py:71
  345.9 73.8 %collective-permute-start.20 = (bf16[704,2048]{1,0:T(8,128)(2,1)}, bf16[704,2048]{1,0:T(8,128)(2,1)}, u32[]{:S(2)}, u32[]{:S(2)}) collective-permute-start(bf16[704,2048]{1,0:T(8,128)(2,1)} %slice.264), channel_id=1, source_target_pairs={{0,1},{1,0},{2,3},{3,2},{4,5},{5,4},{6,7},{7,6},{8,9},{9,8},{10,11... | collective-permute-start | bytes 8650760 | tf_op jit(solution)/shard_map/ppermute | solution.py:71
  361.1 67.4 %collective-permute-start.18 = (bf16[352,2048]{1,0:T(8,128)(2,1)}, bf16[352,2048]{1,0:T(8,128)(2,1)}, u32[]{:S(2)}, u32[]{:S(2)}) collective-permute-start(bf16[352,2048]{1,0:T(8,128)(2,1)} %get-tuple-element.141), channel_id=1, source_target_pairs={{0,4},{1,5},{2,6},{3,7},{4,0},{5,1},{6,2},{7,3},{8,12},{9,13},{10,... | collective-permute-start | bytes 4325384 | tf_op jit(solution)/shard_map/ppermute | solution.py:71
  393.7 31.8 %collective-permute-start.15 = (bf16[160,2048]{1,0:T(8,128)(2,1)}, bf16[160,2048]{1,0:T(8,128)(2,1)S(1)}, u32[]{:S(2)}, u32[]{:S(2)}) collective-permute-start(bf16[160,2048]{1,0:T(8,128)(2,1)} %get-tuple-element.149), channel_id=1, source_target_pairs={{0,2},{1,3},{2,0},{3,1},{4,6},{5,7},{6,4},{7,5},{8,10},{9,11},{10,... | collective-permute-start | bytes 1966088 | tf_op jit(solution)/shard_map/ppermute | solution.py:71
  394.5 31.0 %collective-permute-start.16 = (bf16[160,2048]{1,0:T(8,128)(2,1)}, bf16[160,2048]{1,0:T(8,128)(2,1)}, u32[]{:S(2)}, u32[]{:S(2)}) collective-permute-start(bf16[160,2048]{1,0:T(8,128)(2,1)} %get-tuple-element.151), channel_id=1, source_target_pairs={{0,8},{1,9},{2,10},{3,11},{4,12},{5,13},{6,14},{7,15},{8,0},{9,1},... | collective-permute-start | bytes 1966088 | tf_op jit(solution)/shard_map/ppermute | solution.py:71
  399.3 26.2 %collective-permute-start.17 = (bf16[160,2048]{1,0:T(8,128)(2,1)}, bf16[160,2048]{1,0:T(8,128)(2,1)}, u32[]{:S(2)}, u32[]{:S(2)}) collective-permute-start(bf16[160,2048]{1,0:T(8,128)(2,1)} %get-tuple-element.150), channel_id=1, source_target_pairs={{0,10},{1,11},{2,8},{3,9},{4,14},{5,15},{6,12},{7,13},{8,2},{9,3},... | collective-permute-start | bytes 1966088 | tf_op jit(solution)/shard_map/ppermute | solution.py:71
  430.8 15.1 %copy-start.7 = (f32[8,4,8,256]{3,2,1,0:T(8,128)S(1)}, f32[8,4,8,256]{3,2,1,0:T(8,128)}, u32[]{:S(2)}) copy-start(f32[8,4,8,256]{3,2,1,0:T(8,128)} %shard_map.263) | copy-start | bytes 786436
  430.8 15.1 %copy-start.10 = (s32[36]{0:T(128)S(1)}, s32[36]{0:T(128)}, u32[]{:S(2)}) copy-start(s32[36]{0:T(128)} %copy-done.9) | copy-start | bytes 436
  430.8 15.1 %copy-start.12 = (f32[2,640,128]{2,1,0:T(8,128)S(1)}, f32[2,640,128]{2,1,0:T(8,128)}, u32[]{:S(2)}) copy-start(f32[2,640,128]{2,1,0:T(8,128)} %copy-done.11) | copy-start | bytes 1966084
  458.7 33.5 %collective-permute-start.19 = (bf16[176,2048]{1,0:T(8,128)(2,1)}, bf16[176,2048]{1,0:T(8,128)(2,1)S(1)}, u32[]{:S(2)}, u32[]{:S(2)}) collective-permute-start(bf16[176,2048]{1,0:T(8,128)(2,1)} %add_convert_fusion.10), channel_id=1, source_target_pairs={{0,16},{1,17},{2,18},{3,19},{4,20},{5,21},{6,22},{7,23},{8,24},{9,... | collective-permute-start | bytes 2162696 | tf_op jit(solution)/shard_map/ppermute | solution.py:71
  458.8 36.0 %collective-permute-start.22 = (bf16[352,2048]{1,0:T(8,128)(2,1)}, bf16[352,2048]{1,0:T(8,128)(2,1)S(1)}, u32[]{:S(2)}, u32[]{:S(2)}) collective-permute-start(bf16[352,2048]{1,0:T(8,128)(2,1)} %get-tuple-element.114), channel_id=1, source_target_pairs={{0,4},{1,5},{2,6},{3,7},{4,0},{5,1},{6,2},{7,3},{8,12},{9,13},{10,... | collective-permute-start | bytes 4325384 | tf_op jit(solution)/shard_map/ppermute | solution.py:71
  (80 other events, 369.7 us)

commit v4 on v3

--- a/solution.py
+++ b/solution.py
@@ -99,7 +99,7 @@
     for i, peer in enumerate(peers):
         copy = pltpu.make_async_remote_copy(
             src_ref=in_ref,
-            dst_ref=out_ref.at[slot],
+            dst_ref=out_ref.at[pl.ds(slot * in_ref.shape[0], in_ref.shape[0])],
             send_sem=send_sems.at[i],
             recv_sem=recv_sems.at[i],
             device_id=(peer,),
@@ -107,7 +107,7 @@
         )
         copy.start()
         copies.append(copy)
-    out_ref[slot] = in_ref[...]
+    out_ref[pl.ds(slot * in_ref.shape[0], in_ref.shape[0])] = in_ref[...]
     for copy in copies:
         copy.wait()
 
@@ -117,7 +117,7 @@
     vmem = pl.BlockSpec(memory_space=pltpu.VMEM)
     return pl.pallas_call(
         partial(gather_kernel, lay, masks, slot_of),
-        out_shape=jax.ShapeDtypeStruct((slots,) + value.shape, value.dtype),
+        out_shape=jax.ShapeDtypeStruct((slots * value.shape[0],) + value.shape[1:], value.dtype),
         in_specs=[vmem],
         out_specs=vmem,
         scratch_shapes=[
@@ -183,30 +183,27 @@
 
 
 class WeightGather:
-    def __init__(self, net, own, place, ahead=None):
-        self.net, self.own, self.place, self.ahead = net, own, place, ahead
+    def __init__(self, net, own, place, early=None):
+        self.net, self.own, self.place, self.early = net, own, place, early or {}
         self.bits = net.lay.wbits
         self.pending = {}
 
     def start(self):
         me = self.net.me
-        if self.ahead is None:
-            self.pending[self.bits[0]] = self.net.put(
-                self.own, self.place(me, self.bits[0]), self.bits[0]
-            )
-        for bit in self.bits[1:]:
-            self.pending[bit] = self.net.put(self.own, self.place(me, bit), bit)
+        for bit in self.bits:
+            if bit not in self.early:
+                self.pending[bit] = self.net.put(self.own, self.place(me, bit), bit)
         self.net.move(self.own, self.place(me, 0))
-        if self.ahead is not None:
-            self.pass_on(self.bits[0], self.ahead)
-            self.net.move(self.ahead, self.place(self.net.lay.flip(me, self.bits[0]), self.bits[0]))
+        for bit, block in self.early.items():
+            self.pass_on(bit, block)
+            self.net.move(block, self.place(self.net.lay.flip(me, bit), bit))
 
     def masks(self):
         out = [0]
         for bit in self.bits[:-1]:
             out = out + [m | bit for m in out]
         out = sorted(out[1:], key=lambda m: (bin(m).count("1"), -m))
-        return [m for m in out if self.ahead is None or m != self.bits[0]]
+        return [m for m in out if m not in self.early]
 
     def pass_on(self, mask, block):
         last = max(i for i, bit in enumerate(self.bits) if mask & bit)
@@ -249,11 +246,14 @@
         copy.wait_recv()
 
 
+SCALE = 10_000_000
+
+
 def estimate(micros):
-    return pl.CostEstimate(flops=micros * 1_000_000_000, bytes_accessed=0, transcendentals=0)
-
-
-def net_call(body, lay, values, outs, copies, local, collective_id, name, micros, scratch=(), limit=None):
+    return pl.CostEstimate(flops=micros * SCALE, bytes_accessed=0, transcendentals=0)
+
+
+def net_call(body, lay, values, outs, copies, local, collective_id, name, micros, scratch=()):
     hbm = pl.BlockSpec(memory_space=pl.ANY)
     return pl.pallas_call(
         body,
@@ -269,7 +269,7 @@
         compiler_params=pltpu.CompilerParams(
             collective_id=collective_id,
             has_side_effects=True,
-            vmem_limit_bytes=limit,
+            vmem_limit_bytes=60 << 20,
         ),
         cost_estimate=estimate(micros),
         name=name,
@@ -333,8 +333,8 @@
 
 
 def start_kernel(
-    lay, units, tok, w_in, w_gate, w_forget, w_out, pack,
-    tok_all, mix_all, forget_own, out_own, out_all, every, *rest,
+    lay, units, tok, w_in, w_gate, w_forget, w_out, f_gate, pack,
+    tok_all, mix_all, forget_own, out_own, out_all, f_gate_z, every, *rest,
 ):
     n, W = lay.n, lay.n // 4
     *rooms, send_sems, recv_sems, local_sems = rest
@@ -366,6 +366,7 @@
     own.wait()
     arrived(out_in)
     g_out.start()
+    gate_in = net.put(f_gate, f_gate_z, lay.ZH)
     net.settle()
     for mask in g_in.masks():
         g_in.forward(mask)
@@ -376,7 +377,7 @@
         g_out.forward(mask)
     for gather in (g_in, g_gate, g_forget, g_out):
         gather.end()
-    arrived(rest)
+    arrived(rest + [gate_in])
     arrived(all_in)
     net.finish()
 
@@ -385,49 +386,50 @@
     return lay.tmasks[1:] + lay.wbits
 
 
-def rel_gather(net, own, ahead, out):
-    return WeightGather(net, own, lambda d, m: out.at[net.lay.rel_slot(m)], ahead)
-
-
-def scatter_kernel(lay, blocks, small, weight, ahead, other, got, got_small, weight_all, other_got, *rest):
+def rel_gather(net, own, early, out):
+    return WeightGather(net, own, lambda d, m: out.at[net.lay.rel_slot(m)], early)
+
+
+def branch_kernel(lay, blocks, small, gate, gate_z, down, got_x, got_z, got_small, gate_all, down_y, down_z, *rest):
+    token_rooms, rest = rest[:2], rest[2:]
     *rooms, send_sems, recv_sems, local_sems = rest
     net = Net(lay, group_peers(lay), send_sems, recv_sems, local_sems, rooms)
-    gather = rel_gather(net, weight, ahead, weight_all)
-    waits = token_scatter(net, blocks, got) + token_scatter(net, small, got_small)
+    gather = rel_gather(net, gate, {lay.ZH: gate_z}, gate_all)
     gather.start()
+    waits = [net.put(down, down_z, lay.ZH)]
+    tokens = TokenReduce(net, blocks, got_x, got_z, *token_rooms)
+    waits += token_scatter(net, small, got_small)
     net.settle()
     for mask in gather.masks():
         gather.forward(mask)
-    waits.append(net.put(other, other_got, lay.ybits[0]))
+    waits.append(net.put(down, down_y, lay.ybits[0]))
+    tokens.pass_on()
     gather.end()
+    tokens.end()
     arrived(waits)
     net.finish()
 
 
-def gather_kernel_both(lay, own, weight, ahead, own_all, weight_all, *rest):
+def ffn_kernel(lay, own, up, up_z, down, down_y, down_z, *rest):
+    cot_blocks, (own_all, up_all, down_all, cot_all), rest = rest[:4], rest[4:8], rest[8:]
     *rooms, send_sems, recv_sems, local_sems = rest
     net = Net(lay, group_peers(lay), send_sems, recv_sems, local_sems, rooms)
     first = token_start(net, own, own_all)
-    gather = rel_gather(net, weight, ahead, weight_all)
-    gather.start()
+    g_up = rel_gather(net, up, {lay.ZH: up_z}, up_all)
+    g_down = rel_gather(net, down, {lay.ZH: down_z, lay.ybits[0]: down_y}, down_all)
+    g_up.start()
+    g_down.start()
+    for j, block in enumerate(cot_blocks):
+        net.move(block, cot_all.at[j])
     net.settle()
     rest = token_finish(net, first, own_all)
-    for mask in gather.masks():
-        gather.forward(mask)
-    gather.end()
+    for mask in g_up.masks():
+        g_up.forward(mask)
+    for mask in g_down.masks():
+        g_down.forward(mask)
+    g_up.end()
+    g_down.end()
     arrived(rest)
-    net.finish()
-
-
-def gather_kernel_two(lay, own, small, own_all, small_all, *rest):
-    *rooms, send_sems, recv_sems, local_sems = rest
-    net = Net(lay, lay.tmasks[1:], send_sems, recv_sems, local_sems, rooms)
-    first = token_start(net, own, own_all)
-    net.move(small, small_all.at[0])
-    waits = [net.put(small, small_all.at[j], m) for j, m in enumerate(lay.tmasks) if j]
-    net.settle()
-    rest = token_finish(net, first, own_all)
-    arrived(waits + rest)
     net.finish()
 
 
@@ -444,104 +446,189 @@
 
 
 class WeightReduce:
-    def __init__(self, net, bits, part, place, local, stages, total, away=None):
-        self.net, self.bits, self.part, self.place, self.away = net, bits, part, place, away
+    def __init__(self, net, part, rows, dims, local, stages, total, relative, leaves=None, came=None):
+        self.net, self.part, self.rows, self.relative = net, part, rows, relative
         self.local, self.stages, self.total = local, stages, total
-        self.sent, self.waited = [], -1
-
-    def pick(self, k, i, away):
-        if self.away is not None:
-            return i + (self.stages[k].shape[0] if away and k else 0)
-        side = (self.net.me // self.bits[k]) % 2
-        return 2 * i + (1 - side if away else side)
+        self.leaves, self.came = leaves, came
+        self.first = 0 if leaves is None and came is None else 1
+        self.bits = net.lay.rbits[self.first :]
+        self.dims = [[d for d in dims if d in self.bits]]
+        for bit in self.bits:
+            self.dims.append([d for d in self.dims[-1] if d != bit])
+        self.copy, self.waited = None, -1
+
+    def side(self, k):
+        return 0 if self.relative else (self.net.me // self.bits[k]) % 2
+
+    def cut(self, k, away):
+        index = [slice(None)] * len(self.dims[k])
+        index[self.dims[k].index(self.bits[k])] = 1 - self.side(k) if away else self.side(k)
+        if k:
+            return self.stages[k - 1].at[tuple(index)]
+        return self.part.at[tuple(index) + self.rows]
 
     def start(self):
-        count = self.stages[0].shape[0]
-        self.sent = [
-            self.net.put(
-                (self.part if self.away is None else self.away).at[self.place(self.pick(0, i, True))],
-                self.stages[0].at[i],
-                self.bits[0],
-            )
-            for i in range(count)
-        ]
-        self.loads = [
-            self.net.load(self.part.at[self.place(self.pick(0, i, False))], self.local.at[i])
-            for i in range(count)
-        ]
+        if self.first == 0:
+            self.copy = self.net.put(self.cut(0, True), self.stages[0], self.bits[0])
+            self.loaded = self.net.load(self.cut(0, False), self.local)
+            return
+        index = (slice(None),) * len(self.dims[1]) + self.rows
+        self.loaded = self.net.load(self.part.at[index] if self.rows else self.part, self.local)
+        if self.came is None:
+            block = self.leaves.at[index] if self.rows else self.leaves
+            self.copy = self.net.put(block, self.stages[0], self.bits[0])
+        else:
+            block = self.came.at[index] if self.rows else self.came
+            self.copy = self.net.load(block, self.stages[0])
 
     def wait(self, k):
         if self.waited < k:
-            arrived(self.sent)
+            if k == 0 and self.came is not None:
+                self.copy.wait()
+            else:
+                self.copy.wait_recv()
             self.waited = k
 
-    def add(self, k):
+    def add(self, k, away):
+        if k == 0 and away:
+            self.loaded.wait()
         stage = self.stages[k]
-        count = stage.shape[0]
-        if k == 0:
-            for copy in self.loads:
-                copy.wait()
-
-        def one(i):
-            old = self.local.at[i] if k == 0 else self.stages[k - 1].at[self.pick(k, i, False)]
-            add_rows(self.total if count == 1 else stage.at[i], stage.at[i], old)
-
-        if count == 1:
-            one(0)
-        else:
-            for away in (True, False):
-                for i in range(count // 2):
-                    one(self.pick(k + 1, i, away))
+        old = self.cut(k, False) if k else self.local
+        if k + 1 == len(self.bits):
+            if away:
+                add_rows(self.total, stage, old)
+            return
+        dims = self.dims[k + 1]
+        place = dims.index(self.bits[k + 1])
+        side = 1 - self.side(k + 1) if away else self.side(k + 1)
+        for number in range(1 << (len(dims) - 1)):
+            index = [(number >> j) & 1 for j in range(len(dims) - 1)]
+            index = tuple(index[:place] + [side] + index[place:])
+            add_rows(stage.at[index], stage.at[index], old.at[index])
 
     def send(self, k):
-        self.sent = [
-            self.net.put(self.stages[k - 1].at[self.pick(k, i, True)], self.stages[k].at[i], self.bits[k])
-            for i in range(self.stages[k].shape[0])
-        ]
-
-
-PARTS = (("forget", 0), ("out", 0), ("down", 1), ("gate", 0), ("in", 0))
-
-
-def forget_place(lay, slot):
-    return ((slot // 2) % lay.Y * 2 + slot % 2) * 2 + slot // (2 * lay.Y)
+        self.copy = self.net.put(self.cut(k, True), self.stages[k], self.bits[k])
+
+
+def grad_kernel(lay, own, small, gate, up, down, own_all, small_all, *rest):
+    outs, (room, small_room, *scratch), (send_sems, recv_sems, local_sems) = rest[:6], rest[6:-3], rest[-3:]
+    net = Net(lay, lay.tmasks[1:] + [lay.C], send_sems, recv_sems, local_sems, [room, small_room])
+    first = token_start(net, own, own_all)
+    waits = [net.put(small, small_all.at[j], m) for j, m in enumerate(lay.tmasks) if j]
+    net.move(small, small_all.at[0])
+    dims = part_dims(lay, "up")
+    jobs = []
+    for j, part in enumerate((gate, up, down)):
+        local, stage = scratch[2 * j : 2 * j + 2]
+        jobs.append(WeightReduce(net, part, (), dims, local, [stage], None, True))
+        jobs[-1].start()
+    net.settle()
+    for j, job in enumerate(jobs):
+        job.wait(0)
+        job.add(0, True)
+        net.keep(job.cut(1, True), outs[2 * j + 1])
+        job.add(0, False)
+        net.keep(job.cut(1, False), outs[2 * j])
+        if j == 0:
+            waits += token_finish(net, first, own_all)
+    arrived(waits)
+    net.finish()
+
+
+def row_cuts(name, rows):
+    if name not in ("up", "down") or rows % 16 or rows < 128:
+        return [(0, rows)]
+    first = -(-rows // 32) * 16
+    return [(0, first), (first, rows - first)]
+
+
+PARTS = ("up", "forget", "out", "down", "gate", "in")
+
+
+class TokenReduce:
+    def __init__(self, net, blocks, got_x, got_z, room, other):
+        lay = net.lay
+        self.net, self.room, self.other, self.got_z = net, room, other, got_z
+        self.first = [net.put(blocks.at[3], other, lay.X), net.put(blocks.at[1], got_x, lay.X)]
+        self.loaded = net.load(blocks.at[2], room)
+
+    def pass_on(self):
+        self.first[0].wait_recv()
+        self.loaded.wait()
+        add_rows(self.room, self.room, self.other)
+        self.last = self.net.put(self.room, self.got_z, self.net.lay.ZL)
+
+    def end(self):
+        arrived([self.first[1], self.last])
+
+
+def first_stage(name):
+    return 1 if name in ("up", "down") else 0
+
+
+def part_dims(lay, name):
+    y_bits = list(reversed(lay.ybits))
+    if name == "forget":
+        return y_bits + [lay.C, lay.ZH]
+    if name in ("up", "down"):
+        return [lay.C] + y_bits + [lay.ZH]
+    return [lay.ZH] + y_bits + [lay.C]
+
+
+LAG = 2
 
 
 def reduce_kernel(lay, *refs):
     count = len(PARTS)
     parts, refs = refs[:count], refs[count:]
-    (away, up, du, vectors), refs = refs[:4], refs[4:]
+    (up_came, down_leaves, du, mixed, vectors), refs = refs[:5], refs[5:]
     outs, refs = refs[:count], refs[count:]
-    (got_up, got_du, all_vectors), refs = refs[:3], refs[3:]
+    (du_x, du_z, mixed_x, mixed_z, all_vectors), refs = refs[:5], refs[5:]
+    token_rooms, refs = refs[:4], refs[4:]
     scratch, (send_sems, recv_sems, local_sems) = list(refs[:-3]), refs[-3:]
     net = Net(lay, list(range(1, lay.n)), send_sems, recv_sems, local_sems)
     me = net.me
-    jobs, turns, waits = [], [], []
-    for (name, first), part in zip(PARTS, parts):
-        bits = lay.rbits[first:]
-        local = scratch.pop(0)
-        stages = [scratch.pop(0) for _ in bits]
-        place = partial(forget_place, lay) if name == "forget" else lambda k: k
-        jobs.append(
-            WeightReduce(
-                net, bits, part, place, local, stages, scratch.pop(0), away if name == "down" else None
+    jobs, places, turns, waits = [], [], [], []
+    for name, part, out in zip(PARTS, parts, outs):
+        for first, rows in row_cuts(name, part.shape[-2]):
+            local = scratch.pop(0)
+            stages = [scratch.pop(0) for _ in lay.rbits[first_stage(name) :]]
+            whole = rows == part.shape[-2]
+            at = () if whole else (pl.ds(first, rows),)
+            relative = name in ("up", "down")
+            dims = part_dims(lay, name)
+            jobs.append(
+                WeightReduce(
+                    net,
+                    part,
+                    at,
+                    dims,
+                    local,
+                    stages,
+                    scratch.pop(0),
+                    relative,
+                    down_leaves if name == "down" else None,
+                    up_came if name == "up" else None,
+                )
             )
-        )
-    jobs[0].start()
-    jobs[1].start()
-    jobs[2].start()
-    waits += [net.put(up, got_up, lay.ZH)]
-    waits += token_scatter(net, du, got_du)
-    jobs[3].start()
-    jobs[4].start()
-    waits += [net.put(vectors.at[lay.flip(me, m)], all_vectors.at[me], m) for m in range(1, lay.n)]
-    net.keep(vectors.at[me], all_vectors.at[me])
+            places.append((name, out if whole else out.at[pl.ds(first, rows)]))
+    flows = [[] for _ in lay.rbits]
+    late = []
+    for job, (name, _) in zip(jobs, places):
+        if name in ("gate", "in"):
+            late.append(job)
+        else:
+            job.start()
+            if name == "down":
+                flows[1].append(job)
+    du_sum = TokenReduce(net, du, du_x, du_z, *token_rooms[:2])
 
     def finish(i):
-        total, out = jobs[i].total, outs[i]
-        if PARTS[i][0] == "forget":
+        total = jobs[i].total
+        name, out = places[i]
+        if name == "forget":
             turns.append(Turn(net, forget_from(lay, me), total, out))
-        elif PARTS[i][0] == "out":
+        elif name == "out":
             rows = total.shape[0] // 4
             mine = t_slot(lay, me)
 
@@ -555,23 +642,39 @@
             net.keep(total, out)
 
     depth = len(lay.rbits)
-    for tick in range(count + depth - 1):
-        for stage in range(depth):
-            i = tick - stage
-            valid = 0 <= i < count
-            k = stage - PARTS[i][1] if valid else 0
-            if valid and k >= 0:
-                jobs[i].wait(k)
-                jobs[i].add(k)
-            if stage + 1 < depth:
-                if 0 <= i - 1 < count:
-                    ahead = stage + 1 - PARTS[i - 1][1]
-                    if ahead >= 0:
-                        jobs[i - 1].wait(ahead)
-                if valid and k >= 0:
-                    jobs[i].send(k + 1)
-            elif valid:
+    for tick in range(len(jobs) + depth - 1):
+        for k in range(depth):
+            i = tick - k
+            if not 0 <= i < len(jobs) or k + jobs[i].first >= depth:
+                continue
+            job = jobs[i]
+            job.wait(k)
+            job.add(k, True)
+            flow = k + 1 + job.first
+            if flow == depth:
                 finish(i)
+                continue
+            if len(flows[flow]) >= LAG:
+                behind = flows[flow][-LAG]
+                behind.wait(flow - behind.first)
+            job.send(k + 1)
+            flows[flow].append(job)
+            job.add(k, False)
+        if tick == 0:
+            for job in late:
+                job.start()
+        if tick == 1:
+            waits += [
+                net.put(vectors.at[lay.flip(me, m)], all_vectors.at[me], m) for m in range(1, lay.n)
+            ]
+            net.keep(vectors.at[me], all_vectors.at[me])
+            mixed_sum = TokenReduce(net, mixed, mixed_x, mixed_z, *token_rooms[2:])
+        if tick == 3:
+            du_sum.pass_on()
+        if tick == 5:
+            mixed_sum.pass_on()
+    du_sum.end()
+    mixed_sum.end()
     arrived(waits)
     for turn in turns:
         turn.wait()
@@ -888,7 +991,8 @@
     out_cols = out_cols.transpose(2, 4, 0, 1, 3, 5).reshape(4, r_in, 2 * half)
     units = r_in // r_f
     r_ffn = ffn_gate.shape[0]
-    tok_all, w_mix, _, _, w_out, every = net_call(
+    f_gate = ffn_gate.astype(LOW)
+    tok_all, w_mix, _, _, w_out, gate_z, every = net_call(
         partial(start_kernel, lay, units),
         lay,
         (
@@ -897,6 +1001,7 @@
             gate_proj.astype(LOW).reshape(units, r_f, width),
             forget_proj.astype(LOW).reshape(1, r_f, width),
             out_cols,
+            f_gate,
             packed,
         ),
         [
@@ -905,9 +1010,10 @@
             ((1, r_f, width), LOW),
             ((4, r_in, 2 * half), LOW),
             ((W, 4, r_in, 2 * half), LOW),
+            ((r_ffn, width), LOW),
             ((n, 8, 128), F32),
         ],
-        4 * (W - 1) + 8 + n - 1,
+        4 * (W - 1) + 9 + n - 1,
         24,
         0,
         "start",
@@ -920,10 +1026,7 @@
             pltpu.VMEM((4, r_in, 2 * half), LOW),
         ],
     )
-    f_gate, f_up, f_down = lax.optimization_barrier(
-        (ffn_gate.astype(LOW), ffn_up.astype(LOW), ffn_down.astype(LOW), every)
-    )[:3]
-    gate_z = lay.send(f_gate, lay.ZH)
+    f_up, f_down = ffn_up.astype(LOW), ffn_down.astype(LOW)
     tok_all = tok_all.reshape(total, width)
     w_mix = w_mix.reshape(5 * half, width)
     w_out = w_out.reshape(2, Y, 2, 2, 2, r_in, 2 * half).transpose(0, 3, 1, 4, 2, 5, 6)
@@ -959,9 +1062,9 @@
         3,
         name="gates",
     )(proj, keep, par)
-    summ_all = small_gather(lay, summ, lay.wmasks, partial(w_slot, lay), W, 1).reshape(n, 8, half)
+    summ_all = small_gather(lay, summ, lay.wmasks, partial(w_slot, lay), W, 1)
     cot_blocks = lay.gather_t(tie(cotangent, summ_all))
-    up_z = lay.send(tie(f_up, gate_z, summ_all), lay.ZH)
+    up_z = lay.send(tie(f_up, summ_all), lay.ZH)
     st_re, st_im, be_re, be_im, unit, squares = plain_call(
         partial(state_kernel, half, length, n),
         [wide] * 4 + [((total, 2 * half), LOW), ((total, LANES), F32)],
@@ -974,60 +1077,63 @@
     def t_blocks(value):
         return [value[j * length : (j + 1) * length] for j in range(4)]
 
-    got, got_squares, w_ffn_gate, down_y = net_call(
-        partial(scatter_kernel, lay),
+    branch_x, branch_z, got_squares, w_ffn_gate, down_y, down_z = net_call(
+        partial(branch_kernel, lay),
         lay,
         (branch_low.reshape(4, length, width), squares.reshape(4, length, LANES), f_gate, gate_z, f_down),
         [
-            ((3, length, width), LOW),
+            ((length, width), LOW),
+            ((length, width), LOW),
             ((3, length, LANES), F32),
             ((W, r_ffn, width), LOW),
             ((r_ffn, width), LOW),
+            ((r_ffn, width), LOW),
         ],
-        W - 1 + 7,
-        4,
+        W + 7,
+        6,
         4,
         "branch",
         40,
-        [pltpu.VMEM((r_ffn, width), LOW)] * 2,
+        [pltpu.VMEM((length, width), LOW)] * 2 + [pltpu.VMEM((r_ffn, width), LOW)] * 2,
     )
     w_ffn_gate = w_ffn_gate.reshape(W * r_ffn, width)
-    down_z = lay.send(tie(f_down, up_z, got), lay.ZH)
 
     def own_sum(whole, arrived_parts):
         value = whole[:length].astype(F32)
-        for j in range(3):
-            value = value + arrived_parts[j].astype(F32)
+        for part in arrived_parts:
+            value = value + part.astype(F32)
         return value
 
-    square = own_sum(squares, got_squares)[:, 0:1]
-    branch = own_sum(branch_low, got)
+    square = own_sum(squares, [got_squares[j] for j in range(3)])[:, 0:1]
+    branch = own_sum(branch_low, (branch_x, branch_z))
     r_state = lax.rsqrt(square / width + EPS)
     residual = inputs + r_state * branch
     r_res = lax.rsqrt(jnp.mean(residual * residual, axis=-1, keepdims=True) + EPS)
     ffn_low = (residual * r_res * g_ffn).astype(LOW)
 
-    ffn_all, w_ffn_up = net_call(
-        partial(gather_kernel_both, lay),
+    ffn_all, w_ffn_up, w_down, cot_all = net_call(
+        partial(ffn_kernel, lay),
         lay,
-        (ffn_low, f_up, up_z),
-        [((4, length, width), LOW), ((W, r_ffn, width), LOW)],
-        W - 1 + 4,
-        6,
+        (ffn_low, f_up, up_z, f_down, down_y, down_z, *cot_blocks),
+        [
+            ((4, length, width), LOW),
+            ((W, r_ffn, width), LOW),
+            ((W, r_ffn, width), LOW),
+            ((4, length, width), LOW),
+        ],
+        2 * W + 4,
+        20,
         5,
         "ffn_in",
         40,
-        [pltpu.VMEM((length, width), LOW)] + [pltpu.VMEM((r_ffn, width), LOW)] * 2,
+        [pltpu.VMEM((length, width), LOW)]
+        + [pltpu.VMEM((r_ffn, width), LOW)] * 5
+        + [pltpu.VMEM((length, width), LOW)] * 4,
     )
     ffn_all = ffn_all.reshape(total, width)
     w_ffn_up = w_ffn_up.reshape(W * r_ffn, width)
-    down_pieces = [f_down, down_z]
-    for bit in lay.ybits:
-        first = [down_y] if bit == lay.ybits[0] else []
-        down_pieces = down_pieces + first + [lay.send(v, bit) for v in down_pieces[len(first) :]]
-    down_pieces[0] = tie(f_down, down_z)
-    cot_all = jnp.concatenate(cot_blocks, axis=0)
-    w_down = jnp.concatenate(down_pieces + [lay.send(v, lay.C) for v in down_pieces], axis=0)
+    w_down = w_down.reshape(W * r_ffn, width)
+    cot_all = cot_all.reshape(total, width)
     gate_value = contract(ffn_all, w_ffn_gate)
     up_value = contract(ffn_all, w_ffn_up)
     s_gate = jax.nn.sigmoid(gate_value)
@@ -1040,7 +1146,11 @@
         jnp.dot(grad_gate, w_ffn_gate, preferred_element_type=F32)
         + jnp.dot(grad_up, w_ffn_up, preferred_element_type=F32)
     ).astype(LOW)
-    du = lay.scatter_t(t_blocks(du_low))
+    du_blocks = t_blocks(du_low)
+    du_got = [lay.send(b, m) for b, m in zip(du_blocks[1:], lay.tmasks[1:])]
+    du = du_blocks[0].astype(F32)
+    for got in du_got:
+        du = du + got.astype(F32)
 
     def join(kept, got):
         return kept.astype(F32) + got.astype(F32)
@@ -1048,23 +1158,19 @@
     def split_sum(kept, got):
         rows = kept.shape[0] // 2
         return join(kept[:rows], got[:rows]).astype(LOW), join(kept[rows:], got[rows:]).astype(LOW)
-
-    def over_core(part):
-        rows = part.shape[0] // 2
-        return split_sum(part[:rows], lay.send(part[rows:], lay.C))
 
     def over_y(kept, away):
         for bit in lay.ybits:
             kept, away = split_sum(kept, lay.send(away, bit))
         return kept, away
 
-    left_gate, left_up, left_hidden, _ = lax.optimization_barrier(
-        (grad_gate, grad_up, hidden_low, du_low)
-    )
-    gate_kept, gate_away = over_core(outer_rows(left_gate, ffn_all).astype(LOW))
-    up_kept, up_away = over_core(outer_rows(left_up, ffn_all).astype(LOW))
+    left_gate, left_up, left_hidden, *_ = lax.optimization_barrier(
+        (grad_gate, grad_up, hidden_low, *du_blocks)
+    )
+    gate_part = outer_rows(left_gate, ffn_all).astype(LOW)
+    up_part = outer_rows(left_up, ffn_all).astype(LOW)
     down_part = outer_rows(left_hidden, cot_all).astype(LOW)
-    mixed_low = jnp.dot(left_hidden, w_down, preferred_element_type=F32).astype(LOW)
+    mixed_low = jnp.dot(tie(left_hidden, du_got[0]), w_down, preferred_element_type=F32).astype(LOW)
 
     du_gain = du * g_ffn
     grad_residual = (
@@ -1073,28 +1179,28 @@
         - residual * (r_res * r_res * r_res) * jnp.mean(residual * du_gain, axis=-1, keepdims=True)
     )
     ffn_gain_part = jnp.sum(du * residual * r_res, axis=0)
-    grad_low = tie(grad_residual.astype(LOW), gate_away)
+    grad_low = tie(grad_residual.astype(LOW), mixed_low)
     inner = jnp.sum(grad_low.astype(F32) * branch, axis=-1, keepdims=True) / width
     scale = jnp.where(
         jnp.arange(LANES)[None, :] == 0, r_state, r_state * r_state * r_state * inner
     )
 
-    grad_all, scale_all = net_call(
-        partial(gather_kernel_two, lay),
+    split = (2,) * len(lay.wbits)
+    block = (r_ffn, width)
+    grad_all, scale_all, gate_kept, gate_away, up_kept, up_away, down_kept, down_away = net_call(
+        partial(grad_kernel, lay),
         lay,
-        (grad_low, scale),
-        [((4, length, width), LOW), ((4, length, LANES), F32)],
-        7,
-        4,
+        (grad_low, scale, *[part.reshape(split + block) for part in (gate_part, up_part, down_part)]),
+        [((4, length, width), LOW), ((4, length, LANES), F32)] + [(split[2:] + block, LOW)] * 6,
+        10,
+        13,
         6,
         "grad_in",
         27,
-        [pltpu.VMEM((length, width), LOW), pltpu.VMEM((length, LANES), F32)],
-    )
-    gate_kept, gate_away = over_y(gate_kept, gate_away)
-    mixed_blocks = t_blocks(tie(mixed_low, grad_all))
-    mixed = lay.scatter_t(mixed_blocks)
-    mixed_out = (residual + mixed).astype(LOW)
+        [pltpu.VMEM((length, width), LOW), pltpu.VMEM((length, LANES), F32)]
+        + [pltpu.VMEM(split[1:] + block, LOW)] * 6,
+    )
+    gate_kept, gate_away = over_y(gate_kept.reshape(-1, width), gate_away.reshape(-1, width))
     grad_all = grad_all.reshape(total, width)
     scale_all = scale_all.reshape(total, LANES)
     grad_mid = jnp.dot(grad_all, w_out, preferred_element_type=F32)
@@ -1107,8 +1213,7 @@
         scratch=[pltpu.VMEM((8, 2 * half), F32)],
         name="back_gates",
     )(grad_mid, st_re, st_im, proj, g_out, scale_all, d_re, d_im)
-    back = tie(back, gate_away)
-    back_all = small_gather(lay, back, lay.wmasks, partial(w_slot, lay), W, 2).reshape(n, 8, half)
+    back_all = tie(small_gather(lay, back, lay.wmasks, partial(w_slot, lay), W, 2), gate_away)
     grads, lower_part, angle_part = plain_call(
         partial(adjoint_kernel, half, length, n),
         [((total, 5 * half), LOW), ((8, half), F32), ((8, half), F32)],
@@ -1144,46 +1249,44 @@
 
     grad_w_out = outer_rows(grad_all, mid).astype(LOW).reshape(2, 2, Y, 2, 2, r_in, 2 * half)
     grad_w_out = grad_w_out.transpose(0, 2, 4, 1, 3, 5, 6).reshape(W, 4 * r_in, 2 * half)
-    grad_w_mix = outer_rows(grads, normed).astype(LOW)
-    down_kept, down_away = over_core(down_part)
-    up_kept, up_away = over_y(up_kept, tie(up_away, back_all))
     gate_got = lay.send(tie(gate_away, back_all), lay.ZH)
-    du_mix_low = tie(du_mix_low, mixed_out, gate_got)
-    parts = [
-        grad_w_mix[4 * half :].reshape(W, r_f, width),
-        grad_w_out,
-        down_kept.reshape(W // 4, r_ffn, width),
-        grad_w_mix[2 * half : 4 * half].reshape(W, r_in, width),
-        grad_w_mix[: 2 * half].reshape(W, r_in, width),
-    ]
-    scratch, copies, local_copies = [], 6 + 3 + n + 2, 4
-    for (_, first), part in zip(PARTS, parts):
-        blocks, shape = W // 2 >> first, part.shape[1:]
-        scratch.append(pltpu.VMEM((blocks,) + shape, LOW))
-        local_copies += blocks + 1
-        for _ in lay.rbits[first:]:
-            scratch.append(pltpu.VMEM((blocks,) + shape, LOW))
-            copies += blocks
-            blocks //= 2
-        scratch.append(pltpu.VMEM(shape, F32))
-    forget_proj_grad, out_cols_grad, ffn_down_grad, gate_proj_grad, in_proj_grad, got_up, got_du, owned = net_call(
+    up_came = lay.send(tie(up_away, gate_away, back_all), lay.ybits[0])
+    du_mix_low = tie(du_mix_low, gate_got)
+    part_of = {
+        "forget": outer_rows(grads[:, 4 * half :], normed).astype(LOW).reshape(split + (r_f, width)),
+        "out": grad_w_out.reshape(split + (4 * r_in, 2 * half)),
+        "up": up_kept,
+        "down": down_kept,
+        "gate": outer_rows(tie(gate_low, up_came), normed).astype(LOW).reshape(split + (r_in, width)),
+        "in": outer_rows(grads[:, : 2 * half], normed).astype(LOW).reshape(split + (r_in, width)),
+    }
+    out_of = {name: (part.shape[-2:], F32) for name, part in part_of.items()}
+    out_of["out"] = ((4, r_in, 2 * half), F32)
+    parts = [part_of[name] for name in PARTS]
+    scratch, copies, local_copies = [pltpu.VMEM((length, width), LOW)] * 4, 6 + 3 + n, 8
+    for name, part in zip(PARTS, parts):
+        for _, rows in row_cuts(name, part.shape[-2]):
+            shape, skip = (rows, part.shape[-1]), first_stage(name)
+            scratch.append(pltpu.VMEM(split[1 + skip :] + shape, LOW))
+            for k in range(skip, len(split)):
+                scratch.append(pltpu.VMEM(split[1 + k :] + shape, LOW))
+            scratch.append(pltpu.VMEM(shape, F32))
+            copies += len(split)
+            local_copies += 3
+    *sums, du_x, du_z, mixed_x, mixed_z, owned = net_call(
         partial(reduce_kernel, lay),
         lay,
         (
             *parts,
-            down_away.reshape(W // 4, r_ffn, width),
-            up_away,
+            up_came,
+            down_away,
             du_mix_low.reshape(4, length, width),
+            mixed_low.reshape(4, length, width),
             to_owner,
         ),
         [
-            ((r_f, width), F32),
-            ((4, r_in, 2 * half), F32),
-            ((r_ffn, width), F32),
-            ((r_in, width), F32),
-            ((r_in, width), F32),
-            ((r_ffn, width), LOW),
-            ((3, length, width), LOW),
+            *[out_of[name] for name in PARTS],
+            *[((length, width), LOW)] * 4,
             ((n, 8, 128), F32),
         ],
         copies,
@@ -1192,17 +1295,17 @@
         "reduce",
         120,
         scratch,
-        56 << 20,
     )
     ffn_gate_grad = join(gate_kept, gate_got)
-    ffn_up_grad = join(up_kept, got_up)
+    sum_of = dict(zip(PARTS, sums))
     out_proj_grad = (
-        out_cols_grad.reshape(2, 2, r_in, 2, Y, 2 * r_in)
+        sum_of["out"].reshape(2, 2, r_in, 2, Y, 2 * r_in)
         .transpose(2, 3, 0, 4, 1, 5)
         .reshape(r_in, width)
     )
     owned = jnp.sum(owned, axis=0).reshape(-1)
-    du_mix = own_sum(du_mix_low, got_du)
+    mixed_out = (residual + own_sum(mixed_low, (mixed_x, mixed_z))).astype(LOW)
+    du_mix = own_sum(du_mix_low, (du_x, du_z))
     dg_mix = du_mix * g_mix
     tokens_grad = (
         grad_residual
@@ -1212,13 +1315,13 @@
     return (
         mixed_out,
         tokens_grad,
-        in_proj_grad,
-        forget_proj_grad,
-        gate_proj_grad,
+        sum_of["in"],
+        sum_of["forget"],
+        sum_of["gate"],
         out_proj_grad,
         ffn_gate_grad,
-        ffn_up_grad,
-        ffn_down_grad,
+        sum_of["up"],
+        sum_of["down"],
         owned[0:r_in],
         owned[2 * r_in : 3 * r_in],
         owned[r_in : 2 * r_in],

time: 650 us -> 604 us (0.929)
  Pallas kernels: 364 us -> 406 us
  local copies, waits for them, and re-layouts: 66 us -> 29.7 us
  waiting for transfers between devices: 45.3 us -> 12.6 us
  other arithmetic: 55.7 us -> 35.6 us
  matrix products: 91.7 us -> 102 us
  starting transfers between devices: 17.6 us -> 8.59 us
    pallas_call x5, Pallas kernels: 308 us -> 349 us  [net_call(): pl.pallas_call(body, out_shape=tuple((jax.ShapeDtypeStruct(s, d) for s, d...]
    ppermute x23 -> x10, waiting for transfers between devices: 45.3 us -> 12.6 us  [send(): return lax.ppermute(value, 'dp', [(i, i ^ mask) for i in range(self.n)])]
    unnamed x195 -> x144, local copies, waits for them, and re-layouts: 30.5 us -> 14.5 us
    slice x5 -> x0, local copies, waits for them, and re-layouts: 12.7 us -> none  [the longest x3 5.46 us: over_core(): return split_sum(part[:rows], lay.send(part[rows:], lay.C))]
    convert_element_type x7 -> x5, other arithmetic: 21.5 us -> 9.67 us  [the longest x1 2.95 us: local(): grad_low = tie(grad_residual.astype(LOW), mixed_low)]
    dot_general x5 -> x7, matrix products: 25.8 us -> 35.1 us  [outer_rows(): lax.dot_general(left_rows, right_rows, (((0,), (0,)), ((), ())), preferre...]
    ppermute x23 -> x10, starting transfers between devices: 17.6 us -> 8.59 us  [send(): return lax.ppermute(value, 'dp', [(i, i ^ mask) for i in range(self.n)])]
    convert_element_type x3 -> x1, other arithmetic: 9.36 us -> 2.56 us  [split_sum(): join(kept[rows:], got[rows:]).astype(LOW)]
  transfers between devices with their start and end apart: 23 -> 10, of which waited for: 6 -> 3; matrix products, arithmetic and copies ran while one was open for 20% -> 12% of each run, Pallas kernels for 20% -> 16%
where the time goes in v4:
time: 604 us; the launch traced here: 596 us
  Pallas kernels  406 us (67%)
  matrix products  102 us (17%)
  other arithmetic  35.6 us (6%)
  local copies, waits for them, and re-layouts  29.7 us (5%)
  waiting for transfers between devices  12.6 us (2%)
  starting transfers between devices  8.59 us (1%)
    pallas_call x5, Pallas kernels, net_call(): pl.pallas_call(body, out_shape=tuple((jax.ShapeDtypeStruct(s, d) for s, d...  349 us
    dot_general x5, matrix products, contract(): lax.dot_general(left_rows, right_rows, (((1,), (1,)), ((), ())), preferre...  36.2 us
    dot_general x7, matrix products, outer_rows(): lax.dot_general(left_rows, right_rows, (((0,), (0,)), ((), ())), preferre...  35.1 us
    pallas_call x2, Pallas kernels, small_gather(): pl.pallas_call(partial(gather_kernel, lay, masks, slot_of), out_shape=jax...  27.7 us
    unnamed x144, local copies, waits for them, and re-layouts  14.5 us
    ppermute x10, waiting for transfers between devices, send(): return lax.ppermute(value, 'dp', [(i, i ^ mask) for i in range(self.n)])  12.6 us
  transfers between devices with their start and end apart: 10, of which 3 were waited for; matrix products, arithmetic and copies ran while one was open for 12% of the time, Pallas kernels for 16%

profile of v4, /device:TPU:1, one launch (start us, length us, event | category | flops | bytes accessed | tf_op | source)
XLA Modules:
  0.0 596.3 jit_solution(15054487162175933016)
XLA Ops:
  7.2 84.5 %start.1 = (bf16[4,160,2048]{2,1,0:T(8,128)(2,1)}, bf16[40,32,2048]{2,1,0:T(8,128)(2,1)}, bf16[1,32,2048]{2,1,0:T(8,128)(2,1)}, bf16[4,64,512]{2,1,0:T(8,128)(2,...) custom-call(bf16[160,2048]{1,0:T(8,128)(2,1)} %tok.1, ...), custom_call_target="tpu_custom_call" | custom-call | flops 600000000 | tf_op jit(solution)/shard_map/start/pallas_call | solution.py:258
  99.0 5.2 fusion.35.proj
  104.4 5.8 gates.1
  112.4 12.9 %shard_map.263.summ = f32[32,8,256]{2,1,0:T(8,128)} custom-call(f32[4,8,256]{2,1,0:T(8,128)} %copy-done.19), custom_call_target="tpu_custom_call" | custom-call | flops 100000000 | tf_op jit(solution)/shard_map/pallas_call | solution.py:118
  133.6 7.4 %states.1 = (f32[2,640,128]{2,1,0:T(8,128)S(1)}, f32[2,640,128]{2,1,0:T(8,128)S(1)}, f32[2,640,128]{2,1,0:T(8,128)S(1)}, f32[2,640,128]{2,1,0:T(8,128)S(1)}, bf1...) custom-call(s32[36]{0:T(128)S(1)} %pad_add_fusion.1.ints, f32[32,8,256]{2,1,0:T(8,128)S(1)} %copy-done, ...), custom_call_target="tpu_custom_call" | custom-call | flops 70000000 | tf_op jit(solution)/shard_map/states/pallas_call | solution.py:1068
  141.1 3.0 convolution_convert_fusion.5
  144.1 60.3 %branch.1 = (bf16[160,2048]{1,0:T(8,128)(2,1)}, bf16[160,2048]{1,0:T(8,128)(2,1)}, f32[3,160,128]{2,1,0:T(8,128)}, bf16[8,176,2048]{2,1,0:T(8,128)(2,1)}, bf16[1...) custom-call(bf16[4,160,2048]{2,1,0:T(8,128)(2,1)} %bitcast.122, f32[4,160,128]{2,1,0:T(8,128)} %bitcast.114, ...), custom_call_target="tpu_custom_call" | custom-call | flops 400000000 | tf_op jit(solution)/shard_map/branch/pallas_call | solution.py:258
  205.6 3.0 multiply_reduce_fusion.5
  211.0 52.8 %ffn_in.1 = (bf16[4,160,2048]{2,1,0:T(8,128)(2,1)}, bf16[8,176,2048]{2,1,0:T(8,128)(2,1)}, bf16[8,176,2048]{2,1,0:T(8,128)(2,1)}, bf16[4,160,2048]{2,1,0:T(8,128)(2,1)}) custom-call(bf16[160,2048]{1,0:T(8,128)(2,1)} %multiply_convert_fusion.5.own, bf16[176,2048]{1,0:T(8,128)(2,1)} %convert_element_type.204.up, bf16[176,2048]{1,0:T(8,128)(2,1)} %collective-permute-done.up_z, ...), custom_call_target="tpu_custom_call" | custom-call | flops 400000000 | tf_op jit(solution)/shard_map/ffn_in/pallas_call | solution.py:258
  263.8 9.6 %fusion.36 = f32[640,1408]{1,0:T(8,128)} fusion(bf16[640,2048]{1,0:T(8,128)(2,1)} %bitcast.167, bf16[1408,2048]{1,0:T(8,128)(2,1)} %bitcast.151), kind=kOutput, calls=%fused_computation.147 | convolution fusion | flops 3690987520 | bytes 11993088 | tf_op jit(solution)/shard_map/dot_general | solution.py:20
  273.5 8.8 %fusion.37 = f32[640,1408]{1,0:T(8,128)} fusion(bf16[640,2048]{1,0:T(8,128)(2,1)S(1)} %bitcast.163, bf16[1408,2048]{1,0:T(8,128)(2,1)} %bitcast.147), kind=kOutput, calls=%fused_computation.148 | convolution fusion | flops 3690987520 | bytes 11993088 | tf_op jit(solution)/shard_map/dot_general | solution.py:20
  282.3 9.5 %multiply_convert_fusion.2 = (bf16[640,1408]{1,0:T(8,128)(2,1)}, bf16[640,1408]{1,0:T(8,128)(2,1)}, bf16[640,1408]{1,0:T(8,128)(2,1)}) fusion(f32[640,1408]{1,0:T(8,128)} %fusion.37, f32[640,1408]{1,0:T(8,128)} %fusion.36, bf16[640,2048]{1,0:T(8,128)(2,1)S(1)} %bitcast.164, bf16[1408,2048]{1,0:T(8,128)(2,1)S(1)} %bitcast.157), kind=kOutput, calls=%fused_computation.9 | convolution fusion | flops 3704504320 | bytes 21004288 | tf_op jit(solution)/shard_map/dot_general | solution.py:20
  291.8 5.9 fusion.38
  297.8 4.4 add_convert_fusion
  305.1 6.6 %convolution_convert_fusion = bf16[1408,2048]{1,0:T(8,128)(2,1)} fusion(bf16[640,1408]{1,0:T(8,128)(2,1)S(1)} %copy-done.61, bf16[640,2048]{1,0:T(8,128)(2,1)S(1)} %bitcast.168), kind=kOutput, calls=%fused_computation | convolution fusion | flops 3693871104 | bytes 10190848 | tf_op jit(solution)/shard_map/dot_general | solution.py:26
  311.7 6.5 %convolution_convert_fusion.1 = bf16[1408,2048]{1,0:T(8,128)(2,1)} fusion(bf16[640,1408]{1,0:T(8,128)(2,1)S(1)} %copy-done.60, bf16[640,2048]{1,0:T(8,128)(2,1)S(1)} %bitcast.165), kind=kOutput, calls=%fused_computation.1 | convolution fusion | flops 3693871104 | bytes 10190848 | tf_op jit(solution)/shard_map/dot_general | solution.py:26
  318.2 6.7 %convolution_convert_fusion.2 = bf16[1408,2048]{1,0:T(8,128)(2,1)} fusion(bf16[640,1408]{1,0:T(8,128)(2,1)S(1)} %copy-done.58, bf16[640,2048]{1,0:T(8,128)(2,1)S(1)} %bitcast.166), kind=kOutput, calls=%fused_computation.2 | convolution fusion | flops 3693871104 | bytes 10190848 | tf_op jit(solution)/shard_map/dot_general | solution.py:26
  325.0 5.5 convolution_convert_fusion.4
  330.6 3.0 collective-permute-done.6
  340.1 27.7 %grad_in.1 = (bf16[4,160,2048]{2,1,0:T(8,128)(2,1)}, f32[4,160,128]{2,1,0:T(8,128)}, bf16[2,176,2048]{2,1,0:T(8,128)(2,1)}, bf16[2,176,2048]{2,1,0:T(8,128)(2,1)...) custom-call(bf16[160,2048]{1,0:T(8,128)(2,1)} %copy-done.26, ...), custom_call_target="tpu_custom_call" | custom-call | flops 270000000 | tf_op jit(solution)/shard_map/grad_in/pallas_call | solution.py:258
  369.2 5.1 fusion.39.grad_mid
  374.3 7.2 %back_gates.1 = (f32[2,640,128]{2,1,0:T(8,128)S(1)}, f32[2,640,128]{2,1,0:T(8,128)S(1)}, bf16[640,512]{1,0:T(8,128)(2,1)S(1)}, bf16[640,512]{1,0:T(8,128)(2,1)S(...) custom-call(f32[640,512]{1,0:T(8,128)} %fusion.39.grad_mid, f32[2,640,128]{2,1,0:T(8,128)S(1)} %copy-done.11, ...), custom_call_target="tpu_custom_call" | custom-call | flops 70000000 | tf_op jit(solution)/shard_map/back_gates/pallas_call | solution.py:1207
  384.9 3.7 convolution_convert_fusion.8
  390.2 14.8 %shard_map.264.back = f32[32,8,256]{2,1,0:T(8,128)} custom-call(f32[4,8,256]{2,1,0:T(8,128)} %copy-done.18), custom_call_target="tpu_custom_call" | custom-call | flops 100000000 | tf_op jit(solution)/shard_map/pallas_call | solution.py:118
  408.7 8.5 %adjoints.1 = (bf16[640,1280]{1,0:T(8,128)(2,1)}, f32[8,256]{1,0:T(8,128)S(1)}, f32[8,256]{1,0:T(8,128)S(1)}) custom-call(s32[36]{0:T(128)S(1)} %pad_add_fusion.1.ints, f32[32,8,256]{2,1,0:T(8,128)S(1)} %copy-done, f32[32,8,256]{2,1,0:T(8,128)S(1)} %copy-done.16, f32[2,640,128]{2,1,0:T(8,128)S(1)} %copy-done.4, f32[2,640,128]{2,1,0:T(8,128)S(1)} %copy-done.6, ...), custom_call_target="tpu_custom_call" | custom-call | flops 70000000 | tf_op jit(solution)/shard_map/adjoints/pallas_call | solution.py:1217
  418.5 9.7 %multiply_reduce_fusion = (f32[2048]{0:T(1024)S(1)}, bf16[640,2048]{1,0:T(8,128)(2,1)}, bf16[640,2048]{1,0:T(8,128)(2,1)}) fusion(bf16[4,160,2048]{2,1,0:T(8,128)(2,1)} %get-tuple-element.80, f32[640]{0:T(1024)S(1)} %rsqrt.40, f32[2048]{0:T(1024)S(1)} %mul.322, bf16[640,1280]{1,0:T(8,128)(2,1)} %get-tuple-element.123, bf16[1280,2048]{1,0:T(8,128)(2,1)} %bitcast.159), kind=kOutput, calls=%fused_computation.4 | convolution fusion | flops 3365926912 | bytes 14764544 | tf_op jit(solution)/shard_map/dot_general | solution.py:1225
  429.3 4.0 convolution_convert_fusion.9
  433.3 4.4 convolution_convert_fusion.6
  437.6 4.1 collective-permute-done.9
  444.5 5.5 collective-permute-done.8.refs_6_
  450.0 3.2 convolution_convert_fusion.7
  453.1 124.1 %reduce.6 = (f32[176,2048]{1,0:T(8,128)}, f32[32,2048]{1,0:T(8,128)}, f32[4,64,512]{2,1,0:T(8,128)}, f32[176,2048]{1,0:T(8,128)}, f32[64,2048]{1,0:T(8,128)}, /*...) custom-call(bf16[2,176,2048]{2,1,0:T(8,128)(2,1)} %get-tuple-element, ...), custom_call_target="tpu_custom_call" | custom-call | flops 1200000000 | tf_op jit(solution)/shard_map/reduce/pallas_call | solution.py:258
  (249 shorter events, 71.0 us)
Async XLA Ops:
  5.1 88.1 %copy-start.57 = (s32[32]{0:T(128)S(1)}, s32[32]{0:T(128)}, u32[]{:S(2)}) copy-start(s32[32]{0:T(128)} %param.19) | copy-start | bytes 388
  5.1 88.4 %copy-start.56 = (s32[5]{0:T(128)S(1)}, s32[5]{0:T(128)}, u32[]{:S(2)}) copy-start(s32[5]{0:T(128)} %param.18) | copy-start | bytes 64
  104.2 23.8 %copy-start.34 = (f32[176,2048]{1,0:T(8,128)S(1)}, f32[176,2048]{1,0:T(8,128)}, u32[]{:S(2)}) copy-start(f32[176,2048]{1,0:T(8,128)} %param.25) | copy-start | bytes 4325380
  125.3 85.7 %collective-permute-start.1 = (bf16[160,2048]{1,0:T(8,128)(2,1)}, bf16[160,2048]{1,0:T(8,128)(2,1)}, u32[]{:S(2)}, u32[]{:S(2)}) collective-permute-start(bf16[160,2048]{1,0:T(8,128)(2,1)} %rest_0_), channel_id=1, source_target_pairs={{0,2},{1,3},{2,0},{3,1},{4,6},{5,7},{6,4},{7,5},{8,10},{9,11},{10,... | collective-permute-start | bytes 1966088 | tf_op jit(solution)/shard_map/ppermute | solution.py:71
  125.7 85.4 %collective-permute-start.2 = (bf16[160,2048]{1,0:T(8,128)(2,1)}, bf16[160,2048]{1,0:T(8,128)(2,1)}, u32[]{:S(2)}, u32[]{:S(2)}) collective-permute-start(bf16[160,2048]{1,0:T(8,128)(2,1)} %rest_0_), channel_id=1, source_target_pairs={{0,8},{1,9},{2,10},{3,11},{4,12},{5,13},{6,14},{7,15},{8,0},{9,1},... | collective-permute-start | bytes 1966088 | tf_op jit(solution)/shard_map/ppermute | solution.py:71
  125.7 85.4 %collective-permute-start.3 = (bf16[160,2048]{1,0:T(8,128)(2,1)}, bf16[160,2048]{1,0:T(8,128)(2,1)}, u32[]{:S(2)}, u32[]{:S(2)}) collective-permute-start(bf16[160,2048]{1,0:T(8,128)(2,1)} %rest_0_), channel_id=1, source_target_pairs={{0,10},{1,11},{2,8},{3,9},{4,14},{5,15},{6,12},{7,13},{8,2},{9,3},... | collective-permute-start | bytes 1966088 | tf_op jit(solution)/shard_map/ppermute | solution.py:71
  129.0 82.0 %collective-permute-start = (bf16[176,2048]{1,0:T(8,128)(2,1)}, bf16[176,2048]{1,0:T(8,128)(2,1)}, u32[]{:S(2)}, u32[]{:S(2)}) collective-permute-start(bf16[176,2048]{1,0:T(8,128)(2,1)} %convert_element_type.204.up), channel_id=1, source_target_pairs={{0,16},{1,17},{2,18},{3,19},{4,20},{5,21},{6,22},{7,23},{8,24},{9,... | collective-permute-start | bytes 2162696 | tf_op jit(solution)/shard_map/ppermute | solution.py:71
  131.8 9.3 %copy-start.32 = (bf16[2,2,2,2,2,64,512]{6,5,2,4,1,3,0:T(8,128)(2,1)}, bf16[2,2,2,2,2,64,512]{6,5,2,4,1,3,0:T(8,128)(2,1)S(1)}, u32[]{:S(2)}) copy-start(bf16[2,2,2,2,2,64,512]{6,5,2,4,1,3,0:T(8,128)(2,1)S(1)} %copy.49) | copy-start | bytes 6291460
  144.1 61.5 %copy-start.24 = (bf16[160,2048]{1,0:T(8,128)(2,1)S(1)}, bf16[160,2048]{1,0:T(8,128)(2,1)}, u32[]{:S(2)}) copy-start(bf16[160,2048]{1,0:T(8,128)(2,1)} %tok.1) | copy-start | bytes 1966084
  263.8 9.6 %copy-start.54 = (bf16[4,160,2048]{2,1,0:T(8,128)(2,1)S(1)}, bf16[4,160,2048]{2,1,0:T(8,128)(2,1)}, u32[]{:S(2)}) copy-start(bf16[4,160,2048]{2,1,0:T(8,128)(2,1)} %get-tuple-element.101) | copy-start | bytes 7864324
  263.8 18.5 %slice-start.4 = ((s8[5767168]{0:T(1024)(128)(4,1)}), s8[4194304]{0:T(1024)(128)(4,1)S(1)}, s32[]{:S(2)}) async-start(s8[5767168]{0:T(1024)(128)(4,1)} %bitcast.155), calls=%async_computation.4 | async-start | bytes 8388608
  273.5 8.8 %slice-start.5 = ((s8[5767168]{0:T(1024)(128)(4,1)}), s8[1572864]{0:T(1024)(128)(4,1)S(1)}, s32[]{:S(2)}) async-start(s8[5767168]{0:T(1024)(128)(4,1)} %bitcast.155), calls=%async_computation.5 | async-start | bytes 3145728
  273.5 18.3 %slice-start = ((s8[5767168]{0:T(1024)(128)(4,1)}), s8[4194304]{0:T(1024)(128)(4,1)S(1)}, s32[]{:S(2)}) async-start(s8[5767168]{0:T(1024)(128)(4,1)} %bitcast.148), calls=%async_computation | async-start | bytes 8388608
  282.3 9.5 %slice-start.1 = ((s8[5767168]{0:T(1024)(128)(4,1)}), s8[1572864]{0:T(1024)(128)(4,1)S(1)}, s32[]{:S(2)}) async-start(s8[5767168]{0:T(1024)(128)(4,1)} %bitcast.148), calls=%async_computation.1 | async-start | bytes 3145728
  291.8 5.9 copy-start.59
  297.7 7.4 %copy-start.61 = (bf16[640,1408]{1,0:T(8,128)(2,1)S(1)}, bf16[640,1408]{1,0:T(8,128)(2,1)}, u32[]{:S(2)}) copy-start(bf16[640,1408]{1,0:T(8,128)(2,1)} %get-tuple-element.105) | copy-start | bytes 5406724
  302.4 22.6 %collective-permute-start.4 = (bf16[160,2048]{1,0:T(8,128)(2,1)S(1)}, bf16[160,2048]{1,0:T(8,128)(2,1)S(1)}, u32[]{:S(2)}, u32[]{:S(2)}) collective-permute-start(bf16[160,2048]{1,0:T(8,128)(2,1)S(1)} %get-tuple-element.161), channel_id=1, source_target_pairs={{0,2},{1,3},{2,0},{3,1},{4,6},{5,7},{6,4},{7,5},{8,10},{9,11},{10,... | collective-permute-start | bytes 1966088 | tf_op jit(solution)/shard_map/ppermute | solution.py:71
  303.7 26.8 %collective-permute-start.5 = (bf16[160,2048]{1,0:T(8,128)(2,1)S(1)}, bf16[160,2048]{1,0:T(8,128)(2,1)S(1)}, u32[]{:S(2)}, u32[]{:S(2)}) collective-permute-start(bf16[160,2048]{1,0:T(8,128)(2,1)S(1)} %get-tuple-element.163), channel_id=1, source_target_pairs={{0,8},{1,9},{2,10},{3,11},{4,12},{5,13},{6,14},{7,15},{8,0},{9,1},... | collective-permute-start | bytes 1966088 | tf_op jit(solution)/shard_map/ppermute | solution.py:71
  304.1 29.5 %collective-permute-start.6 = (bf16[160,2048]{1,0:T(8,128)(2,1)S(1)}, bf16[160,2048]{1,0:T(8,128)(2,1)S(1)}, u32[]{:S(2)}, u32[]{:S(2)}) collective-permute-start(bf16[160,2048]{1,0:T(8,128)(2,1)S(1)} %get-tuple-element.162), channel_id=1, source_target_pairs={{0,10},{1,11},{2,8},{3,9},{4,14},{5,15},{6,12},{7,13},{8,2},{9,3},... | collective-permute-start | bytes 1966088 | tf_op jit(solution)/shard_map/ppermute | solution.py:71
  305.1 6.6 %copy-start.60 = (bf16[640,1408]{1,0:T(8,128)(2,1)S(1)}, bf16[640,1408]{1,0:T(8,128)(2,1)}, u32[]{:S(2)}) copy-start(bf16[640,1408]{1,0:T(8,128)(2,1)} %get-tuple-element.108) | copy-start | bytes 5406724
  311.7 6.5 %copy-start.58 = (bf16[640,1408]{1,0:T(8,128)(2,1)S(1)}, bf16[640,1408]{1,0:T(8,128)(2,1)}, u32[]{:S(2)}) copy-start(bf16[640,1408]{1,0:T(8,128)(2,1)} %get-tuple-element.107) | copy-start | bytes 5406724
  311.7 13.3 %slice-start.2 = ((s8[5767168]{0:T(1024)(128)(4,1)}), s8[4194304]{0:T(1024)(128)(4,1)S(1)}, s32[]{:S(2)}) async-start(s8[5767168]{0:T(1024)(128)(4,1)} %bitcast.152), calls=%async_computation.2 | async-start | bytes 8388608
  318.2 6.8 %slice-start.3 = ((s8[5767168]{0:T(1024)(128)(4,1)}), s8[1572864]{0:T(1024)(128)(4,1)S(1)}, s32[]{:S(2)}) async-start(s8[5767168]{0:T(1024)(128)(4,1)} %bitcast.152), calls=%async_computation.3 | async-start | bytes 3145728
  325.0 8.6 %copy-start.20 = (f32[160,2048]{1,0:T(8,128)S(1)}, f32[160,2048]{1,0:T(8,128)}, u32[]{:S(2)}) copy-start(f32[160,2048]{1,0:T(8,128)} %get-tuple-element.153) | copy-start | bytes 3932164
  367.8 37.3 %collective-permute-start.7 = (bf16[352,2048]{1,0:T(8,128)(2,1)}, bf16[352,2048]{1,0:T(8,128)(2,1)}, u32[]{:S(2)}, u32[]{:S(2)}) collective-permute-start(bf16[352,2048]{1,0:T(8,128)(2,1)} %bitcast.169), channel_id=1, source_target_pairs={{0,4},{1,5},{2,6},{3,7},{4,0},{5,1},{6,2},{7,3},{8,12},{9,13},{10,... | collective-permute-start | bytes 4325384 | tf_op jit(solution)/shard_map/ppermute | solution.py:71
  369.2 5.1 copy-start.15
  407.6 34.1 %collective-permute-start.9 = (bf16[176,2048]{1,0:T(8,128)(2,1)}, bf16[176,2048]{1,0:T(8,128)(2,1)}, u32[]{:S(2)}, u32[]{:S(2)}) collective-permute-start(bf16[176,2048]{1,0:T(8,128)(2,1)} %fusion.2), channel_id=1, source_target_pairs={{0,16},{1,17},{2,18},{3,19},{4,20},{5,21},{6,22},{7,23},{8,24},{9,... | collective-permute-start | bytes 2162696 | tf_op jit(solution)/shard_map/ppermute | solution.py:71
  417.2 32.8 %collective-permute-start.8 = (bf16[2,176,2048]{2,1,0:T(8,128)(2,1)}, bf16[2,176,2048]{2,1,0:T(8,128)(2,1)S(1)}, u32[]{:S(2)}, u32[]{:S(2)}) collective-permute-start(bf16[2,176,2048]{2,1,0:T(8,128)(2,1)} %get-tuple-element.127), channel_id=1, source_target_pairs={{0,4},{1,5},{2,6},{3,7},{4,0},{5,1},{6,2},{7,3},{8,12},{9,13},{10,... | collective-permute-start | bytes 4325384 | tf_op jit(solution)/shard_map/ppermute | solution.py:71
  433.3 8.5 %copy-start.33 = (bf16[2,176,2048]{2,1,0:T(8,128)(2,1)S(1)}, bf16[2,176,2048]{2,1,0:T(8,128)(2,1)}, u32[]{:S(2)}) copy-start(bf16[2,176,2048]{2,1,0:T(8,128)(2,1)} %get-tuple-element.115) | copy-start | bytes 4325380
  577.3 7.2 %copy-start.25 = (bf16[160,2048]{1,0:T(8,128)(2,1)S(1)}, bf16[160,2048]{1,0:T(8,128)(2,1)}, u32[]{:S(2)}) copy-start(bf16[160,2048]{1,0:T(8,128)(2,1)} %tok.1) | copy-start | bytes 1966084
  577.3 7.2 %copy-start.30 = (bf16[160,2048]{1,0:T(8,128)(2,1)S(1)}, bf16[160,2048]{1,0:T(8,128)(2,1)}, u32[]{:S(2)}) copy-start(bf16[160,2048]{1,0:T(8,128)(2,1)} %get-tuple-element.137) | copy-start | bytes 1966084
  577.3 7.2 %copy-start.31 = (bf16[160,2048]{1,0:T(8,128)(2,1)S(1)}, bf16[160,2048]{1,0:T(8,128)(2,1)}, u32[]{:S(2)}) copy-start(bf16[160,2048]{1,0:T(8,128)(2,1)} %get-tuple-element.138) | copy-start | bytes 1966084
  (46 other events, 120.8 us)

commit v5 on v4

--- a/solution.py
+++ b/solution.py
@@ -366,7 +366,7 @@
     own.wait()
     arrived(out_in)
     g_out.start()
-    gate_in = net.put(f_gate, f_gate_z, lay.ZH)
+    gate_in = net.put(f_gate.at[pl.ds(0, f_gate_z.shape[0])], f_gate_z, lay.ZH)
     net.settle()
     for mask in g_in.masks():
         g_in.forward(mask)
@@ -386,49 +386,70 @@
     return lay.tmasks[1:] + lay.wbits
 
 
-def rel_gather(net, own, early, out):
-    return WeightGather(net, own, lambda d, m: out.at[net.lay.rel_slot(m)], early)
-
-
-def branch_kernel(lay, blocks, small, gate, gate_z, down, got_x, got_z, got_small, gate_all, down_y, down_z, *rest):
+def rel_gather(net, own, early, out, cut):
+    rows = pl.ds(*cut)
+    early = {bit: block if block.shape[0] == cut[1] else block.at[rows] for bit, block in early.items()}
+    return WeightGather(net, own.at[rows], lambda d, m: out.at[net.lay.rel_slot(m), rows], early)
+
+
+def branch_kernel(lay, cuts, blocks, small, gate, up, down, *rest):
+    pieces = len(cuts)
+    gate_z, rest = rest[:pieces], rest[pieces:]
+    (got_x, got_z, got_small, gate_all, down_y, down_z), rest = rest[:6], rest[6:]
+    up_z, rest = rest[: pieces - 1], rest[pieces - 1 :]
     token_rooms, rest = rest[:2], rest[2:]
     *rooms, send_sems, recv_sems, local_sems = rest
     net = Net(lay, group_peers(lay), send_sems, recv_sems, local_sems, rooms)
-    gather = rel_gather(net, gate, {lay.ZH: gate_z}, gate_all)
-    gather.start()
-    waits = [net.put(down, down_z, lay.ZH)]
+    gathers = [rel_gather(net, gate, {lay.ZH: z}, gate_all, cut) for cut, z in zip(cuts, gate_z)]
+    for gather in gathers:
+        gather.start()
     tokens = TokenReduce(net, blocks, got_x, got_z, *token_rooms)
+    waits = [net.put(up.at[pl.ds(*cut)], z, lay.ZH) for cut, z in zip(cuts[1:], up_z)]
     waits += token_scatter(net, small, got_small)
     net.settle()
-    for mask in gather.masks():
-        gather.forward(mask)
+    arrived(waits[: pieces - 1])
+    waits = waits[pieces - 1 :]
+    waits.append(net.put(down.at[pl.ds(*cuts[0])], down_z, lay.ZH))
+    for gather in gathers:
+        for mask in gather.masks():
+            gather.forward(mask)
     waits.append(net.put(down, down_y, lay.ybits[0]))
     tokens.pass_on()
-    gather.end()
+    for gather in gathers:
+        gather.end()
     tokens.end()
     arrived(waits)
     net.finish()
 
 
-def ffn_kernel(lay, own, up, up_z, down, down_y, down_z, *rest):
+def ffn_kernel(lay, cuts, own, up, down, down_y, down_z, *rest):
+    pieces = len(cuts)
+    up_z, rest = rest[:pieces], rest[pieces:]
     cot_blocks, (own_all, up_all, down_all, cot_all), rest = rest[:4], rest[4:8], rest[8:]
     *rooms, send_sems, recv_sems, local_sems = rest
     net = Net(lay, group_peers(lay), send_sems, recv_sems, local_sems, rooms)
+    gathers = []
+    for i, cut in enumerate(cuts):
+        early = {lay.ybits[0]: down_y}
+        if i == 0:
+            early[lay.ZH] = down_z
+        gathers.append(rel_gather(net, down, early, down_all, cut))
+    for cut, z in zip(cuts, up_z):
+        gathers.append(rel_gather(net, up, {lay.ZH: z}, up_all, cut))
+    gathers[pieces - 1].start()
     first = token_start(net, own, own_all)
-    g_up = rel_gather(net, up, {lay.ZH: up_z}, up_all)
-    g_down = rel_gather(net, down, {lay.ZH: down_z, lay.ybits[0]: down_y}, down_all)
-    g_up.start()
-    g_down.start()
+    for i, gather in enumerate(gathers):
+        if i != pieces - 1:
+            gather.start()
     for j, block in enumerate(cot_blocks):
         net.move(block, cot_all.at[j])
     net.settle()
     rest = token_finish(net, first, own_all)
-    for mask in g_up.masks():
-        g_up.forward(mask)
-    for mask in g_down.masks():
-        g_down.forward(mask)
-    g_up.end()
-    g_down.end()
+    for gather in gathers[pieces:] + gathers[:pieces]:
+        for mask in gather.masks():
+            gather.forward(mask)
+    for gather in gathers:
+        gather.end()
     arrived(rest)
     net.finish()
 
@@ -991,8 +1012,9 @@
     out_cols = out_cols.transpose(2, 4, 0, 1, 3, 5).reshape(4, r_in, 2 * half)
     units = r_in // r_f
     r_ffn = ffn_gate.shape[0]
+    cuts = row_cuts("up", r_ffn)
     f_gate = ffn_gate.astype(LOW)
-    tok_all, w_mix, _, _, w_out, gate_z, every = net_call(
+    tok_all, w_mix, _, _, w_out, gate_za, every = net_call(
         partial(start_kernel, lay, units),
         lay,
         (
@@ -1010,7 +1032,7 @@
             ((1, r_f, width), LOW),
             ((4, r_in, 2 * half), LOW),
             ((W, 4, r_in, 2 * half), LOW),
-            ((r_ffn, width), LOW),
+            ((cuts[0][1], width), LOW),
             ((n, 8, 128), F32),
         ],
         4 * (W - 1) + 9 + n - 1,
@@ -1027,6 +1049,9 @@
         ],
     )
     f_up, f_down = ffn_up.astype(LOW), ffn_down.astype(LOW)
+    gate_z = [gate_za]
+    if len(cuts) > 1:
+        gate_z.append(lay.send(tie(ffn_gate[cuts[1][0] :].astype(LOW), tok_all), lay.ZH))
     tok_all = tok_all.reshape(total, width)
     w_mix = w_mix.reshape(5 * half, width)
     w_out = w_out.reshape(2, Y, 2, 2, 2, r_in, 2 * half).transpose(0, 3, 1, 4, 2, 5, 6)
@@ -1062,9 +1087,10 @@
         3,
         name="gates",
     )(proj, keep, par)
+    summ = tie(summ, gate_z[-1])
     summ_all = small_gather(lay, summ, lay.wmasks, partial(w_slot, lay), W, 1)
     cot_blocks = lay.gather_t(tie(cotangent, summ_all))
-    up_z = lay.send(tie(f_up, summ_all), lay.ZH)
+    up_z = [lay.send(tie(ffn_up[: cuts[0][1]].astype(LOW), summ_all), lay.ZH)]
     st_re, st_im, be_re, be_im, unit, squares = plain_call(
         partial(state_kernel, half, length, n),
         [wide] * 4 + [((total, 2 * half), LOW), ((total, LANES), F32)],
@@ -1072,29 +1098,38 @@
         smem=1,
         name="states",
     )(ints, summ_all, d_re, d_im, v_re, v_im, proj, g_out)
-    branch_low = contract(unit, w_out).astype(LOW)
+    branch_low = tie(contract(unit, w_out).astype(LOW), up_z[0])
 
     def t_blocks(value):
         return [value[j * length : (j + 1) * length] for j in range(4)]
 
-    branch_x, branch_z, got_squares, w_ffn_gate, down_y, down_z = net_call(
-        partial(branch_kernel, lay),
+    branch_x, branch_z, got_squares, w_ffn_gate, down_y, down_z, *up_zb = net_call(
+        partial(branch_kernel, lay, cuts),
         lay,
-        (branch_low.reshape(4, length, width), squares.reshape(4, length, LANES), f_gate, gate_z, f_down),
+        (
+            branch_low.reshape(4, length, width),
+            squares.reshape(4, length, LANES),
+            f_gate,
+            f_up,
+            f_down,
+            *gate_z,
+        ),
         [
             ((length, width), LOW),
             ((length, width), LOW),
             ((3, length, LANES), F32),
             ((W, r_ffn, width), LOW),
             ((r_ffn, width), LOW),
-            ((r_ffn, width), LOW),
-        ],
-        W + 7,
-        6,
+            ((cuts[0][1], width), LOW),
+        ]
+        + [((rows, width), LOW) for _, rows in cuts[1:]],
+        2 * W + 10,
+        12,
         4,
         "branch",
         40,
-        [pltpu.VMEM((length, width), LOW)] * 2 + [pltpu.VMEM((r_ffn, width), LOW)] * 2,
+        [pltpu.VMEM((length, width), LOW)] * 2
+        + [pltpu.VMEM((rows, width), LOW) for _, rows in cuts for _ in range(2)],
     )
     w_ffn_gate = w_ffn_gate.reshape(W * r_ffn, width)
 
@@ -1111,24 +1146,30 @@
     r_res = lax.rsqrt(jnp.mean(residual * residual, axis=-1, keepdims=True) + EPS)
     ffn_low = (residual * r_res * g_ffn).astype(LOW)
 
+    tok_room = pltpu.VMEM((length, width), LOW)
+    rooms = [pltpu.VMEM((rows, width), LOW) for _, rows in cuts]
+    last = len(cuts) - 1
+    down_rooms = [[room] * (3 if i == 0 else 2) for i, room in enumerate(rooms)]
     ffn_all, w_ffn_up, w_down, cot_all = net_call(
-        partial(ffn_kernel, lay),
+        partial(ffn_kernel, lay, cuts),
         lay,
-        (ffn_low, f_up, up_z, f_down, down_y, down_z, *cot_blocks),
+        (ffn_low, f_up, f_down, down_y, down_z, *up_z, *up_zb, *cot_blocks),
         [
             ((4, length, width), LOW),
             ((W, r_ffn, width), LOW),
             ((W, r_ffn, width), LOW),
             ((4, length, width), LOW),
         ],
-        2 * W + 4,
-        20,
+        4 * W + 8,
+        32,
         5,
         "ffn_in",
         40,
-        [pltpu.VMEM((length, width), LOW)]
-        + [pltpu.VMEM((r_ffn, width), LOW)] * 5
-        + [pltpu.VMEM((length, width), LOW)] * 4,
+        down_rooms[last]
+        + [tok_room]
+        + [room for i in range(last) for room in down_rooms[i]]
+        + [room for room in rooms for _ in range(2)]
+        + [tok_room] * 4,
     )
     ffn_all = ffn_all.reshape(total, width)
     w_ffn_up = w_ffn_up.reshape(W * r_ffn, width)

time: 604 us -> 592 us (0.980)
  Pallas kernels: 406 us -> 392 us
    pallas_call x5, Pallas kernels: 349 us -> 335 us  [net_call(): pl.pallas_call(body, out_shape=tuple((jax.ShapeDtypeStruct(s, d) for s, d...]
    unnamed x144 -> x152, local copies, waits for them, and re-layouts: 14.5 us -> 16.2 us
    ppermute x10 -> x11, waiting for transfers between devices: 12.6 us -> 14.2 us  [send(): return lax.ppermute(value, 'dp', [(i, i ^ mask) for i in range(self.n)])]
  transfers between devices with their start and end apart: 10 -> 11, of which waited for: 3 -> 4; matrix products, arithmetic and copies ran while one was open for 12% -> 14% of each run, Pallas kernels for 16% -> 17%
where the time goes in v5:
time: 592 us; the launch traced here: 585 us
  Pallas kernels  392 us (66%)
  matrix products  102 us (17%)
  other arithmetic  33.5 us (6%)
  local copies, waits for them, and re-layouts  32.7 us (6%)
  waiting for transfers between devices  14.2 us (2%)
  starting transfers between devices  8.42 us (1%)
    pallas_call x5, Pallas kernels, net_call(): pl.pallas_call(body, out_shape=tuple((jax.ShapeDtypeStruct(s, d) for s, d...  335 us
    dot_general x5, matrix products, contract(): lax.dot_general(left_rows, right_rows, (((1,), (1,)), ((), ())), preferre...  36.2 us
    dot_general x7, matrix products, outer_rows(): lax.dot_general(left_rows, right_rows, (((0,), (0,)), ((), ())), preferre...  35.1 us
    pallas_call x2, Pallas kernels, small_gather(): pl.pallas_call(partial(gather_kernel, lay, masks, slot_of), out_shape=jax...  28.2 us
    unnamed x152, local copies, waits for them, and re-layouts  16.2 us
    ppermute x11, waiting for transfers between devices, send(): return lax.ppermute(value, 'dp', [(i, i ^ mask) for i in range(self.n)])  14.2 us
  transfers between devices with their start and end apart: 11, of which 4 were waited for; matrix products, arithmetic and copies ran while one was open for 14% of the time, Pallas kernels for 17%

profile of v5, /device:TPU:1, one launch (start us, length us, event | category | flops | bytes accessed | tf_op | source)
XLA Modules:
  0.0 584.8 jit_solution(13002423311247945265)
XLA Ops:
  6.4 72.0 %start.1 = (bf16[4,160,2048]{2,1,0:T(8,128)(2,1)}, bf16[40,32,2048]{2,1,0:T(8,128)(2,1)}, bf16[1,32,2048]{2,1,0:T(8,128)(2,1)}, bf16[4,64,512]{2,1,0:T(8,128)(2,...) custom-call(bf16[160,2048]{1,0:T(8,128)(2,1)} %tok.1, ...), custom_call_target="tpu_custom_call" | custom-call | flops 600000000 | tf_op jit(solution)/shard_map/start/pallas_call | solution.py:258
  87.9 5.2 fusion.35.proj
  93.2 5.7 gates.1
  101.2 12.2 %shard_map.263.summ = f32[32,8,256]{2,1,0:T(8,128)} custom-call(f32[4,8,256]{2,1,0:T(8,128)} %copy-done.19), custom_call_target="tpu_custom_call" | custom-call | flops 100000000 | tf_op jit(solution)/shard_map/pallas_call | solution.py:118
  113.6 3.2 copy.49
  122.7 7.6 %states.1 = (f32[2,640,128]{2,1,0:T(8,128)S(1)}, f32[2,640,128]{2,1,0:T(8,128)S(1)}, f32[2,640,128]{2,1,0:T(8,128)S(1)}, f32[2,640,128]{2,1,0:T(8,128)S(1)}, bf1...) custom-call(s32[36]{0:T(128)S(1)} %pad_add_fusion.1.ints, f32[32,8,256]{2,1,0:T(8,128)S(1)} %copy-done, ...), custom_call_target="tpu_custom_call" | custom-call | flops 70000000 | tf_op jit(solution)/shard_map/states/pallas_call | solution.py:1094
  130.4 3.0 convolution_convert_fusion.5
  134.6 56.8 %branch.1 = (bf16[160,2048]{1,0:T(8,128)(2,1)}, bf16[160,2048]{1,0:T(8,128)(2,1)}, f32[3,160,128]{2,1,0:T(8,128)}, bf16[8,176,2048]{2,1,0:T(8,128)(2,1)}, bf16[1...) custom-call(bf16[4,160,2048]{2,1,0:T(8,128)(2,1)} %bitcast.122, f32[4,160,128]{2,1,0:T(8,128)} %bitcast.114, ...), custom_call_target="tpu_custom_call" | custom-call | flops 400000000 | tf_op jit(solution)/shard_map/branch/pallas_call | solution.py:258
  196.6 53.6 %ffn_in.1 = (bf16[4,160,2048]{2,1,0:T(8,128)(2,1)}, bf16[8,176,2048]{2,1,0:T(8,128)(2,1)}, bf16[8,176,2048]{2,1,0:T(8,128)(2,1)}, bf16[4,160,2048]{2,1,0:T(8,128)(2,1)}) custom-call(bf16[160,2048]{1,0:T(8,128)(2,1)} %multiply_convert_fusion.5.own, bf16[176,2048]{1,0:T(8,128)(2,1)} %copy-done.26, bf16[176,2048]{1,0:T(8,128)(2,1)} %convert_element_type.199.down, ...), custom_call_target="tpu_custom_call" | custom-call | flops 400000000 | tf_op jit(solution)/shard_map/ffn_in/pallas_call | solution.py:258
  250.3 9.6 %fusion.36 = f32[640,1408]{1,0:T(8,128)} fusion(bf16[640,2048]{1,0:T(8,128)(2,1)} %bitcast.167, bf16[1408,2048]{1,0:T(8,128)(2,1)} %bitcast.151), kind=kOutput, calls=%fused_computation.147 | convolution fusion | flops 3690987520 | bytes 11993088 | tf_op jit(solution)/shard_map/dot_general | solution.py:20
  259.9 8.8 %fusion.37 = f32[640,1408]{1,0:T(8,128)} fusion(bf16[640,2048]{1,0:T(8,128)(2,1)S(1)} %bitcast.163, bf16[1408,2048]{1,0:T(8,128)(2,1)} %bitcast.147), kind=kOutput, calls=%fused_computation.148 | convolution fusion | flops 3690987520 | bytes 11993088 | tf_op jit(solution)/shard_map/dot_general | solution.py:20
  268.8 9.5 %multiply_convert_fusion.2 = (bf16[640,1408]{1,0:T(8,128)(2,1)}, bf16[640,1408]{1,0:T(8,128)(2,1)}, bf16[640,1408]{1,0:T(8,128)(2,1)}) fusion(f32[640,1408]{1,0:T(8,128)} %fusion.37, f32[640,1408]{1,0:T(8,128)} %fusion.36, bf16[640,2048]{1,0:T(8,128)(2,1)S(1)} %bitcast.164, bf16[1408,2048]{1,0:T(8,128)(2,1)S(1)} %bitcast.157), kind=kOutput, calls=%fused_computation.9 | convolution fusion | flops 3704504320 | bytes 21004288 | tf_op jit(solution)/shard_map/dot_general | solution.py:20
  278.3 5.9 %fusion.38 = f32[640,2048]{1,0:T(8,128)S(1)} fusion(bf16[640,1408]{1,0:T(8,128)(2,1)} %get-tuple-element.116, bf16[1408,2048]{1,0:T(8,128)(2,1)S(1)} %bitcast.158), kind=kOutput, calls=%fused_computation.149 | convolution fusion | flops 3690987520 | bytes 12812288 | tf_op jit(solution)/shard_map/dot_general | solution.py:1188
  284.2 4.4 add_convert_fusion
  292.5 6.6 %convolution_convert_fusion = bf16[1408,2048]{1,0:T(8,128)(2,1)} fusion(bf16[640,1408]{1,0:T(8,128)(2,1)S(1)} %copy-done.65, bf16[640,2048]{1,0:T(8,128)(2,1)S(1)} %bitcast.168), kind=kOutput, calls=%fused_computation | convolution fusion | flops 3693871104 | bytes 10190848 | tf_op jit(solution)/shard_map/dot_general | solution.py:26
  299.1 6.5 %convolution_convert_fusion.1 = bf16[1408,2048]{1,0:T(8,128)(2,1)} fusion(bf16[640,1408]{1,0:T(8,128)(2,1)S(1)} %copy-done.62, bf16[640,2048]{1,0:T(8,128)(2,1)S(1)} %bitcast.165), kind=kOutput, calls=%fused_computation.1 | convolution fusion | flops 3693871104 | bytes 10190848 | tf_op jit(solution)/shard_map/dot_general | solution.py:26
  305.7 6.7 %convolution_convert_fusion.2 = bf16[1408,2048]{1,0:T(8,128)(2,1)} fusion(bf16[640,1408]{1,0:T(8,128)(2,1)S(1)} %copy-done.64, bf16[640,2048]{1,0:T(8,128)(2,1)S(1)} %bitcast.166), kind=kOutput, calls=%fused_computation.2 | convolution fusion | flops 3693871104 | bytes 10190848 | tf_op jit(solution)/shard_map/dot_general | solution.py:26
  312.4 5.6 convolution_convert_fusion.4
  318.0 3.4 collective-permute-done.7
  327.9 27.5 %grad_in.1 = (bf16[4,160,2048]{2,1,0:T(8,128)(2,1)}, f32[4,160,128]{2,1,0:T(8,128)}, bf16[2,176,2048]{2,1,0:T(8,128)(2,1)}, bf16[2,176,2048]{2,1,0:T(8,128)(2,1)...) custom-call(bf16[160,2048]{1,0:T(8,128)(2,1)} %copy-done.28, ...), custom_call_target="tpu_custom_call" | custom-call | flops 270000000 | tf_op jit(solution)/shard_map/grad_in/pallas_call | solution.py:258
  355.6 5.1 fusion.39.grad_mid
  360.7 7.2 %back_gates.1 = (f32[2,640,128]{2,1,0:T(8,128)S(1)}, f32[2,640,128]{2,1,0:T(8,128)S(1)}, bf16[640,512]{1,0:T(8,128)(2,1)S(1)}, bf16[640,512]{1,0:T(8,128)(2,1)S(...) custom-call(f32[640,512]{1,0:T(8,128)} %fusion.39.grad_mid, f32[2,640,128]{2,1,0:T(8,128)S(1)} %copy-done.11, ...), custom_call_target="tpu_custom_call" | custom-call | flops 70000000 | tf_op jit(solution)/shard_map/back_gates/pallas_call | solution.py:1248
  371.3 3.7 convolution_convert_fusion.8
  376.6 16.0 %shard_map.264.back = f32[32,8,256]{2,1,0:T(8,128)} custom-call(f32[4,8,256]{2,1,0:T(8,128)} %copy-done.18), custom_call_target="tpu_custom_call" | custom-call | flops 100000000 | tf_op jit(solution)/shard_map/pallas_call | solution.py:118
  396.2 8.5 %adjoints.1 = (bf16[640,1280]{1,0:T(8,128)(2,1)}, f32[8,256]{1,0:T(8,128)S(1)}, f32[8,256]{1,0:T(8,128)S(1)}) custom-call(s32[36]{0:T(128)S(1)} %pad_add_fusion.1.ints, f32[32,8,256]{2,1,0:T(8,128)S(1)} %copy-done, f32[32,8,256]{2,1,0:T(8,128)S(1)} %copy-done.16, f32[2,640,128]{2,1,0:T(8,128)S(1)} %copy-done.4, f32[2,640,128]{2,1,0:T(8,128)S(1)} %copy-done.6, ...), custom_call_target="tpu_custom_call" | custom-call | flops 70000000 | tf_op jit(solution)/shard_map/adjoints/pallas_call | solution.py:1258
  405.4 9.7 %multiply_reduce_fusion = (f32[2048]{0:T(1024)S(1)}, bf16[640,2048]{1,0:T(8,128)(2,1)}, bf16[640,2048]{1,0:T(8,128)(2,1)}) fusion(bf16[4,160,2048]{2,1,0:T(8,128)(2,1)} %get-tuple-element.84, f32[640]{0:T(1024)S(1)} %rsqrt.40, f32[2048]{0:T(1024)S(1)} %mul.322, bf16[640,1280]{1,0:T(8,128)(2,1)} %get-tuple-element.131, bf16[1280,2048]{1,0:T(8,128)(2,1)} %bitcast.159), kind=kOutput, calls=%fused_computation.4 | convolution fusion | flops 3365926912 | bytes 14764544 | tf_op jit(solution)/shard_map/dot_general | solution.py:1266
  416.2 4.0 convolution_convert_fusion.9
  420.2 4.4 convolution_convert_fusion.6
  424.6 5.3 collective-permute-done.10
  432.7 5.0 collective-permute-done.9.refs_6_
  437.7 3.2 convolution_convert_fusion.7
  440.9 124.8 %reduce.6 = (f32[176,2048]{1,0:T(8,128)}, f32[32,2048]{1,0:T(8,128)}, f32[4,64,512]{2,1,0:T(8,128)}, f32[176,2048]{1,0:T(8,128)}, f32[64,2048]{1,0:T(8,128)}, /*...) custom-call(bf16[2,176,2048]{2,1,0:T(8,128)(2,1)} %get-tuple-element, ...), custom_call_target="tpu_custom_call" | custom-call | flops 1200000000 | tf_op jit(solution)/shard_map/reduce/pallas_call | solution.py:258
  (261 shorter events, 71.8 us)
Async XLA Ops:
  78.4 22.8 %collective-permute-start = (bf16[80,2048]{1,0:T(8,128)(2,1)S(1)}, bf16[80,2048]{1,0:T(8,128)(2,1)S(1)}, u32[]{:S(2)}, u32[]{:S(2)}) collective-permute-start(bf16[80,2048]{1,0:T(8,128)(2,1)S(1)} %slice.131), channel_id=1, source_target_pairs={{0,16},{1,17},{2,18},{3,19},{4,20},{5,21},{6,22},{7,23},{8,24},{9,... | collective-permute-start | bytes 983048 | tf_op jit(solution)/shard_map/ppermute | solution.py:71
  101.2 12.3 %copy-start.49 = (bf16[80,2048]{1,0:T(8,128)(2,1)}, bf16[80,2048]{1,0:T(8,128)(2,1)S(1)}, u32[]{:S(2)}) copy-start(bf16[80,2048]{1,0:T(8,128)(2,1)S(1)} %collective-permute-done.rest_1_) | copy-start | bytes 983044
  113.4 20.5 %collective-permute-start.1 = (bf16[96,2048]{1,0:T(8,128)(2,1)S(1)}, bf16[96,2048]{1,0:T(8,128)(2,1)S(1)}, u32[]{:S(2)}, u32[]{:S(2)}) collective-permute-start(bf16[96,2048]{1,0:T(8,128)(2,1)S(1)} %slice.133), channel_id=1, source_target_pairs={{0,16},{1,17},{2,18},{3,19},{4,20},{5,21},{6,22},{7,23},{8,24},{9,... | collective-permute-start | bytes 1179656 | tf_op jit(solution)/shard_map/ppermute | solution.py:71
  117.8 78.8 %collective-permute-start.2 = (bf16[160,2048]{1,0:T(8,128)(2,1)}, bf16[160,2048]{1,0:T(8,128)(2,1)}, u32[]{:S(2)}, u32[]{:S(2)}) collective-permute-start(bf16[160,2048]{1,0:T(8,128)(2,1)} %rest_2_), channel_id=1, source_target_pairs={{0,2},{1,3},{2,0},{3,1},{4,6},{5,7},{6,4},{7,5},{8,10},{9,11},{10,... | collective-permute-start | bytes 1966088 | tf_op jit(solution)/shard_map/ppermute | solution.py:71
  118.1 78.6 %collective-permute-start.3 = (bf16[160,2048]{1,0:T(8,128)(2,1)}, bf16[160,2048]{1,0:T(8,128)(2,1)}, u32[]{:S(2)}, u32[]{:S(2)}) collective-permute-start(bf16[160,2048]{1,0:T(8,128)(2,1)} %rest_2_), channel_id=1, source_target_pairs={{0,8},{1,9},{2,10},{3,11},{4,12},{5,13},{6,14},{7,15},{8,0},{9,1},... | collective-permute-start | bytes 1966088 | tf_op jit(solution)/shard_map/ppermute | solution.py:71
  120.7 75.9 %collective-permute-start.4 = (bf16[160,2048]{1,0:T(8,128)(2,1)}, bf16[160,2048]{1,0:T(8,128)(2,1)}, u32[]{:S(2)}, u32[]{:S(2)}) collective-permute-start(bf16[160,2048]{1,0:T(8,128)(2,1)} %rest_2_), channel_id=1, source_target_pairs={{0,10},{1,11},{2,8},{3,9},{4,14},{5,15},{6,12},{7,13},{8,2},{9,3},... | collective-permute-start | bytes 1966088 | tf_op jit(solution)/shard_map/ppermute | solution.py:71
  122.7 7.7 %copy-start.34 = (bf16[2,2,2,2,2,64,512]{6,5,2,4,1,3,0:T(8,128)(2,1)S(1)}, bf16[2,2,2,2,2,64,512]{6,5,2,4,1,3,0:T(8,128)(2,1)}, u32[]{:S(2)}) copy-start(bf16[2,2,2,2,2,64,512]{6,5,2,4,1,3,0:T(8,128)(2,1)} %copy.49) | copy-start | bytes 6291460
  134.6 57.9 %copy-start.24 = (bf16[160,2048]{1,0:T(8,128)(2,1)S(1)}, bf16[160,2048]{1,0:T(8,128)(2,1)}, u32[]{:S(2)}) copy-start(bf16[160,2048]{1,0:T(8,128)(2,1)} %tok.1) | copy-start | bytes 1966084
  250.3 9.7 %copy-start.58 = (bf16[4,160,2048]{2,1,0:T(8,128)(2,1)S(1)}, bf16[4,160,2048]{2,1,0:T(8,128)(2,1)}, u32[]{:S(2)}) copy-start(bf16[4,160,2048]{2,1,0:T(8,128)(2,1)} %get-tuple-element.109) | copy-start | bytes 7864324
  250.3 18.5 %slice-start.4 = ((s8[5767168]{0:T(1024)(128)(4,1)}), s8[4194304]{0:T(1024)(128)(4,1)S(1)}, s32[]{:S(2)}) async-start(s8[5767168]{0:T(1024)(128)(4,1)} %bitcast.155), calls=%async_computation.4 | async-start | bytes 8388608
  259.9 8.8 %slice-start.5 = ((s8[5767168]{0:T(1024)(128)(4,1)}), s8[1572864]{0:T(1024)(128)(4,1)S(1)}, s32[]{:S(2)}) async-start(s8[5767168]{0:T(1024)(128)(4,1)} %bitcast.155), calls=%async_computation.5 | async-start | bytes 3145728
  259.9 24.3 %slice-start = ((s8[5767168]{0:T(1024)(128)(4,1)}), s8[4194304]{0:T(1024)(128)(4,1)S(1)}, s32[]{:S(2)}) async-start(s8[5767168]{0:T(1024)(128)(4,1)} %bitcast.148), calls=%async_computation | async-start | bytes 8388608
  268.8 15.4 %slice-start.1 = ((s8[5767168]{0:T(1024)(128)(4,1)}), s8[1572864]{0:T(1024)(128)(4,1)S(1)}, s32[]{:S(2)}) async-start(s8[5767168]{0:T(1024)(128)(4,1)} %bitcast.148), calls=%async_computation.1 | async-start | bytes 3145728
  278.3 6.0 %copy-start.63 = (bf16[640,1408]{1,0:T(8,128)(2,1)S(1)}, bf16[640,1408]{1,0:T(8,128)(2,1)}, u32[]{:S(2)}) copy-start(bf16[640,1408]{1,0:T(8,128)(2,1)} %get-tuple-element.115) | copy-start | bytes 5406724
  284.2 8.3 %copy-start.65 = (bf16[640,1408]{1,0:T(8,128)(2,1)S(1)}, bf16[640,1408]{1,0:T(8,128)(2,1)}, u32[]{:S(2)}) copy-start(bf16[640,1408]{1,0:T(8,128)(2,1)} %get-tuple-element.113) | copy-start | bytes 5406724
  288.9 23.5 %collective-permute-start.5 = (bf16[160,2048]{1,0:T(8,128)(2,1)S(1)}, bf16[160,2048]{1,0:T(8,128)(2,1)S(1)}, u32[]{:S(2)}, u32[]{:S(2)}) collective-permute-start(bf16[160,2048]{1,0:T(8,128)(2,1)S(1)} %get-tuple-element.169), channel_id=1, source_target_pairs={{0,2},{1,3},{2,0},{3,1},{4,6},{5,7},{6,4},{7,5},{8,10},{9,11},{10,... | collective-permute-start | bytes 1966088 | tf_op jit(solution)/shard_map/ppermute | solution.py:71
  291.3 26.7 %collective-permute-start.6 = (bf16[160,2048]{1,0:T(8,128)(2,1)S(1)}, bf16[160,2048]{1,0:T(8,128)(2,1)S(1)}, u32[]{:S(2)}, u32[]{:S(2)}) collective-permute-start(bf16[160,2048]{1,0:T(8,128)(2,1)S(1)} %get-tuple-element.171), channel_id=1, source_target_pairs={{0,8},{1,9},{2,10},{3,11},{4,12},{5,13},{6,14},{7,15},{8,0},{9,1},... | collective-permute-start | bytes 1966088 | tf_op jit(solution)/shard_map/ppermute | solution.py:71
  291.3 30.1 %collective-permute-start.7 = (bf16[160,2048]{1,0:T(8,128)(2,1)S(1)}, bf16[160,2048]{1,0:T(8,128)(2,1)S(1)}, u32[]{:S(2)}, u32[]{:S(2)}) collective-permute-start(bf16[160,2048]{1,0:T(8,128)(2,1)S(1)} %get-tuple-element.170), channel_id=1, source_target_pairs={{0,10},{1,11},{2,8},{3,9},{4,14},{5,15},{6,12},{7,13},{8,2},{9,3},... | collective-permute-start | bytes 1966088 | tf_op jit(solution)/shard_map/ppermute | solution.py:71
  292.5 6.6 %copy-start.62 = (bf16[640,1408]{1,0:T(8,128)(2,1)S(1)}, bf16[640,1408]{1,0:T(8,128)(2,1)}, u32[]{:S(2)}) copy-start(bf16[640,1408]{1,0:T(8,128)(2,1)} %get-tuple-element.116) | copy-start | bytes 5406724
  299.1 6.5 %copy-start.64 = (bf16[640,1408]{1,0:T(8,128)(2,1)S(1)}, bf16[640,1408]{1,0:T(8,128)(2,1)}, u32[]{:S(2)}) copy-start(bf16[640,1408]{1,0:T(8,128)(2,1)} %get-tuple-element.115) | copy-start | bytes 5406724
  299.1 13.3 %slice-start.2 = ((s8[5767168]{0:T(1024)(128)(4,1)}), s8[4194304]{0:T(1024)(128)(4,1)S(1)}, s32[]{:S(2)}) async-start(s8[5767168]{0:T(1024)(128)(4,1)} %bitcast.152), calls=%async_computation.2 | async-start | bytes 8388608
  305.7 6.8 %slice-start.3 = ((s8[5767168]{0:T(1024)(128)(4,1)}), s8[1572864]{0:T(1024)(128)(4,1)S(1)}, s32[]{:S(2)}) async-start(s8[5767168]{0:T(1024)(128)(4,1)} %bitcast.152), calls=%async_computation.3 | async-start | bytes 3145728
  312.4 9.0 %copy-start.21 = (f32[160,2048]{1,0:T(8,128)S(1)}, f32[160,2048]{1,0:T(8,128)}, u32[]{:S(2)}) copy-start(f32[160,2048]{1,0:T(8,128)} %copy-done.20) | copy-start | bytes 3932164
  355.3 37.3 %collective-permute-start.8 = (bf16[352,2048]{1,0:T(8,128)(2,1)}, bf16[352,2048]{1,0:T(8,128)(2,1)}, u32[]{:S(2)}, u32[]{:S(2)}) collective-permute-start(bf16[352,2048]{1,0:T(8,128)(2,1)} %bitcast.169), channel_id=1, source_target_pairs={{0,4},{1,5},{2,6},{3,7},{4,0},{5,1},{6,2},{7,3},{8,12},{9,13},{10,... | collective-permute-start | bytes 4325384 | tf_op jit(solution)/shard_map/ppermute | solution.py:71
  355.6 5.1 copy-start.13
  355.6 5.1 copy-start.15
  395.2 34.7 %collective-permute-start.10 = (bf16[176,2048]{1,0:T(8,128)(2,1)}, bf16[176,2048]{1,0:T(8,128)(2,1)}, u32[]{:S(2)}, u32[]{:S(2)}) collective-permute-start(bf16[176,2048]{1,0:T(8,128)(2,1)} %fusion.2), channel_id=1, source_target_pairs={{0,16},{1,17},{2,18},{3,19},{4,20},{5,21},{6,22},{7,23},{8,24},{9,... | collective-permute-start | bytes 2162696 | tf_op jit(solution)/shard_map/ppermute | solution.py:71
  404.6 33.1 %collective-permute-start.9 = (bf16[2,176,2048]{2,1,0:T(8,128)(2,1)}, bf16[2,176,2048]{2,1,0:T(8,128)(2,1)S(1)}, u32[]{:S(2)}, u32[]{:S(2)}) collective-permute-start(bf16[2,176,2048]{2,1,0:T(8,128)(2,1)} %get-tuple-element.135), channel_id=1, source_target_pairs={{0,4},{1,5},{2,6},{3,7},{4,0},{5,1},{6,2},{7,3},{8,12},{9,13},{10,... | collective-permute-start | bytes 4325384 | tf_op jit(solution)/shard_map/ppermute | solution.py:71
  420.2 9.8 %copy-start.35 = (bf16[2,176,2048]{2,1,0:T(8,128)(2,1)S(1)}, bf16[2,176,2048]{2,1,0:T(8,128)(2,1)}, u32[]{:S(2)}) copy-start(bf16[2,176,2048]{2,1,0:T(8,128)(2,1)} %get-tuple-element.123) | copy-start | bytes 4325380
  565.7 7.2 %copy-start.25 = (bf16[160,2048]{1,0:T(8,128)(2,1)S(1)}, bf16[160,2048]{1,0:T(8,128)(2,1)}, u32[]{:S(2)}) copy-start(bf16[160,2048]{1,0:T(8,128)(2,1)} %tok.1) | copy-start | bytes 1966084
  565.8 7.2 %copy-start.32 = (bf16[160,2048]{1,0:T(8,128)(2,1)S(1)}, bf16[160,2048]{1,0:T(8,128)(2,1)}, u32[]{:S(2)}) copy-start(bf16[160,2048]{1,0:T(8,128)(2,1)} %get-tuple-element.145) | copy-start | bytes 1966084
  565.8 7.2 %copy-start.33 = (bf16[160,2048]{1,0:T(8,128)(2,1)S(1)}, bf16[160,2048]{1,0:T(8,128)(2,1)}, u32[]{:S(2)}) copy-start(bf16[160,2048]{1,0:T(8,128)(2,1)} %get-tuple-element.146) | copy-start | bytes 1966084
  (51 other events, 135.0 us)

commit v6 on v5

--- a/solution.py
+++ b/solution.py
@@ -333,10 +333,12 @@
 
 
 def start_kernel(
-    lay, units, tok, w_in, w_gate, w_forget, w_out, f_gate, pack,
-    tok_all, mix_all, forget_own, out_own, out_all, f_gate_z, every, *rest,
+    lay, units, cuts, tok, w_in, w_gate, w_forget, w_out, pack, wide_0, wide_1, wide_2,
+    tok_all, mix_all, forget_own, out_own, out_all, f_gate_z, every, low_0, low_1, low_2, up_a, *rest,
 ):
     n, W = lay.n, lay.n // 4
+    gate_b, rest = rest[: len(cuts) - 1], rest[len(cuts) - 1 :]
+    wide_rooms, low_rooms, rest = rest[:3], rest[3:6], rest[6:]
     *rooms, send_sems, recv_sems, local_sems = rest
     net = Net(lay, list(range(1, n)), send_sems, recv_sems, local_sems, rooms)
     me = net.me
@@ -349,15 +351,22 @@
     g_forget = WeightGather(
         net, forget_own, lambda d, m: mix_all.at[pl.ds(2 * W * units + f_slot(lay, d), 1)]
     )
-    g_out = WeightGather(net, out_own, lambda d, m: out_all.at[w_slot(lay, d)])
+
+    def out_place(d, m):
+        zhi, _, y, _, c = lay.parts(d)
+        return out_all.at[zhi, :, y, :, c]
+
+    g_out = WeightGather(net, out_own, out_place)
     turn = Turn(net, forget_to(lay, me), w_forget, forget_own)
     g_in.start()
     g_gate.start()
-    mine = t_slot(lay, me)
+    def square(d):
+        _, zlo, _, x, _ = lay.parts(d)
+        return zlo, x
+
+    mine = square(me)
     own = net.load(w_out.at[mine], out_own.at[mine])
-    out_in = [
-        net.put(w_out.at[t_slot(lay, lay.flip(me, m))], out_own.at[mine], m) for m in lay.tmasks[1:]
-    ]
+    out_in = [net.put(w_out.at[square(lay.flip(me, m))], out_own.at[mine], m) for m in lay.tmasks[1:]]
     first = token_start(net, tok, tok_all)
     all_in = [net.put(pack, every.at[me], m) for m in range(1, n)]
     net.keep(pack, every.at[me])
@@ -366,8 +375,18 @@
     own.wait()
     arrived(out_in)
     g_out.start()
-    gate_in = net.put(f_gate.at[pl.ds(0, f_gate_z.shape[0])], f_gate_z, lay.ZH)
     net.settle()
+    wide = [net.load(w, room) for w, room in zip((wide_0, wide_1, wide_2), wide_rooms)]
+    for copy, src, room, low in zip(wide, wide_rooms, low_rooms, (low_0, low_1, low_2)):
+        copy.wait()
+        cast_rows(room, src)
+        if low is low_0:
+            gate_in = net.put(room.at[pl.ds(*cuts[0])], f_gate_z, lay.ZH)
+            for cut, out in zip(cuts[1:], gate_b):
+                net.keep(room.at[pl.ds(*cut)], out)
+        if low is low_1:
+            net.keep(room.at[pl.ds(*cuts[0])], up_a)
+        net.keep(room, low)
     for mask in g_in.masks():
         g_in.forward(mask)
         g_gate.forward(mask)
@@ -559,11 +578,23 @@
 def row_cuts(name, rows):
     if name not in ("up", "down") or rows % 16 or rows < 128:
         return [(0, rows)]
-    first = -(-rows // 32) * 16
+    first = rows // 32 * 16
     return [(0, first), (first, rows - first)]
 
 
 PARTS = ("up", "forget", "out", "down", "gate", "in")
+
+
+def cast_rows(out, src):
+    rows = src.shape[0]
+    tile = 16 if rows % 16 == 0 else rows
+
+    def body(i, _):
+        at = pl.ds(pl.multiple_of(i * tile, tile), tile)
+        out[at, :] = src[at, :].astype(out.dtype)
+        return 0
+
+    lax.fori_loop(0, rows // tile, body, 0)
 
 
 class TokenReduce:
@@ -663,24 +694,27 @@
             net.keep(total, out)
 
     depth = len(lay.rbits)
-    for tick in range(len(jobs) + depth - 1):
-        for k in range(depth):
+    for tick in range(len(jobs) + depth):
+        for k in range(depth + 1):
             i = tick - k
-            if not 0 <= i < len(jobs) or k + jobs[i].first >= depth:
+            if not 0 <= i < len(jobs):
                 continue
             job = jobs[i]
-            job.wait(k)
-            job.add(k, True)
-            flow = k + 1 + job.first
-            if flow == depth:
+            last = depth - 1 - job.first
+            if k < last:
+                job.wait(k)
+                job.add(k, True)
+                flow = k + 1 + job.first
+                if len(flows[flow]) >= LAG:
+                    behind = flows[flow][-LAG]
+                    behind.wait(flow - behind.first)
+                job.send(k + 1)
+                flows[flow].append(job)
+                job.add(k, False)
+            elif k == last + 1:
+                job.wait(last)
+                job.add(last, True)
                 finish(i)
-                continue
-            if len(flows[flow]) >= LAG:
-                behind = flows[flow][-LAG]
-                behind.wait(flow - behind.first)
-            job.send(k + 1)
-            flows[flow].append(job)
-            job.add(k, False)
         if tick == 0:
             for job in late:
                 job.start()
@@ -1009,13 +1043,12 @@
     pack_rows = -(-packed.shape[0] // 128)
     packed = jnp.pad(packed, (0, 8 * 128 - packed.shape[0])).reshape(8, 128)
     out_cols = out_proj.astype(LOW).reshape(r_in, 2, 2, Y, 2, 2 * r_in)
-    out_cols = out_cols.transpose(2, 4, 0, 1, 3, 5).reshape(4, r_in, 2 * half)
+    out_cols = out_cols.transpose(2, 4, 0, 1, 3, 5).reshape(2, 2, r_in, 2 * half)
     units = r_in // r_f
     r_ffn = ffn_gate.shape[0]
     cuts = row_cuts("up", r_ffn)
-    f_gate = ffn_gate.astype(LOW)
-    tok_all, w_mix, _, _, w_out, gate_za, every = net_call(
-        partial(start_kernel, lay, units),
+    tok_all, w_mix, _, _, w_out, gate_za, every, f_gate, f_up, f_down, up_a, *gate_b = net_call(
+        partial(start_kernel, lay, units, cuts),
         lay,
         (
             tokens,
@@ -1023,38 +1056,44 @@
             gate_proj.astype(LOW).reshape(units, r_f, width),
             forget_proj.astype(LOW).reshape(1, r_f, width),
             out_cols,
-            f_gate,
             packed,
+            ffn_gate,
+            ffn_up,
+            ffn_down,
         ),
         [
             ((4, length, width), LOW),
             ((W * (2 * units + 1), r_f, width), LOW),
             ((1, r_f, width), LOW),
-            ((4, r_in, 2 * half), LOW),
-            ((W, 4, r_in, 2 * half), LOW),
+            ((2, 2, r_in, 2 * half), LOW),
+            ((2, 2, Y, 2, 2, r_in, 2 * half), LOW),
             ((cuts[0][1], width), LOW),
             ((n, 8, 128), F32),
+            *[((r_ffn, width), LOW)] * 3,
+            *[((rows, width), LOW) for _, rows in cuts],
         ],
         4 * (W - 1) + 9 + n - 1,
-        24,
+        32,
         0,
         "start",
         60,
         [
+            *[pltpu.VMEM((r_ffn, width), F32)] * 3,
+            *[pltpu.VMEM((r_ffn, width), LOW)] * 3,
             pltpu.VMEM((units, r_f, width), LOW),
             pltpu.VMEM((units, r_f, width), LOW),
             pltpu.VMEM((length, width), LOW),
             pltpu.VMEM((1, r_f, width), LOW),
-            pltpu.VMEM((4, r_in, 2 * half), LOW),
+            pltpu.VMEM((2, 2, r_in, 2 * half), LOW),
         ],
     )
-    f_up, f_down = ffn_up.astype(LOW), ffn_down.astype(LOW)
+    cot_own = tie(cotangent, tok_all)
+    cot_x, cot_z = lay.send(cot_own, lay.X), lay.send(cot_own, lay.ZL)
     gate_z = [gate_za]
     if len(cuts) > 1:
-        gate_z.append(lay.send(tie(ffn_gate[cuts[1][0] :].astype(LOW), tok_all), lay.ZH))
+        gate_z.append(lay.send(gate_b[0], lay.ZH))
     tok_all = tok_all.reshape(total, width)
     w_mix = w_mix.reshape(5 * half, width)
-    w_out = w_out.reshape(2, Y, 2, 2, 2, r_in, 2 * half).transpose(0, 3, 1, 4, 2, 5, 6)
     w_out = w_out.reshape(width, 2 * half)
     every = every[:, :pack_rows, :].reshape(n, pack_rows * 128)
     g_mix = every[:, 0:r_in].reshape(1, width)
@@ -1087,10 +1126,10 @@
         3,
         name="gates",
     )(proj, keep, par)
-    summ = tie(summ, gate_z[-1])
+    summ = tie(summ, gate_z[-1], cot_x, cot_z)
     summ_all = small_gather(lay, summ, lay.wmasks, partial(w_slot, lay), W, 1)
-    cot_blocks = lay.gather_t(tie(cotangent, summ_all))
-    up_z = [lay.send(tie(ffn_up[: cuts[0][1]].astype(LOW), summ_all), lay.ZH)]
+    cot_blocks = [cotangent, cot_x, cot_z, lay.send(tie(cot_z, summ_all), lay.X)]
+    up_z = [lay.send(tie(up_a, summ_all), lay.ZH)]
     st_re, st_im, be_re, be_im, unit, squares = plain_call(
         partial(state_kernel, half, length, n),
         [wide] * 4 + [((total, 2 * half), LOW), ((total, LANES), F32)],
@@ -1298,7 +1337,7 @@
         "out": grad_w_out.reshape(split + (4 * r_in, 2 * half)),
         "up": up_kept,
         "down": down_kept,
-        "gate": outer_rows(tie(gate_low, up_came), normed).astype(LOW).reshape(split + (r_in, width)),
+        "gate": outer_rows(gate_low, normed).astype(LOW).reshape(split + (r_in, width)),
         "in": outer_rows(grads[:, : 2 * half], normed).astype(LOW).reshape(split + (r_in, width)),
     }
     out_of = {name: (part.shape[-2:], F32) for name, part in part_of.items()}

time: 592 us -> 580 us (0.980)
  Pallas kernels: 392 us -> 381 us
    pallas_call x5, Pallas kernels: 335 us -> 326 us  [net_call(): pl.pallas_call(body, out_shape=tuple((jax.ShapeDtypeStruct(s, d) for s, d...]
    unnamed x152 -> x150, local copies, waits for them, and re-layouts: 16.2 us -> 17.8 us
  transfers between devices with their start and end apart: 11 -> 11, of which waited for: 4 -> 6; matrix products, arithmetic and copies ran while one was open for 14% -> 14% of each run, Pallas kernels for 17% -> 16%
where the time goes in v6:
time: 580 us; the launch traced here: 572 us
  Pallas kernels  381 us (66%)
  matrix products  102 us (18%)
  local copies, waits for them, and re-layouts  30.9 us (5%)
  other arithmetic  30.1 us (5%)
  waiting for transfers between devices  16.3 us (3%)
  starting transfers between devices  10.4 us (2%)
    pallas_call x5, Pallas kernels, net_call(): pl.pallas_call(body, out_shape=tuple((jax.ShapeDtypeStruct(s, d) for s, d...  326 us
    dot_general x5, matrix products, contract(): lax.dot_general(left_rows, right_rows, (((1,), (1,)), ((), ())), preferre...  36.2 us
    dot_general x7, matrix products, outer_rows(): lax.dot_general(left_rows, right_rows, (((0,), (0,)), ((), ())), preferre...  35.2 us
    pallas_call x2, Pallas kernels, small_gather(): pl.pallas_call(partial(gather_kernel, lay, masks, slot_of), out_shape=jax...  26.6 us
    unnamed x150, local copies, waits for them, and re-layouts  17.8 us
    ppermute x11, waiting for transfers between devices, send(): return lax.ppermute(value, 'dp', [(i, i ^ mask) for i in range(self.n)])  16.3 us
  transfers between devices with their start and end apart: 11, of which 6 were waited for; matrix products, arithmetic and copies ran while one was open for 14% of the time, Pallas kernels for 16%

profile of v6, /device:TPU:1, one launch (start us, length us, event | category | flops | bytes accessed | tf_op | source)
XLA Modules:
  0.0 572.4 jit_solution(836500621998262480)
XLA Ops:
  5.9 70.7 %start.1 = (bf16[4,160,2048]{2,1,0:T(8,128)(2,1)}, bf16[40,32,2048]{2,1,0:T(8,128)(2,1)}, bf16[1,32,2048]{2,1,0:T(8,128)(2,1)}, bf16[2,2,64,512]{3,2,1,0:T(8,128...) custom-call(bf16[160,2048]{1,0:T(8,128)(2,1)} %tok.1, ...), custom_call_target="tpu_custom_call" | custom-call | flops 600000000 | tf_op jit(solution)/shard_map/start/pallas_call | solution.py:258
  86.2 5.3 fusion.35.proj
  91.6 5.2 gates.1
  101.8 12.1 %shard_map.263.summ = f32[32,8,256]{2,1,0:T(8,128)} custom-call(f32[4,8,256]{2,1,0:T(8,128)} %copy-done.19), custom_call_target="tpu_custom_call" | custom-call | flops 100000000 | tf_op jit(solution)/shard_map/pallas_call | solution.py:118
  116.0 7.5 %states.1 = (f32[2,640,128]{2,1,0:T(8,128)S(1)}, f32[2,640,128]{2,1,0:T(8,128)S(1)}, f32[2,640,128]{2,1,0:T(8,128)S(1)}, f32[2,640,128]{2,1,0:T(8,128)S(1)}, bf1...) custom-call(s32[36]{0:T(128)S(1)} %pad_add_fusion.1.ints, f32[32,8,256]{2,1,0:T(8,128)S(1)} %copy-done, ...), custom_call_target="tpu_custom_call" | custom-call | flops 70000000 | tf_op jit(solution)/shard_map/states/pallas_call | solution.py:1133
  124.0 3.0 convolution_convert_fusion.5
  127.0 4.2 collective-permute-done.3.rest_0_
  131.2 50.2 %branch.1 = (bf16[160,2048]{1,0:T(8,128)(2,1)}, bf16[160,2048]{1,0:T(8,128)(2,1)}, f32[3,160,128]{2,1,0:T(8,128)}, bf16[8,176,2048]{2,1,0:T(8,128)(2,1)}, bf16[1...) custom-call(bf16[4,160,2048]{2,1,0:T(8,128)(2,1)} %bitcast.119, f32[4,160,128]{2,1,0:T(8,128)} %bitcast.111, ...), custom_call_target="tpu_custom_call" | custom-call | flops 400000000 | tf_op jit(solution)/shard_map/branch/pallas_call | solution.py:258
  186.6 54.1 %ffn_in.1 = (bf16[4,160,2048]{2,1,0:T(8,128)(2,1)}, bf16[8,176,2048]{2,1,0:T(8,128)(2,1)}, bf16[8,176,2048]{2,1,0:T(8,128)(2,1)}, bf16[4,160,2048]{2,1,0:T(8,128)(2,1)}) custom-call(bf16[160,2048]{1,0:T(8,128)(2,1)} %multiply_convert_fusion.5.own, bf16[176,2048]{1,0:T(8,128)(2,1)} %get-tuple-element.106.up, bf16[176,2048]{1,0:T(8,128)(2,1)} %get-tuple-element.107.down, ...), custom_call_target="tpu_custom_call" | custom-call | flops 400000000 | tf_op jit(solution)/shard_map/ffn_in/pallas_call | solution.py:258
  240.7 9.6 %fusion.36 = f32[640,1408]{1,0:T(8,128)} fusion(bf16[640,2048]{1,0:T(8,128)(2,1)} %bitcast.161, bf16[1408,2048]{1,0:T(8,128)(2,1)} %bitcast.145), kind=kOutput, calls=%fused_computation.147 | convolution fusion | flops 3690987520 | bytes 11993088 | tf_op jit(solution)/shard_map/dot_general | solution.py:20
  250.4 8.8 %fusion.37 = f32[640,1408]{1,0:T(8,128)} fusion(bf16[640,2048]{1,0:T(8,128)(2,1)S(1)} %bitcast.157, bf16[1408,2048]{1,0:T(8,128)(2,1)} %bitcast.141), kind=kOutput, calls=%fused_computation.148 | convolution fusion | flops 3690987520 | bytes 11993088 | tf_op jit(solution)/shard_map/dot_general | solution.py:20
  259.2 9.5 %multiply_convert_fusion.2 = (bf16[640,1408]{1,0:T(8,128)(2,1)}, bf16[640,1408]{1,0:T(8,128)(2,1)}, bf16[640,1408]{1,0:T(8,128)(2,1)}) fusion(f32[640,1408]{1,0:T(8,128)} %fusion.37, f32[640,1408]{1,0:T(8,128)} %fusion.36, bf16[640,2048]{1,0:T(8,128)(2,1)S(1)} %bitcast.158, bf16[1408,2048]{1,0:T(8,128)(2,1)S(1)} %bitcast.151), kind=kOutput, calls=%fused_computation.9 | convolution fusion | flops 3704504320 | bytes 21004288 | tf_op jit(solution)/shard_map/dot_general | solution.py:20
  268.7 5.9 %fusion.38 = f32[640,2048]{1,0:T(8,128)S(1)} fusion(bf16[640,1408]{1,0:T(8,128)(2,1)} %get-tuple-element.125, bf16[1408,2048]{1,0:T(8,128)(2,1)S(1)} %bitcast.152), kind=kOutput, calls=%fused_computation.149 | convolution fusion | flops 3690987520 | bytes 12812288 | tf_op jit(solution)/shard_map/dot_general | solution.py:1227
  274.7 4.4 add_convert_fusion
  282.1 6.6 %convolution_convert_fusion = bf16[1408,2048]{1,0:T(8,128)(2,1)} fusion(bf16[640,1408]{1,0:T(8,128)(2,1)S(1)} %copy-done.64, bf16[640,2048]{1,0:T(8,128)(2,1)S(1)} %bitcast.162), kind=kOutput, calls=%fused_computation | convolution fusion | flops 3693871104 | bytes 10190848 | tf_op jit(solution)/shard_map/dot_general | solution.py:26
  288.7 6.5 %convolution_convert_fusion.1 = bf16[1408,2048]{1,0:T(8,128)(2,1)} fusion(bf16[640,1408]{1,0:T(8,128)(2,1)S(1)} %copy-done.61, bf16[640,2048]{1,0:T(8,128)(2,1)S(1)} %bitcast.159), kind=kOutput, calls=%fused_computation.1 | convolution fusion | flops 3693871104 | bytes 10190848 | tf_op jit(solution)/shard_map/dot_general | solution.py:26
  295.2 6.5 %convolution_convert_fusion.2 = bf16[1408,2048]{1,0:T(8,128)(2,1)} fusion(bf16[640,1408]{1,0:T(8,128)(2,1)S(1)} %copy-done.63, bf16[640,2048]{1,0:T(8,128)(2,1)S(1)} %bitcast.160), kind=kOutput, calls=%fused_computation.2 | convolution fusion | flops 3693871104 | bytes 10190848 | tf_op jit(solution)/shard_map/dot_general | solution.py:26
  301.7 5.7 %convolution_convert_fusion.4 = bf16[640,2048]{1,0:T(8,128)(2,1)} fusion(bf16[640,1408]{1,0:T(8,128)(2,1)S(1)} %copy-done.64, bf16[1408,2048]{1,0:T(8,128)(2,1)S(1)} %bitcast.148), kind=kOutput, calls=%fused_computation.15 | convolution fusion | flops 3692298240 | bytes 10190848 | tf_op jit(solution)/shard_map/dot_general | solution.py:1253
  307.5 3.1 collective-permute-done.7
  311.3 3.0 fusion.27
  317.1 26.3 %grad_in.1 = (bf16[4,160,2048]{2,1,0:T(8,128)(2,1)}, f32[4,160,128]{2,1,0:T(8,128)}, bf16[2,176,2048]{2,1,0:T(8,128)(2,1)}, bf16[2,176,2048]{2,1,0:T(8,128)(2,1)...) custom-call(bf16[160,2048]{1,0:T(8,128)(2,1)} %copy-done.29, ...), custom_call_target="tpu_custom_call" | custom-call | flops 270000000 | tf_op jit(solution)/shard_map/grad_in/pallas_call | solution.py:258
  346.0 5.1 fusion.39.grad_mid
  351.1 7.2 %back_gates.1 = (f32[2,640,128]{2,1,0:T(8,128)S(1)}, f32[2,640,128]{2,1,0:T(8,128)S(1)}, bf16[640,512]{1,0:T(8,128)(2,1)S(1)}, bf16[640,512]{1,0:T(8,128)(2,1)S(...) custom-call(f32[640,512]{1,0:T(8,128)} %fusion.39.grad_mid, f32[2,640,128]{2,1,0:T(8,128)S(1)} %copy-done.12, ...), custom_call_target="tpu_custom_call" | custom-call | flops 70000000 | tf_op jit(solution)/shard_map/back_gates/pallas_call | solution.py:1287
  361.7 3.7 convolution_convert_fusion.8
  367.0 14.5 %shard_map.264.back = f32[32,8,256]{2,1,0:T(8,128)} custom-call(f32[4,8,256]{2,1,0:T(8,128)} %copy-done.20), custom_call_target="tpu_custom_call" | custom-call | flops 100000000 | tf_op jit(solution)/shard_map/pallas_call | solution.py:118
  386.0 8.5 %adjoints.1 = (bf16[640,1280]{1,0:T(8,128)(2,1)}, f32[8,256]{1,0:T(8,128)S(1)}, f32[8,256]{1,0:T(8,128)S(1)}) custom-call(s32[36]{0:T(128)S(1)} %pad_add_fusion.1.ints, f32[32,8,256]{2,1,0:T(8,128)S(1)} %copy-done.1, f32[32,8,256]{2,1,0:T(8,128)S(1)} %copy-done.17, f32[2,640,128]{2,1,0:T(8,128)S(1)} %copy-done.5, f32[2,640,128]{2,1,0:T(8,128)S(1)} %copy-done.7, ...), custom_call_target="tpu_custom_call" | custom-call | flops 70000000 | tf_op jit(solution)/shard_map/adjoints/pallas_call | solution.py:1297
  396.1 8.9 %multiply_reduce_fusion = (f32[2048]{0:T(1024)S(1)}, bf16[640,2048]{1,0:T(8,128)(2,1)S(1)}, bf16[640,2048]{1,0:T(8,128)(2,1)}) fusion(bf16[4,160,2048]{2,1,0:T(8,128)(2,1)} %get-tuple-element.88, f32[640]{0:T(1024)S(1)} %rsqrt.40, f32[2048]{0:T(1024)S(1)} %mul.322, bf16[640,1280]{1,0:T(8,128)(2,1)} %get-tuple-element.140, bf16[1280,2048]{1,0:T(8,128)(2,1)} %bitcast.153), kind=kOutput, calls=%fused_computation.4 | convolution fusion | flops 3365926912 | bytes 14764544 | tf_op jit(solution)/shard_map/dot_general | solution.py:1305
  405.0 4.8 convolution_convert_fusion.6
  410.8 4.0 convolution_convert_fusion.9
  414.8 3.2 convolution_convert_fusion.7
  421.0 6.3 %collective-permute-done.9.refs_6_ = bf16[2,176,2048]{2,1,0:T(8,128)(2,1)S(1)} collective-permute-done((bf16[2,176,2048]{2,1,0:T(8,128)(2,1)}, bf16[2,176,2048]{2,1,0:T(8,128)(2,1)S(1)}, u32[]{:S(2)}, u32[]{:S(2)}) %collective-permute-start.9) | collective-permute-done | bytes 1441824 | tf_op jit(solution)/shard_map/ppermute | solution.py:71
  428.4 124.9 %reduce.6 = (f32[176,2048]{1,0:T(8,128)}, f32[32,2048]{1,0:T(8,128)}, f32[4,64,512]{2,1,0:T(8,128)}, f32[176,2048]{1,0:T(8,128)}, f32[64,2048]{1,0:T(8,128)}, /*...) custom-call(bf16[2,176,2048]{2,1,0:T(8,128)(2,1)} %get-tuple-element, ...), custom_call_target="tpu_custom_call" | custom-call | flops 1200000000 | tf_op jit(solution)/shard_map/reduce/pallas_call | solution.py:258
  (253 shorter events, 71.1 us)
Async XLA Ops:
  76.6 7.1 %copy-start.28 = (bf16[4,160,2048]{2,1,0:T(8,128)(2,1)S(1)}, bf16[4,160,2048]{2,1,0:T(8,128)(2,1)}, u32[]{:S(2)}) copy-start(bf16[4,160,2048]{2,1,0:T(8,128)(2,1)} %get-tuple-element.88) | copy-start | bytes 7864324
  76.6 25.2 %collective-permute-start.2 = (bf16[160,2048]{1,0:T(8,128)(2,1)}, bf16[160,2048]{1,0:T(8,128)(2,1)}, u32[]{:S(2)}, u32[]{:S(2)}) collective-permute-start(bf16[160,2048]{1,0:T(8,128)(2,1)} %rest_2_.1), channel_id=1, source_target_pairs={{0,8},{1,9},{2,10},{3,11},{4,12},{5,13},{6,14},{7,15},{8,0},{9,1},... | collective-permute-start | bytes 1966088 | tf_op jit(solution)/shard_map/ppermute | solution.py:71
  76.7 25.1 %collective-permute-start.1 = (bf16[160,2048]{1,0:T(8,128)(2,1)}, bf16[160,2048]{1,0:T(8,128)(2,1)}, u32[]{:S(2)}, u32[]{:S(2)}) collective-permute-start(bf16[160,2048]{1,0:T(8,128)(2,1)} %rest_2_.1), channel_id=1, source_target_pairs={{0,2},{1,3},{2,0},{3,1},{4,6},{5,7},{6,4},{7,5},{8,10},{9,11},{10,... | collective-permute-start | bytes 1966088 | tf_op jit(solution)/shard_map/ppermute | solution.py:71
  77.0 22.8 %collective-permute-start = (bf16[96,2048]{1,0:T(8,128)(2,1)}, bf16[96,2048]{1,0:T(8,128)(2,1)S(1)}, u32[]{:S(2)}, u32[]{:S(2)}) collective-permute-start(bf16[96,2048]{1,0:T(8,128)(2,1)} %get-tuple-element.92), channel_id=1, source_target_pairs={{0,16},{1,17},{2,18},{3,19},{4,20},{5,21},{6,22},{7,23},{8,24},{9,... | collective-permute-start | bytes 1179656 | tf_op jit(solution)/shard_map/ppermute | solution.py:71
  91.5 22.4 %copy-start.58 = (bf16[80,2048]{1,0:T(8,128)(2,1)S(1)}, bf16[80,2048]{1,0:T(8,128)(2,1)}, u32[]{:S(2)}) copy-start(bf16[80,2048]{1,0:T(8,128)(2,1)} %get-tuple-element.103) | copy-start | bytes 983044
  99.8 23.8 %copy-start.45 = (bf16[96,2048]{1,0:T(8,128)(2,1)}, bf16[96,2048]{1,0:T(8,128)(2,1)S(1)}, u32[]{:S(2)}) copy-start(bf16[96,2048]{1,0:T(8,128)(2,1)S(1)} %collective-permute-done.rest_1_) | copy-start | bytes 1179652
  113.9 17.3 %collective-permute-start.3 = (bf16[80,2048]{1,0:T(8,128)(2,1)S(1)}, bf16[80,2048]{1,0:T(8,128)(2,1)S(1)}, u32[]{:S(2)}, u32[]{:S(2)}) collective-permute-start(bf16[80,2048]{1,0:T(8,128)(2,1)S(1)} %copy-done.58), channel_id=1, source_target_pairs={{0,16},{1,17},{2,18},{3,19},{4,20},{5,21},{6,22},{7,23},{8,24},{9,... | collective-permute-start | bytes 983048 | tf_op jit(solution)/shard_map/ppermute | solution.py:71
  116.0 7.9 %copy-start.57 = (bf16[2,2,2,2,2,64,512]{6,5,4,3,2,1,0:T(8,128)(2,1)S(1)}, bf16[2,2,2,2,2,64,512]{6,5,4,3,2,1,0:T(8,128)(2,1)}, u32[]{:S(2)}) copy-start(bf16[2,2,2,2,2,64,512]{6,5,4,3,2,1,0:T(8,128)(2,1)} %get-tuple-element.101) | copy-start | bytes 6291460
  123.6 62.9 %collective-permute-start.4 = (bf16[160,2048]{1,0:T(8,128)(2,1)}, bf16[160,2048]{1,0:T(8,128)(2,1)}, u32[]{:S(2)}, u32[]{:S(2)}) collective-permute-start(bf16[160,2048]{1,0:T(8,128)(2,1)} %collective-permute-done.2.rest_4_), channel_id=1, source_target_pairs={{0,2},{1,3},{2,0},{3,1},{4,6},{5,7},{6,4},{7,5},{8,10},{9,11},{10,... | collective-permute-start | bytes 1966088 | tf_op jit(solution)/shard_map/ppermute | solution.py:71
  131.2 50.2 %copy-start.46 = (bf16[80,2048]{1,0:T(8,128)(2,1)}, bf16[80,2048]{1,0:T(8,128)(2,1)S(1)}, u32[]{:S(2)}) copy-start(bf16[80,2048]{1,0:T(8,128)(2,1)S(1)} %collective-permute-done.3.rest_0_) | copy-start | bytes 983044
  131.2 51.3 %copy-start.26 = (bf16[160,2048]{1,0:T(8,128)(2,1)S(1)}, bf16[160,2048]{1,0:T(8,128)(2,1)}, u32[]{:S(2)}) copy-start(bf16[160,2048]{1,0:T(8,128)(2,1)} %tok.1) | copy-start | bytes 1966084
  240.7 9.7 %copy-start.55 = (bf16[4,160,2048]{2,1,0:T(8,128)(2,1)S(1)}, bf16[4,160,2048]{2,1,0:T(8,128)(2,1)}, u32[]{:S(2)}) copy-start(bf16[4,160,2048]{2,1,0:T(8,128)(2,1)} %get-tuple-element.118) | copy-start | bytes 7864324
  240.7 18.5 %slice-start.4 = ((s8[5767168]{0:T(1024)(128)(4,1)}), s8[4194304]{0:T(1024)(128)(4,1)S(1)}, s32[]{:S(2)}) async-start(s8[5767168]{0:T(1024)(128)(4,1)} %bitcast.149), calls=%async_computation.4 | async-start | bytes 8388608
  250.4 8.8 %slice-start.5 = ((s8[5767168]{0:T(1024)(128)(4,1)}), s8[1572864]{0:T(1024)(128)(4,1)S(1)}, s32[]{:S(2)}) async-start(s8[5767168]{0:T(1024)(128)(4,1)} %bitcast.149), calls=%async_computation.5 | async-start | bytes 3145728
  250.4 24.3 %slice-start = ((s8[5767168]{0:T(1024)(128)(4,1)}), s8[4194304]{0:T(1024)(128)(4,1)S(1)}, s32[]{:S(2)}) async-start(s8[5767168]{0:T(1024)(128)(4,1)} %bitcast.142), calls=%async_computation | async-start | bytes 8388608
  259.2 15.4 %slice-start.1 = ((s8[5767168]{0:T(1024)(128)(4,1)}), s8[1572864]{0:T(1024)(128)(4,1)S(1)}, s32[]{:S(2)}) async-start(s8[5767168]{0:T(1024)(128)(4,1)} %bitcast.142), calls=%async_computation.1 | async-start | bytes 3145728
  274.7 7.4 %copy-start.64 = (bf16[640,1408]{1,0:T(8,128)(2,1)S(1)}, bf16[640,1408]{1,0:T(8,128)(2,1)}, u32[]{:S(2)}) copy-start(bf16[640,1408]{1,0:T(8,128)(2,1)} %get-tuple-element.122) | copy-start | bytes 5406724
  279.4 22.4 %collective-permute-start.5 = (bf16[160,2048]{1,0:T(8,128)(2,1)S(1)}, bf16[160,2048]{1,0:T(8,128)(2,1)S(1)}, u32[]{:S(2)}, u32[]{:S(2)}) collective-permute-start(bf16[160,2048]{1,0:T(8,128)(2,1)S(1)} %get-tuple-element.177), channel_id=1, source_target_pairs={{0,2},{1,3},{2,0},{3,1},{4,6},{5,7},{6,4},{7,5},{8,10},{9,11},{10,... | collective-permute-start | bytes 1966088 | tf_op jit(solution)/shard_map/ppermute | solution.py:71
  279.8 27.7 %collective-permute-start.6 = (bf16[160,2048]{1,0:T(8,128)(2,1)S(1)}, bf16[160,2048]{1,0:T(8,128)(2,1)S(1)}, u32[]{:S(2)}, u32[]{:S(2)}) collective-permute-start(bf16[160,2048]{1,0:T(8,128)(2,1)S(1)} %get-tuple-element.179), channel_id=1, source_target_pairs={{0,8},{1,9},{2,10},{3,11},{4,12},{5,13},{6,14},{7,15},{8,0},{9,1},... | collective-permute-start | bytes 1966088 | tf_op jit(solution)/shard_map/ppermute | solution.py:71
  281.1 29.5 %collective-permute-start.7 = (bf16[160,2048]{1,0:T(8,128)(2,1)S(1)}, bf16[160,2048]{1,0:T(8,128)(2,1)S(1)}, u32[]{:S(2)}, u32[]{:S(2)}) collective-permute-start(bf16[160,2048]{1,0:T(8,128)(2,1)S(1)} %get-tuple-element.178), channel_id=1, source_target_pairs={{0,10},{1,11},{2,8},{3,9},{4,14},{5,15},{6,12},{7,13},{8,2},{9,3},... | collective-permute-start | bytes 1966088 | tf_op jit(solution)/shard_map/ppermute | solution.py:71
  282.1 6.6 %copy-start.61 = (bf16[640,1408]{1,0:T(8,128)(2,1)S(1)}, bf16[640,1408]{1,0:T(8,128)(2,1)}, u32[]{:S(2)}) copy-start(bf16[640,1408]{1,0:T(8,128)(2,1)} %get-tuple-element.125) | copy-start | bytes 5406724
  288.6 6.5 %copy-start.63 = (bf16[640,1408]{1,0:T(8,128)(2,1)S(1)}, bf16[640,1408]{1,0:T(8,128)(2,1)}, u32[]{:S(2)}) copy-start(bf16[640,1408]{1,0:T(8,128)(2,1)} %get-tuple-element.124) | copy-start | bytes 5406724
  288.7 13.1 %slice-start.2 = ((s8[5767168]{0:T(1024)(128)(4,1)}), s8[4194304]{0:T(1024)(128)(4,1)S(1)}, s32[]{:S(2)}) async-start(s8[5767168]{0:T(1024)(128)(4,1)} %bitcast.146), calls=%async_computation.2 | async-start | bytes 8388608
  295.2 6.5 %slice-start.3 = ((s8[5767168]{0:T(1024)(128)(4,1)}), s8[1572864]{0:T(1024)(128)(4,1)S(1)}, s32[]{:S(2)}) async-start(s8[5767168]{0:T(1024)(128)(4,1)} %bitcast.146), calls=%async_computation.3 | async-start | bytes 3145728
  301.7 8.9 %copy-start.22 = (f32[160,2048]{1,0:T(8,128)S(1)}, f32[160,2048]{1,0:T(8,128)}, u32[]{:S(2)}) copy-start(f32[160,2048]{1,0:T(8,128)} %copy-done.21) | copy-start | bytes 3932164
  343.4 38.3 %collective-permute-start.8 = (bf16[352,2048]{1,0:T(8,128)(2,1)}, bf16[352,2048]{1,0:T(8,128)(2,1)}, u32[]{:S(2)}, u32[]{:S(2)}) collective-permute-start(bf16[352,2048]{1,0:T(8,128)(2,1)} %bitcast.165), channel_id=1, source_target_pairs={{0,4},{1,5},{2,6},{3,7},{4,0},{5,1},{6,2},{7,3},{8,12},{9,13},{10,... | collective-permute-start | bytes 4325384 | tf_op jit(solution)/shard_map/ppermute | solution.py:71
  367.0 18.0 %copy-start.1 = (f32[32,8,256]{2,1,0:T(8,128)S(1)}, f32[32,8,256]{2,1,0:T(8,128)}, u32[]{:S(2)}) copy-start(f32[32,8,256]{2,1,0:T(8,128)} %shard_map.263.summ) | copy-start | bytes 786436
  384.2 34.0 %collective-permute-start.10 = (bf16[176,2048]{1,0:T(8,128)(2,1)}, bf16[176,2048]{1,0:T(8,128)(2,1)}, u32[]{:S(2)}, u32[]{:S(2)}) collective-permute-start(bf16[176,2048]{1,0:T(8,128)(2,1)} %fusion.2), channel_id=1, source_target_pairs={{0,16},{1,17},{2,18},{3,19},{4,20},{5,21},{6,22},{7,23},{8,24},{9,... | collective-permute-start | bytes 2162696 | tf_op jit(solution)/shard_map/ppermute | solution.py:71
  394.6 32.8 %collective-permute-start.9 = (bf16[2,176,2048]{2,1,0:T(8,128)(2,1)}, bf16[2,176,2048]{2,1,0:T(8,128)(2,1)S(1)}, u32[]{:S(2)}, u32[]{:S(2)}) collective-permute-start(bf16[2,176,2048]{2,1,0:T(8,128)(2,1)} %get-tuple-element.144), channel_id=1, source_target_pairs={{0,4},{1,5},{2,6},{3,7},{4,0},{5,1},{6,2},{7,3},{8,12},{9,13},{10,... | collective-permute-start | bytes 4325384 | tf_op jit(solution)/shard_map/ppermute | solution.py:71
  553.4 7.2 %copy-start.27 = (bf16[160,2048]{1,0:T(8,128)(2,1)S(1)}, bf16[160,2048]{1,0:T(8,128)(2,1)}, u32[]{:S(2)}) copy-start(bf16[160,2048]{1,0:T(8,128)(2,1)} %tok.1) | copy-start | bytes 1966084
  553.4 7.2 %copy-start.33 = (bf16[160,2048]{1,0:T(8,128)(2,1)S(1)}, bf16[160,2048]{1,0:T(8,128)(2,1)}, u32[]{:S(2)}) copy-start(bf16[160,2048]{1,0:T(8,128)(2,1)} %get-tuple-element.153) | copy-start | bytes 1966084
  553.4 7.2 %copy-start.34 = (bf16[160,2048]{1,0:T(8,128)(2,1)S(1)}, bf16[160,2048]{1,0:T(8,128)(2,1)}, u32[]{:S(2)}) copy-start(bf16[160,2048]{1,0:T(8,128)(2,1)} %get-tuple-element.154) | copy-start | bytes 1966084
  (50 other events, 151.6 us)

commit v7 on v6

--- a/solution.py
+++ b/solution.py
@@ -687,9 +687,24 @@
             def cut(slot):
                 return total.at[pl.ds(pl.multiple_of(slot * rows, rows), rows)]
 
-            net.keep(cut(mine), out.at[mine])
-            for m in lay.tmasks[1:]:
-                waits.append(net.put(cut(t_slot(lay, lay.flip(me, m))), out.at[mine], m))
+            run = total.shape[1] // (2 * lay.Y)
+            if run % LANES:
+                net.keep(cut(mine), out.at[mine])
+                for m in lay.tmasks[1:]:
+                    waits.append(net.put(cut(t_slot(lay, lay.flip(me, m))), out.at[mine], m))
+                return
+            for block in range(2 * lay.Y):
+                zhi, y = block // lay.Y, block % lay.Y
+                start = (((zhi * 2 + mine // 2) * lay.Y + y) * 2 + mine % 2) * run
+                there = out.at[:, pl.ds(pl.multiple_of(start, LANES), run)]
+                lanes_here = pl.ds(block * run, run)
+
+                def piece(slot):
+                    return total.at[pl.ds(pl.multiple_of(slot * rows, rows), rows), lanes_here]
+
+                net.keep(piece(mine), there)
+                for m in lay.tmasks[1:]:
+                    waits.append(net.put(piece(t_slot(lay, lay.flip(me, m))), there, m))
         else:
             net.keep(total, out)
 
@@ -1341,9 +1356,10 @@
         "in": outer_rows(grads[:, : 2 * half], normed).astype(LOW).reshape(split + (r_in, width)),
     }
     out_of = {name: (part.shape[-2:], F32) for name, part in part_of.items()}
-    out_of["out"] = ((4, r_in, 2 * half), F32)
+    in_place = 2 * r_in % LANES == 0
+    out_of["out"] = ((r_in, width) if in_place else (4, r_in, 2 * half), F32)
     parts = [part_of[name] for name in PARTS]
-    scratch, copies, local_copies = [pltpu.VMEM((length, width), LOW)] * 4, 6 + 3 + n, 8
+    scratch, copies, local_copies = [pltpu.VMEM((length, width), LOW)] * 4, 18 + n, 12
     for name, part in zip(PARTS, parts):
         for _, rows in row_cuts(name, part.shape[-2]):
             shape, skip = (rows, part.shape[-1]), first_stage(name)
@@ -1378,11 +1394,10 @@
     )
     ffn_gate_grad = join(gate_kept, gate_got)
     sum_of = dict(zip(PARTS, sums))
-    out_proj_grad = (
-        sum_of["out"].reshape(2, 2, r_in, 2, Y, 2 * r_in)
-        .transpose(2, 3, 0, 4, 1, 5)
-        .reshape(r_in, width)
-    )
+    out_proj_grad = sum_of["out"]
+    if not in_place:
+        out_proj_grad = out_proj_grad.reshape(2, 2, r_in, 2, Y, 2 * r_in)
+        out_proj_grad = out_proj_grad.transpose(2, 3, 0, 4, 1, 5).reshape(r_in, width)
     owned = jnp.sum(owned, axis=0).reshape(-1)
     mixed_out = (residual + own_sum(mixed_low, (mixed_x, mixed_z))).astype(LOW)
     du_mix = own_sum(du_mix_low, (du_x, du_z))

time: 580 us -> 577 us (level)
    unnamed x150 -> x153, local copies, waits for them, and re-layouts: 17.8 us -> 18.6 us
where the time goes in v7:
time: 577 us; the launch traced here: 569 us
  Pallas kernels  381 us (66%)
  matrix products  102 us (18%)
  other arithmetic  30.5 us (5%)
  local copies, waits for them, and re-layouts  26.8 us (5%)
  waiting for transfers between devices  16.3 us (3%)
  starting transfers between devices  10.3 us (2%)
    pallas_call x5, Pallas kernels, net_call(): pl.pallas_call(body, out_shape=tuple((jax.ShapeDtypeStruct(s, d) for s, d...  326 us
    dot_general x5, matrix products, contract(): lax.dot_general(left_rows, right_rows, (((1,), (1,)), ((), ())), preferre...  36.2 us
    dot_general x7, matrix products, outer_rows(): lax.dot_general(left_rows, right_rows, (((0,), (0,)), ((), ())), preferre...  35.3 us
    pallas_call x2, Pallas kernels, small_gather(): pl.pallas_call(partial(gather_kernel, lay, masks, slot_of), out_shape=jax...  26.7 us
    unnamed x153, local copies, waits for them, and re-layouts  18.6 us
    ppermute x11, waiting for transfers between devices, send(): return lax.ppermute(value, 'dp', [(i, i ^ mask) for i in range(self.n)])  16.3 us
  transfers between devices with their start and end apart: 11, of which 6 were waited for; matrix products, arithmetic and copies ran while one was open for 14% of the time, Pallas kernels for 16%

profile of v7, /device:TPU:1, one launch (start us, length us, event | category | flops | bytes accessed | tf_op | source)
XLA Modules:
  0.0 568.6 jit_solution(7184547754906709528)
XLA Ops:
  5.9 70.7 %start.1 = (bf16[4,160,2048]{2,1,0:T(8,128)(2,1)}, bf16[40,32,2048]{2,1,0:T(8,128)(2,1)}, bf16[1,32,2048]{2,1,0:T(8,128)(2,1)}, bf16[2,2,64,512]{3,2,1,0:T(8,128...) custom-call(bf16[160,2048]{1,0:T(8,128)(2,1)} %tok.1, ...), custom_call_target="tpu_custom_call" | custom-call | flops 600000000 | tf_op jit(solution)/shard_map/start/pallas_call | solution.py:258
  86.2 5.3 fusion.35.proj
  91.6 5.2 gates.1
  101.8 12.1 %shard_map.263.summ = f32[32,8,256]{2,1,0:T(8,128)} custom-call(f32[4,8,256]{2,1,0:T(8,128)} %copy-done.19), custom_call_target="tpu_custom_call" | custom-call | flops 100000000 | tf_op jit(solution)/shard_map/pallas_call | solution.py:118
  116.0 7.5 %states.1 = (f32[2,640,128]{2,1,0:T(8,128)S(1)}, f32[2,640,128]{2,1,0:T(8,128)S(1)}, f32[2,640,128]{2,1,0:T(8,128)S(1)}, f32[2,640,128]{2,1,0:T(8,128)S(1)}, bf1...) custom-call(s32[36]{0:T(128)S(1)} %pad_add_fusion.1.ints, f32[32,8,256]{2,1,0:T(8,128)S(1)} %copy-done, ...), custom_call_target="tpu_custom_call" | custom-call | flops 70000000 | tf_op jit(solution)/shard_map/states/pallas_call | solution.py:1148
  124.0 3.0 convolution_convert_fusion.5
  127.0 4.2 collective-permute-done.3.rest_0_
  131.2 50.2 %branch.1 = (bf16[160,2048]{1,0:T(8,128)(2,1)}, bf16[160,2048]{1,0:T(8,128)(2,1)}, f32[3,160,128]{2,1,0:T(8,128)}, bf16[8,176,2048]{2,1,0:T(8,128)(2,1)}, bf16[1...) custom-call(bf16[4,160,2048]{2,1,0:T(8,128)(2,1)} %bitcast.118, f32[4,160,128]{2,1,0:T(8,128)} %bitcast.110, ...), custom_call_target="tpu_custom_call" | custom-call | flops 400000000 | tf_op jit(solution)/shard_map/branch/pallas_call | solution.py:258
  186.6 54.1 %ffn_in.1 = (bf16[4,160,2048]{2,1,0:T(8,128)(2,1)}, bf16[8,176,2048]{2,1,0:T(8,128)(2,1)}, bf16[8,176,2048]{2,1,0:T(8,128)(2,1)}, bf16[4,160,2048]{2,1,0:T(8,128)(2,1)}) custom-call(bf16[160,2048]{1,0:T(8,128)(2,1)} %multiply_convert_fusion.5.own, bf16[176,2048]{1,0:T(8,128)(2,1)} %get-tuple-element.106.up, bf16[176,2048]{1,0:T(8,128)(2,1)} %get-tuple-element.107.down, ...), custom_call_target="tpu_custom_call" | custom-call | flops 400000000 | tf_op jit(solution)/shard_map/ffn_in/pallas_call | solution.py:258
  240.7 9.6 %fusion.36 = f32[640,1408]{1,0:T(8,128)} fusion(bf16[640,2048]{1,0:T(8,128)(2,1)} %bitcast.159, bf16[1408,2048]{1,0:T(8,128)(2,1)} %bitcast.143), kind=kOutput, calls=%fused_computation.147 | convolution fusion | flops 3690987520 | bytes 11993088 | tf_op jit(solution)/shard_map/dot_general | solution.py:20
  250.4 8.8 %fusion.37 = f32[640,1408]{1,0:T(8,128)} fusion(bf16[640,2048]{1,0:T(8,128)(2,1)S(1)} %bitcast.155, bf16[1408,2048]{1,0:T(8,128)(2,1)} %bitcast.139), kind=kOutput, calls=%fused_computation.148 | convolution fusion | flops 3690987520 | bytes 11993088 | tf_op jit(solution)/shard_map/dot_general | solution.py:20
  259.2 9.5 %multiply_convert_fusion.2 = (bf16[640,1408]{1,0:T(8,128)(2,1)}, bf16[640,1408]{1,0:T(8,128)(2,1)}, bf16[640,1408]{1,0:T(8,128)(2,1)}) fusion(f32[640,1408]{1,0:T(8,128)} %fusion.37, f32[640,1408]{1,0:T(8,128)} %fusion.36, bf16[640,2048]{1,0:T(8,128)(2,1)S(1)} %bitcast.156, bf16[1408,2048]{1,0:T(8,128)(2,1)S(1)} %bitcast.149), kind=kOutput, calls=%fused_computation.9 | convolution fusion | flops 3704504320 | bytes 21004288 | tf_op jit(solution)/shard_map/dot_general | solution.py:20
  268.7 5.9 %fusion.38 = f32[640,2048]{1,0:T(8,128)S(1)} fusion(bf16[640,1408]{1,0:T(8,128)(2,1)} %get-tuple-element.125, bf16[1408,2048]{1,0:T(8,128)(2,1)S(1)} %bitcast.150), kind=kOutput, calls=%fused_computation.149 | convolution fusion | flops 3690987520 | bytes 12812288 | tf_op jit(solution)/shard_map/dot_general | solution.py:1242
  274.7 4.4 add_convert_fusion
  282.1 6.6 %convolution_convert_fusion = bf16[1408,2048]{1,0:T(8,128)(2,1)} fusion(bf16[640,1408]{1,0:T(8,128)(2,1)S(1)} %copy-done.65, bf16[640,2048]{1,0:T(8,128)(2,1)S(1)} %bitcast.160), kind=kOutput, calls=%fused_computation | convolution fusion | flops 3693871104 | bytes 10190848 | tf_op jit(solution)/shard_map/dot_general | solution.py:26
  288.7 6.5 %convolution_convert_fusion.1 = bf16[1408,2048]{1,0:T(8,128)(2,1)} fusion(bf16[640,1408]{1,0:T(8,128)(2,1)S(1)} %copy-done.62, bf16[640,2048]{1,0:T(8,128)(2,1)S(1)} %bitcast.157), kind=kOutput, calls=%fused_computation.1 | convolution fusion | flops 3693871104 | bytes 10190848 | tf_op jit(solution)/shard_map/dot_general | solution.py:26
  295.2 6.5 %convolution_convert_fusion.2 = bf16[1408,2048]{1,0:T(8,128)(2,1)} fusion(bf16[640,1408]{1,0:T(8,128)(2,1)S(1)} %copy-done.64, bf16[640,2048]{1,0:T(8,128)(2,1)S(1)} %bitcast.158), kind=kOutput, calls=%fused_computation.2 | convolution fusion | flops 3693871104 | bytes 10190848 | tf_op jit(solution)/shard_map/dot_general | solution.py:26
  301.8 5.8 %convolution_convert_fusion.4 = bf16[640,2048]{1,0:T(8,128)(2,1)} fusion(bf16[640,1408]{1,0:T(8,128)(2,1)S(1)} %copy-done.65, bf16[1408,2048]{1,0:T(8,128)(2,1)S(1)} %bitcast.146), kind=kOutput, calls=%fused_computation.15 | convolution fusion | flops 3692298240 | bytes 10190848 | tf_op jit(solution)/shard_map/dot_general | solution.py:1268
  307.5 3.1 collective-permute-done.7
  311.3 2.9 fusion.27
  317.1 26.3 %grad_in.1 = (bf16[4,160,2048]{2,1,0:T(8,128)(2,1)}, f32[4,160,128]{2,1,0:T(8,128)}, bf16[2,176,2048]{2,1,0:T(8,128)(2,1)}, bf16[2,176,2048]{2,1,0:T(8,128)(2,1)...) custom-call(bf16[160,2048]{1,0:T(8,128)(2,1)} %copy-done.29, ...), custom_call_target="tpu_custom_call" | custom-call | flops 270000000 | tf_op jit(solution)/shard_map/grad_in/pallas_call | solution.py:258
  346.0 5.1 fusion.39.grad_mid
  351.1 7.2 %back_gates.1 = (f32[2,640,128]{2,1,0:T(8,128)S(1)}, f32[2,640,128]{2,1,0:T(8,128)S(1)}, bf16[640,512]{1,0:T(8,128)(2,1)S(1)}, bf16[640,512]{1,0:T(8,128)(2,1)S(...) custom-call(f32[640,512]{1,0:T(8,128)} %fusion.39.grad_mid, f32[2,640,128]{2,1,0:T(8,128)S(1)} %copy-done.12, ...), custom_call_target="tpu_custom_call" | custom-call | flops 70000000 | tf_op jit(solution)/shard_map/back_gates/pallas_call | solution.py:1302
  361.7 3.7 convolution_convert_fusion.8
  367.0 14.6 %shard_map.264.back = f32[32,8,256]{2,1,0:T(8,128)} custom-call(f32[4,8,256]{2,1,0:T(8,128)} %copy-done.20), custom_call_target="tpu_custom_call" | custom-call | flops 100000000 | tf_op jit(solution)/shard_map/pallas_call | solution.py:118
  386.0 8.5 %adjoints.1 = (bf16[640,1280]{1,0:T(8,128)(2,1)}, f32[8,256]{1,0:T(8,128)S(1)}, f32[8,256]{1,0:T(8,128)S(1)}) custom-call(s32[36]{0:T(128)S(1)} %pad_add_fusion.1.ints, f32[32,8,256]{2,1,0:T(8,128)S(1)} %copy-done.1, f32[32,8,256]{2,1,0:T(8,128)S(1)} %copy-done.17, f32[2,640,128]{2,1,0:T(8,128)S(1)} %copy-done.5, f32[2,640,128]{2,1,0:T(8,128)S(1)} %copy-done.7, ...), custom_call_target="tpu_custom_call" | custom-call | flops 70000000 | tf_op jit(solution)/shard_map/adjoints/pallas_call | solution.py:1312
  396.1 8.9 %multiply_reduce_fusion = (f32[2048]{0:T(1024)S(1)}, bf16[640,2048]{1,0:T(8,128)(2,1)S(1)}, bf16[640,2048]{1,0:T(8,128)(2,1)}) fusion(bf16[4,160,2048]{2,1,0:T(8,128)(2,1)} %get-tuple-element.88, f32[640]{0:T(1024)S(1)} %rsqrt.40, f32[2048]{0:T(1024)S(1)} %mul.322, bf16[640,1280]{1,0:T(8,128)(2,1)} %get-tuple-element.140, bf16[1280,2048]{1,0:T(8,128)(2,1)} %bitcast.151), kind=kOutput, calls=%fused_computation.4 | convolution fusion | flops 3365926912 | bytes 14764544 | tf_op jit(solution)/shard_map/dot_general | solution.py:1320
  405.0 4.8 convolution_convert_fusion.6
  410.9 4.0 convolution_convert_fusion.9
  414.8 3.2 convolution_convert_fusion.7
  421.0 6.4 %collective-permute-done.9.refs_6_ = bf16[2,176,2048]{2,1,0:T(8,128)(2,1)S(1)} collective-permute-done((bf16[2,176,2048]{2,1,0:T(8,128)(2,1)}, bf16[2,176,2048]{2,1,0:T(8,128)(2,1)S(1)}, u32[]{:S(2)}, u32[]{:S(2)}) %collective-permute-start.9) | collective-permute-done | bytes 1441824 | tf_op jit(solution)/shard_map/ppermute | solution.py:71
  428.5 124.9 %reduce.6 = (f32[176,2048]{1,0:T(8,128)}, f32[32,2048]{1,0:T(8,128)}, f32[64,2048]{1,0:T(8,128)}, f32[176,2048]{1,0:T(8,128)}, f32[64,2048]{1,0:T(8,128)}, /*ind...) custom-call(bf16[2,176,2048]{2,1,0:T(8,128)(2,1)} %get-tuple-element, ...), custom_call_target="tpu_custom_call" | custom-call | flops 1200000000 | tf_op jit(solution)/shard_map/reduce/pallas_call | solution.py:258
  (253 shorter events, 67.3 us)
Async XLA Ops:
  76.6 6.1 %copy-start.61 = (s32[32]{0:T(128)S(1)}, s32[32]{0:T(128)}, u32[]{:S(2)}) copy-start(s32[32]{0:T(128)} %param.19) | copy-start | bytes 388
  76.6 6.4 %copy-start.60 = (s32[5]{0:T(128)S(1)}, s32[5]{0:T(128)}, u32[]{:S(2)}) copy-start(s32[5]{0:T(128)} %param.18) | copy-start | bytes 64
  76.6 7.1 %copy-start.28 = (bf16[4,160,2048]{2,1,0:T(8,128)(2,1)S(1)}, bf16[4,160,2048]{2,1,0:T(8,128)(2,1)}, u32[]{:S(2)}) copy-start(bf16[4,160,2048]{2,1,0:T(8,128)(2,1)} %get-tuple-element.88) | copy-start | bytes 7864324
  76.6 25.2 %collective-permute-start.2 = (bf16[160,2048]{1,0:T(8,128)(2,1)}, bf16[160,2048]{1,0:T(8,128)(2,1)}, u32[]{:S(2)}, u32[]{:S(2)}) collective-permute-start(bf16[160,2048]{1,0:T(8,128)(2,1)} %rest_2_.1), channel_id=1, source_target_pairs={{0,8},{1,9},{2,10},{3,11},{4,12},{5,13},{6,14},{7,15},{8,0},{9,1},... | collective-permute-start | bytes 1966088 | tf_op jit(solution)/shard_map/ppermute | solution.py:71
  76.7 25.1 %collective-permute-start.1 = (bf16[160,2048]{1,0:T(8,128)(2,1)}, bf16[160,2048]{1,0:T(8,128)(2,1)}, u32[]{:S(2)}, u32[]{:S(2)}) collective-permute-start(bf16[160,2048]{1,0:T(8,128)(2,1)} %rest_2_.1), channel_id=1, source_target_pairs={{0,2},{1,3},{2,0},{3,1},{4,6},{5,7},{6,4},{7,5},{8,10},{9,11},{10,... | collective-permute-start | bytes 1966088 | tf_op jit(solution)/shard_map/ppermute | solution.py:71
  77.0 22.8 %collective-permute-start = (bf16[96,2048]{1,0:T(8,128)(2,1)}, bf16[96,2048]{1,0:T(8,128)(2,1)S(1)}, u32[]{:S(2)}, u32[]{:S(2)}) collective-permute-start(bf16[96,2048]{1,0:T(8,128)(2,1)} %get-tuple-element.92), channel_id=1, source_target_pairs={{0,16},{1,17},{2,18},{3,19},{4,20},{5,21},{6,22},{7,23},{8,24},{9,... | collective-permute-start | bytes 1179656 | tf_op jit(solution)/shard_map/ppermute | solution.py:71
  91.5 22.4 %copy-start.59 = (bf16[80,2048]{1,0:T(8,128)(2,1)S(1)}, bf16[80,2048]{1,0:T(8,128)(2,1)}, u32[]{:S(2)}) copy-start(bf16[80,2048]{1,0:T(8,128)(2,1)} %get-tuple-element.103) | copy-start | bytes 983044
  99.8 23.8 %copy-start.46 = (bf16[96,2048]{1,0:T(8,128)(2,1)}, bf16[96,2048]{1,0:T(8,128)(2,1)S(1)}, u32[]{:S(2)}) copy-start(bf16[96,2048]{1,0:T(8,128)(2,1)S(1)} %collective-permute-done.rest_1_) | copy-start | bytes 1179652
  113.9 17.3 %collective-permute-start.3 = (bf16[80,2048]{1,0:T(8,128)(2,1)S(1)}, bf16[80,2048]{1,0:T(8,128)(2,1)S(1)}, u32[]{:S(2)}, u32[]{:S(2)}) collective-permute-start(bf16[80,2048]{1,0:T(8,128)(2,1)S(1)} %copy-done.59), channel_id=1, source_target_pairs={{0,16},{1,17},{2,18},{3,19},{4,20},{5,21},{6,22},{7,23},{8,24},{9,... | collective-permute-start | bytes 983048 | tf_op jit(solution)/shard_map/ppermute | solution.py:71
  116.0 7.9 %copy-start.58 = (bf16[2,2,2,2,2,64,512]{6,5,4,3,2,1,0:T(8,128)(2,1)S(1)}, bf16[2,2,2,2,2,64,512]{6,5,4,3,2,1,0:T(8,128)(2,1)}, u32[]{:S(2)}) copy-start(bf16[2,2,2,2,2,64,512]{6,5,4,3,2,1,0:T(8,128)(2,1)} %get-tuple-element.101) | copy-start | bytes 6291460
  123.6 62.9 %collective-permute-start.4 = (bf16[160,2048]{1,0:T(8,128)(2,1)}, bf16[160,2048]{1,0:T(8,128)(2,1)}, u32[]{:S(2)}, u32[]{:S(2)}) collective-permute-start(bf16[160,2048]{1,0:T(8,128)(2,1)} %collective-permute-done.2.rest_4_), channel_id=1, source_target_pairs={{0,2},{1,3},{2,0},{3,1},{4,6},{5,7},{6,4},{7,5},{8,10},{9,11},{10,... | collective-permute-start | bytes 1966088 | tf_op jit(solution)/shard_map/ppermute | solution.py:71
  131.2 50.2 %copy-start.47 = (bf16[80,2048]{1,0:T(8,128)(2,1)}, bf16[80,2048]{1,0:T(8,128)(2,1)S(1)}, u32[]{:S(2)}) copy-start(bf16[80,2048]{1,0:T(8,128)(2,1)S(1)} %collective-permute-done.3.rest_0_) | copy-start | bytes 983044
  131.2 51.3 %copy-start.26 = (bf16[160,2048]{1,0:T(8,128)(2,1)S(1)}, bf16[160,2048]{1,0:T(8,128)(2,1)}, u32[]{:S(2)}) copy-start(bf16[160,2048]{1,0:T(8,128)(2,1)} %tok.1) | copy-start | bytes 1966084
  240.7 9.7 %copy-start.56 = (bf16[4,160,2048]{2,1,0:T(8,128)(2,1)S(1)}, bf16[4,160,2048]{2,1,0:T(8,128)(2,1)}, u32[]{:S(2)}) copy-start(bf16[4,160,2048]{2,1,0:T(8,128)(2,1)} %get-tuple-element.118) | copy-start | bytes 7864324
  240.7 18.5 %slice-start.4 = ((s8[5767168]{0:T(1024)(128)(4,1)}), s8[4194304]{0:T(1024)(128)(4,1)S(1)}, s32[]{:S(2)}) async-start(s8[5767168]{0:T(1024)(128)(4,1)} %bitcast.147), calls=%async_computation.4 | async-start | bytes 8388608
  250.4 8.8 %slice-start.5 = ((s8[5767168]{0:T(1024)(128)(4,1)}), s8[1572864]{0:T(1024)(128)(4,1)S(1)}, s32[]{:S(2)}) async-start(s8[5767168]{0:T(1024)(128)(4,1)} %bitcast.147), calls=%async_computation.5 | async-start | bytes 3145728
  250.4 24.3 %slice-start = ((s8[5767168]{0:T(1024)(128)(4,1)}), s8[4194304]{0:T(1024)(128)(4,1)S(1)}, s32[]{:S(2)}) async-start(s8[5767168]{0:T(1024)(128)(4,1)} %bitcast.140), calls=%async_computation | async-start | bytes 8388608
  259.2 15.4 %slice-start.1 = ((s8[5767168]{0:T(1024)(128)(4,1)}), s8[1572864]{0:T(1024)(128)(4,1)S(1)}, s32[]{:S(2)}) async-start(s8[5767168]{0:T(1024)(128)(4,1)} %bitcast.140), calls=%async_computation.1 | async-start | bytes 3145728
  274.7 7.4 %copy-start.65 = (bf16[640,1408]{1,0:T(8,128)(2,1)S(1)}, bf16[640,1408]{1,0:T(8,128)(2,1)}, u32[]{:S(2)}) copy-start(bf16[640,1408]{1,0:T(8,128)(2,1)} %get-tuple-element.122) | copy-start | bytes 5406724
  279.3 22.4 %collective-permute-start.5 = (bf16[160,2048]{1,0:T(8,128)(2,1)S(1)}, bf16[160,2048]{1,0:T(8,128)(2,1)S(1)}, u32[]{:S(2)}, u32[]{:S(2)}) collective-permute-start(bf16[160,2048]{1,0:T(8,128)(2,1)S(1)} %get-tuple-element.177), channel_id=1, source_target_pairs={{0,2},{1,3},{2,0},{3,1},{4,6},{5,7},{6,4},{7,5},{8,10},{9,11},{10,... | collective-permute-start | bytes 1966088 | tf_op jit(solution)/shard_map/ppermute | solution.py:71
  279.8 27.8 %collective-permute-start.6 = (bf16[160,2048]{1,0:T(8,128)(2,1)S(1)}, bf16[160,2048]{1,0:T(8,128)(2,1)S(1)}, u32[]{:S(2)}, u32[]{:S(2)}) collective-permute-start(bf16[160,2048]{1,0:T(8,128)(2,1)S(1)} %get-tuple-element.179), channel_id=1, source_target_pairs={{0,8},{1,9},{2,10},{3,11},{4,12},{5,13},{6,14},{7,15},{8,0},{9,1},... | collective-permute-start | bytes 1966088 | tf_op jit(solution)/shard_map/ppermute | solution.py:71
  281.1 29.5 %collective-permute-start.7 = (bf16[160,2048]{1,0:T(8,128)(2,1)S(1)}, bf16[160,2048]{1,0:T(8,128)(2,1)S(1)}, u32[]{:S(2)}, u32[]{:S(2)}) collective-permute-start(bf16[160,2048]{1,0:T(8,128)(2,1)S(1)} %get-tuple-element.178), channel_id=1, source_target_pairs={{0,10},{1,11},{2,8},{3,9},{4,14},{5,15},{6,12},{7,13},{8,2},{9,3},... | collective-permute-start | bytes 1966088 | tf_op jit(solution)/shard_map/ppermute | solution.py:71
  282.1 6.6 %copy-start.62 = (bf16[640,1408]{1,0:T(8,128)(2,1)S(1)}, bf16[640,1408]{1,0:T(8,128)(2,1)}, u32[]{:S(2)}) copy-start(bf16[640,1408]{1,0:T(8,128)(2,1)} %get-tuple-element.125) | copy-start | bytes 5406724
  288.6 6.5 %copy-start.64 = (bf16[640,1408]{1,0:T(8,128)(2,1)S(1)}, bf16[640,1408]{1,0:T(8,128)(2,1)}, u32[]{:S(2)}) copy-start(bf16[640,1408]{1,0:T(8,128)(2,1)} %get-tuple-element.124) | copy-start | bytes 5406724
  288.6 13.1 %slice-start.2 = ((s8[5767168]{0:T(1024)(128)(4,1)}), s8[4194304]{0:T(1024)(128)(4,1)S(1)}, s32[]{:S(2)}) async-start(s8[5767168]{0:T(1024)(128)(4,1)} %bitcast.144), calls=%async_computation.2 | async-start | bytes 8388608
  295.2 6.6 %slice-start.3 = ((s8[5767168]{0:T(1024)(128)(4,1)}), s8[1572864]{0:T(1024)(128)(4,1)S(1)}, s32[]{:S(2)}) async-start(s8[5767168]{0:T(1024)(128)(4,1)} %bitcast.144), calls=%async_computation.3 | async-start | bytes 3145728
  301.7 8.9 %copy-start.22 = (f32[160,2048]{1,0:T(8,128)S(1)}, f32[160,2048]{1,0:T(8,128)}, u32[]{:S(2)}) copy-start(f32[160,2048]{1,0:T(8,128)} %copy-done.21) | copy-start | bytes 3932164
  343.4 38.2 %collective-permute-start.8 = (bf16[352,2048]{1,0:T(8,128)(2,1)}, bf16[352,2048]{1,0:T(8,128)(2,1)}, u32[]{:S(2)}, u32[]{:S(2)}) collective-permute-start(bf16[352,2048]{1,0:T(8,128)(2,1)} %bitcast.163), channel_id=1, source_target_pairs={{0,4},{1,5},{2,6},{3,7},{4,0},{5,1},{6,2},{7,3},{8,12},{9,13},{10,... | collective-permute-start | bytes 4325384 | tf_op jit(solution)/shard_map/ppermute | solution.py:71
  367.0 18.1 %copy-start.1 = (f32[32,8,256]{2,1,0:T(8,128)S(1)}, f32[32,8,256]{2,1,0:T(8,128)}, u32[]{:S(2)}) copy-start(f32[32,8,256]{2,1,0:T(8,128)} %shard_map.263.summ) | copy-start | bytes 786436
  384.2 34.0 %collective-permute-start.10 = (bf16[176,2048]{1,0:T(8,128)(2,1)}, bf16[176,2048]{1,0:T(8,128)(2,1)}, u32[]{:S(2)}, u32[]{:S(2)}) collective-permute-start(bf16[176,2048]{1,0:T(8,128)(2,1)} %fusion.2), channel_id=1, source_target_pairs={{0,16},{1,17},{2,18},{3,19},{4,20},{5,21},{6,22},{7,23},{8,24},{9,... | collective-permute-start | bytes 2162696 | tf_op jit(solution)/shard_map/ppermute | solution.py:71
  394.6 32.8 %collective-permute-start.9 = (bf16[2,176,2048]{2,1,0:T(8,128)(2,1)}, bf16[2,176,2048]{2,1,0:T(8,128)(2,1)S(1)}, u32[]{:S(2)}, u32[]{:S(2)}) collective-permute-start(bf16[2,176,2048]{2,1,0:T(8,128)(2,1)} %get-tuple-element.144), channel_id=1, source_target_pairs={{0,4},{1,5},{2,6},{3,7},{4,0},{5,1},{6,2},{7,3},{8,12},{9,13},{10,... | collective-permute-start | bytes 4325384 | tf_op jit(solution)/shard_map/ppermute | solution.py:71
  428.5 127.2 %copy-start.27 = (bf16[160,2048]{1,0:T(8,128)(2,1)S(1)}, bf16[160,2048]{1,0:T(8,128)(2,1)}, u32[]{:S(2)}) copy-start(bf16[160,2048]{1,0:T(8,128)(2,1)} %tok.1) | copy-start | bytes 1966084
  (51 other events, 152.7 us)
